TPU v7x, 256 devices: a whole 4x4x8 slice. The times are simulated.
256 devices in a mesh: gx: 16 (over x_lo, y, core), gy: 16 (over x_hi, z).
Axes of the slice: x: 4 (x_hi: 2, x_lo: 2; x = x_hi * 2 + x_lo), y: 4, z: 8, core: 2. Of those that a mesh axis runs over, the one named last changes fastest.
Arguments:
- concentration: float32 [512, 512, 256], P('gx', 'gy'), may hold values from 0 to 1
- order_field: float32 [512, 512, 256], P('gx', 'gy'), may hold values from 0 to 1
- phase_labels: int32 [512, 512, 256], P('gx', 'gy'), may hold values from 0 to 2
- displacement: float32 [3, 256, 128, 256], P(None, 'gx', 'gy'), may hold values from -4 to 4
- body_load: float32 [3, 256, 128, 256], P(None, 'gx', 'gy'), may hold values from -6 to 6
Outputs:
- concentration_out: float32 [512, 512, 256], P('gx', 'gy')
- order_out: float32 [512, 512, 256], P('gx', 'gy')
- displacement_out: float32 [3, 256, 128, 256], P(None, 'gx', 'gy')
- energy_tiles: float32 [256, 256, 128], P('gx', 'gy')
All inputs are finite; a program needn't handle non-finite values.
Results may differ from a plain program's by a relative error of at most 0.0003.
Values sent between devices are 32-bit elements; how exact they have to be, the bound alone decides.
A program may use at most 192 MiB of HBM per device.

v0:
```python
import jax
import jax.numpy as jnp
from jax import lax
from jax.sharding import PartitionSpec as P

STEPS = 4


rate_conc = 0.15
rate_order = 0.15
well_height = 1.0
drive_coupling = 0.5
spring_term = 0.2
first_weight = 0.5956
second_weight = 2.695


def padded_2(block, sides, width):
    for axis, dim in sides:
        count = lax.axis_size(axis)
        forward = [(i, i + 1) for i in range(count - 1)]
        backward = [(target, source) for source, target in forward]
        low = lax.ppermute(
            lax.slice_in_dim(block, block.shape[dim] - width, None, axis=dim), axis, forward
        )
        high = lax.ppermute(lax.slice_in_dim(block, 0, width, axis=dim), axis, backward)
        block = jnp.concatenate([low, block, high], axis=dim)
    return block


def fine_laplace(padded):
    zpad = jnp.pad(padded, ((0, 0), (0, 0), (1, 1)))
    center = zpad[1:-1, 1:-1, 1:-1]
    total = zpad[2:, 1:-1, 1:-1] + zpad[:-2, 1:-1, 1:-1]
    total = total + zpad[1:-1, 2:, 1:-1] + zpad[1:-1, :-2, 1:-1]
    total = total + zpad[1:-1, 1:-1, 2:] + zpad[1:-1, 1:-1, :-2]
    return total - 6.0 * center


def advance(conc_pad, order_pad, mobility):
    chem = conc_pad - order_pad * order_pad * (3.0 - 2.0 * order_pad)
    conc_in = conc_pad[1:-1, 1:-1]
    order_in = order_pad[1:-1, 1:-1]
    chem_in = chem[1:-1, 1:-1]
    conc_new = conc_in + rate_conc * fine_laplace(chem)
    dh_term = 6.0 * order_in * (1.0 - order_in)
    dg_term = 2.0 * order_in * (1.0 - order_in) * (1.0 - 2.0 * order_in)
    order_new = order_in + mobility * (
        rate_order * fine_laplace(order_pad)
        - well_height * dg_term
        + drive_coupling * chem_in * dh_term
    )
    return (conc_new, order_new)


def mobility_of(labels):
    return (0.5 * (labels == 0) + 1.0 * (labels == 1) + 0.25 * (labels == 2)).astype(jnp.float32)


def restrict(order_out):
    sx, sy, sz = order_out.shape
    sq = (order_out * order_out).reshape(sx // 2, 2, sy // 2, 2, sz // 2, 2)
    return 0.1 + 0.125 * jnp.sum(sq, axis=(1, 3, 5))


def shifted(padded):
    return [
        padded[..., 2:, 1:-1, 1:-1],
        padded[..., :-2, 1:-1, 1:-1],
        padded[..., 1:-1, 2:, 1:-1],
        padded[..., 1:-1, :-2, 1:-1],
        padded[..., 1:-1, 1:-1, 2:],
        padded[..., 1:-1, 1:-1, :-2],
    ]


def face_terms(stiff_pad):
    center = stiff_pad[1:-1, 1:-1, 1:-1]
    faces = [0.5 * (center + other) for other in shifted(stiff_pad)]
    diag = faces[0] + faces[1] + faces[2] + faces[3] + faces[4] + faces[5] + spring_term * center
    return (faces, diag)


def apply_op(disp_pad, faces, diag):
    center = disp_pad[:, 1:-1, 1:-1, 1:-1]
    result = diag * center
    for face, other in zip(faces, shifted(disp_pad)):
        result = result - face * other
    return result


def strain_energy(disp_pad, faces):
    center = disp_pad[:, 1:-1, 1:-1, 1:-1]
    total = jnp.zeros(center.shape, jnp.float32)
    for face, other in zip(faces, shifted(disp_pad)):
        diff = center - other
        total = total + face * diff * diff
    return 0.25 * jnp.sum(total, axis=0)


def disp_padded(disp):
    rimmed = padded_2(disp, (("gx", 1), ("gy", 2)), 1)
    return jnp.pad(rimmed, ((0, 0), (0, 0), (0, 0), (1, 1)))


def on_device(concentration, order_field, phase_labels, displacement, body_load):
    mobility = mobility_of(phase_labels)
    conc, order = (concentration, order_field)
    for step in range(STEPS):
        both = padded_2(jnp.stack([conc, order]), (("gx", 1), ("gy", 2)), 1)
        conc, order = advance(both[0], both[1], mobility)
    coarse = jnp.transpose(restrict(order), (0, 2, 1))
    stiff = lax.all_to_all(coarse, "gy", split_axis=1, concat_axis=2, tiled=True)
    stiff_pad = padded_2(stiff, (("gx", 0), ("gy", 1)), 1)
    faces, diag = face_terms(jnp.pad(stiff_pad, ((0, 0), (0, 0), (1, 1))))
    disp = displacement
    for weight in (first_weight, second_weight):
        disp = disp + weight * (body_load - apply_op(disp_padded(disp), faces, diag)) / diag
    energy = strain_energy(disp_padded(disp), faces)
    tiles = lax.all_to_all(energy, "gy", split_axis=2, concat_axis=1, tiled=True)
    return (conc, order, disp, jnp.transpose(tiles, (0, 2, 1)))


def solution(mesh):
    return jax.shard_map(
        on_device,
        mesh=mesh,
        in_specs=(
            P("gx", "gy", None),
            P("gx", "gy", None),
            P("gx", "gy", None),
            P(None, "gx", "gy", None),
            P(None, "gx", "gy", None),
        ),
        out_specs=(
            P("gx", "gy", None),
            P("gx", "gy", None),
            P(None, "gx", "gy", None),
            P("gx", "gy", None),
        ),
        check_vma=False,
    )
```

profile of v0, /device:TPU:2, one launch (start us, length us, event | category | flops | bytes accessed | tf_op | source)
XLA Modules:
  0.0 317.2 jit_solution(5278059448493687318)
XLA Ops:
  1.6 1.9 collective-permute-start
  3.5 5.8 %collective-permute-start.1 = (f32[2,1,32,256]{3,2,1,0:T(8,128)S(1)}, f32[2,1,32,256]{3,2,1,0:T(8,128)S(1)}, u32[]{:S(2)}, u32[]{:S(2)}) collective-permute-start(f32[2,1,32,256]{3,2,1,0:T(8,128)S(1)} %get-tuple-element.48), channel_id=1, source_target_pairs={{16,0},{32,16},{48,32},{64,48},{80,64},{96,80},{112,96},{128,112},... | collective-permute-start | bytes 196616 | tf_op jit(solution)/shard_map/ppermute | solution.py:26
  9.3 1.9 collective-permute-done.1
  11.3 3.8 %collective-permute-start.2 = (f32[2,34,1,256]{3,2,1,0:T(1,128)S(1)}, f32[2,34,1,256]{3,2,1,0:T(1,128)S(1)}, u32[]{:S(2)}, u32[]{:S(2)}) collective-permute-start(f32[2,34,1,256]{3,2,1,0:T(1,128)S(1)} %get-tuple-element.39), channel_id=1, source_target_pairs={{0,1},{1,2},{2,3},{3,4},{4,5},{5,6},{6,7},{7,8},{8,9},{9,10},{10,1... | collective-permute-start | bytes 208904 | tf_op jit(solution)/shard_map/ppermute | solution.py:23
  15.1 1.3 collective-permute-start.3
  17.1 4.3 %collective-permute-done.3 = f32[2,34,1,256]{3,2,1,0:T(1,128)S(1)} collective-permute-done((f32[2,34,1,256]{3,2,1,0:T(1,128)S(1)}, f32[2,34,1,256]{3,2,1,0:T(1,128)S(1)}, u32[]{:S(2)}, u32[]{:S(2)}) %collective-permute-start.3) | collective-permute-done | bytes 69664 | tf_op jit(solution)/shard_map/ppermute | solution.py:26
  23.2 3.1 fusion.6
  26.3 1.9 collective-permute-start.4
  28.2 5.8 %collective-permute-start.5 = (f32[2,1,32,256]{3,2,1,0:T(8,128)S(1)}, f32[2,1,32,256]{3,2,1,0:T(8,128)S(1)}, u32[]{:S(2)}, u32[]{:S(2)}) collective-permute-start(f32[2,1,32,256]{3,2,1,0:T(8,128)S(1)} %get-tuple-element.46), channel_id=1, source_target_pairs={{16,0},{32,16},{48,32},{64,48},{80,64},{96,80},{112,96},{128,112},... | collective-permute-start | bytes 196616 | tf_op jit(solution)/shard_map/ppermute | solution.py:26
  34.0 1.9 collective-permute-done.5
  36.0 3.8 %collective-permute-start.6 = (f32[2,34,1,256]{3,2,1,0:T(1,128)S(1)}, f32[2,34,1,256]{3,2,1,0:T(1,128)S(1)}, u32[]{:S(2)}, u32[]{:S(2)}) collective-permute-start(f32[2,34,1,256]{3,2,1,0:T(1,128)S(1)} %get-tuple-element.37), channel_id=1, source_target_pairs={{0,1},{1,2},{2,3},{3,4},{4,5},{5,6},{6,7},{7,8},{8,9},{9,10},{10,1... | collective-permute-start | bytes 208904 | tf_op jit(solution)/shard_map/ppermute | solution.py:23
  39.8 1.3 collective-permute-start.7
  41.7 5.3 %collective-permute-done.7 = f32[2,34,1,256]{3,2,1,0:T(1,128)S(1)} collective-permute-done((f32[2,34,1,256]{3,2,1,0:T(1,128)S(1)}, f32[2,34,1,256]{3,2,1,0:T(1,128)S(1)}, u32[]{:S(2)}, u32[]{:S(2)}) %collective-permute-start.7) | collective-permute-done | bytes 69664 | tf_op jit(solution)/shard_map/ppermute | solution.py:26
  47.9 3.1 fusion.21
  51.0 1.9 collective-permute-start.8
  52.9 5.8 %collective-permute-start.9 = (f32[2,1,32,256]{3,2,1,0:T(8,128)S(1)}, f32[2,1,32,256]{3,2,1,0:T(8,128)S(1)}, u32[]{:S(2)}, u32[]{:S(2)}) collective-permute-start(f32[2,1,32,256]{3,2,1,0:T(8,128)S(1)} %get-tuple-element.44), channel_id=1, source_target_pairs={{16,0},{32,16},{48,32},{64,48},{80,64},{96,80},{112,96},{128,112},... | collective-permute-start | bytes 196616 | tf_op jit(solution)/shard_map/ppermute | solution.py:26
  58.7 1.9 collective-permute-done.9
  60.7 5.1 %collective-permute-start.10 = (f32[2,34,1,256]{3,2,1,0:T(1,128)S(1)}, f32[2,34,1,256]{3,2,1,0:T(1,128)S(1)}, u32[]{:S(2)}, u32[]{:S(2)}) collective-permute-start(f32[2,34,1,256]{3,2,1,0:T(1,128)S(1)} %get-tuple-element.35), channel_id=1, source_target_pairs={{0,1},{1,2},{2,3},{3,4},{4,5},{5,6},{6,7},{7,8},{8,9},{9,10},{10,1... | collective-permute-start | bytes 208904 | tf_op jit(solution)/shard_map/ppermute | solution.py:23
  67.7 4.3 %collective-permute-done.11 = f32[2,34,1,256]{3,2,1,0:T(1,128)S(1)} collective-permute-done((f32[2,34,1,256]{3,2,1,0:T(1,128)S(1)}, f32[2,34,1,256]{3,2,1,0:T(1,128)S(1)}, u32[]{:S(2)}, u32[]{:S(2)}) %collective-permute-start.11) | collective-permute-done | bytes 69664 | tf_op jit(solution)/shard_map/ppermute | solution.py:26
  72.9 3.1 fusion.36
  76.0 2.1 collective-permute-start.12
  78.1 5.8 %collective-permute-start.13 = (f32[2,1,32,256]{3,2,1,0:T(8,128)S(1)}, f32[2,1,32,256]{3,2,1,0:T(8,128)S(1)}, u32[]{:S(2)}, u32[]{:S(2)}) collective-permute-start(f32[2,1,32,256]{3,2,1,0:T(8,128)S(1)} %get-tuple-element.42), channel_id=1, source_target_pairs={{16,0},{32,16},{48,32},{64,48},{80,64},{96,80},{112,96},{128,112},... | collective-permute-start | bytes 196616 | tf_op jit(solution)/shard_map/ppermute | solution.py:26
  83.8 1.9 collective-permute-done.13
  85.8 3.9 %collective-permute-start.14 = (f32[2,34,1,256]{3,2,1,0:T(1,128)S(1)}, f32[2,34,1,256]{3,2,1,0:T(1,128)S(1)}, u32[]{:S(2)}, u32[]{:S(2)}) collective-permute-start(f32[2,34,1,256]{3,2,1,0:T(1,128)S(1)} %get-tuple-element.33), channel_id=1, source_target_pairs={{0,1},{1,2},{2,3},{3,4},{4,5},{5,6},{6,7},{7,8},{8,9},{9,10},{10,1... | collective-permute-start | bytes 208904 | tf_op jit(solution)/shard_map/ppermute | solution.py:23
  91.1 1.9 collective-permute-start.21
  93.0 5.9 %collective-permute-start.20 = (f32[3,1,8,256]{3,2,1,0:T(8,128)S(1)}, f32[3,1,8,256]{3,2,1,0:T(8,128)S(1)}, u32[]{:S(2)}, u32[]{:S(2)}) collective-permute-start(f32[3,1,8,256]{3,2,1,0:T(8,128)S(1)} %get-tuple-element.70), channel_id=1, source_target_pairs={{16,0},{32,16},{48,32},{64,48},{80,64},{96,80},{112,96},{128,112},... | collective-permute-start | bytes 73736 | tf_op jit(solution)/shard_map/ppermute | solution.py:26
  99.8 4.1 %fusion.110 = (f32[32,32,256]{2,1,0:T(8,128)S(1)}, f32[32,32,256]{2,1,0:T(8,128)}, f32[32,32,256]{2,1,0:T(8,128)}) fusion(f32[34,34,256]{2,1,0:T(8,128)S(1)} %multiply_subtract_fusion, f32[34,34,256]{2,1,0:T(8,128)S(1)} %get-tuple-element.25, s32[32,32,256]{2,1,0:T(8,128)S(1)} %copy-done, f32[34,34,256]{2,1,0:T(8,128)S(1)} %get-tuple-element.26), kind=kLoop, calls=%fused_computation.259 | loop fusion | flops 9961472 | bytes 18513920 | tf_op jit(solution)/shard_map/mul | solution.py:62
  104.0 68.4 %reshape.20 = f32[16,2,16,2,128,2]{5,4,3,2,1,0:T(8,128)} reshape(f32[32,32,256]{2,1,0:T(8,128)S(1)} %get-tuple-element.23) | data formatting | bytes 2097152 | tf_op jit(solution)/shard_map/reshape | solution.py:62
  172.3 20.8 %reduce_sum.18 = f32[16,16,128]{2,1,0:T(8,128)S(1)} reduce(f32[16,2,16,2,128,2]{5,4,3,2,1,0:T(8,128)} %reshape.20, f32[]{:T(128)} %constant.18.clone.1), dimensions={1,3,5}, to_apply=%region_0.1 | reduce | flops 229376 | bytes 1179652 | tf_op jit(solution)/shard_map/reduce_sum | solution.py:63
  194.7 11.6 %all-to-all-start = ((f32[16,1,2048]{2,1,0:T(1,128)}), f32[16,1,2048]{2,1,0:T(1,128)S(1)}, u32[]{:S(2)}, u32[]{:S(2)}) async-start(f32[16,1,2048]{2,1,0:T(1,128)} %reshape.21), calls=%async_computation | async-start | bytes 262144 | tf_op jit(solution)/shard_map/all_to_all | solution.py:113
  206.4 10.0 %all-to-all-done = f32[16,1,2048]{2,1,0:T(1,128)S(1)} async-done(((f32[16,1,2048]{2,1,0:T(1,128)}), f32[16,1,2048]{2,1,0:T(1,128)S(1)}, u32[]{:S(2)}, u32[]{:S(2)}) %all-to-all-start) | async-done | bytes 131104 | tf_op jit(solution)/shard_map/all_to_all | solution.py:113
  218.7 1.9 collective-permute-start.17
  222.0 4.5 %collective-permute-start.23 = (f32[3,18,1,256]{3,2,1,0:T(1,128)S(1)}, f32[3,18,1,256]{3,2,1,0:T(1,128)S(1)}, u32[]{:S(2)}, u32[]{:S(2)}) collective-permute-start(f32[3,18,1,256]{3,2,1,0:T(1,128)S(1)} %get-tuple-element.64), channel_id=1, source_target_pairs={{0,1},{1,2},{2,3},{3,4},{4,5},{5,6},{6,7},{7,8},{8,9},{9,10},{10,1... | collective-permute-start | bytes 165896 | tf_op jit(solution)/shard_map/ppermute | solution.py:23
  227.7 5.2 %collective-permute-start.16 = (f32[1,8,256]{2,1,0:T(8,128)S(1)}, f32[1,8,256]{2,1,0:T(8,128)S(1)}, u32[]{:S(2)}, u32[]{:S(2)}) collective-permute-start(f32[1,8,256]{2,1,0:T(8,128)S(1)} %slice.563), channel_id=1, source_target_pairs={{16,0},{32,16},{48,32},{64,48},{80,64},{96,80},{112,96},{128,112},... | collective-permute-start | bytes 24584 | tf_op jit(solution)/shard_map/ppermute | solution.py:26
  233.0 1.3 collective-permute-done.16
  235.6 4.5 %collective-permute-start.19 = (f32[18,1,256]{2,1,0:T(1,128)S(1)}, f32[18,1,256]{2,1,0:T(1,128)S(1)}, u32[]{:S(2)}, u32[]{:S(2)}) collective-permute-start(f32[18,1,256]{2,1,0:T(1,128)S(1)} %get-tuple-element.72), channel_id=1, source_target_pairs={{0,1},{1,2},{2,3},{3,4},{4,5},{5,6},{6,7},{7,8},{8,9},{9,10},{10,1... | collective-permute-start | bytes 55304 | tf_op jit(solution)/shard_map/ppermute | solution.py:23
  242.6 5.1 %collective-permute-start.24 = (f32[3,1,8,256]{3,2,1,0:T(8,128)S(1)}, f32[3,1,8,256]{3,2,1,0:T(8,128)S(1)}, u32[]{:S(2)}, u32[]{:S(2)}) collective-permute-start(f32[3,1,8,256]{3,2,1,0:T(8,128)S(1)} %get-tuple-element.69), channel_id=1, source_target_pairs={{16,0},{32,16},{48,32},{64,48},{80,64},{96,80},{112,96},{128,112},... | collective-permute-start | bytes 73736 | tf_op jit(solution)/shard_map/ppermute | solution.py:26
  247.7 1.9 collective-permute-start.25
  249.6 5.3 %collective-permute-done.25 = f32[3,1,8,256]{3,2,1,0:T(8,128)S(1)} collective-permute-done((f32[3,1,8,256]{3,2,1,0:T(8,128)S(1)}, f32[3,1,8,256]{3,2,1,0:T(8,128)S(1)}, u32[]{:S(2)}, u32[]{:S(2)}) %collective-permute-start.25) | collective-permute-done | bytes 24608 | tf_op jit(solution)/shard_map/ppermute | solution.py:23
  255.0 1.3 collective-permute-start.26
  256.3 4.5 %collective-permute-start.27 = (f32[3,18,1,256]{3,2,1,0:T(1,128)S(1)}, f32[3,18,1,256]{3,2,1,0:T(1,128)S(1)}, u32[]{:S(2)}, u32[]{:S(2)}) collective-permute-start(f32[3,18,1,256]{3,2,1,0:T(1,128)S(1)} %get-tuple-element.62), channel_id=1, source_target_pairs={{0,1},{1,2},{2,3},{3,4},{4,5},{5,6},{6,7},{7,8},{8,9},{9,10},{10,1... | collective-permute-start | bytes 165896 | tf_op jit(solution)/shard_map/ppermute | solution.py:23
  261.1 1.6 collective-permute-done.27
  264.0 1.9 collective-permute-start.28
  265.9 2.4 collective-permute-start.29
  268.4 5.2 %collective-permute-done.29 = f32[3,1,8,256]{3,2,1,0:T(8,128)S(1)} collective-permute-done((f32[3,1,8,256]{3,2,1,0:T(8,128)S(1)}, f32[3,1,8,256]{3,2,1,0:T(8,128)S(1)}, u32[]{:S(2)}, u32[]{:S(2)}) %collective-permute-start.29) | collective-permute-done | bytes 24608 | tf_op jit(solution)/shard_map/ppermute | solution.py:23
  274.9 4.8 %collective-permute-start.31 = (f32[3,18,1,256]{3,2,1,0:T(1,128)S(1)}, f32[3,18,1,256]{3,2,1,0:T(1,128)S(1)}, u32[]{:S(2)}, u32[]{:S(2)}) collective-permute-start(f32[3,18,1,256]{3,2,1,0:T(1,128)S(1)} %get-tuple-element.60), channel_id=1, source_target_pairs={{0,1},{1,2},{2,3},{3,4},{4,5},{5,6},{6,7},{7,8},{8,9},{9,10},{10,1... | collective-permute-start | bytes 165896 | tf_op jit(solution)/shard_map/ppermute | solution.py:23
  279.7 1.6 collective-permute-done.31
  283.5 30.4 %all_to_all.36 = f32[16,1,2048]{2,1,0:T(1,128)S(1)} all-to-all(f32[16,1,2048]{2,1,0:T(1,128)S(1)} %reshape.23), channel_id=1, replica_groups=mesh['gx'=16,'gy'=16] {'gy'}, dimensions={0} | all-to-all | bytes 262144 | tf_op jit(solution)/shard_map/all_to_all | solution.py:120
  (99 shorter events, 28.7 us)
Async XLA Ops:
  0.6 10.6 %copy-start.2 = (f32[32,32,256]{2,1,0:T(8,128)S(1)}, f32[32,32,256]{2,1,0:T(8,128)}, u32[]{:S(2)}) copy-start(f32[32,32,256]{2,1,0:T(8,128)} %param.5) | copy-start | bytes 3145732
  0.6 10.6 %copy-start.1 = (f32[32,32,256]{2,1,0:T(8,128)S(1)}, f32[32,32,256]{2,1,0:T(8,128)}, u32[]{:S(2)}) copy-start(f32[32,32,256]{2,1,0:T(8,128)} %param.6) | copy-start | bytes 3145732
  1.6 7.7 %collective-permute-start = (f32[2,1,32,256]{3,2,1,0:T(8,128)S(1)}, f32[2,1,32,256]{3,2,1,0:T(8,128)S(1)}, u32[]{:S(2)}, u32[]{:S(2)}) collective-permute-start(f32[2,1,32,256]{3,2,1,0:T(8,128)S(1)} %get-tuple-element.47), channel_id=1, source_target_pairs={{0,16},{16,32},{32,48},{48,64},{64,80},{80,96},{96,112},{112,128},... | collective-permute-start | bytes 196616 | tf_op jit(solution)/shard_map/ppermute | solution.py:23
  3.5 7.6 %collective-permute-start.1 = (f32[2,1,32,256]{3,2,1,0:T(8,128)S(1)}, f32[2,1,32,256]{3,2,1,0:T(8,128)S(1)}, u32[]{:S(2)}, u32[]{:S(2)}) collective-permute-start(f32[2,1,32,256]{3,2,1,0:T(8,128)S(1)} %get-tuple-element.48), channel_id=1, source_target_pairs={{16,0},{32,16},{48,32},{64,48},{80,64},{96,80},{112,96},{128,112},... | collective-permute-start | bytes 196616 | tf_op jit(solution)/shard_map/ppermute | solution.py:26
  11.3 5.8 %collective-permute-start.2 = (f32[2,34,1,256]{3,2,1,0:T(1,128)S(1)}, f32[2,34,1,256]{3,2,1,0:T(1,128)S(1)}, u32[]{:S(2)}, u32[]{:S(2)}) collective-permute-start(f32[2,34,1,256]{3,2,1,0:T(1,128)S(1)} %get-tuple-element.39), channel_id=1, source_target_pairs={{0,1},{1,2},{2,3},{3,4},{4,5},{5,6},{6,7},{7,8},{8,9},{9,10},{10,1... | collective-permute-start | bytes 208904 | tf_op jit(solution)/shard_map/ppermute | solution.py:23
  15.1 6.2 %collective-permute-start.3 = (f32[2,34,1,256]{3,2,1,0:T(1,128)S(1)}, f32[2,34,1,256]{3,2,1,0:T(1,128)S(1)}, u32[]{:S(2)}, u32[]{:S(2)}) collective-permute-start(f32[2,34,1,256]{3,2,1,0:T(1,128)S(1)} %get-tuple-element.40), channel_id=1, source_target_pairs={{1,0},{2,1},{3,2},{4,3},{5,4},{6,5},{7,6},{8,7},{9,8},{10,9},{11,1... | collective-permute-start | bytes 208904 | tf_op jit(solution)/shard_map/ppermute | solution.py:26
  22.0 1.2 copy-start
  26.3 7.7 %collective-permute-start.4 = (f32[2,1,32,256]{3,2,1,0:T(8,128)S(1)}, f32[2,1,32,256]{3,2,1,0:T(8,128)S(1)}, u32[]{:S(2)}, u32[]{:S(2)}) collective-permute-start(f32[2,1,32,256]{3,2,1,0:T(8,128)S(1)} %get-tuple-element.45), channel_id=1, source_target_pairs={{0,16},{16,32},{32,48},{48,64},{64,80},{80,96},{96,112},{112,128},... | collective-permute-start | bytes 196616 | tf_op jit(solution)/shard_map/ppermute | solution.py:23
  28.2 7.6 %collective-permute-start.5 = (f32[2,1,32,256]{3,2,1,0:T(8,128)S(1)}, f32[2,1,32,256]{3,2,1,0:T(8,128)S(1)}, u32[]{:S(2)}, u32[]{:S(2)}) collective-permute-start(f32[2,1,32,256]{3,2,1,0:T(8,128)S(1)} %get-tuple-element.46), channel_id=1, source_target_pairs={{16,0},{32,16},{48,32},{64,48},{80,64},{96,80},{112,96},{128,112},... | collective-permute-start | bytes 196616 | tf_op jit(solution)/shard_map/ppermute | solution.py:26
  36.0 5.8 %collective-permute-start.6 = (f32[2,34,1,256]{3,2,1,0:T(1,128)S(1)}, f32[2,34,1,256]{3,2,1,0:T(1,128)S(1)}, u32[]{:S(2)}, u32[]{:S(2)}) collective-permute-start(f32[2,34,1,256]{3,2,1,0:T(1,128)S(1)} %get-tuple-element.37), channel_id=1, source_target_pairs={{0,1},{1,2},{2,3},{3,4},{4,5},{5,6},{6,7},{7,8},{8,9},{9,10},{10,1... | collective-permute-start | bytes 208904 | tf_op jit(solution)/shard_map/ppermute | solution.py:23
  39.8 7.2 %collective-permute-start.7 = (f32[2,34,1,256]{3,2,1,0:T(1,128)S(1)}, f32[2,34,1,256]{3,2,1,0:T(1,128)S(1)}, u32[]{:S(2)}, u32[]{:S(2)}) collective-permute-start(f32[2,34,1,256]{3,2,1,0:T(1,128)S(1)} %get-tuple-element.38), channel_id=1, source_target_pairs={{1,0},{2,1},{3,2},{4,3},{5,4},{6,5},{7,6},{8,7},{9,8},{10,9},{11,1... | collective-permute-start | bytes 208904 | tf_op jit(solution)/shard_map/ppermute | solution.py:26
  51.0 7.7 %collective-permute-start.8 = (f32[2,1,32,256]{3,2,1,0:T(8,128)S(1)}, f32[2,1,32,256]{3,2,1,0:T(8,128)S(1)}, u32[]{:S(2)}, u32[]{:S(2)}) collective-permute-start(f32[2,1,32,256]{3,2,1,0:T(8,128)S(1)} %get-tuple-element.43), channel_id=1, source_target_pairs={{0,16},{16,32},{32,48},{48,64},{64,80},{80,96},{96,112},{112,128},... | collective-permute-start | bytes 196616 | tf_op jit(solution)/shard_map/ppermute | solution.py:23
  52.9 7.6 %collective-permute-start.9 = (f32[2,1,32,256]{3,2,1,0:T(8,128)S(1)}, f32[2,1,32,256]{3,2,1,0:T(8,128)S(1)}, u32[]{:S(2)}, u32[]{:S(2)}) collective-permute-start(f32[2,1,32,256]{3,2,1,0:T(8,128)S(1)} %get-tuple-element.44), channel_id=1, source_target_pairs={{16,0},{32,16},{48,32},{64,48},{80,64},{96,80},{112,96},{128,112},... | collective-permute-start | bytes 196616 | tf_op jit(solution)/shard_map/ppermute | solution.py:26
  60.7 7.1 %collective-permute-start.10 = (f32[2,34,1,256]{3,2,1,0:T(1,128)S(1)}, f32[2,34,1,256]{3,2,1,0:T(1,128)S(1)}, u32[]{:S(2)}, u32[]{:S(2)}) collective-permute-start(f32[2,34,1,256]{3,2,1,0:T(1,128)S(1)} %get-tuple-element.35), channel_id=1, source_target_pairs={{0,1},{1,2},{2,3},{3,4},{4,5},{5,6},{6,7},{7,8},{8,9},{9,10},{10,1... | collective-permute-start | bytes 208904 | tf_op jit(solution)/shard_map/ppermute | solution.py:23
  65.8 6.2 %collective-permute-start.11 = (f32[2,34,1,256]{3,2,1,0:T(1,128)S(1)}, f32[2,34,1,256]{3,2,1,0:T(1,128)S(1)}, u32[]{:S(2)}, u32[]{:S(2)}) collective-permute-start(f32[2,34,1,256]{3,2,1,0:T(1,128)S(1)} %get-tuple-element.36), channel_id=1, source_target_pairs={{1,0},{2,1},{3,2},{4,3},{5,4},{6,5},{7,6},{8,7},{9,8},{10,9},{11,1... | collective-permute-start | bytes 208904 | tf_op jit(solution)/shard_map/ppermute | solution.py:26
  76.0 15.0 %copy-start.4 = (f32[3,16,8,256]{3,2,1,0:T(8,128)S(1)}, f32[3,16,8,256]{3,2,1,0:T(8,128)}, u32[]{:S(2)}) copy-start(f32[3,16,8,256]{3,2,1,0:T(8,128)} %param.8) | copy-start | bytes 1179652
  76.0 7.8 %collective-permute-start.12 = (f32[2,1,32,256]{3,2,1,0:T(8,128)S(1)}, f32[2,1,32,256]{3,2,1,0:T(8,128)S(1)}, u32[]{:S(2)}, u32[]{:S(2)}) collective-permute-start(f32[2,1,32,256]{3,2,1,0:T(8,128)S(1)} %get-tuple-element.41), channel_id=1, source_target_pairs={{0,16},{16,32},{32,48},{48,64},{64,80},{80,96},{96,112},{112,128},... | collective-permute-start | bytes 196616 | tf_op jit(solution)/shard_map/ppermute | solution.py:23
  78.1 7.6 %collective-permute-start.13 = (f32[2,1,32,256]{3,2,1,0:T(8,128)S(1)}, f32[2,1,32,256]{3,2,1,0:T(8,128)S(1)}, u32[]{:S(2)}, u32[]{:S(2)}) collective-permute-start(f32[2,1,32,256]{3,2,1,0:T(8,128)S(1)} %get-tuple-element.42), channel_id=1, source_target_pairs={{16,0},{32,16},{48,32},{64,48},{80,64},{96,80},{112,96},{128,112},... | collective-permute-start | bytes 196616 | tf_op jit(solution)/shard_map/ppermute | solution.py:26
  85.8 13.1 %collective-permute-start.14 = (f32[2,34,1,256]{3,2,1,0:T(1,128)S(1)}, f32[2,34,1,256]{3,2,1,0:T(1,128)S(1)}, u32[]{:S(2)}, u32[]{:S(2)}) collective-permute-start(f32[2,34,1,256]{3,2,1,0:T(1,128)S(1)} %get-tuple-element.33), channel_id=1, source_target_pairs={{0,1},{1,2},{2,3},{3,4},{4,5},{5,6},{6,7},{7,8},{8,9},{9,10},{10,1... | collective-permute-start | bytes 208904 | tf_op jit(solution)/shard_map/ppermute | solution.py:23
  89.7 9.2 %collective-permute-start.15 = (f32[2,34,1,256]{3,2,1,0:T(1,128)S(1)}, f32[2,34,1,256]{3,2,1,0:T(1,128)S(1)}, u32[]{:S(2)}, u32[]{:S(2)}) collective-permute-start(f32[2,34,1,256]{3,2,1,0:T(1,128)S(1)} %get-tuple-element.34), channel_id=1, source_target_pairs={{1,0},{2,1},{3,2},{4,3},{5,4},{6,5},{7,6},{8,7},{9,8},{10,9},{11,1... | collective-permute-start | bytes 208904 | tf_op jit(solution)/shard_map/ppermute | solution.py:26
  91.1 115.2 %collective-permute-start.21 = (f32[3,1,8,256]{3,2,1,0:T(8,128)S(1)}, f32[3,1,8,256]{3,2,1,0:T(8,128)S(1)}, u32[]{:S(2)}, u32[]{:S(2)}) collective-permute-start(f32[3,1,8,256]{3,2,1,0:T(8,128)S(1)} %get-tuple-element.71), channel_id=1, source_target_pairs={{0,16},{16,32},{32,48},{48,64},{64,80},{80,96},{96,112},{112,128},... | collective-permute-start | bytes 73736 | tf_op jit(solution)/shard_map/ppermute | solution.py:23
  93.0 113.4 %collective-permute-start.20 = (f32[3,1,8,256]{3,2,1,0:T(8,128)S(1)}, f32[3,1,8,256]{3,2,1,0:T(8,128)S(1)}, u32[]{:S(2)}, u32[]{:S(2)}) collective-permute-start(f32[3,1,8,256]{3,2,1,0:T(8,128)S(1)} %get-tuple-element.70), channel_id=1, source_target_pairs={{16,0},{32,16},{48,32},{64,48},{80,64},{96,80},{112,96},{128,112},... | collective-permute-start | bytes 73736 | tf_op jit(solution)/shard_map/ppermute | solution.py:26
  194.7 21.7 %all-to-all-start = ((f32[16,1,2048]{2,1,0:T(1,128)}), f32[16,1,2048]{2,1,0:T(1,128)S(1)}, u32[]{:S(2)}, u32[]{:S(2)}) async-start(f32[16,1,2048]{2,1,0:T(1,128)} %reshape.21), calls=%async_computation | async-start | bytes 262144 | tf_op jit(solution)/shard_map/all_to_all | solution.py:113
  218.7 14.2 %collective-permute-start.17 = (f32[1,8,256]{2,1,0:T(8,128)S(1)}, f32[1,8,256]{2,1,0:T(8,128)S(1)}, u32[]{:S(2)}, u32[]{:S(2)}) collective-permute-start(f32[1,8,256]{2,1,0:T(8,128)S(1)} %slice.566), channel_id=1, source_target_pairs={{0,16},{16,32},{32,48},{48,64},{64,80},{80,96},{96,112},{112,128},... | collective-permute-start | bytes 24584 | tf_op jit(solution)/shard_map/ppermute | solution.py:23
  220.7 19.5 %collective-permute-start.22 = (f32[3,18,1,256]{3,2,1,0:T(1,128)S(1)}, f32[3,18,1,256]{3,2,1,0:T(1,128)S(1)}, u32[]{:S(2)}, u32[]{:S(2)}) collective-permute-start(f32[3,18,1,256]{3,2,1,0:T(1,128)S(1)} %get-tuple-element.65), channel_id=1, source_target_pairs={{1,0},{2,1},{3,2},{4,3},{5,4},{6,5},{7,6},{8,7},{9,8},{10,9},{11,1... | collective-permute-start | bytes 165896 | tf_op jit(solution)/shard_map/ppermute | solution.py:26
  222.0 18.2 %collective-permute-start.23 = (f32[3,18,1,256]{3,2,1,0:T(1,128)S(1)}, f32[3,18,1,256]{3,2,1,0:T(1,128)S(1)}, u32[]{:S(2)}, u32[]{:S(2)}) collective-permute-start(f32[3,18,1,256]{3,2,1,0:T(1,128)S(1)} %get-tuple-element.64), channel_id=1, source_target_pairs={{0,1},{1,2},{2,3},{3,4},{4,5},{5,6},{6,7},{7,8},{8,9},{9,10},{10,1... | collective-permute-start | bytes 165896 | tf_op jit(solution)/shard_map/ppermute | solution.py:23
  227.7 6.5 %collective-permute-start.16 = (f32[1,8,256]{2,1,0:T(8,128)S(1)}, f32[1,8,256]{2,1,0:T(8,128)S(1)}, u32[]{:S(2)}, u32[]{:S(2)}) collective-permute-start(f32[1,8,256]{2,1,0:T(8,128)S(1)} %slice.563), channel_id=1, source_target_pairs={{16,0},{32,16},{48,32},{64,48},{80,64},{96,80},{112,96},{128,112},... | collective-permute-start | bytes 24584 | tf_op jit(solution)/shard_map/ppermute | solution.py:26
  234.3 6.7 %collective-permute-start.18 = (f32[18,1,256]{2,1,0:T(1,128)S(1)}, f32[18,1,256]{2,1,0:T(1,128)S(1)}, u32[]{:S(2)}, u32[]{:S(2)}) collective-permute-start(f32[18,1,256]{2,1,0:T(1,128)S(1)} %get-tuple-element.73), channel_id=1, source_target_pairs={{1,0},{2,1},{3,2},{4,3},{5,4},{6,5},{7,6},{8,7},{9,8},{10,9},{11,1... | collective-permute-start | bytes 55304 | tf_op jit(solution)/shard_map/ppermute | solution.py:26
  235.6 6.0 %collective-permute-start.19 = (f32[18,1,256]{2,1,0:T(1,128)S(1)}, f32[18,1,256]{2,1,0:T(1,128)S(1)}, u32[]{:S(2)}, u32[]{:S(2)}) collective-permute-start(f32[18,1,256]{2,1,0:T(1,128)S(1)} %get-tuple-element.72), channel_id=1, source_target_pairs={{0,1},{1,2},{2,3},{3,4},{4,5},{5,6},{6,7},{7,8},{8,9},{9,10},{10,1... | collective-permute-start | bytes 55304 | tf_op jit(solution)/shard_map/ppermute | solution.py:23
  241.0 1.1 copy-start.5
  242.6 7.0 %collective-permute-start.24 = (f32[3,1,8,256]{3,2,1,0:T(8,128)S(1)}, f32[3,1,8,256]{3,2,1,0:T(8,128)S(1)}, u32[]{:S(2)}, u32[]{:S(2)}) collective-permute-start(f32[3,1,8,256]{3,2,1,0:T(8,128)S(1)} %get-tuple-element.69), channel_id=1, source_target_pairs={{16,0},{32,16},{48,32},{64,48},{80,64},{96,80},{112,96},{128,112},... | collective-permute-start | bytes 73736 | tf_op jit(solution)/shard_map/ppermute | solution.py:26
  247.7 7.3 %collective-permute-start.25 = (f32[3,1,8,256]{3,2,1,0:T(8,128)S(1)}, f32[3,1,8,256]{3,2,1,0:T(8,128)S(1)}, u32[]{:S(2)}, u32[]{:S(2)}) collective-permute-start(f32[3,1,8,256]{3,2,1,0:T(8,128)S(1)} %get-tuple-element.68), channel_id=1, source_target_pairs={{0,16},{16,32},{32,48},{48,64},{64,80},{80,96},{96,112},{112,128},... | collective-permute-start | bytes 73736 | tf_op jit(solution)/shard_map/ppermute | solution.py:23
  255.0 6.0 %collective-permute-start.26 = (f32[3,18,1,256]{3,2,1,0:T(1,128)S(1)}, f32[3,18,1,256]{3,2,1,0:T(1,128)S(1)}, u32[]{:S(2)}, u32[]{:S(2)}) collective-permute-start(f32[3,18,1,256]{3,2,1,0:T(1,128)S(1)} %get-tuple-element.63), channel_id=1, source_target_pairs={{1,0},{2,1},{3,2},{4,3},{5,4},{6,5},{7,6},{8,7},{9,8},{10,9},{11,1... | collective-permute-start | bytes 165896 | tf_op jit(solution)/shard_map/ppermute | solution.py:26
  256.3 6.3 %collective-permute-start.27 = (f32[3,18,1,256]{3,2,1,0:T(1,128)S(1)}, f32[3,18,1,256]{3,2,1,0:T(1,128)S(1)}, u32[]{:S(2)}, u32[]{:S(2)}) collective-permute-start(f32[3,18,1,256]{3,2,1,0:T(1,128)S(1)} %get-tuple-element.62), channel_id=1, source_target_pairs={{0,1},{1,2},{2,3},{3,4},{4,5},{5,6},{6,7},{7,8},{8,9},{9,10},{10,1... | collective-permute-start | bytes 165896 | tf_op jit(solution)/shard_map/ppermute | solution.py:23
  264.0 18.7 %copy-start.3 = (f32[3,16,8,256]{3,2,1,0:T(8,128)}, f32[3,16,8,256]{3,2,1,0:T(8,128)S(1)}, u32[]{:S(2)}) copy-start(f32[3,16,8,256]{3,2,1,0:T(8,128)S(1)} %fusion.74) | copy-start | bytes 1179652
  264.0 4.3 %collective-permute-start.28 = (f32[3,1,8,256]{3,2,1,0:T(8,128)S(1)}, f32[3,1,8,256]{3,2,1,0:T(8,128)S(1)}, u32[]{:S(2)}, u32[]{:S(2)}) collective-permute-start(f32[3,1,8,256]{3,2,1,0:T(8,128)S(1)} %get-tuple-element.67), channel_id=1, source_target_pairs={{16,0},{32,16},{48,32},{64,48},{80,64},{96,80},{112,96},{128,112},... | collective-permute-start | bytes 73736 | tf_op jit(solution)/shard_map/ppermute | solution.py:26
  265.9 7.6 %collective-permute-start.29 = (f32[3,1,8,256]{3,2,1,0:T(8,128)S(1)}, f32[3,1,8,256]{3,2,1,0:T(8,128)S(1)}, u32[]{:S(2)}, u32[]{:S(2)}) collective-permute-start(f32[3,1,8,256]{3,2,1,0:T(8,128)S(1)} %get-tuple-element.66), channel_id=1, source_target_pairs={{0,16},{16,32},{32,48},{48,64},{64,80},{80,96},{96,112},{112,128},... | collective-permute-start | bytes 73736 | tf_op jit(solution)/shard_map/ppermute | solution.py:23
  273.6 6.1 %collective-permute-start.30 = (f32[3,18,1,256]{3,2,1,0:T(1,128)S(1)}, f32[3,18,1,256]{3,2,1,0:T(1,128)S(1)}, u32[]{:S(2)}, u32[]{:S(2)}) collective-permute-start(f32[3,18,1,256]{3,2,1,0:T(1,128)S(1)} %get-tuple-element.61), channel_id=1, source_target_pairs={{1,0},{2,1},{3,2},{4,3},{5,4},{6,5},{7,6},{8,7},{9,8},{10,9},{11,1... | collective-permute-start | bytes 165896 | tf_op jit(solution)/shard_map/ppermute | solution.py:26
  274.9 6.3 %collective-permute-start.31 = (f32[3,18,1,256]{3,2,1,0:T(1,128)S(1)}, f32[3,18,1,256]{3,2,1,0:T(1,128)S(1)}, u32[]{:S(2)}, u32[]{:S(2)}) collective-permute-start(f32[3,18,1,256]{3,2,1,0:T(1,128)S(1)} %get-tuple-element.60), channel_id=1, source_target_pairs={{0,1},{1,2},{2,3},{3,4},{4,5},{5,6},{6,7},{7,8},{8,9},{9,10},{10,1... | collective-permute-start | bytes 165896 | tf_op jit(solution)/shard_map/ppermute | solution.py:23
where the time goes:
time: 318 us; the launch traced here: 317 us
  starting transfers between devices  114 us (36%)
  local copies, waits for them, and re-layouts  77.3 us (24%)
  waiting for transfers between devices  49 us (15%)
  other arithmetic  44.8 us (14%)
  blocking collectives  30.4 us (10%)
    reshape x1, local copies, waits for them, and re-layouts, restrict(): sq = (order_out * order_out).reshape(sx // 2, 2, sy // 2, 2, sz // 2, 2)  68.4 us
    ppermute x16, starting transfers between devices, padded_2(): lax.ppermute(lax.slice_in_dim(block, 0, width, axis=dim), axis, backward)  51.5 us
    ppermute x16, starting transfers between devices, padded_2(): lax.ppermute(lax.slice_in_dim(block, block.shape[dim] - width, None, axis...  51.1 us
    all_to_all x1, blocking collectives, on_device(): lax.all_to_all(energy, 'gy', split_axis=2, concat_axis=1, tiled=True)  30.4 us
    ppermute x16, waiting for transfers between devices, padded_2(): lax.ppermute(lax.slice_in_dim(block, 0, width, axis=dim), axis, backward)  22.9 us
    reduce_sum x1, other arithmetic, restrict(): return 0.1 + 0.125 * jnp.sum(sq, axis=(1, 3, 5))  20.8 us
    ppermute x16, waiting for transfers between devices, padded_2(): lax.ppermute(lax.slice_in_dim(block, block.shape[dim] - width, None, axis...  16.1 us
    all_to_all x1, starting transfers between devices, on_device(): lax.all_to_all(coarse, 'gy', split_axis=1, concat_axis=2, tiled=True)  11.6 us
  transfers between devices with their start and end apart: 33, of which 18 were waited for; matrix products, arithmetic and copies ran while one was open for 31% of the time, Pallas kernels for 0%

commit v1 on v0

v1 whole, which is shorter than its diff:
```python
import jax
import jax.numpy as jnp
import numpy as np
from jax import lax
from jax.sharding import PartitionSpec as P

STEPS = 4
FINE_HALO = 4
MECH_HALO = 3

rate_conc = 0.15
rate_order = 0.15
well_height = 1.0
drive_coupling = 0.5
spring_term = 0.2
first_weight = 0.5956
second_weight = 2.695


def padded_2(block, sides, width):
    for axis, dim in sides:
        count = lax.axis_size(axis)
        forward = [(i, i + 1) for i in range(count - 1)]
        backward = [(target, source) for source, target in forward]
        low = lax.ppermute(
            lax.slice_in_dim(block, block.shape[dim] - width, None, axis=dim), axis, forward
        )
        high = lax.ppermute(lax.slice_in_dim(block, 0, width, axis=dim), axis, backward)
        block = jnp.concatenate([low, block, high], axis=dim)
    return block


def fine_laplace(padded):
    zpad = jnp.pad(padded, ((0, 0), (0, 0), (1, 1)))
    center = zpad[1:-1, 1:-1, 1:-1]
    total = zpad[2:, 1:-1, 1:-1] + zpad[:-2, 1:-1, 1:-1]
    total = total + zpad[1:-1, 2:, 1:-1] + zpad[1:-1, :-2, 1:-1]
    total = total + zpad[1:-1, 1:-1, 2:] + zpad[1:-1, 1:-1, :-2]
    return total - 6.0 * center


def advance(conc_pad, order_pad, mob_pad, last):
    chem = conc_pad - order_pad * order_pad * (3.0 - 2.0 * order_pad)
    conc_in = conc_pad[1:-1, 1:-1]
    order_in = order_pad[1:-1, 1:-1]
    chem_in = chem[1:-1, 1:-1]
    mobility = mob_pad[1:-1, 1:-1]
    conc_new = conc_in + rate_conc * fine_laplace(chem)
    dh_term = 6.0 * order_in * (1.0 - order_in)
    dg_term = 2.0 * order_in * (1.0 - order_in) * (1.0 - 2.0 * order_in)
    order_new = order_in + mobility * (
        rate_order * fine_laplace(order_pad)
        - well_height * dg_term
        + drive_coupling * chem_in * dh_term
    )
    if not last:
        conc_new = jnp.where(mobility > 0, conc_new, 0.0)
    return conc_new, order_new, mobility


def mobility_of(labels):
    return (0.5 * (labels == 0) + 1.0 * (labels == 1) + 0.25 * (labels == 2)).astype(jnp.float32)


def restrict_xzy(order_out):
    sx, sy, sz = order_out.shape
    sq = order_out * order_out
    sq = sq.reshape(sx // 2, 2, sy, sz).sum(axis=1)
    sq = sq.reshape(sx // 2, sy // 2, 2, sz).sum(axis=2)
    pairs = jnp.asarray(np.repeat(np.eye(sz // 2, dtype=np.float32), 2, axis=0))
    summed = jnp.einsum("xyz,zw->xwy", sq, pairs, precision=lax.Precision.HIGHEST)
    return 0.1 + 0.125 * summed


def y_shift(v, step):
    if step > 0:
        return jnp.pad(v[..., step:], [(0, 0)] * (v.ndim - 1) + [(0, step)])
    return jnp.pad(v[..., :step], [(0, 0)] * (v.ndim - 1) + [(-step, 0)])


def face_terms(stiff_pad):
    center = stiff_pad[1:-1, 1:-1]
    others = [stiff_pad[2:, 1:-1], stiff_pad[:-2, 1:-1], stiff_pad[1:-1, 2:], stiff_pad[1:-1, :-2],
              y_shift(center, 1), y_shift(center, -1)]
    faces = [0.5 * (center + other) for other in others]
    diag = faces[0] + faces[1] + faces[2] + faces[3] + faces[4] + faces[5] + spring_term * center
    return faces, diag, center


def neighbours(u_pad):
    center = u_pad[:, 1:-1, 1:-1]
    return center, [u_pad[:, 2:, 1:-1], u_pad[:, :-2, 1:-1], u_pad[:, 1:-1, 2:], u_pad[:, 1:-1, :-2],
                    y_shift(center, 1), y_shift(center, -1)]


def apply_op(u_pad, faces, diag):
    center, others = neighbours(u_pad)
    result = diag * center
    for face, other in zip(faces, others):
        result = result - face * other
    return result, center


def strain_energy(u_pad, faces):
    center, others = neighbours(u_pad)
    total = jnp.zeros(center.shape, jnp.float32)
    for face, other in zip(faces, others):
        diff = center - other
        total = total + face * diff * diff
    return 0.25 * jnp.sum(total, axis=0)


def on_device(concentration, order_field, phase_labels, displacement, body_load):
    h = FINE_HALO
    fields = jnp.stack([concentration, order_field, mobility_of(phase_labels)])
    fields = padded_2(fields, (("gx", 1), ("gy", 2)), h)
    conc, order, mob = fields[0], fields[1], fields[2]
    for step in range(STEPS):
        conc, order, mob = advance(conc, order, mob, step == STEPS - 1)

    m = MECH_HALO
    ub = padded_2(jnp.concatenate([displacement, body_load]), (("gx", 1), ("gy", 2)), m)
    disp, load = ub[:3], ub[3:]

    coarse = restrict_xzy(order)
    stiff = lax.all_to_all(coarse, "gy", split_axis=1, concat_axis=2, tiled=True)
    stiff_pad = padded_2(stiff, (("gx", 0), ("gy", 1)), m)

    faces, diag, center = face_terms(stiff_pad)
    for weight in (first_weight, second_weight):
        load = load[:, 1:-1, 1:-1]
        result, u_c = apply_op(disp, faces, diag)
        new = u_c + weight * (load - result) / diag
        disp = jnp.where(center > 0, new, 0.0)
        faces = [f[1:-1, 1:-1] for f in faces]
        diag = diag[1:-1, 1:-1]
        center = center[1:-1, 1:-1]
    energy = strain_energy(disp, faces)
    disp = disp[:, 1:-1, 1:-1]
    tiles = lax.all_to_all(energy, "gy", split_axis=2, concat_axis=1, tiled=True)
    return (conc, order, disp, jnp.transpose(tiles, (0, 2, 1)))


def solution(mesh):
    return jax.shard_map(
        on_device,
        mesh=mesh,
        in_specs=(
            P("gx", "gy", None),
            P("gx", "gy", None),
            P("gx", "gy", None),
            P(None, "gx", "gy", None),
            P(None, "gx", "gy", None),
        ),
        out_specs=(
            P("gx", "gy", None),
            P("gx", "gy", None),
            P(None, "gx", "gy", None),
            P("gx", "gy", None),
        ),
        check_vma=False,
    )
```

time: 318 us -> 135 us (0.42)
  local copies, waits for them, and re-layouts: 77.3 us -> 17.9 us
  starting transfers between devices: 114 us -> 60.5 us
  blocking collectives: 30.4 us -> 0 us
  waiting for transfers between devices: 49 us -> 22.5 us
  other arithmetic: 44.8 us -> 30.6 us
    reshape x1 -> x0, local copies, waits for them, and re-layouts: 68.4 us -> none  [restrict(): sq = (order_out * order_out).reshape(sx // 2, 2, sy // 2, 2, sz // 2, 2)]
    ppermute x16 -> x6, starting transfers between devices: 51.5 us -> 13.8 us  [padded_2(): lax.ppermute(lax.slice_in_dim(block, 0, width, axis=dim), axis, backward)]
    all_to_all x1 -> x0, blocking collectives: 30.4 us -> none  [on_device(): lax.all_to_all(energy, 'gy', split_axis=2, concat_axis=1, tiled=True)]
    ppermute x16 -> x6, starting transfers between devices: 51.1 us -> 21.1 us  [padded_2(): lax.ppermute(lax.slice_in_dim(block, block.shape[dim] - width, None, axis...]
    ppermute x16 -> x6, waiting for transfers between devices: 22.9 us -> 3.2 us  [padded_2(): lax.ppermute(lax.slice_in_dim(block, 0, width, axis=dim), axis, backward)]
    reduce_sum x1 -> x2, other arithmetic: 20.8 us -> 2.69 us  [the longest x1 2.4 us: restrict_xzy(): sq = sq.reshape(sx // 2, 2, sy, sz).sum(axis=1)]
    sub x4, other arithmetic: 0.91 us -> 14.1 us  [advance(): chem = conc_pad - order_pad * order_pad * (3.0 - 2.0 * order_pad)]
    all_to_all x0 -> x1, starting transfers between devices: none -> 11.1 us  [on_device(): lax.all_to_all(energy, 'gy', split_axis=2, concat_axis=1, tiled=True)]
  transfers between devices with their start and end apart: 33 -> 14, of which waited for: 18 -> 7; matrix products, arithmetic and copies ran while one was open for 31% -> 26% of each run, Pallas kernels for 0% -> 0%
where the time goes in v1:
time: 135 us; the launch traced here: 133 us
  starting transfers between devices  60.5 us (45%)
  other arithmetic  30.6 us (23%)
  waiting for transfers between devices  22.5 us (17%)
  local copies, waits for them, and re-layouts  17.9 us (13%)
    ppermute x6, starting transfers between devices, padded_2(): lax.ppermute(lax.slice_in_dim(block, block.shape[dim] - width, None, axis...  21.1 us
    all_to_all x1, starting transfers between devices, on_device(): lax.all_to_all(coarse, 'gy', split_axis=1, concat_axis=2, tiled=True)  14.6 us
    sub x4, other arithmetic, advance(): chem = conc_pad - order_pad * order_pad * (3.0 - 2.0 * order_pad)  14.1 us
    ppermute x6, starting transfers between devices, padded_2(): lax.ppermute(lax.slice_in_dim(block, 0, width, axis=dim), axis, backward)  13.8 us
    all_to_all x1, starting transfers between devices, on_device(): lax.all_to_all(energy, 'gy', split_axis=2, concat_axis=1, tiled=True)  11.1 us
    ppermute x6, waiting for transfers between devices, padded_2(): lax.ppermute(lax.slice_in_dim(block, block.shape[dim] - width, None, axis...  10.5 us
    all_to_all x1, waiting for transfers between devices, on_device(): lax.all_to_all(energy, 'gy', split_axis=2, concat_axis=1, tiled=True)  7.35 us
    unnamed x29, local copies, waits for them, and re-layouts  6.86 us
  transfers between devices with their start and end apart: 14, of which 7 were waited for; matrix products, arithmetic and copies ran while one was open for 26% of the time, Pallas kernels for 0%

profile of v1, /device:TPU:2, one launch (start us, length us, event | category | flops | bytes accessed | tf_op | source)
XLA Modules:
  0.0 133.2 jit_solution(16922649125582475896)
XLA Ops:
  0.7 1.6 %add_bitcast_fusion = f32[1,32,32,256]{3,2,1,0:T(8,128)S(1)} fusion(s32[32,32,256]{2,1,0:T(8,128)} %param.8), kind=kLoop, calls=%fused_computation.109 | loop fusion | flops 2097152 | bytes 2097152 | tf_op jit(solution)/shard_map/stack | solution.py:115
  2.5 4.3 %collective-permute-start.1 = (f32[3,4,32,256]{3,2,1,0:T(8,128)S(1)}, f32[3,4,32,256]{3,2,1,0:T(8,128)S(1)}, u32[]{:S(2)}, u32[]{:S(2)}) collective-permute-start(f32[3,4,32,256]{3,2,1,0:T(8,128)S(1)} %get-tuple-element.56), channel_id=1, source_target_pairs={{16,0},{32,16},{48,32},{64,48},{80,64},{96,80},{112,96},{128,112},... | collective-permute-start | bytes 1179656 | tf_op jit(solution)/shard_map/ppermute | solution.py:28
  6.9 2.1 %collective-permute-start = (f32[3,4,32,256]{3,2,1,0:T(8,128)S(1)}, f32[3,4,32,256]{3,2,1,0:T(8,128)S(1)}, u32[]{:S(2)}, u32[]{:S(2)}) collective-permute-start(f32[3,4,32,256]{3,2,1,0:T(8,128)S(1)} %get-tuple-element.55), channel_id=1, source_target_pairs={{0,16},{16,32},{32,48},{48,64},{64,80},{80,96},{96,112},{112,128},... | collective-permute-start | bytes 1179656 | tf_op jit(solution)/shard_map/ppermute | solution.py:25
  9.0 3.2 %collective-permute-done.1 = f32[3,4,32,256]{3,2,1,0:T(8,128)S(1)} collective-permute-done((f32[3,4,32,256]{3,2,1,0:T(8,128)S(1)}, f32[3,4,32,256]{3,2,1,0:T(8,128)S(1)}, u32[]{:S(2)}, u32[]{:S(2)}) %collective-permute-start.1) | collective-permute-done | bytes 393248 | tf_op jit(solution)/shard_map/ppermute | solution.py:28
  12.2 6.1 %collective-permute-done = f32[3,4,32,256]{3,2,1,0:T(8,128)S(1)} collective-permute-done((f32[3,4,32,256]{3,2,1,0:T(8,128)S(1)}, f32[3,4,32,256]{3,2,1,0:T(8,128)S(1)}, u32[]{:S(2)}, u32[]{:S(2)}) %collective-permute-start) | collective-permute-done | bytes 393248 | tf_op jit(solution)/shard_map/ppermute | solution.py:25
  18.4 1.3 collective-permute-start.3
  19.7 4.6 %collective-permute-start.2 = (f32[3,40,4,256]{3,2,1,0:T(4,128)S(1)}, f32[3,40,4,256]{3,2,1,0:T(4,128)S(1)}, u32[]{:S(2)}, u32[]{:S(2)}) collective-permute-start(f32[3,40,4,256]{3,2,1,0:T(4,128)S(1)} %get-tuple-element.53), channel_id=1, source_target_pairs={{0,1},{1,2},{2,3},{3,4},{4,5},{5,6},{6,7},{7,8},{8,9},{9,10},{10,1... | collective-permute-start | bytes 1474568 | tf_op jit(solution)/shard_map/ppermute | solution.py:25
  24.6 0.9 fusion.104
  25.5 1.9 %collective-permute-start.9 = (f32[6,3,8,256]{3,1,2,0:T(4,128)}, f32[6,3,8,256]{3,1,2,0:T(4,128)S(1)}, u32[]{:S(2)}, u32[]{:S(2)}) collective-permute-start(f32[6,3,8,256]{3,1,2,0:T(4,128)} %get-tuple-element.66), channel_id=1, source_target_pairs={{16,0},{32,16},{48,32},{64,48},{80,64},{96,80},{112,96},{128,112},... | collective-permute-start | bytes 442376 | tf_op jit(solution)/shard_map/ppermute | solution.py:28
  27.4 2.4 %collective-permute-start.8 = (f32[6,3,8,256]{3,1,2,0:T(4,128)}, f32[6,3,8,256]{3,1,2,0:T(4,128)}, u32[]{:S(2)}, u32[]{:S(2)}) collective-permute-start(f32[6,3,8,256]{3,1,2,0:T(4,128)} %get-tuple-element.65), channel_id=1, source_target_pairs={{0,16},{16,32},{32,48},{48,64},{64,80},{80,96},{96,112},{112,128},... | collective-permute-start | bytes 442376 | tf_op jit(solution)/shard_map/ppermute | solution.py:25
  29.9 0.7 collective-permute-done.2
  30.6 1.0 pad_maximum_fusion
  32.3 4.5 %multiply_subtract_fusion.1 = (f32[38,38,256]{2,1,0:T(8,128)S(1)}, f32[38,38,256]{2,1,0:T(8,128)S(1)}, f32[38,38,256]{2,1,0:T(8,128)S(1)}) fusion(f32[40,40,256]{2,1,0:T(8,128)S(1)} %multiply_subtract_fusion, f32[40,40,256]{2,1,0:T(8,128)S(1)} %get-tuple-element.51, f32[40,40,256]{2,1,0:T(8,128)S(1)} %get-tuple-element.52, ...), kind=kLoop, calls=%fused_computation.42 | loop fusion | flops 13307904 | bytes 26390528 | tf_op jit(solution)/shard_map/sub | solution.py:43
  36.8 4.5 %multiply_subtract_fusion.2 = (f32[36,36,256]{2,1,0:T(8,128)S(1)}, f32[36,36,256]{2,1,0:T(8,128)S(1)}, f32[36,36,256]{2,1,0:T(8,128)S(1)}) fusion(f32[38,38,256]{2,1,0:T(8,128)S(1)} %get-tuple-element.47, f32[38,38,256]{2,1,0:T(8,128)S(1)} %get-tuple-element.48, f32[40,40,256]{2,1,0:T(8,128)S(1)} %get-tuple-element.52, f32[38,38,256]{2,1,0:T(8,128)S(1)} %get-tuple-element.49), kind=kLoop, calls=%fused_computation.63 | loop fusion | flops 11943936 | bytes 24788992 | tf_op jit(solution)/shard_map/sub | solution.py:43
  41.3 4.9 %multiply_subtract_fusion.3 = (f32[34,34,256]{2,1,0:T(8,128)S(1)}, f32[34,34,256]{2,1,0:T(8,128)S(1)}, f32[34,34,256]{2,1,0:T(8,128)}) fusion(f32[36,36,256]{2,1,0:T(8,128)S(1)} %get-tuple-element.44, f32[36,36,256]{2,1,0:T(8,128)S(1)} %get-tuple-element.45, f32[40,40,256]{2,1,0:T(8,128)S(1)} %get-tuple-element.52, f32[36,36,256]{2,1,0:T(8,128)S(1)} %get-tuple-element.46), kind=kLoop, calls=%fused_computation.84 | loop fusion | flops 10653696 | bytes 23212032 | tf_op jit(solution)/shard_map/sub | solution.py:43
  46.2 2.4 %bitcast_reduce_fusion = (f32[16,32,256]{2,1,0:T(8,128)S(1)}, f32[32,32,256]{2,1,0:T(8,128)}) fusion(f32[34,34,256]{2,1,0:T(8,128)S(1)} %get-tuple-element.41, f32[34,34,256]{2,1,0:T(8,128)S(1)} %get-tuple-element.42, f32[40,40,256]{2,1,0:T(8,128)S(1)} %get-tuple-element.52), kind=kLoop, calls=%fused_computation.107 | loop fusion | flops 5636096 | bytes 10305536 | tf_op jit(solution)/shard_map/reduce_sum | solution.py:68
  49.3 0.5 copy.190
  49.8 1.0 reshape.42
  50.9 14.6 %all-to-all-start = ((f32[16,1,2048]{2,1,0:T(1,128)}), f32[16,1,2048]{2,1,0:T(1,128)S(1)}, u32[]{:S(2)}, u32[]{:S(2)}) async-start(f32[16,1,2048]{2,1,0:T(1,128)} %reshape.42), calls=%async_computation | async-start | bytes 262144 | tf_op jit(solution)/shard_map/all_to_all | solution.py:126
  65.5 2.0 %pad_maximum_fusion.9 = (f32[6,22,3,256]{3,1,2,0:T(8,128)}, f32[6,22,3,256]{3,1,2,0:T(8,128)}) fusion(f32[6,3,8,256]{3,1,2,0:T(4,128)S(1)} %collective-permute-done.9, f32[6,16,8,256]{3,1,2,0:T(8,128)S(1)} %copy_dynamic-update-slice_fusion, f32[6,3,8,256]{3,1,2,0:T(4,128)} %collective-permute-done.8), kind=kLoop, calls=%fused_computation.154 | loop fusion | flops 405504 | bytes 1892352 | tf_op jit(solution)/shard_map/slice | solution.py:26
  67.5 1.3 collective-permute-start.11
  68.8 5.3 %collective-permute-start.10 = (f32[6,22,3,256]{3,1,2,0:T(8,128)}, f32[6,22,3,256]{3,1,2,0:T(8,128)}, u32[]{:S(2)}, u32[]{:S(2)}) collective-permute-start(f32[6,22,3,256]{3,1,2,0:T(8,128)} %get-tuple-element.59), channel_id=1, source_target_pairs={{0,1},{1,2},{2,3},{3,4},{4,5},{5,6},{6,7},{7,8},{8,9},{9,10},{10,1... | collective-permute-start | bytes 1216520 | tf_op jit(solution)/shard_map/ppermute | solution.py:25
  74.1 1.4 %all-to-all-done = f32[16,1,2048]{2,1,0:T(1,128)S(1)} async-done(((f32[16,1,2048]{2,1,0:T(1,128)}), f32[16,1,2048]{2,1,0:T(1,128)S(1)}, u32[]{:S(2)}, u32[]{:S(2)}) %all-to-all-start) | async-done | bytes 131104 | tf_op jit(solution)/shard_map/all_to_all | solution.py:126
  75.5 0.6 broadcast.198
  76.1 0.9 reduce
  77.9 0.5 copy-done.2
  78.5 3.7 %collective-permute-start.5 = (f32[3,8,256]{2,0,1:T(4,128)S(1)}, f32[3,8,256]{2,0,1:T(4,128)S(1)}, u32[]{:S(2)}, u32[]{:S(2)}) collective-permute-start(f32[3,8,256]{2,0,1:T(4,128)S(1)} %reshape.41), channel_id=1, source_target_pairs={{16,0},{32,16},{48,32},{64,48},{80,64},{96,80},{112,96},{128,112},... | collective-permute-start | bytes 73736 | tf_op jit(solution)/shard_map/ppermute | solution.py:28
  82.3 0.8 reshape.39
  83.0 2.0 %collective-permute-start.4 = (f32[3,8,256]{2,0,1:T(4,128)}, f32[3,8,256]{2,0,1:T(4,128)S(1)}, u32[]{:S(2)}, u32[]{:S(2)}) collective-permute-start(f32[3,8,256]{2,0,1:T(4,128)} %reshape.39), channel_id=1, source_target_pairs={{0,16},{16,32},{32,48},{48,64},{64,80},{80,96},{96,112},{112,128},... | collective-permute-start | bytes 73736 | tf_op jit(solution)/shard_map/ppermute | solution.py:25
  85.1 1.8 %pad_maximum_fusion.1 = f32[6,22,14,256]{3,1,2,0:T(8,128)S(1)} fusion(f32[6,22,3,256]{3,1,2,0:T(8,128)} %collective-permute-done.11, f32[6,3,8,256]{3,1,2,0:T(4,128)} %copy-done.7, f32[6,16,8,256]{3,1,2,0:T(8,128)} %copy-done.4, f32[6,3,8,256]{3,1,2,0:T(4,128)} %collective-permute-done.8, f32[6,22,3,256]{3,1,2,0:T(8,128)} %collective-permute-done.10), kind=kLoop, calls=%fused_computation.17 | loop fusion | flops 1892352 | bytes 3784704 | tf_op jit(solution)/shard_map/concatenate | solution.py:29
  86.9 1.6 %copy.207 = f32[16,8,16,16]{3,2,0,1:T(8,128)} copy(f32[16,8,16,16]{3,0,1,2:T(8,128)S(1)} %bitcast.58) | data formatting | bytes 262144 | tf_op jit(solution)/shard_map/all_to_all | solution.py:126
  88.5 2.3 %reshape.40 = f32[16,8,256]{2,0,1:T(8,128)} reshape(f32[16,8,16,16]{3,2,0,1:T(8,128)} %copy.207) | data formatting | bytes 262144 | tf_op jit(solution)/shard_map/all_to_all | solution.py:126
  90.7 2.1 %collective-permute-done.4 = f32[3,8,256]{2,0,1:T(4,128)S(1)} collective-permute-done((f32[3,8,256]{2,0,1:T(4,128)}, f32[3,8,256]{2,0,1:T(4,128)S(1)}, u32[]{:S(2)}, u32[]{:S(2)}) %collective-permute-start.4) | collective-permute-done | bytes 24608 | tf_op jit(solution)/shard_map/ppermute | solution.py:25
  92.8 0.8 pad_maximum_fusion.16
  93.7 1.3 collective-permute-start.7
  95.0 4.7 %collective-permute-start.6 = (f32[22,3,256]{2,0,1:T(8,128)S(1)}, f32[22,3,256]{2,0,1:T(8,128)S(1)}, u32[]{:S(2)}, u32[]{:S(2)}) collective-permute-start(f32[22,3,256]{2,0,1:T(8,128)S(1)} %get-tuple-element.73), channel_id=1, source_target_pairs={{0,1},{1,2},{2,3},{3,4},{4,5},{5,6},{6,7},{7,8},{8,9},{9,10},{10,1... | collective-permute-start | bytes 202760 | tf_op jit(solution)/shard_map/ppermute | solution.py:25
  100.0 1.6 %collective-permute-done.6 = f32[22,3,256]{2,0,1:T(8,128)S(1)} collective-permute-done((f32[22,3,256]{2,0,1:T(8,128)S(1)}, f32[22,3,256]{2,0,1:T(8,128)S(1)}, u32[]{:S(2)}, u32[]{:S(2)}) %collective-permute-start.6) | collective-permute-done | bytes 67616 | tf_op jit(solution)/shard_map/ppermute | solution.py:25
  102.6 1.0 fusion.67
  103.8 0.8 fusion.78
  105.2 1.3 copy.200
  106.6 2.3 %reshape.44 = f32[16,1,2048]{2,1,0:T(1,128)} reshape(f32[256,8,16]{2,1,0:T(8,128)} %bitcast.60) | data formatting | bytes 262144
  108.8 11.1 %all-to-all-start.1 = ((f32[16,1,2048]{2,1,0:T(1,128)}), f32[16,1,2048]{2,1,0:T(1,128)S(1)}, u32[]{:S(2)}, u32[]{:S(2)}) async-start(f32[16,1,2048]{2,1,0:T(1,128)} %reshape.44), calls=%async_computation.1 | async-start | bytes 262144 | tf_op jit(solution)/shard_map/all_to_all | solution.py:140
  119.9 1.7 %fusion.48 = f32[32,32,256]{2,1,0:T(8,128)} fusion(f32[34,34,256]{2,1,0:T(8,128)S(1)} %get-tuple-element.41, f32[34,34,256]{2,1,0:T(8,128)S(1)} %copy-done.5), kind=kLoop, calls=%fused_computation.92 | loop fusion | flops 2359296 | bytes 8732672 | tf_op jit(solution)/shard_map/add | solution.py:48
  121.7 1.0 copy.203
  122.6 7.3 %all-to-all-done.1 = f32[16,1,2048]{2,1,0:T(1,128)S(1)} async-done(((f32[16,1,2048]{2,1,0:T(1,128)}), f32[16,1,2048]{2,1,0:T(1,128)S(1)}, u32[]{:S(2)}, u32[]{:S(2)}) %all-to-all-start.1) | async-done | bytes 131104 | tf_op jit(solution)/shard_map/all_to_all | solution.py:140
  130.0 0.9 reduce.1
  131.3 0.9 copy.202
  132.2 1.0 copy.204
  (66 shorter events, 5.4 us)
Async XLA Ops:
  0.6 1.7 %copy-start = (f32[32,32,256]{2,1,0:T(8,128)S(1)}, f32[32,32,256]{2,1,0:T(8,128)}, u32[]{:S(2)}) copy-start(f32[32,32,256]{2,1,0:T(8,128)} %param.7) | copy-start | bytes 3145732
  0.6 1.8 %copy-start.1 = (f32[32,32,256]{2,1,0:T(8,128)S(1)}, f32[32,32,256]{2,1,0:T(8,128)}, u32[]{:S(2)}) copy-start(f32[32,32,256]{2,1,0:T(8,128)} %param.6) | copy-start | bytes 3145732
  2.5 9.6 %collective-permute-start.1 = (f32[3,4,32,256]{3,2,1,0:T(8,128)S(1)}, f32[3,4,32,256]{3,2,1,0:T(8,128)S(1)}, u32[]{:S(2)}, u32[]{:S(2)}) collective-permute-start(f32[3,4,32,256]{3,2,1,0:T(8,128)S(1)} %get-tuple-element.56), channel_id=1, source_target_pairs={{16,0},{32,16},{48,32},{64,48},{80,64},{96,80},{112,96},{128,112},... | collective-permute-start | bytes 1179656 | tf_op jit(solution)/shard_map/ppermute | solution.py:28
  6.9 17.4 %copy-start.8 = (f32[3,16,8,256]{3,2,1,0:T(8,128)S(1)}, f32[3,16,8,256]{3,2,1,0:T(8,128)}, u32[]{:S(2)}) copy-start(f32[3,16,8,256]{3,2,1,0:T(8,128)} %param.9) | copy-start | bytes 1179652
  6.9 17.6 %copy-start.9 = (f32[3,16,8,256]{3,2,1,0:T(8,128)S(1)}, f32[3,16,8,256]{3,2,1,0:T(8,128)}, u32[]{:S(2)}) copy-start(f32[3,16,8,256]{3,2,1,0:T(8,128)} %param.10) | copy-start | bytes 1179652
  6.9 11.3 %collective-permute-start = (f32[3,4,32,256]{3,2,1,0:T(8,128)S(1)}, f32[3,4,32,256]{3,2,1,0:T(8,128)S(1)}, u32[]{:S(2)}, u32[]{:S(2)}) collective-permute-start(f32[3,4,32,256]{3,2,1,0:T(8,128)S(1)} %get-tuple-element.55), channel_id=1, source_target_pairs={{0,16},{16,32},{32,48},{48,64},{64,80},{80,96},{96,112},{112,128},... | collective-permute-start | bytes 1179656 | tf_op jit(solution)/shard_map/ppermute | solution.py:25
  18.4 11.4 %collective-permute-start.3 = (f32[3,40,4,256]{3,2,1,0:T(4,128)S(1)}, f32[3,40,4,256]{3,2,1,0:T(4,128)S(1)}, u32[]{:S(2)}, u32[]{:S(2)}) collective-permute-start(f32[3,40,4,256]{3,2,1,0:T(4,128)S(1)} %get-tuple-element.54), channel_id=1, source_target_pairs={{1,0},{2,1},{3,2},{4,3},{5,4},{6,5},{7,6},{8,7},{9,8},{10,9},{11,1... | collective-permute-start | bytes 1474568 | tf_op jit(solution)/shard_map/ppermute | solution.py:28
  19.7 10.9 %collective-permute-start.2 = (f32[3,40,4,256]{3,2,1,0:T(4,128)S(1)}, f32[3,40,4,256]{3,2,1,0:T(4,128)S(1)}, u32[]{:S(2)}, u32[]{:S(2)}) collective-permute-start(f32[3,40,4,256]{3,2,1,0:T(4,128)S(1)} %get-tuple-element.53), channel_id=1, source_target_pairs={{0,1},{1,2},{2,3},{3,4},{4,5},{5,6},{6,7},{7,8},{8,9},{9,10},{10,1... | collective-permute-start | bytes 1474568 | tf_op jit(solution)/shard_map/ppermute | solution.py:25
  24.6 40.9 %copy-start.4 = (f32[6,16,8,256]{3,1,2,0:T(8,128)}, f32[6,16,8,256]{3,1,2,0:T(8,128)S(1)}, u32[]{:S(2)}) copy-start(f32[6,16,8,256]{3,1,2,0:T(8,128)S(1)} %copy_dynamic-update-slice_fusion) | copy-start | bytes 2359300
  25.5 39.9 %collective-permute-start.9 = (f32[6,3,8,256]{3,1,2,0:T(4,128)}, f32[6,3,8,256]{3,1,2,0:T(4,128)S(1)}, u32[]{:S(2)}, u32[]{:S(2)}) collective-permute-start(f32[6,3,8,256]{3,1,2,0:T(4,128)} %get-tuple-element.66), channel_id=1, source_target_pairs={{16,0},{32,16},{48,32},{64,48},{80,64},{96,80},{112,96},{128,112},... | collective-permute-start | bytes 442376 | tf_op jit(solution)/shard_map/ppermute | solution.py:28
  27.4 38.0 %collective-permute-start.8 = (f32[6,3,8,256]{3,1,2,0:T(4,128)}, f32[6,3,8,256]{3,1,2,0:T(4,128)}, u32[]{:S(2)}, u32[]{:S(2)}) collective-permute-start(f32[6,3,8,256]{3,1,2,0:T(4,128)} %get-tuple-element.65), channel_id=1, source_target_pairs={{0,16},{16,32},{32,48},{48,64},{64,80},{80,96},{96,112},{112,128},... | collective-permute-start | bytes 442376 | tf_op jit(solution)/shard_map/ppermute | solution.py:25
  46.1 2.7 %copy-start.10 = (f32[256,128,1]{1,0,2:T(8,128)S(1)}, f32[256,128,1]{1,0,2:T(8,128)}, u32[]{:S(2)}) copy-start(f32[256,128,1]{1,0,2:T(8,128)} %constant.99) | copy-start | bytes 393220
  50.9 24.6 %all-to-all-start = ((f32[16,1,2048]{2,1,0:T(1,128)}), f32[16,1,2048]{2,1,0:T(1,128)S(1)}, u32[]{:S(2)}, u32[]{:S(2)}) async-start(f32[16,1,2048]{2,1,0:T(1,128)} %reshape.42), calls=%async_computation | async-start | bytes 262144 | tf_op jit(solution)/shard_map/all_to_all | solution.py:126
  65.5 12.0 %copy-start.7 = (f32[6,3,8,256]{3,1,2,0:T(4,128)}, f32[6,3,8,256]{3,1,2,0:T(4,128)S(1)}, u32[]{:S(2)}) copy-start(f32[6,3,8,256]{3,1,2,0:T(4,128)S(1)} %collective-permute-done.9) | copy-start | bytes 442372
  67.5 17.5 %collective-permute-start.11 = (f32[6,22,3,256]{3,1,2,0:T(8,128)}, f32[6,22,3,256]{3,1,2,0:T(8,128)}, u32[]{:S(2)}, u32[]{:S(2)}) collective-permute-start(f32[6,22,3,256]{3,1,2,0:T(8,128)} %get-tuple-element.60), channel_id=1, source_target_pairs={{1,0},{2,1},{3,2},{4,3},{5,4},{6,5},{7,6},{8,7},{9,8},{10,9},{11,1... | collective-permute-start | bytes 1216520 | tf_op jit(solution)/shard_map/ppermute | solution.py:28
  68.8 16.3 %collective-permute-start.10 = (f32[6,22,3,256]{3,1,2,0:T(8,128)}, f32[6,22,3,256]{3,1,2,0:T(8,128)}, u32[]{:S(2)}, u32[]{:S(2)}) collective-permute-start(f32[6,22,3,256]{3,1,2,0:T(8,128)} %get-tuple-element.59), channel_id=1, source_target_pairs={{0,1},{1,2},{2,3},{3,4},{4,5},{5,6},{6,7},{7,8},{8,9},{9,10},{10,1... | collective-permute-start | bytes 1216520 | tf_op jit(solution)/shard_map/ppermute | solution.py:25
  77.4 1.0 copy-start.2
  78.5 12.2 %collective-permute-start.5 = (f32[3,8,256]{2,0,1:T(4,128)S(1)}, f32[3,8,256]{2,0,1:T(4,128)S(1)}, u32[]{:S(2)}, u32[]{:S(2)}) collective-permute-start(f32[3,8,256]{2,0,1:T(4,128)S(1)} %reshape.41), channel_id=1, source_target_pairs={{16,0},{32,16},{48,32},{64,48},{80,64},{96,80},{112,96},{128,112},... | collective-permute-start | bytes 73736 | tf_op jit(solution)/shard_map/ppermute | solution.py:28
  83.0 3.9 %copy-start.3 = (f32[128,16,16]{2,1,0:T(8,128)S(1)}, f32[128,16,16]{2,1,0:T(8,128)}, u32[]{:S(2)}) copy-start(f32[128,16,16]{2,1,0:T(8,128)} %copy-done.2) | copy-start | bytes 393220
  83.0 9.8 %collective-permute-start.4 = (f32[3,8,256]{2,0,1:T(4,128)}, f32[3,8,256]{2,0,1:T(4,128)S(1)}, u32[]{:S(2)}, u32[]{:S(2)}) collective-permute-start(f32[3,8,256]{2,0,1:T(4,128)} %reshape.39), channel_id=1, source_target_pairs={{0,16},{16,32},{32,48},{48,64},{64,80},{80,96},{96,112},{112,128},... | collective-permute-start | bytes 73736 | tf_op jit(solution)/shard_map/ppermute | solution.py:25
  93.7 6.3 %collective-permute-start.7 = (f32[22,3,256]{2,0,1:T(8,128)S(1)}, f32[22,3,256]{2,0,1:T(8,128)S(1)}, u32[]{:S(2)}, u32[]{:S(2)}) collective-permute-start(f32[22,3,256]{2,0,1:T(8,128)S(1)} %get-tuple-element.74), channel_id=1, source_target_pairs={{1,0},{2,1},{3,2},{4,3},{5,4},{6,5},{7,6},{8,7},{9,8},{10,9},{11,1... | collective-permute-start | bytes 202760 | tf_op jit(solution)/shard_map/ppermute | solution.py:28
  95.0 6.7 %copy-start.6 = (f32[16,8,256]{2,0,1:T(8,128)S(1)}, f32[16,8,256]{2,0,1:T(8,128)}, u32[]{:S(2)}) copy-start(f32[16,8,256]{2,0,1:T(8,128)} %reshape.40) | copy-start | bytes 393220
  95.0 6.7 %collective-permute-start.6 = (f32[22,3,256]{2,0,1:T(8,128)S(1)}, f32[22,3,256]{2,0,1:T(8,128)S(1)}, u32[]{:S(2)}, u32[]{:S(2)}) collective-permute-start(f32[22,3,256]{2,0,1:T(8,128)S(1)} %get-tuple-element.73), channel_id=1, source_target_pairs={{0,1},{1,2},{2,3},{3,4},{4,5},{5,6},{6,7},{7,8},{8,9},{9,10},{10,1... | collective-permute-start | bytes 202760 | tf_op jit(solution)/shard_map/ppermute | solution.py:25
  105.2 14.7 %copy-start.5 = (f32[34,34,256]{2,1,0:T(8,128)S(1)}, f32[34,34,256]{2,1,0:T(8,128)}, u32[]{:S(2)}) copy-start(f32[34,34,256]{2,1,0:T(8,128)} %get-tuple-element.43) | copy-start | bytes 3551236
  108.8 21.2 %all-to-all-start.1 = ((f32[16,1,2048]{2,1,0:T(1,128)}), f32[16,1,2048]{2,1,0:T(1,128)S(1)}, u32[]{:S(2)}, u32[]{:S(2)}) async-start(f32[16,1,2048]{2,1,0:T(1,128)} %reshape.44), calls=%async_computation.1 | async-start | bytes 262144 | tf_op jit(solution)/shard_map/all_to_all | solution.py:140

commit v2 on v1

--- a/solution.py
+++ b/solution.py
@@ -28,6 +28,36 @@
         high = lax.ppermute(lax.slice_in_dim(block, 0, width, axis=dim), axis, backward)
         block = jnp.concatenate([low, block, high], axis=dim)
     return block
+
+
+def halo_2d(block, dims, width):
+    (ax0, d0), (ax1, d1) = dims
+    n0, n1 = lax.axis_size(ax0), lax.axis_size(ax1)
+    w = width
+
+    def part(v, dim, side):
+        if side > 0:
+            return lax.slice_in_dim(v, v.shape[dim] - w, None, axis=dim)
+        if side < 0:
+            return lax.slice_in_dim(v, 0, w, axis=dim)
+        return v
+
+    got = {}
+    for s0 in (-1, 0, 1):
+        for s1 in (-1, 0, 1):
+            if s0 == 0 and s1 == 0:
+                continue
+            piece = part(part(block, d0, s0), d1, s1)
+            pairs = []
+            for i in range(n0):
+                for j in range(n1):
+                    ti, tj = i + s0, j + s1
+                    if 0 <= ti < n0 and 0 <= tj < n1:
+                        pairs.append((i * n1 + j, ti * n1 + tj))
+            got[(s0, s1)] = lax.ppermute(piece, (ax0, ax1), pairs)
+    got[(0, 0)] = block
+    rows = [jnp.concatenate([got[(s0, 1)], got[(s0, 0)], got[(s0, -1)]], axis=d1) for s0 in (1, 0, -1)]
+    return jnp.concatenate(rows, axis=d0)
 
 
 def fine_laplace(padded):
@@ -113,18 +143,18 @@
 def on_device(concentration, order_field, phase_labels, displacement, body_load):
     h = FINE_HALO
     fields = jnp.stack([concentration, order_field, mobility_of(phase_labels)])
-    fields = padded_2(fields, (("gx", 1), ("gy", 2)), h)
+    fields = halo_2d(fields, (("gx", 1), ("gy", 2)), h)
     conc, order, mob = fields[0], fields[1], fields[2]
     for step in range(STEPS):
         conc, order, mob = advance(conc, order, mob, step == STEPS - 1)
 
     m = MECH_HALO
-    ub = padded_2(jnp.concatenate([displacement, body_load]), (("gx", 1), ("gy", 2)), m)
+    ub = halo_2d(jnp.concatenate([displacement, body_load]), (("gx", 1), ("gy", 2)), m)
     disp, load = ub[:3], ub[3:]
 
     coarse = restrict_xzy(order)
     stiff = lax.all_to_all(coarse, "gy", split_axis=1, concat_axis=2, tiled=True)
-    stiff_pad = padded_2(stiff, (("gx", 0), ("gy", 1)), m)
+    stiff_pad = halo_2d(stiff, (("gx", 0), ("gy", 1)), m)
 
     faces, diag, center = face_terms(stiff_pad)
     for weight in (first_weight, second_weight):

time: 135 us -> 201 us (1.49)
  starting transfers between devices: 60.5 us -> 114 us
  local copies, waits for them, and re-layouts: 17.9 us -> 28.6 us
  other arithmetic: 30.6 us -> 33 us
    ppermute x12 -> x24, starting transfers between devices: 34.9 us -> 76.5 us  [halo_2d(): got[s0, s1] = lax.ppermute(piece, (ax0, ax1), pairs)]
    all_to_all x1, starting transfers between devices: 14.6 us -> 22.5 us  [on_device(): lax.all_to_all(coarse, 'gy', split_axis=1, concat_axis=2, tiled=True)]
    slice x6 -> x11, local copies, waits for them, and re-layouts: 1.91 us -> 8.15 us  [the longest x9 6.38 us: part(): return lax.slice_in_dim(v, v.shape[dim] - w, None, axis=dim)]
    ppermute x12 -> x24, waiting for transfers between devices: 13.7 us -> 7.53 us  [halo_2d(): got[s0, s1] = lax.ppermute(piece, (ax0, ax1), pairs)]
    all_to_all x1, waiting for transfers between devices: 1.38 us -> 7.48 us  [on_device(): lax.all_to_all(coarse, 'gy', split_axis=1, concat_axis=2, tiled=True)]
    concatenate x3, other arithmetic: 2.85 us -> 6.65 us  [halo_2d(): return jnp.concatenate(rows, axis=d0)]
    all_to_all x1, starting transfers between devices: 11.1 us -> 14.8 us  [on_device(): lax.all_to_all(energy, 'gy', split_axis=2, concat_axis=1, tiled=True)]
    slice x4 -> x3, other arithmetic: 3.11 us -> 0.26 us  [part(): return lax.slice_in_dim(v, v.shape[dim] - w, None, axis=dim)]
  transfers between devices with their start and end apart: 14 -> 26, of which waited for: 7 -> 5; matrix products, arithmetic and copies ran while one was open for 26% -> 19% of each run, Pallas kernels for 0% -> 0%
where the time goes in v2:
time: 201 us; the launch traced here: 200 us
  starting transfers between devices  114 us (57%)
  other arithmetic  33 us (16%)
  local copies, waits for them, and re-layouts  28.6 us (14%)
  waiting for transfers between devices  22.4 us (11%)
    ppermute x24, starting transfers between devices, halo_2d(): got[s0, s1] = lax.ppermute(piece, (ax0, ax1), pairs)  76.5 us
    all_to_all x1, starting transfers between devices, on_device(): lax.all_to_all(coarse, 'gy', split_axis=1, concat_axis=2, tiled=True)  22.5 us
    all_to_all x1, starting transfers between devices, on_device(): lax.all_to_all(energy, 'gy', split_axis=2, concat_axis=1, tiled=True)  14.8 us
    sub x4, other arithmetic, advance(): chem = conc_pad - order_pad * order_pad * (3.0 - 2.0 * order_pad)  14.1 us
    unnamed x31, local copies, waits for them, and re-layouts  8.93 us
    ppermute x24, waiting for transfers between devices, halo_2d(): got[s0, s1] = lax.ppermute(piece, (ax0, ax1), pairs)  7.53 us
    all_to_all x1, waiting for transfers between devices, on_device(): lax.all_to_all(coarse, 'gy', split_axis=1, concat_axis=2, tiled=True)  7.48 us
    all_to_all x1, waiting for transfers between devices, on_device(): lax.all_to_all(energy, 'gy', split_axis=2, concat_axis=1, tiled=True)  7.34 us
  transfers between devices with their start and end apart: 26, of which 5 were waited for; matrix products, arithmetic and copies ran while one was open for 19% of the time, Pallas kernels for 0%

profile of v2, /device:TPU:2, one launch (start us, length us, event | category | flops | bytes accessed | tf_op | source)
XLA Modules:
  0.0 199.6 jit_solution(13484975278665444291)
XLA Ops:
  0.7 1.6 add_bitcast_fusion
  2.5 1.3 collective-permute-start.7
  3.9 4.3 %collective-permute-start.6 = (f32[3,4,32,256]{3,2,1,0:T(8,128)S(1)}, f32[3,4,32,256]{3,2,1,0:T(8,128)S(1)}, u32[]{:S(2)}, u32[]{:S(2)}) collective-permute-start(f32[3,4,32,256]{3,2,1,0:T(8,128)S(1)} %get-tuple-element.58), channel_id=1, source_target_pairs={{16,0},{17,1},{18,2},{19,3},{20,4},{21,5},{22,6},{23,7},{24,8},{25... | collective-permute-start | bytes 1179656 | tf_op jit(solution)/shard_map/ppermute | solution.py:57
  8.3 4.7 %collective-permute-start.5 = (f32[3,4,4,256]{3,2,1,0:T(4,128)S(1)}, f32[3,4,4,256]{3,2,1,0:T(4,128)S(1)}, u32[]{:S(2)}, u32[]{:S(2)}) collective-permute-start(f32[3,4,4,256]{3,2,1,0:T(4,128)S(1)} %get-tuple-element.54), channel_id=1, source_target_pairs={{16,1},{17,2},{18,3},{19,4},{20,5},{21,6},{22,7},{23,8},{24,9},{25... | collective-permute-start | bytes 147464 | tf_op jit(solution)/shard_map/ppermute | solution.py:57
  13.1 1.3 collective-permute-start.4
  14.4 4.6 %collective-permute-start.3 = (f32[3,32,4,256]{3,2,1,0:T(4,128)S(1)}, f32[3,32,4,256]{3,2,1,0:T(4,128)S(1)}, u32[]{:S(2)}, u32[]{:S(2)}) collective-permute-start(f32[3,32,4,256]{3,2,1,0:T(4,128)S(1)} %get-tuple-element.59), channel_id=1, source_target_pairs={{0,1},{1,2},{2,3},{3,4},{4,5},{5,6},{6,7},{7,8},{8,9},{9,10},{10,1... | collective-permute-start | bytes 1179656 | tf_op jit(solution)/shard_map/ppermute | solution.py:57
  19.4 1.3 collective-permute-start.2
  20.7 1.9 collective-permute-start.1
  23.5 4.4 %collective-permute-done.2 = f32[3,4,4,256]{3,2,1,0:T(4,128)S(1)} collective-permute-done((f32[3,4,4,256]{3,2,1,0:T(4,128)S(1)}, f32[3,4,4,256]{3,2,1,0:T(4,128)S(1)}, u32[]{:S(2)}, u32[]{:S(2)}) %collective-permute-start.2) | collective-permute-done | bytes 49184 | tf_op jit(solution)/shard_map/ppermute | solution.py:57
  27.9 3.3 %collective-permute-start = (f32[3,4,4,256]{3,2,1,0:T(4,128)S(1)}, f32[3,4,4,256]{3,2,1,0:T(4,128)S(1)}, u32[]{:S(2)}, u32[]{:S(2)}) collective-permute-start(f32[3,4,4,256]{3,2,1,0:T(4,128)S(1)} %get-tuple-element.53), channel_id=1, source_target_pairs={{0,17},{1,18},{2,19},{3,20},{4,21},{5,22},{6,23},{7,24},{8,25},{9,... | collective-permute-start | bytes 147464 | tf_op jit(solution)/shard_map/ppermute | solution.py:57
  31.3 1.8 collective-permute-done
  33.1 1.3 collective-permute-start.23
  34.4 8.2 %collective-permute-start.21 = (f32[6,3,3,256]{3,1,2,0:T(4,128)S(1)}, f32[6,3,3,256]{3,1,2,0:T(4,128)S(1)}, u32[]{:S(2)}, u32[]{:S(2)}) collective-permute-start(f32[6,3,3,256]{3,1,2,0:T(4,128)S(1)} %get-tuple-element.69), channel_id=1, source_target_pairs={{16,1},{17,2},{18,3},{19,4},{20,5},{21,6},{22,7},{23,8},{24,9},{25... | collective-permute-start | bytes 165896 | tf_op jit(solution)/shard_map/ppermute | solution.py:57
  42.5 1.3 collective-permute-start.20
  43.8 7.6 %collective-permute-start.19 = (f32[6,16,3,256]{3,1,2,0:T(8,128)S(1)}, f32[6,16,3,256]{3,1,2,0:T(8,128)}, u32[]{:S(2)}, u32[]{:S(2)}) collective-permute-start(f32[6,16,3,256]{3,1,2,0:T(8,128)S(1)} %get-tuple-element.73), channel_id=1, source_target_pairs={{0,1},{1,2},{2,3},{3,4},{4,5},{5,6},{6,7},{7,8},{8,9},{9,10},{10,1... | collective-permute-start | bytes 884744 | tf_op jit(solution)/shard_map/ppermute | solution.py:57
  51.5 1.3 collective-permute-start.18
  52.8 3.9 %maximum_maximum_fusion = f32[3,40,40,256]{3,2,1,0:T(8,128)S(1)} fusion(f32[3,4,4,256]{3,2,1,0:T(4,128)S(1)} %collective-permute-done.7, f32[3,4,32,256]{3,2,1,0:T(8,128)S(1)} %collective-permute-done.6, f32[3,4,4,256]{3,2,1,0:T(4,128)S(1)} %collective-permute-done.5, f32[3,32,4,256]{3,2,1,0:T(4,128)S(1)} %collective-permute-done.4, ...), kind=kLoop, calls=%fused_computation | loop fusion | flops 12288000 | bytes 9830400 | tf_op jit(solution)/shard_map/concatenate | solution.py:60
  57.3 4.5 %multiply_subtract_fusion.1 = (f32[38,38,256]{2,1,0:T(8,128)S(1)}, f32[38,38,256]{2,1,0:T(8,128)S(1)}, f32[38,38,256]{2,1,0:T(8,128)S(1)}) fusion(f32[40,40,256]{2,1,0:T(8,128)S(1)} %multiply_subtract_fusion, f32[40,40,256]{2,1,0:T(8,128)S(1)} %get-tuple-element.51, f32[40,40,256]{2,1,0:T(8,128)S(1)} %get-tuple-element.52, ...), kind=kLoop, calls=%fused_computation.42 | loop fusion | flops 13307904 | bytes 26390528 | tf_op jit(solution)/shard_map/sub | solution.py:73
  61.9 4.5 %multiply_subtract_fusion.2 = (f32[36,36,256]{2,1,0:T(8,128)S(1)}, f32[36,36,256]{2,1,0:T(8,128)S(1)}, f32[36,36,256]{2,1,0:T(8,128)S(1)}) fusion(f32[38,38,256]{2,1,0:T(8,128)S(1)} %get-tuple-element.47, f32[38,38,256]{2,1,0:T(8,128)S(1)} %get-tuple-element.48, f32[40,40,256]{2,1,0:T(8,128)S(1)} %get-tuple-element.52, f32[38,38,256]{2,1,0:T(8,128)S(1)} %get-tuple-element.49), kind=kLoop, calls=%fused_computation.63 | loop fusion | flops 11943936 | bytes 24788992 | tf_op jit(solution)/shard_map/sub | solution.py:73
  66.4 4.8 %multiply_subtract_fusion.3 = (f32[34,34,256]{2,1,0:T(8,128)S(1)}, f32[34,34,256]{2,1,0:T(8,128)S(1)}, f32[34,34,256]{2,1,0:T(8,128)}) fusion(f32[36,36,256]{2,1,0:T(8,128)S(1)} %get-tuple-element.44, f32[36,36,256]{2,1,0:T(8,128)S(1)} %get-tuple-element.45, f32[40,40,256]{2,1,0:T(8,128)S(1)} %get-tuple-element.52, f32[36,36,256]{2,1,0:T(8,128)S(1)} %get-tuple-element.46), kind=kLoop, calls=%fused_computation.84 | loop fusion | flops 10653696 | bytes 23212032 | tf_op jit(solution)/shard_map/sub | solution.py:73
  71.2 2.4 %bitcast_reduce_fusion = (f32[16,32,256]{2,1,0:T(8,128)S(1)}, f32[32,32,256]{2,1,0:T(8,128)}) fusion(f32[34,34,256]{2,1,0:T(8,128)S(1)} %get-tuple-element.41, f32[34,34,256]{2,1,0:T(8,128)S(1)} %get-tuple-element.42, f32[40,40,256]{2,1,0:T(8,128)S(1)} %get-tuple-element.52), kind=kLoop, calls=%fused_computation.107 | loop fusion | flops 5636096 | bytes 10305536 | tf_op jit(solution)/shard_map/reduce_sum | solution.py:98
  73.9 1.9 collective-permute-start.22
  75.9 2.4 %collective-permute-start.17 = (f32[6,3,8,256]{3,1,2,0:T(4,128)}, f32[6,3,8,256]{3,1,2,0:T(4,128)}, u32[]{:S(2)}, u32[]{:S(2)}) collective-permute-start(f32[6,3,8,256]{3,1,2,0:T(4,128)} %get-tuple-element.71), channel_id=1, source_target_pairs={{0,16},{1,17},{2,18},{3,19},{4,20},{5,21},{6,22},{7,23},{8,24},{9,... | collective-permute-start | bytes 442376 | tf_op jit(solution)/shard_map/ppermute | solution.py:57
  78.3 6.0 %collective-permute-start.16 = (f32[6,3,3,256]{3,1,2,0:T(4,128)S(1)}, f32[6,3,3,256]{3,1,2,0:T(4,128)}, u32[]{:S(2)}, u32[]{:S(2)}) collective-permute-start(f32[6,3,3,256]{3,1,2,0:T(4,128)S(1)} %get-tuple-element.67), channel_id=1, source_target_pairs={{0,17},{1,18},{2,19},{3,20},{4,21},{5,22},{6,23},{7,24},{8,25},{9,... | collective-permute-start | bytes 165896 | tf_op jit(solution)/shard_map/ppermute | solution.py:57
  86.3 22.5 %all-to-all-start = ((f32[16,1,2048]{2,1,0:T(1,128)}), f32[16,1,2048]{2,1,0:T(1,128)}, u32[]{:S(2)}, u32[]{:S(2)}) async-start(f32[16,1,2048]{2,1,0:T(1,128)} %reshape.42), calls=%async_computation | async-start | bytes 262144 | tf_op jit(solution)/shard_map/all_to_all | solution.py:156
  109.6 1.9 maximum_maximum_fusion.1
  111.5 7.5 %all-to-all-done = f32[16,1,2048]{2,1,0:T(1,128)} async-done(((f32[16,1,2048]{2,1,0:T(1,128)}), f32[16,1,2048]{2,1,0:T(1,128)}, u32[]{:S(2)}, u32[]{:S(2)}) %all-to-all-start) | async-done | bytes 131104 | tf_op jit(solution)/shard_map/all_to_all | solution.py:156
  119.5 2.4 %reduce = f32[16,2048]{1,0:T(8,128)} reduce(f32[16,1,2048]{2,1,0:T(1,128)} %all-to-all-done, f32[]{:T(128)} %broadcast.198), dimensions={1}, to_apply=%all_to_all.26.reduce_sub_computation | reduce | bytes 262148 | tf_op jit(solution)/shard_map/all_to_all | solution.py:156
  121.9 2.2 %reshape.43 = f32[128,16,16]{2,1,0:T(8,128)} reshape(f32[16,2048]{1,0:T(8,128)} %reduce) | data formatting | bytes 262144
  124.1 1.6 copy.235
  127.1 1.1 reshape.41
  128.8 2.1 %collective-permute-start.14 = (f32[3,8,256]{2,0,1:T(4,128)S(1)}, f32[3,8,256]{2,0,1:T(4,128)S(1)}, u32[]{:S(2)}, u32[]{:S(2)}) collective-permute-start(f32[3,8,256]{2,0,1:T(4,128)S(1)} %reshape.41), channel_id=1, source_target_pairs={{16,0},{17,1},{18,2},{19,3},{20,4},{21,5},{22,6},{23,7},{24,8},{25... | collective-permute-start | bytes 73736 | tf_op jit(solution)/shard_map/ppermute | solution.py:57
  130.9 1.7 copy.222
  134.2 2.2 %collective-permute-start.9 = (f32[3,8,256]{2,0,1:T(4,128)S(1)}, f32[3,8,256]{2,0,1:T(4,128)}, u32[]{:S(2)}, u32[]{:S(2)}) collective-permute-start(f32[3,8,256]{2,0,1:T(4,128)S(1)} %reshape.39), channel_id=1, source_target_pairs={{0,16},{1,17},{2,18},{3,19},{4,20},{5,21},{6,22},{7,23},{8,24},{9,... | collective-permute-start | bytes 73736 | tf_op jit(solution)/shard_map/ppermute | solution.py:57
  136.4 1.3 collective-permute-start.15
  137.7 7.8 %collective-permute-start.13 = (f32[3,3,256]{2,0,1:T(4,128)}, f32[3,3,256]{2,0,1:T(4,128)}, u32[]{:S(2)}, u32[]{:S(2)}) collective-permute-start(f32[3,3,256]{2,0,1:T(4,128)} %get-tuple-element.85), channel_id=1, source_target_pairs={{16,1},{17,2},{18,3},{19,4},{20,5},{21,6},{22,7},{23,8},{24,9},{25... | collective-permute-start | bytes 27656 | tf_op jit(solution)/shard_map/ppermute | solution.py:57
  145.5 2.8 %copy.224 = f32[16,8,16,16]{3,2,0,1:T(8,128)} copy(f32[16,8,16,16]{3,0,1,2:T(8,128)} %bitcast.60) | data formatting | bytes 262144 | tf_op jit(solution)/shard_map/all_to_all | solution.py:156
  148.3 2.3 %reshape.40 = f32[16,8,256]{2,0,1:T(8,128)} reshape(f32[16,8,16,16]{3,2,0,1:T(8,128)} %copy.224) | data formatting | bytes 262144 | tf_op jit(solution)/shard_map/all_to_all | solution.py:156
  150.6 1.3 collective-permute-start.10
  152.7 1.3 collective-permute-start.12
  154.0 5.3 %collective-permute-start.11 = (f32[16,3,256]{2,0,1:T(8,128)S(1)}, f32[16,3,256]{2,0,1:T(8,128)S(1)}, u32[]{:S(2)}, u32[]{:S(2)}) collective-permute-start(f32[16,3,256]{2,0,1:T(8,128)S(1)} %get-tuple-element.81), channel_id=1, source_target_pairs={{0,1},{1,2},{2,3},{3,4},{4,5},{5,6},{6,7},{7,8},{8,9},{9,10},{10,1... | collective-permute-start | bytes 147464 | tf_op jit(solution)/shard_map/ppermute | solution.py:57
  159.3 2.5 %collective-permute-start.8 = (f32[3,3,256]{2,0,1:T(4,128)}, f32[3,3,256]{2,0,1:T(4,128)S(1)}, u32[]{:S(2)}, u32[]{:S(2)}) collective-permute-start(f32[3,3,256]{2,0,1:T(4,128)} %get-tuple-element.83), channel_id=1, source_target_pairs={{0,17},{1,18},{2,19},{3,20},{4,21},{5,22},{6,23},{7,24},{8,25},{9,... | collective-permute-start | bytes 27656 | tf_op jit(solution)/shard_map/ppermute | solution.py:57
  162.2 1.3 collective-permute-done.8
  167.9 1.3 copy.214
  169.3 2.3 %reshape.44 = f32[16,1,2048]{2,1,0:T(1,128)} reshape(f32[256,8,16]{2,1,0:T(8,128)} %bitcast.62) | data formatting | bytes 262144
  171.5 14.8 %all-to-all-start.1 = ((f32[16,1,2048]{2,1,0:T(1,128)}), f32[16,1,2048]{2,1,0:T(1,128)S(1)}, u32[]{:S(2)}, u32[]{:S(2)}) async-start(f32[16,1,2048]{2,1,0:T(1,128)} %reshape.44), calls=%async_computation.1 | async-start | bytes 262144 | tf_op jit(solution)/shard_map/all_to_all | solution.py:170
  186.4 1.7 fusion.48
  189.1 7.3 %all-to-all-done.1 = f32[16,1,2048]{2,1,0:T(1,128)S(1)} async-done(((f32[16,1,2048]{2,1,0:T(1,128)}), f32[16,1,2048]{2,1,0:T(1,128)S(1)}, u32[]{:S(2)}, u32[]{:S(2)}) %all-to-all-start.1) | async-done | bytes 131104 | tf_op jit(solution)/shard_map/all_to_all | solution.py:170
  (96 shorter events, 19.0 us)
Async XLA Ops:
  0.6 1.7 copy-start
  0.6 1.8 copy-start.1
  2.5 16.8 %collective-permute-start.7 = (f32[3,4,4,256]{3,2,1,0:T(4,128)S(1)}, f32[3,4,4,256]{3,2,1,0:T(4,128)S(1)}, u32[]{:S(2)}, u32[]{:S(2)}) collective-permute-start(f32[3,4,4,256]{3,2,1,0:T(4,128)S(1)} %get-tuple-element.56), channel_id=1, source_target_pairs={{17,0},{18,1},{19,2},{20,3},{21,4},{22,5},{23,6},{24,7},{25,8},{26... | collective-permute-start | bytes 147464 | tf_op jit(solution)/shard_map/ppermute | solution.py:57
  3.9 30.4 %collective-permute-start.6 = (f32[3,4,32,256]{3,2,1,0:T(8,128)S(1)}, f32[3,4,32,256]{3,2,1,0:T(8,128)S(1)}, u32[]{:S(2)}, u32[]{:S(2)}) collective-permute-start(f32[3,4,32,256]{3,2,1,0:T(8,128)S(1)} %get-tuple-element.58), channel_id=1, source_target_pairs={{16,0},{17,1},{18,2},{19,3},{20,4},{21,5},{22,6},{23,7},{24,8},{25... | collective-permute-start | bytes 1179656 | tf_op jit(solution)/shard_map/ppermute | solution.py:57
  8.3 10.8 %copy-start.5 = (f32[3,16,8,256]{3,2,1,0:T(8,128)S(1)}, f32[3,16,8,256]{3,2,1,0:T(8,128)}, u32[]{:S(2)}) copy-start(f32[3,16,8,256]{3,2,1,0:T(8,128)} %param.9) | copy-start | bytes 1179652
  8.3 10.9 %copy-start.6 = (f32[3,16,8,256]{3,2,1,0:T(8,128)S(1)}, f32[3,16,8,256]{3,2,1,0:T(8,128)}, u32[]{:S(2)}) copy-start(f32[3,16,8,256]{3,2,1,0:T(8,128)} %param.10) | copy-start | bytes 1179652
  8.3 12.4 %collective-permute-start.5 = (f32[3,4,4,256]{3,2,1,0:T(4,128)S(1)}, f32[3,4,4,256]{3,2,1,0:T(4,128)S(1)}, u32[]{:S(2)}, u32[]{:S(2)}) collective-permute-start(f32[3,4,4,256]{3,2,1,0:T(4,128)S(1)} %get-tuple-element.54), channel_id=1, source_target_pairs={{16,1},{17,2},{18,3},{19,4},{20,5},{21,6},{22,7},{23,8},{24,9},{25... | collective-permute-start | bytes 147464 | tf_op jit(solution)/shard_map/ppermute | solution.py:57
  13.1 29.4 %collective-permute-start.4 = (f32[3,32,4,256]{3,2,1,0:T(4,128)S(1)}, f32[3,32,4,256]{3,2,1,0:T(4,128)S(1)}, u32[]{:S(2)}, u32[]{:S(2)}) collective-permute-start(f32[3,32,4,256]{3,2,1,0:T(4,128)S(1)} %get-tuple-element.60), channel_id=1, source_target_pairs={{1,0},{2,1},{3,2},{4,3},{5,4},{6,5},{7,6},{8,7},{9,8},{10,9},{11,1... | collective-permute-start | bytes 1179656 | tf_op jit(solution)/shard_map/ppermute | solution.py:57
  14.4 29.4 %collective-permute-start.3 = (f32[3,32,4,256]{3,2,1,0:T(4,128)S(1)}, f32[3,32,4,256]{3,2,1,0:T(4,128)S(1)}, u32[]{:S(2)}, u32[]{:S(2)}) collective-permute-start(f32[3,32,4,256]{3,2,1,0:T(4,128)S(1)} %get-tuple-element.59), channel_id=1, source_target_pairs={{0,1},{1,2},{2,3},{3,4},{4,5},{5,6},{6,7},{7,8},{8,9},{9,10},{10,1... | collective-permute-start | bytes 1179656 | tf_op jit(solution)/shard_map/ppermute | solution.py:57
  19.3 32.2 %copy-start.2 = (f32[6,16,8,256]{3,1,2,0:T(8,128)}, f32[6,16,8,256]{3,1,2,0:T(8,128)S(1)}, u32[]{:S(2)}) copy-start(f32[6,16,8,256]{3,1,2,0:T(8,128)S(1)} %copy_dynamic-update-slice_fusion) | copy-start | bytes 2359300
  19.4 8.5 %collective-permute-start.2 = (f32[3,4,4,256]{3,2,1,0:T(4,128)S(1)}, f32[3,4,4,256]{3,2,1,0:T(4,128)S(1)}, u32[]{:S(2)}, u32[]{:S(2)}) collective-permute-start(f32[3,4,4,256]{3,2,1,0:T(4,128)S(1)} %get-tuple-element.55), channel_id=1, source_target_pairs={{1,16},{2,17},{3,18},{4,19},{5,20},{6,21},{7,22},{8,23},{9,24},{10... | collective-permute-start | bytes 147464 | tf_op jit(solution)/shard_map/ppermute | solution.py:57
  20.7 30.8 %collective-permute-start.1 = (f32[3,4,32,256]{3,2,1,0:T(8,128)S(1)}, f32[3,4,32,256]{3,2,1,0:T(8,128)S(1)}, u32[]{:S(2)}, u32[]{:S(2)}) collective-permute-start(f32[3,4,32,256]{3,2,1,0:T(8,128)S(1)} %get-tuple-element.57), channel_id=1, source_target_pairs={{0,16},{1,17},{2,18},{3,19},{4,20},{5,21},{6,22},{7,23},{8,24},{9,... | collective-permute-start | bytes 1179656 | tf_op jit(solution)/shard_map/ppermute | solution.py:57
  27.9 5.2 %collective-permute-start = (f32[3,4,4,256]{3,2,1,0:T(4,128)S(1)}, f32[3,4,4,256]{3,2,1,0:T(4,128)S(1)}, u32[]{:S(2)}, u32[]{:S(2)}) collective-permute-start(f32[3,4,4,256]{3,2,1,0:T(4,128)S(1)} %get-tuple-element.53), channel_id=1, source_target_pairs={{0,17},{1,18},{2,19},{3,20},{4,21},{5,22},{6,23},{7,24},{8,25},{9,... | collective-permute-start | bytes 147464 | tf_op jit(solution)/shard_map/ppermute | solution.py:57
  33.1 40.8 %collective-permute-start.23 = (f32[6,3,3,256]{3,1,2,0:T(4,128)S(1)}, f32[6,3,3,256]{3,1,2,0:T(4,128)S(1)}, u32[]{:S(2)}, u32[]{:S(2)}) collective-permute-start(f32[6,3,3,256]{3,1,2,0:T(4,128)S(1)} %get-tuple-element.68), channel_id=1, source_target_pairs={{17,0},{18,1},{19,2},{20,3},{21,4},{22,5},{23,6},{24,7},{25,8},{26... | collective-permute-start | bytes 165896 | tf_op jit(solution)/shard_map/ppermute | solution.py:57
  34.4 41.5 %collective-permute-start.21 = (f32[6,3,3,256]{3,1,2,0:T(4,128)S(1)}, f32[6,3,3,256]{3,1,2,0:T(4,128)S(1)}, u32[]{:S(2)}, u32[]{:S(2)}) collective-permute-start(f32[6,3,3,256]{3,1,2,0:T(4,128)S(1)} %get-tuple-element.69), channel_id=1, source_target_pairs={{16,1},{17,2},{18,3},{19,4},{20,5},{21,6},{22,7},{23,8},{24,9},{25... | collective-permute-start | bytes 165896 | tf_op jit(solution)/shard_map/ppermute | solution.py:57
  42.5 66.3 %collective-permute-start.20 = (f32[6,16,3,256]{3,1,2,0:T(8,128)S(1)}, f32[6,16,3,256]{3,1,2,0:T(8,128)S(1)}, u32[]{:S(2)}, u32[]{:S(2)}) collective-permute-start(f32[6,16,3,256]{3,1,2,0:T(8,128)S(1)} %get-tuple-element.74), channel_id=1, source_target_pairs={{1,0},{2,1},{3,2},{4,3},{5,4},{6,5},{7,6},{8,7},{9,8},{10,9},{11,1... | collective-permute-start | bytes 884744 | tf_op jit(solution)/shard_map/ppermute | solution.py:57
  43.8 65.7 %collective-permute-start.19 = (f32[6,16,3,256]{3,1,2,0:T(8,128)S(1)}, f32[6,16,3,256]{3,1,2,0:T(8,128)}, u32[]{:S(2)}, u32[]{:S(2)}) collective-permute-start(f32[6,16,3,256]{3,1,2,0:T(8,128)S(1)} %get-tuple-element.73), channel_id=1, source_target_pairs={{0,1},{1,2},{2,3},{3,4},{4,5},{5,6},{6,7},{7,8},{8,9},{9,10},{10,1... | collective-permute-start | bytes 884744 | tf_op jit(solution)/shard_map/ppermute | solution.py:57
  51.5 26.8 %collective-permute-start.18 = (f32[6,3,3,256]{3,1,2,0:T(4,128)S(1)}, f32[6,3,3,256]{3,1,2,0:T(4,128)S(1)}, u32[]{:S(2)}, u32[]{:S(2)}) collective-permute-start(f32[6,3,3,256]{3,1,2,0:T(4,128)S(1)} %get-tuple-element.70), channel_id=1, source_target_pairs={{1,16},{2,17},{3,18},{4,19},{5,20},{6,21},{7,22},{8,23},{9,24},{10... | collective-permute-start | bytes 165896 | tf_op jit(solution)/shard_map/ppermute | solution.py:57
  71.2 13.1 %copy-start.8 = (f32[256,128,1]{1,0,2:T(8,128)S(1)}, f32[256,128,1]{1,0,2:T(8,128)}, u32[]{:S(2)}) copy-start(f32[256,128,1]{1,0,2:T(8,128)} %constant.99) | copy-start | bytes 393220
  73.9 10.4 %copy-start.9 = (f32[6,3,3,256]{3,1,2,0:T(4,128)}, f32[6,3,3,256]{3,1,2,0:T(4,128)S(1)}, u32[]{:S(2)}) copy-start(f32[6,3,3,256]{3,1,2,0:T(4,128)S(1)} %collective-permute-done.23) | copy-start | bytes 165892
  73.9 34.9 %collective-permute-start.22 = (f32[6,3,8,256]{3,1,2,0:T(4,128)}, f32[6,3,8,256]{3,1,2,0:T(4,128)}, u32[]{:S(2)}, u32[]{:S(2)}) collective-permute-start(f32[6,3,8,256]{3,1,2,0:T(4,128)} %get-tuple-element.72), channel_id=1, source_target_pairs={{16,0},{17,1},{18,2},{19,3},{20,4},{21,5},{22,6},{23,7},{24,8},{25... | collective-permute-start | bytes 442376 | tf_op jit(solution)/shard_map/ppermute | solution.py:57
  75.9 8.4 %copy-start.10 = (f32[6,3,3,256]{3,1,2,0:T(4,128)}, f32[6,3,3,256]{3,1,2,0:T(4,128)S(1)}, u32[]{:S(2)}) copy-start(f32[6,3,3,256]{3,1,2,0:T(4,128)S(1)} %collective-permute-done.21) | copy-start | bytes 165892
  75.9 33.0 %collective-permute-start.17 = (f32[6,3,8,256]{3,1,2,0:T(4,128)}, f32[6,3,8,256]{3,1,2,0:T(4,128)}, u32[]{:S(2)}, u32[]{:S(2)}) collective-permute-start(f32[6,3,8,256]{3,1,2,0:T(4,128)} %get-tuple-element.71), channel_id=1, source_target_pairs={{0,16},{1,17},{2,18},{3,19},{4,20},{5,21},{6,22},{7,23},{8,24},{9,... | collective-permute-start | bytes 442376 | tf_op jit(solution)/shard_map/ppermute | solution.py:57
  78.3 6.0 %copy-start.11 = (f32[6,3,3,256]{3,1,2,0:T(4,128)}, f32[6,3,3,256]{3,1,2,0:T(4,128)S(1)}, u32[]{:S(2)}) copy-start(f32[6,3,3,256]{3,1,2,0:T(4,128)S(1)} %collective-permute-done.18) | copy-start | bytes 165892
  78.3 30.5 %collective-permute-start.16 = (f32[6,3,3,256]{3,1,2,0:T(4,128)S(1)}, f32[6,3,3,256]{3,1,2,0:T(4,128)}, u32[]{:S(2)}, u32[]{:S(2)}) collective-permute-start(f32[6,3,3,256]{3,1,2,0:T(4,128)S(1)} %get-tuple-element.67), channel_id=1, source_target_pairs={{0,17},{1,18},{2,19},{3,20},{4,21},{5,22},{6,23},{7,24},{8,25},{9,... | collective-permute-start | bytes 165896 | tf_op jit(solution)/shard_map/ppermute | solution.py:57
  86.3 32.7 %all-to-all-start = ((f32[16,1,2048]{2,1,0:T(1,128)}), f32[16,1,2048]{2,1,0:T(1,128)}, u32[]{:S(2)}, u32[]{:S(2)}) async-start(f32[16,1,2048]{2,1,0:T(1,128)} %reshape.42), calls=%async_computation | async-start | bytes 262144 | tf_op jit(solution)/shard_map/all_to_all | solution.py:156
  108.9 0.7 copy-start.7
  128.8 34.7 %collective-permute-start.14 = (f32[3,8,256]{2,0,1:T(4,128)S(1)}, f32[3,8,256]{2,0,1:T(4,128)S(1)}, u32[]{:S(2)}, u32[]{:S(2)}) collective-permute-start(f32[3,8,256]{2,0,1:T(4,128)S(1)} %reshape.41), channel_id=1, source_target_pairs={{16,0},{17,1},{18,2},{19,3},{20,4},{21,5},{22,6},{23,7},{24,8},{25... | collective-permute-start | bytes 73736 | tf_op jit(solution)/shard_map/ppermute | solution.py:57
  134.2 29.2 %collective-permute-start.9 = (f32[3,8,256]{2,0,1:T(4,128)S(1)}, f32[3,8,256]{2,0,1:T(4,128)}, u32[]{:S(2)}, u32[]{:S(2)}) collective-permute-start(f32[3,8,256]{2,0,1:T(4,128)S(1)} %reshape.39), channel_id=1, source_target_pairs={{0,16},{1,17},{2,18},{3,19},{4,20},{5,21},{6,22},{7,23},{8,24},{9,... | collective-permute-start | bytes 73736 | tf_op jit(solution)/shard_map/ppermute | solution.py:57
  136.4 16.3 %collective-permute-start.15 = (f32[3,3,256]{2,0,1:T(4,128)}, f32[3,3,256]{2,0,1:T(4,128)}, u32[]{:S(2)}, u32[]{:S(2)}) collective-permute-start(f32[3,3,256]{2,0,1:T(4,128)} %get-tuple-element.86), channel_id=1, source_target_pairs={{17,0},{18,1},{19,2},{20,3},{21,4},{22,5},{23,6},{24,7},{25,8},{26... | collective-permute-start | bytes 27656 | tf_op jit(solution)/shard_map/ppermute | solution.py:57
  137.7 16.3 %collective-permute-start.13 = (f32[3,3,256]{2,0,1:T(4,128)}, f32[3,3,256]{2,0,1:T(4,128)}, u32[]{:S(2)}, u32[]{:S(2)}) collective-permute-start(f32[3,3,256]{2,0,1:T(4,128)} %get-tuple-element.85), channel_id=1, source_target_pairs={{16,1},{17,2},{18,3},{19,4},{20,5},{21,6},{22,7},{23,8},{24,9},{25... | collective-permute-start | bytes 27656 | tf_op jit(solution)/shard_map/ppermute | solution.py:57
  150.6 8.7 %collective-permute-start.10 = (f32[3,3,256]{2,0,1:T(4,128)}, f32[3,3,256]{2,0,1:T(4,128)S(1)}, u32[]{:S(2)}, u32[]{:S(2)}) collective-permute-start(f32[3,3,256]{2,0,1:T(4,128)} %get-tuple-element.84), channel_id=1, source_target_pairs={{1,16},{2,17},{3,18},{4,19},{5,20},{6,21},{7,22},{8,23},{9,24},{10... | collective-permute-start | bytes 27656 | tf_op jit(solution)/shard_map/ppermute | solution.py:57
  152.7 10.8 %collective-permute-start.12 = (f32[16,3,256]{2,0,1:T(8,128)S(1)}, f32[16,3,256]{2,0,1:T(8,128)S(1)}, u32[]{:S(2)}, u32[]{:S(2)}) collective-permute-start(f32[16,3,256]{2,0,1:T(8,128)S(1)} %get-tuple-element.82), channel_id=1, source_target_pairs={{1,0},{2,1},{3,2},{4,3},{5,4},{6,5},{7,6},{8,7},{9,8},{10,9},{11,1... | collective-permute-start | bytes 147464 | tf_op jit(solution)/shard_map/ppermute | solution.py:57
  154.0 9.5 %collective-permute-start.11 = (f32[16,3,256]{2,0,1:T(8,128)S(1)}, f32[16,3,256]{2,0,1:T(8,128)S(1)}, u32[]{:S(2)}, u32[]{:S(2)}) collective-permute-start(f32[16,3,256]{2,0,1:T(8,128)S(1)} %get-tuple-element.81), channel_id=1, source_target_pairs={{0,1},{1,2},{2,3},{3,4},{4,5},{5,6},{6,7},{7,8},{8,9},{9,10},{10,1... | collective-permute-start | bytes 147464 | tf_op jit(solution)/shard_map/ppermute | solution.py:57
  159.3 4.2 %copy-start.4 = (f32[16,8,256]{2,0,1:T(8,128)S(1)}, f32[16,8,256]{2,0,1:T(8,128)}, u32[]{:S(2)}) copy-start(f32[16,8,256]{2,0,1:T(8,128)} %reshape.40) | copy-start | bytes 393220
  159.3 4.1 %collective-permute-start.8 = (f32[3,3,256]{2,0,1:T(4,128)}, f32[3,3,256]{2,0,1:T(4,128)S(1)}, u32[]{:S(2)}, u32[]{:S(2)}) collective-permute-start(f32[3,3,256]{2,0,1:T(4,128)} %get-tuple-element.83), channel_id=1, source_target_pairs={{0,17},{1,18},{2,19},{3,20},{4,21},{5,22},{6,23},{7,24},{8,25},{9,... | collective-permute-start | bytes 27656 | tf_op jit(solution)/shard_map/ppermute | solution.py:57
  167.9 18.5 %copy-start.3 = (f32[34,34,256]{2,1,0:T(8,128)S(1)}, f32[34,34,256]{2,1,0:T(8,128)}, u32[]{:S(2)}) copy-start(f32[34,34,256]{2,1,0:T(8,128)} %get-tuple-element.43) | copy-start | bytes 3551236
  171.5 24.9 %all-to-all-start.1 = ((f32[16,1,2048]{2,1,0:T(1,128)}), f32[16,1,2048]{2,1,0:T(1,128)S(1)}, u32[]{:S(2)}, u32[]{:S(2)}) async-start(f32[16,1,2048]{2,1,0:T(1,128)} %reshape.44), calls=%async_computation.1 | async-start | bytes 262144 | tf_op jit(solution)/shard_map/all_to_all | solution.py:170

commit v3 on v1

--- a/solution.py
+++ b/solution.py
@@ -1,7 +1,11 @@
 import jax
 import jax.numpy as jnp
+import functools
+
 import numpy as np
 from jax import lax
+from jax.experimental import pallas as pl
+from jax.experimental.pallas import tpu as pltpu
 from jax.sharding import PartitionSpec as P
 
 STEPS = 4
@@ -15,6 +19,52 @@
 spring_term = 0.2
 first_weight = 0.5956
 second_weight = 2.695
+
+
+MESH = pl.DeviceIdType.MESH
+
+
+def exchange_kernel(n, src_ref, out_ref, recv, send_sem, recv_sem):
+    me = lax.axis_index("gy")
+    row = lax.axis_index("gx")
+    barrier = pltpu.get_barrier_semaphore()
+    for d in range(1, n):
+        peer = lax.rem(me + d, n)
+        pl.semaphore_signal(barrier, inc=1, device_id=(row, peer), device_id_type=MESH)
+    pl.semaphore_wait(barrier, n - 1)
+    copies = []
+    for d in range(1, n):
+        peer = lax.rem(me + d, n)
+        copy = pltpu.make_async_remote_copy(
+            src_ref=src_ref.at[peer],
+            dst_ref=recv.at[me],
+            send_sem=send_sem.at[d],
+            recv_sem=recv_sem.at[d],
+            device_id=(row, peer),
+            device_id_type=MESH,
+        )
+        copy.start()
+        copies.append(copy)
+    recv[me] = src_ref[me]
+    for copy in copies:
+        copy.wait()
+    out_ref[...] = recv[...]
+
+
+def all_to_all_gy(src, cid):
+    n = src.shape[0]
+    return pl.pallas_call(
+        functools.partial(exchange_kernel, n),
+        out_shape=jax.ShapeDtypeStruct(src.shape, src.dtype),
+        in_specs=[pl.BlockSpec(memory_space=pltpu.VMEM)],
+        out_specs=pl.BlockSpec(memory_space=pltpu.VMEM),
+        scratch_shapes=[
+            pltpu.VMEM(src.shape, src.dtype),
+            pltpu.SemaphoreType.DMA((n,)),
+            pltpu.SemaphoreType.DMA((n,)),
+        ],
+        compiler_params=pltpu.CompilerParams(collective_id=cid, has_side_effects=True),
+    )(src)
 
 
 def padded_2(block, sides, width):
@@ -123,7 +173,12 @@
     disp, load = ub[:3], ub[3:]
 
     coarse = restrict_xzy(order)
-    stiff = lax.all_to_all(coarse, "gy", split_axis=1, concat_axis=2, tiled=True)
+    n = lax.axis_size("gy")
+    cx, cz, cy = coarse.shape
+    zc = cz // n
+    src = coarse.reshape(cx, n, zc, cy).transpose(1, 0, 2, 3).reshape(n, cx, zc * cy)
+    got = all_to_all_gy(src, 0)
+    stiff = got.reshape(n, cx, zc, cy).transpose(1, 2, 0, 3).reshape(cx, zc, n * cy)
     stiff_pad = padded_2(stiff, (("gx", 0), ("gy", 1)), m)
 
     faces, diag, center = face_terms(stiff_pad)
@@ -137,8 +192,10 @@
         center = center[1:-1, 1:-1]
     energy = strain_energy(disp, faces)
     disp = disp[:, 1:-1, 1:-1]
-    tiles = lax.all_to_all(energy, "gy", split_axis=2, concat_axis=1, tiled=True)
-    return (conc, order, disp, jnp.transpose(tiles, (0, 2, 1)))
+    src = energy.reshape(cx, zc, n, cy).transpose(2, 0, 1, 3).reshape(n, cx, zc * cy)
+    got = all_to_all_gy(src, 1)
+    tiles = got.reshape(n, cx, zc, cy).transpose(1, 3, 0, 2).reshape(cx, cy, n * zc)
+    return (conc, order, disp, tiles)
 
 
 def solution(mesh):

time: 135 us -> 150 us (1.11)
  Pallas kernels: 0 us -> 40.2 us
  starting transfers between devices: 60.5 us -> 36.5 us
  local copies, waits for them, and re-layouts: 17.9 us -> 27.1 us
  waiting for transfers between devices: 22.5 us -> 16.7 us
  other arithmetic: 30.6 us -> 25.8 us
    pallas_call x0 -> x2, Pallas kernels: none -> 40.2 us  [all_to_all_gy(): pl.pallas_call(functools.partial(exchange_kernel, n), out_shape=jax.Shape...]
    all_to_all x2 -> x0, starting transfers between devices: 25.6 us -> none  [the longest x1 14.6 us: on_device(): lax.all_to_all(coarse, 'gy', split_axis=1, concat_axis=2, tiled=True)]
    reshape x0 -> x9, local copies, waits for them, and re-layouts: none -> 13.3 us  [the longest x4 7.24 us: on_device(): got.reshape(n, cx, zc, cy).transpose(1, 2, 0, 3).reshape(cx, zc, n * cy)]
    all_to_all x2 -> x0, waiting for transfers between devices: 8.73 us -> none  [the longest x1 7.35 us: on_device(): lax.all_to_all(energy, 'gy', split_axis=2, concat_axis=1, tiled=True)]
    all_to_all x5 -> x0, local copies, waits for them, and re-layouts: 5.69 us -> none  [the longest x4 4.76 us: on_device(): lax.all_to_all(coarse, 'gy', split_axis=1, concat_axis=2, tiled=True)]
    ppermute x6, waiting for transfers between devices: 3.2 us -> 7.72 us  [padded_2(): lax.ppermute(lax.slice_in_dim(block, 0, width, axis=dim), axis, backward)]
    ppermute x6, starting transfers between devices: 13.8 us -> 16.9 us  [padded_2(): lax.ppermute(lax.slice_in_dim(block, 0, width, axis=dim), axis, backward)]
    slice x4, other arithmetic: 3.11 us -> 0.38 us  [padded_2(): lax.slice_in_dim(block, block.shape[dim] - width, None, axis=dim)]
  transfers between devices with their start and end apart: 14 -> 12, of which waited for: 7 -> 7; matrix products, arithmetic and copies ran while one was open for 26% -> 7% of each run, Pallas kernels for 0% -> 0%
where the time goes in v3:
time: 150 us; the launch traced here: 149 us
  Pallas kernels  40.2 us (27%)
  starting transfers between devices  36.5 us (24%)
  local copies, waits for them, and re-layouts  27.1 us (18%)
  other arithmetic  25.8 us (17%)
  waiting for transfers between devices  16.7 us (11%)
    pallas_call x2, Pallas kernels, all_to_all_gy(): pl.pallas_call(functools.partial(exchange_kernel, n), out_shape=jax.Shape...  40.2 us
    ppermute x6, starting transfers between devices, padded_2(): lax.ppermute(lax.slice_in_dim(block, block.shape[dim] - width, None, axis...  19.6 us
    ppermute x6, starting transfers between devices, padded_2(): lax.ppermute(lax.slice_in_dim(block, 0, width, axis=dim), axis, backward)  16.9 us
    sub x4, other arithmetic, advance(): chem = conc_pad - order_pad * order_pad * (3.0 - 2.0 * order_pad)  14.1 us
    ppermute x6, waiting for transfers between devices, padded_2(): lax.ppermute(lax.slice_in_dim(block, block.shape[dim] - width, None, axis...  9 us
    ppermute x6, waiting for transfers between devices, padded_2(): lax.ppermute(lax.slice_in_dim(block, 0, width, axis=dim), axis, backward)  7.72 us
    reshape x4, local copies, waits for them, and re-layouts, on_device(): got.reshape(n, cx, zc, cy).transpose(1, 2, 0, 3).reshape(cx, zc, n * cy)  7.24 us
    unnamed x19, local copies, waits for them, and re-layouts  4.45 us
  transfers between devices with their start and end apart: 12, of which 7 were waited for; matrix products, arithmetic and copies ran while one was open for 7% of the time, Pallas kernels for 0%

profile of v3, /device:TPU:2, one launch (start us, length us, event | category | flops | bytes accessed | tf_op | source)
XLA Modules:
  0.0 148.7 jit_solution(9441398099828188790)
XLA Ops:
  0.7 1.6 %add_bitcast_fusion = f32[1,32,32,256]{3,2,1,0:T(8,128)S(1)} fusion(s32[32,32,256]{2,1,0:T(8,128)} %param.8), kind=kLoop, calls=%fused_computation.110 | loop fusion | flops 2097152 | bytes 2097152 | tf_op jit(solution)/shard_map/stack | solution.py:165
  2.5 4.5 %collective-permute-start.1 = (f32[3,4,32,256]{3,2,1,0:T(8,128)S(1)}, f32[3,4,32,256]{3,2,1,0:T(8,128)S(1)}, u32[]{:S(2)}, u32[]{:S(2)}) collective-permute-start(f32[3,4,32,256]{3,2,1,0:T(8,128)S(1)} %get-tuple-element.56), channel_id=1, source_target_pairs={{16,0},{32,16},{48,32},{64,48},{80,64},{96,80},{112,96},{128,112},... | collective-permute-start | bytes 1179656 | tf_op jit(solution)/shard_map/ppermute | solution.py:78
  7.0 1.9 %collective-permute-start = (f32[3,4,32,256]{3,2,1,0:T(8,128)S(1)}, f32[3,4,32,256]{3,2,1,0:T(8,128)S(1)}, u32[]{:S(2)}, u32[]{:S(2)}) collective-permute-start(f32[3,4,32,256]{3,2,1,0:T(8,128)S(1)} %get-tuple-element.55), channel_id=1, source_target_pairs={{0,16},{16,32},{32,48},{48,64},{64,80},{80,96},{96,112},{112,128},... | collective-permute-start | bytes 1179656 | tf_op jit(solution)/shard_map/ppermute | solution.py:75
  9.3 5.8 %collective-permute-start.9 = (f32[6,3,8,256]{3,1,2,0:T(4,128)S(1)}, f32[6,3,8,256]{3,1,2,0:T(4,128)S(1)}, u32[]{:S(2)}, u32[]{:S(2)}) collective-permute-start(f32[6,3,8,256]{3,1,2,0:T(4,128)S(1)} %get-tuple-element.66), channel_id=1, source_target_pairs={{16,0},{32,16},{48,32},{64,48},{80,64},{96,80},{112,96},{128,112},... | collective-permute-start | bytes 442376 | tf_op jit(solution)/shard_map/ppermute | solution.py:78
  15.1 1.9 %collective-permute-start.8 = (f32[6,3,8,256]{3,1,2,0:T(4,128)S(1)}, f32[6,3,8,256]{3,1,2,0:T(4,128)S(1)}, u32[]{:S(2)}, u32[]{:S(2)}) collective-permute-start(f32[6,3,8,256]{3,1,2,0:T(4,128)S(1)} %get-tuple-element.65), channel_id=1, source_target_pairs={{0,16},{16,32},{32,48},{48,64},{64,80},{80,96},{96,112},{112,128},... | collective-permute-start | bytes 442376 | tf_op jit(solution)/shard_map/ppermute | solution.py:75
  17.0 1.2 collective-permute-done.9
  18.2 5.9 %collective-permute-done.8 = f32[6,3,8,256]{3,1,2,0:T(4,128)S(1)} collective-permute-done((f32[6,3,8,256]{3,1,2,0:T(4,128)S(1)}, f32[6,3,8,256]{3,1,2,0:T(4,128)S(1)}, u32[]{:S(2)}, u32[]{:S(2)}) %collective-permute-start.8) | collective-permute-done | bytes 147488 | tf_op jit(solution)/shard_map/ppermute | solution.py:75
  24.3 1.3 collective-permute-start.11
  25.6 4.6 %collective-permute-start.10 = (f32[6,22,3,256]{3,1,2,0:T(8,128)S(1)}, f32[6,22,3,256]{3,1,2,0:T(8,128)S(1)}, u32[]{:S(2)}, u32[]{:S(2)}) collective-permute-start(f32[6,22,3,256]{3,1,2,0:T(8,128)S(1)} %get-tuple-element.59), channel_id=1, source_target_pairs={{0,1},{1,2},{2,3},{3,4},{4,5},{5,6},{6,7},{7,8},{8,9},{9,10},{10,1... | collective-permute-start | bytes 1216520 | tf_op jit(solution)/shard_map/ppermute | solution.py:75
  30.4 1.3 collective-permute-start.3
  31.7 4.6 %collective-permute-start.2 = (f32[3,40,4,256]{3,2,1,0:T(4,128)S(1)}, f32[3,40,4,256]{3,2,1,0:T(4,128)S(1)}, u32[]{:S(2)}, u32[]{:S(2)}) collective-permute-start(f32[3,40,4,256]{3,2,1,0:T(4,128)S(1)} %get-tuple-element.53), channel_id=1, source_target_pairs={{0,1},{1,2},{2,3},{3,4},{4,5},{5,6},{6,7},{7,8},{8,9},{9,10},{10,1... | collective-permute-start | bytes 1474568 | tf_op jit(solution)/shard_map/ppermute | solution.py:75
  36.3 2.6 %collective-permute-done.11 = f32[6,22,3,256]{3,1,2,0:T(8,128)S(1)} collective-permute-done((f32[6,22,3,256]{3,1,2,0:T(8,128)S(1)}, f32[6,22,3,256]{3,1,2,0:T(8,128)S(1)}, u32[]{:S(2)}, u32[]{:S(2)}) %collective-permute-start.11) | collective-permute-done | bytes 405536 | tf_op jit(solution)/shard_map/ppermute | solution.py:78
  38.9 1.2 collective-permute-done.10
  40.4 3.8 %collective-permute-done.3 = f32[3,40,4,256]{3,2,1,0:T(4,128)S(1)} collective-permute-done((f32[3,40,4,256]{3,2,1,0:T(4,128)S(1)}, f32[3,40,4,256]{3,2,1,0:T(4,128)S(1)}, u32[]{:S(2)}, u32[]{:S(2)}) %collective-permute-start.3) | collective-permute-done | bytes 491552 | tf_op jit(solution)/shard_map/ppermute | solution.py:78
  44.2 1.2 collective-permute-done.2
  45.4 1.0 pad_maximum_fusion
  47.0 4.5 %multiply_subtract_fusion.1 = (f32[38,38,256]{2,1,0:T(8,128)S(1)}, f32[38,38,256]{2,1,0:T(8,128)S(1)}, f32[38,38,256]{2,1,0:T(8,128)S(1)}) fusion(f32[40,40,256]{2,1,0:T(8,128)S(1)} %multiply_subtract_fusion, f32[40,40,256]{2,1,0:T(8,128)S(1)} %get-tuple-element.51, f32[40,40,256]{2,1,0:T(8,128)S(1)} %get-tuple-element.52, ...), kind=kLoop, calls=%fused_computation.42 | loop fusion | flops 13307904 | bytes 26390528 | tf_op jit(solution)/shard_map/sub | solution.py:93
  51.6 4.5 %multiply_subtract_fusion.2 = (f32[36,36,256]{2,1,0:T(8,128)S(1)}, f32[36,36,256]{2,1,0:T(8,128)S(1)}, f32[36,36,256]{2,1,0:T(8,128)S(1)}) fusion(f32[38,38,256]{2,1,0:T(8,128)S(1)} %get-tuple-element.47, f32[38,38,256]{2,1,0:T(8,128)S(1)} %get-tuple-element.48, f32[40,40,256]{2,1,0:T(8,128)S(1)} %get-tuple-element.52, f32[38,38,256]{2,1,0:T(8,128)S(1)} %get-tuple-element.49), kind=kLoop, calls=%fused_computation.63 | loop fusion | flops 11943936 | bytes 24788992 | tf_op jit(solution)/shard_map/sub | solution.py:93
  56.0 4.9 %multiply_subtract_fusion.3 = (f32[34,34,256]{2,1,0:T(8,128)S(1)}, f32[34,34,256]{2,1,0:T(8,128)S(1)}, f32[34,34,256]{2,1,0:T(8,128)}) fusion(f32[36,36,256]{2,1,0:T(8,128)S(1)} %get-tuple-element.44, f32[36,36,256]{2,1,0:T(8,128)S(1)} %get-tuple-element.45, f32[40,40,256]{2,1,0:T(8,128)S(1)} %get-tuple-element.52, f32[36,36,256]{2,1,0:T(8,128)S(1)} %get-tuple-element.46), kind=kLoop, calls=%fused_computation.84 | loop fusion | flops 10653696 | bytes 23212032 | tf_op jit(solution)/shard_map/sub | solution.py:93
  60.9 2.4 %bitcast_reduce_fusion = (f32[16,32,256]{2,1,0:T(8,128)S(1)}, f32[32,32,256]{2,1,0:T(8,128)}) fusion(f32[34,34,256]{2,1,0:T(8,128)S(1)} %get-tuple-element.41, f32[34,34,256]{2,1,0:T(8,128)S(1)} %get-tuple-element.42, f32[40,40,256]{2,1,0:T(8,128)S(1)} %get-tuple-element.52), kind=kLoop, calls=%fused_computation.107 | loop fusion | flops 5636096 | bytes 10305536 | tf_op jit(solution)/shard_map/reduce_sum | solution.py:118
  63.6 1.1 fusion.43
  64.8 2.2 %copy.182 = f32[16,128,16]{2,1,0:T(8,128)} copy(f32[16,128,16]{1,2,0:T(8,128)} %fusion.43) | data formatting | bytes 262144 | tf_op jit(solution)/shard_map/add | solution.py:122
  67.0 2.2 %reshape.71 = f32[16,16,128]{2,0,1:T(8,128)} reshape(f32[16,16,8,16]{3,2,0,1:T(8,128)} %bitcast.54) | data formatting | bytes 262144 | tf_op jit(solution)/shard_map/reshape | solution.py:179
  69.2 1.6 %copy.195.src_ref = f32[16,16,128]{2,1,0:T(8,128)} copy(f32[16,16,128]{2,0,1:T(8,128)} %reshape.71) | data formatting | bytes 262144 | tf_op jit(solution)/shard_map/reshape | solution.py:179
  70.8 24.0 %shard_map.93 = f32[16,16,128]{2,1,0:T(8,128)} custom-call(f32[16,16,128]{2,1,0:T(8,128)} %copy.195.src_ref), custom_call_target="tpu_custom_call" | custom-call | tf_op jit(solution)/shard_map/pallas_call | solution.py:56
  94.8 2.2 %reshape.65 = f32[16,16,8,16]{3,2,1,0:T(8,128)} reshape(f32[16,16,128]{2,1,0:T(8,128)} %shard_map.93) | data formatting | bytes 262144 | tf_op jit(solution)/shard_map/reshape | solution.py:181
  97.0 1.8 %copy.205 = f32[16,16,8,16]{3,0,2,1:T(8,128)S(1)} copy(f32[16,16,8,16]{3,2,1,0:T(8,128)} %reshape.65) | data formatting | bytes 262144 | tf_op jit(solution)/shard_map/reshape | solution.py:181
  98.8 1.0 copy-done.2
  99.8 0.8 fusion.102
  100.6 1.0 slice.525
  101.6 2.8 %collective-permute-start.5 = (f32[3,8,256]{2,0,1:T(4,128)S(1)}, f32[3,8,256]{2,0,1:T(4,128)S(1)}, u32[]{:S(2)}, u32[]{:S(2)}) collective-permute-start(f32[3,8,256]{2,0,1:T(4,128)S(1)} %copy.186), channel_id=1, source_target_pairs={{16,0},{32,16},{48,32},{64,48},{80,64},{96,80},{112,96},{128,112},... | collective-permute-start | bytes 73736 | tf_op jit(solution)/shard_map/ppermute | solution.py:78
  104.5 1.1 slice.523
  106.2 2.1 %collective-permute-start.4 = (f32[3,8,256]{2,0,1:T(4,128)}, f32[3,8,256]{2,0,1:T(4,128)S(1)}, u32[]{:S(2)}, u32[]{:S(2)}) collective-permute-start(f32[3,8,256]{2,0,1:T(4,128)} %copy.185), channel_id=1, source_target_pairs={{0,16},{16,32},{32,48},{48,64},{64,80},{80,96},{96,112},{112,128},... | collective-permute-start | bytes 73736 | tf_op jit(solution)/shard_map/ppermute | solution.py:75
  108.3 1.5 %fusion.101 = (f32[3,20,12,255]{3,1,2,0:T(8,128)}, f32[3,20,12,255]{3,1,2,0:T(8,128)}) fusion(f32[6,22,14,256]{3,1,2,0:T(8,128)S(1)} %pad_maximum_fusion.1), kind=kLoop, calls=%fused_computation.190 | loop fusion | bytes 2937600 | tf_op jit(solution)/shard_map/slice | solution.py:127
  109.8 2.3 %reshape.66 = f32[16,8,256]{2,1,0:T(8,128)} reshape(f32[16,8,16,16]{3,2,1,0:T(8,128)} %bitcast.53) | data formatting | bytes 262144 | tf_op jit(solution)/shard_map/reshape | solution.py:181
  112.0 0.9 copy.187
  113.0 0.7 collective-permute-done.4
  113.7 1.3 collective-permute-start.7
  115.0 4.5 %collective-permute-start.6 = (f32[22,3,256]{2,0,1:T(8,128)S(1)}, f32[22,3,256]{2,0,1:T(8,128)S(1)}, u32[]{:S(2)}, u32[]{:S(2)}) collective-permute-start(f32[22,3,256]{2,0,1:T(8,128)S(1)} %get-tuple-element.73), channel_id=1, source_target_pairs={{0,1},{1,2},{2,3},{3,4},{4,5},{5,6},{6,7},{7,8},{8,9},{9,10},{10,1... | collective-permute-start | bytes 202760 | tf_op jit(solution)/shard_map/ppermute | solution.py:75
  119.6 3.1 %fusion.48 = f32[32,32,256]{2,1,0:T(8,128)} fusion(f32[34,34,256]{2,1,0:T(8,128)S(1)} %get-tuple-element.41, f32[34,34,256]{2,1,0:T(8,128)} %get-tuple-element.43), kind=kLoop, calls=%fused_computation.92 | loop fusion | flops 2359296 | bytes 8732672 | tf_op jit(solution)/shard_map/add | solution.py:98
  123.6 0.9 copy-done.3
  124.8 1.0 fusion.67
  126.1 0.8 fusion.78
  127.5 1.0 copy.193
  129.2 1.0 reshape.67.src_ref
  130.2 16.2 %shard_map.94 = f32[16,16,128]{2,1,0:T(8,128)} custom-call(f32[16,16,128]{2,1,0:T(8,128)} %reshape.67.src_ref), custom_call_target="tpu_custom_call" | custom-call | tf_op jit(solution)/shard_map/pallas_call | solution.py:56
  146.4 1.2 reshape.68
  147.7 1.0 copy.194
  (58 shorter events, 5.5 us)
Async XLA Ops:
  0.6 1.7 %copy-start = (f32[32,32,256]{2,1,0:T(8,128)S(1)}, f32[32,32,256]{2,1,0:T(8,128)}, u32[]{:S(2)}) copy-start(f32[32,32,256]{2,1,0:T(8,128)} %param.7) | copy-start | bytes 3145732
  0.6 1.8 %copy-start.1 = (f32[32,32,256]{2,1,0:T(8,128)S(1)}, f32[32,32,256]{2,1,0:T(8,128)}, u32[]{:S(2)}) copy-start(f32[32,32,256]{2,1,0:T(8,128)} %param.6) | copy-start | bytes 3145732
  2.5 6.5 %copy-start.5 = (f32[3,16,8,256]{3,2,1,0:T(8,128)S(1)}, f32[3,16,8,256]{3,2,1,0:T(8,128)}, u32[]{:S(2)}) copy-start(f32[3,16,8,256]{3,2,1,0:T(8,128)} %param.9) | copy-start | bytes 1179652
  2.5 6.6 %copy-start.6 = (f32[3,16,8,256]{3,2,1,0:T(8,128)S(1)}, f32[3,16,8,256]{3,2,1,0:T(8,128)}, u32[]{:S(2)}) copy-start(f32[3,16,8,256]{3,2,1,0:T(8,128)} %param.10) | copy-start | bytes 1179652
  2.5 27.6 %collective-permute-start.1 = (f32[3,4,32,256]{3,2,1,0:T(8,128)S(1)}, f32[3,4,32,256]{3,2,1,0:T(8,128)S(1)}, u32[]{:S(2)}, u32[]{:S(2)}) collective-permute-start(f32[3,4,32,256]{3,2,1,0:T(8,128)S(1)} %get-tuple-element.56), channel_id=1, source_target_pairs={{16,0},{32,16},{48,32},{64,48},{80,64},{96,80},{112,96},{128,112},... | collective-permute-start | bytes 1179656 | tf_op jit(solution)/shard_map/ppermute | solution.py:78
  7.0 23.2 %collective-permute-start = (f32[3,4,32,256]{3,2,1,0:T(8,128)S(1)}, f32[3,4,32,256]{3,2,1,0:T(8,128)S(1)}, u32[]{:S(2)}, u32[]{:S(2)}) collective-permute-start(f32[3,4,32,256]{3,2,1,0:T(8,128)S(1)} %get-tuple-element.55), channel_id=1, source_target_pairs={{0,16},{16,32},{32,48},{48,64},{64,80},{80,96},{96,112},{112,128},... | collective-permute-start | bytes 1179656 | tf_op jit(solution)/shard_map/ppermute | solution.py:75
  9.3 8.9 %collective-permute-start.9 = (f32[6,3,8,256]{3,1,2,0:T(4,128)S(1)}, f32[6,3,8,256]{3,1,2,0:T(4,128)S(1)}, u32[]{:S(2)}, u32[]{:S(2)}) collective-permute-start(f32[6,3,8,256]{3,1,2,0:T(4,128)S(1)} %get-tuple-element.66), channel_id=1, source_target_pairs={{16,0},{32,16},{48,32},{64,48},{80,64},{96,80},{112,96},{128,112},... | collective-permute-start | bytes 442376 | tf_op jit(solution)/shard_map/ppermute | solution.py:78
  15.1 9.1 %collective-permute-start.8 = (f32[6,3,8,256]{3,1,2,0:T(4,128)S(1)}, f32[6,3,8,256]{3,1,2,0:T(4,128)S(1)}, u32[]{:S(2)}, u32[]{:S(2)}) collective-permute-start(f32[6,3,8,256]{3,1,2,0:T(4,128)S(1)} %get-tuple-element.65), channel_id=1, source_target_pairs={{0,16},{16,32},{32,48},{48,64},{64,80},{80,96},{96,112},{112,128},... | collective-permute-start | bytes 442376 | tf_op jit(solution)/shard_map/ppermute | solution.py:75
  24.3 14.6 %collective-permute-start.11 = (f32[6,22,3,256]{3,1,2,0:T(8,128)S(1)}, f32[6,22,3,256]{3,1,2,0:T(8,128)S(1)}, u32[]{:S(2)}, u32[]{:S(2)}) collective-permute-start(f32[6,22,3,256]{3,1,2,0:T(8,128)S(1)} %get-tuple-element.60), channel_id=1, source_target_pairs={{1,0},{2,1},{3,2},{4,3},{5,4},{6,5},{7,6},{8,7},{9,8},{10,9},{11,1... | collective-permute-start | bytes 1216520 | tf_op jit(solution)/shard_map/ppermute | solution.py:78
  25.6 14.5 %collective-permute-start.10 = (f32[6,22,3,256]{3,1,2,0:T(8,128)S(1)}, f32[6,22,3,256]{3,1,2,0:T(8,128)S(1)}, u32[]{:S(2)}, u32[]{:S(2)}) collective-permute-start(f32[6,22,3,256]{3,1,2,0:T(8,128)S(1)} %get-tuple-element.59), channel_id=1, source_target_pairs={{0,1},{1,2},{2,3},{3,4},{4,5},{5,6},{6,7},{7,8},{8,9},{9,10},{10,1... | collective-permute-start | bytes 1216520 | tf_op jit(solution)/shard_map/ppermute | solution.py:75
  30.4 13.8 %collective-permute-start.3 = (f32[3,40,4,256]{3,2,1,0:T(4,128)S(1)}, f32[3,40,4,256]{3,2,1,0:T(4,128)S(1)}, u32[]{:S(2)}, u32[]{:S(2)}) collective-permute-start(f32[3,40,4,256]{3,2,1,0:T(4,128)S(1)} %get-tuple-element.54), channel_id=1, source_target_pairs={{1,0},{2,1},{3,2},{4,3},{5,4},{6,5},{7,6},{8,7},{9,8},{10,9},{11,1... | collective-permute-start | bytes 1474568 | tf_op jit(solution)/shard_map/ppermute | solution.py:78
  31.7 13.7 %collective-permute-start.2 = (f32[3,40,4,256]{3,2,1,0:T(4,128)S(1)}, f32[3,40,4,256]{3,2,1,0:T(4,128)S(1)}, u32[]{:S(2)}, u32[]{:S(2)}) collective-permute-start(f32[3,40,4,256]{3,2,1,0:T(4,128)S(1)} %get-tuple-element.53), channel_id=1, source_target_pairs={{0,1},{1,2},{2,3},{3,4},{4,5},{5,6},{6,7},{7,8},{8,9},{9,10},{10,1... | collective-permute-start | bytes 1474568 | tf_op jit(solution)/shard_map/ppermute | solution.py:75
  60.9 2.7 %copy-start.7 = (f32[256,128,1]{1,0,2:T(8,128)S(1)}, f32[256,128,1]{1,0,2:T(8,128)}, u32[]{:S(2)}) copy-start(f32[256,128,1]{1,0,2:T(8,128)} %constant.99) | copy-start | bytes 393220
  98.8 1.0 copy-start.2
  101.6 11.3 %collective-permute-start.5 = (f32[3,8,256]{2,0,1:T(4,128)S(1)}, f32[3,8,256]{2,0,1:T(4,128)S(1)}, u32[]{:S(2)}, u32[]{:S(2)}) collective-permute-start(f32[3,8,256]{2,0,1:T(4,128)S(1)} %copy.186), channel_id=1, source_target_pairs={{16,0},{32,16},{48,32},{64,48},{80,64},{96,80},{112,96},{128,112},... | collective-permute-start | bytes 73736 | tf_op jit(solution)/shard_map/ppermute | solution.py:78
  106.2 7.5 %collective-permute-start.4 = (f32[3,8,256]{2,0,1:T(4,128)}, f32[3,8,256]{2,0,1:T(4,128)S(1)}, u32[]{:S(2)}, u32[]{:S(2)}) collective-permute-start(f32[3,8,256]{2,0,1:T(4,128)} %copy.185), channel_id=1, source_target_pairs={{0,16},{16,32},{32,48},{48,64},{64,80},{80,96},{96,112},{112,128},... | collective-permute-start | bytes 73736 | tf_op jit(solution)/shard_map/ppermute | solution.py:75
  113.7 8.9 %collective-permute-start.7 = (f32[22,3,256]{2,0,1:T(8,128)S(1)}, f32[22,3,256]{2,0,1:T(8,128)S(1)}, u32[]{:S(2)}, u32[]{:S(2)}) collective-permute-start(f32[22,3,256]{2,0,1:T(8,128)S(1)} %get-tuple-element.74), channel_id=1, source_target_pairs={{1,0},{2,1},{3,2},{4,3},{5,4},{6,5},{7,6},{8,7},{9,8},{10,9},{11,1... | collective-permute-start | bytes 202760 | tf_op jit(solution)/shard_map/ppermute | solution.py:78
  115.0 7.6 %collective-permute-start.6 = (f32[22,3,256]{2,0,1:T(8,128)S(1)}, f32[22,3,256]{2,0,1:T(8,128)S(1)}, u32[]{:S(2)}, u32[]{:S(2)}) collective-permute-start(f32[22,3,256]{2,0,1:T(8,128)S(1)} %get-tuple-element.73), channel_id=1, source_target_pairs={{0,1},{1,2},{2,3},{3,4},{4,5},{5,6},{6,7},{7,8},{8,9},{9,10},{10,1... | collective-permute-start | bytes 202760 | tf_op jit(solution)/shard_map/ppermute | solution.py:75
  123.4 1.2 copy-start.3
  123.4 1.4 copy-start.4

commit v4 on v1

--- a/solution.py
+++ b/solution.py
@@ -112,19 +112,34 @@
 
 def on_device(concentration, order_field, phase_labels, displacement, body_load):
     h = FINE_HALO
+    m = MECH_HALO
+    hx = h + 2 * m
     fields = jnp.stack([concentration, order_field, mobility_of(phase_labels)])
-    fields = padded_2(fields, (("gx", 1), ("gy", 2)), h)
+    fields = padded_2(fields, (("gx", 1),), hx)
+    fields = padded_2(fields, (("gy", 2),), h)
     conc, order, mob = fields[0], fields[1], fields[2]
     for step in range(STEPS):
         conc, order, mob = advance(conc, order, mob, step == STEPS - 1)
+    fx = concentration.shape[0]
+    conc = conc[2 * m:2 * m + fx]
+    order_x = order
+    order = order[2 * m:2 * m + fx]
 
-    m = MECH_HALO
     ub = padded_2(jnp.concatenate([displacement, body_load]), (("gx", 1), ("gy", 2)), m)
     disp, load = ub[:3], ub[3:]
 
-    coarse = restrict_xzy(order)
-    stiff = lax.all_to_all(coarse, "gy", split_axis=1, concat_axis=2, tiled=True)
-    stiff_pad = padded_2(stiff, (("gx", 0), ("gy", 1)), m)
+    coarse = restrict_xzy(order_x)
+    cx, cz, cy = coarse.shape
+    bx = cx - 2 * m
+    n = lax.axis_size("gy")
+    gxi = lax.axis_index("gx")
+    xg = gxi * bx - m + lax.broadcasted_iota(jnp.int32, (cx, 1, 1), 0)
+    coarse = jnp.where((xg >= 0) & (xg < bx * lax.axis_size("gx")), coarse, 0.0)
+    zc = cz // n
+    zpad = jnp.pad(coarse, ((0, 0), (m, m), (0, 0)))
+    windows = jnp.stack([zpad[:, j * zc:j * zc + zc + 2 * m] for j in range(n)])
+    got = lax.all_to_all(windows, "gy", split_axis=0, concat_axis=0, tiled=True)
+    stiff_pad = got.transpose(1, 2, 0, 3).reshape(cx, zc + 2 * m, n * cy)
 
     faces, diag, center = face_terms(stiff_pad)
     for weight in (first_weight, second_weight):

time: 135 us -> 175 us (1.30)
  local copies, waits for them, and re-layouts: 17.9 us -> 47.7 us
  starting transfers between devices: 60.5 us -> 32.8 us
  waiting for transfers between devices: 22.5 us -> 43.5 us
  other arithmetic: 30.6 us -> 48.2 us
    ppermute x6 -> x4, waiting for transfers between devices: 3.2 us -> 22 us  [padded_2(): lax.ppermute(lax.slice_in_dim(block, 0, width, axis=dim), axis, backward)]
    unnamed x29 -> x54, local copies, waits for them, and re-layouts: 6.86 us -> 25 us
    all_to_all x1, starting transfers between devices: 14.6 us -> 4.21 us  [on_device(): got = lax.all_to_all(windows, 'gy', split_axis=0, concat_axis=0, tiled=True)]
    sub x4, other arithmetic: 14.1 us -> 23 us  [advance(): chem = conc_pad - order_pad * order_pad * (3.0 - 2.0 * order_pad)]
    transpose x0 -> x2, local copies, waits for them, and re-layouts: none -> 6.82 us  [on_device(): stiff_pad = got.transpose(1, 2, 0, 3).reshape(cx, zc + 2 * m, n * cy)]
    all_to_all x1, starting transfers between devices: 11.1 us -> 4.67 us  [on_device(): lax.all_to_all(energy, 'gy', split_axis=2, concat_axis=1, tiled=True)]
    ppermute x6 -> x4, starting transfers between devices: 21.1 us -> 15.1 us  [padded_2(): lax.ppermute(lax.slice_in_dim(block, block.shape[dim] - width, None, axis...]
    mul x0 -> x1, other arithmetic: none -> 5.31 us  [restrict_xzy(): sq = order_out * order_out]
  transfers between devices with their start and end apart: 14 -> 10, of which waited for: 7 -> 6; matrix products, arithmetic and copies ran while one was open for 26% -> 37% of each run, Pallas kernels for 0% -> 0%
where the time goes in v4:
time: 175 us; the launch traced here: 174 us
  other arithmetic  48.2 us (28%)
  local copies, waits for them, and re-layouts  47.7 us (27%)
  waiting for transfers between devices  43.5 us (25%)
  starting transfers between devices  32.8 us (19%)
    unnamed x54, local copies, waits for them, and re-layouts  25 us
    sub x4, other arithmetic, advance(): chem = conc_pad - order_pad * order_pad * (3.0 - 2.0 * order_pad)  23 us
    ppermute x4, waiting for transfers between devices, padded_2(): lax.ppermute(lax.slice_in_dim(block, 0, width, axis=dim), axis, backward)  22 us
    ppermute x4, starting transfers between devices, padded_2(): lax.ppermute(lax.slice_in_dim(block, block.shape[dim] - width, None, axis...  15.1 us
    ppermute x4, waiting for transfers between devices, padded_2(): lax.ppermute(lax.slice_in_dim(block, block.shape[dim] - width, None, axis...  11.3 us
    ppermute x4, starting transfers between devices, padded_2(): lax.ppermute(lax.slice_in_dim(block, 0, width, axis=dim), axis, backward)  8.8 us
    transpose x2, local copies, waits for them, and re-layouts, on_device(): stiff_pad = got.transpose(1, 2, 0, 3).reshape(cx, zc + 2 * m, n * cy)  6.82 us
    mul x1, other arithmetic, restrict_xzy(): sq = order_out * order_out  5.31 us
  transfers between devices with their start and end apart: 10, of which 6 were waited for; matrix products, arithmetic and copies ran while one was open for 37% of the time, Pallas kernels for 0%

profile of v4, /device:TPU:2, one launch (start us, length us, event | category | flops | bytes accessed | tf_op | source)
XLA Modules:
  0.0 173.8 jit_solution(15231712206772372271)
XLA Ops:
  0.7 1.6 add_bitcast_fusion
  2.6 4.3 %collective-permute-start.1 = (f32[3,10,32,256]{3,2,1,0:T(8,128)S(1)}, f32[3,10,32,256]{3,2,1,0:T(8,128)S(1)}, u32[]{:S(2)}, u32[]{:S(2)}) collective-permute-start(f32[3,10,32,256]{3,2,1,0:T(8,128)S(1)} %get-tuple-element.48), channel_id=1, source_target_pairs={{16,0},{32,16},{48,32},{64,48},{80,64},{96,80},{112,96},{128,112},... | collective-permute-start | bytes 2949128 | tf_op jit(solution)/shard_map/ppermute | solution.py:28
  7.0 1.9 %collective-permute-start = (f32[3,10,32,256]{3,2,1,0:T(8,128)S(1)}, f32[3,10,32,256]{3,2,1,0:T(8,128)S(1)}, u32[]{:S(2)}, u32[]{:S(2)}) collective-permute-start(f32[3,10,32,256]{3,2,1,0:T(8,128)S(1)} %get-tuple-element.47), channel_id=1, source_target_pairs={{0,16},{16,32},{32,48},{48,64},{64,80},{80,96},{96,112},{112,128},... | collective-permute-start | bytes 2949128 | tf_op jit(solution)/shard_map/ppermute | solution.py:25
  9.1 9.5 %collective-permute-done.1 = f32[3,10,32,256]{3,2,1,0:T(8,128)S(1)} collective-permute-done((f32[3,10,32,256]{3,2,1,0:T(8,128)S(1)}, f32[3,10,32,256]{3,2,1,0:T(8,128)S(1)}, u32[]{:S(2)}, u32[]{:S(2)}) %collective-permute-start.1) | collective-permute-done | bytes 983072 | tf_op jit(solution)/shard_map/ppermute | solution.py:28
  18.6 5.9 %collective-permute-done = f32[3,10,32,256]{3,2,1,0:T(8,128)S(1)} collective-permute-done((f32[3,10,32,256]{3,2,1,0:T(8,128)S(1)}, f32[3,10,32,256]{3,2,1,0:T(8,128)S(1)}, u32[]{:S(2)}, u32[]{:S(2)}) %collective-permute-start) | collective-permute-done | bytes 983072 | tf_op jit(solution)/shard_map/ppermute | solution.py:25
  24.5 1.4 pad_maximum_fusion.9
  25.9 1.3 collective-permute-start.3
  27.1 5.4 %collective-permute-start.2 = (f32[3,52,4,256]{3,2,1,0:T(4,128)}, f32[3,52,4,256]{3,2,1,0:T(4,128)}, u32[]{:S(2)}, u32[]{:S(2)}) collective-permute-start(f32[3,52,4,256]{3,2,1,0:T(4,128)} %get-tuple-element.45), channel_id=1, source_target_pairs={{0,1},{1,2},{2,3},{3,4},{4,5},{5,6},{6,7},{7,8},{8,9},{9,10},{10,1... | collective-permute-start | bytes 1916936 | tf_op jit(solution)/shard_map/ppermute | solution.py:25
  32.7 0.9 copy-done.2
  33.6 0.8 fusion.119
  34.4 1.9 %collective-permute-start.5 = (f32[6,3,8,256]{3,1,2,0:T(4,128)}, f32[6,3,8,256]{3,1,2,0:T(4,128)S(1)}, u32[]{:S(2)}, u32[]{:S(2)}) collective-permute-start(f32[6,3,8,256]{3,1,2,0:T(4,128)} %get-tuple-element.61), channel_id=1, source_target_pairs={{16,0},{32,16},{48,32},{64,48},{80,64},{96,80},{112,96},{128,112},... | collective-permute-start | bytes 442376 | tf_op jit(solution)/shard_map/ppermute | solution.py:28
  36.3 2.4 %collective-permute-start.4 = (f32[6,3,8,256]{3,1,2,0:T(4,128)}, f32[6,3,8,256]{3,1,2,0:T(4,128)S(1)}, u32[]{:S(2)}, u32[]{:S(2)}) collective-permute-start(f32[6,3,8,256]{3,1,2,0:T(4,128)} %get-tuple-element.60), channel_id=1, source_target_pairs={{0,16},{16,32},{32,48},{48,64},{64,80},{80,96},{96,112},{112,128},... | collective-permute-start | bytes 442376 | tf_op jit(solution)/shard_map/ppermute | solution.py:25
  38.8 12.5 %collective-permute-done.5 = f32[6,3,8,256]{3,1,2,0:T(4,128)S(1)} collective-permute-done((f32[6,3,8,256]{3,1,2,0:T(4,128)}, f32[6,3,8,256]{3,1,2,0:T(4,128)S(1)}, u32[]{:S(2)}, u32[]{:S(2)}) %collective-permute-start.5) | collective-permute-done | bytes 147488 | tf_op jit(solution)/shard_map/ppermute | solution.py:28
  51.2 5.3 %collective-permute-done.4 = f32[6,3,8,256]{3,1,2,0:T(4,128)S(1)} collective-permute-done((f32[6,3,8,256]{3,1,2,0:T(4,128)}, f32[6,3,8,256]{3,1,2,0:T(4,128)S(1)}, u32[]{:S(2)}, u32[]{:S(2)}) %collective-permute-start.4) | collective-permute-done | bytes 147488 | tf_op jit(solution)/shard_map/ppermute | solution.py:25
  56.5 2.1 %pad_maximum_fusion.12 = (f32[6,22,3,256]{3,1,2,0:T(8,128)}, f32[6,22,3,256]{3,1,2,0:T(8,128)}) fusion(f32[6,3,8,256]{3,1,2,0:T(4,128)S(1)} %collective-permute-done.5, f32[6,16,8,256]{3,1,2,0:T(8,128)} %copy-done.2, f32[6,3,8,256]{3,1,2,0:T(4,128)S(1)} %collective-permute-done.4), kind=kLoop, calls=%fused_computation.156 | loop fusion | flops 405504 | bytes 1892352 | tf_op jit(solution)/shard_map/slice | solution.py:26
  58.7 1.3 collective-permute-start.7
  59.9 5.4 %collective-permute-start.6 = (f32[6,22,3,256]{3,1,2,0:T(8,128)}, f32[6,22,3,256]{3,1,2,0:T(8,128)}, u32[]{:S(2)}, u32[]{:S(2)}) collective-permute-start(f32[6,22,3,256]{3,1,2,0:T(8,128)} %get-tuple-element.56), channel_id=1, source_target_pairs={{0,1},{1,2},{2,3},{3,4},{4,5},{5,6},{6,7},{7,8},{8,9},{9,10},{10,1... | collective-permute-start | bytes 1216520 | tf_op jit(solution)/shard_map/ppermute | solution.py:25
  65.3 2.4 %pad_maximum_fusion = f32[3,52,40,256]{3,2,1,0:T(8,128)S(1)} fusion(f32[3,52,4,256]{3,2,1,0:T(4,128)} %collective-permute-done.3, f32[3,10,32,256]{3,2,1,0:T(8,128)S(1)} %copy-done.9, f32[1,32,32,256]{3,2,1,0:T(8,128)S(1)} %add_bitcast_fusion, f32[1,32,32,256]{3,2,1,0:T(8,128)S(1)} %bitcast.104, f32[1,32,32,256]{3,2,1,0:T(8,128)S(1)} %bitcast.107, ...), kind=kLoop, calls=%fused_computation | loop fusion | flops 9584640 | bytes 12779520 | tf_op jit(solution)/shard_map/concatenate | solution.py:29
  68.5 7.0 %multiply_subtract_fusion.1 = (f32[50,38,256]{2,1,0:T(8,128)S(1)}, f32[50,38,256]{2,1,0:T(8,128)S(1)}, f32[50,38,256]{2,1,0:T(8,128)}) fusion(f32[52,40,256]{2,1,0:T(8,128)S(1)} %multiply_subtract_fusion, f32[52,40,256]{2,1,0:T(8,128)S(1)} %get-tuple-element.43, f32[52,40,256]{2,1,0:T(8,128)S(1)} %get-tuple-element.44, f32[52,40,256]{2,1,0:T(8,128)S(1)} %get-tuple-element.42), kind=kLoop, calls=%fused_computation.42 | loop fusion | flops 17510400 | bytes 34672640 | tf_op jit(solution)/shard_map/sub | solution.py:43
  75.5 8.0 %multiply_subtract_fusion.2 = (f32[48,36,256]{2,1,0:T(8,128)S(1)}, f32[48,36,256]{2,1,0:T(8,128)S(1)}, f32[48,36,256]{2,1,0:T(8,128)}) fusion(f32[50,38,256]{2,1,0:T(8,128)S(1)} %get-tuple-element.39, f32[50,38,256]{2,1,0:T(8,128)S(1)} %get-tuple-element.40, f32[52,40,256]{2,1,0:T(8,128)S(1)} %get-tuple-element.44, f32[50,38,256]{2,1,0:T(8,128)} %get-tuple-element.41), kind=kLoop, calls=%fused_computation.63 | loop fusion | flops 15925248 | bytes 32800768 | tf_op jit(solution)/shard_map/sub | solution.py:43
  83.5 7.7 %multiply_subtract_fusion.3 = (f32[46,34,256]{2,1,0:T(8,128)S(1)}, f32[46,34,256]{2,1,0:T(8,128)S(1)}, f32[46,34,256]{2,1,0:T(8,128)}) fusion(f32[48,36,256]{2,1,0:T(8,128)S(1)} %get-tuple-element.36, f32[48,36,256]{2,1,0:T(8,128)S(1)} %get-tuple-element.37, f32[52,40,256]{2,1,0:T(8,128)S(1)} %get-tuple-element.44, f32[48,36,256]{2,1,0:T(8,128)} %get-tuple-element.38), kind=kLoop, calls=%fused_computation.84 | loop fusion | flops 14413824 | bytes 31064064 | tf_op jit(solution)/shard_map/sub | solution.py:43
  91.2 5.3 %fusion.109 = (f32[44,32,256]{2,1,0:T(8,128)S(1)}, f32[44,32,256]{2,1,0:T(8,128)}, f32[44,32,256]{2,1,0:T(8,128)}, f32[44,32,256]{2,1,0:T(8,128)}, f32[44,32,256...) fusion(f32[46,34,256]{2,1,0:T(8,128)S(1)} %get-tuple-element.33, ...), kind=kLoop, calls=%fused_computation.218 | loop fusion | flops 8290304 | bytes 29720576 | tf_op jit(solution)/shard_map/mul | solution.py:67
  97.1 0.9 reduce_sum.28
  110.2 0.8 fusion.90
  111.0 3.3 %copy.62 = f32[16,22,14,16]{1,3,2,0:T(8,128)S(1)} copy(f32[16,22,14,16]{2,3,1,0:T(8,128)} %fusion.90) | data formatting | bytes 630784 | tf_op jit(solution)/shard_map/stack | solution.py:140
  114.4 2.5 %reshape.52 = f32[16,1,4928]{2,1,0:T(1,128)} reshape(f32[16,14,16,22]{3,2,1,0:T(8,128)S(1)} %bitcast.108) | data formatting | bytes 630784
  116.9 4.2 %all-to-all-start = ((f32[16,1,4928]{2,1,0:T(1,128)}), f32[16,1,4928]{2,1,0:T(1,128)}, u32[]{:S(2)}, u32[]{:S(2)}) async-start(f32[16,1,4928]{2,1,0:T(1,128)} %reshape.52), calls=%async_computation | async-start | bytes 638976 | tf_op jit(solution)/shard_map/all_to_all | solution.py:141
  121.2 1.4 pad_maximum_fusion.1
  122.6 1.2 fusion.117
  124.4 1.4 slice.672
  125.8 1.0 slice.695
  126.8 5.0 %all-to-all-done = f32[16,1,4928]{2,1,0:T(1,128)} async-done(((f32[16,1,4928]{2,1,0:T(1,128)}), f32[16,1,4928]{2,1,0:T(1,128)}, u32[]{:S(2)}, u32[]{:S(2)}) %all-to-all-start) | async-done | bytes 315424 | tf_op jit(solution)/shard_map/all_to_all | solution.py:141
  132.4 2.4 %reduce = f32[16,4928]{1,0:T(8,128)S(1)} reduce(f32[16,1,4928]{2,1,0:T(1,128)} %all-to-all-done, f32[]{:T(128)} %broadcast.223), dimensions={1}, to_apply=%all_to_all.16.reduce_sub_computation | reduce | bytes 630788 | tf_op jit(solution)/shard_map/all_to_all | solution.py:141
  134.8 3.4 %reshape.53 = f32[16,14,16,22]{3,2,1,0:T(8,128)} reshape(f32[16,4928]{1,0:T(8,128)S(1)} %reduce) | data formatting | bytes 630784
  138.2 2.9 %bitcast_bitcast_fusion = f32[22,14,16,16]{0,3,1,2:T(8,128)} fusion(f32[16,14,16,22]{3,2,1,0:T(8,128)} %reshape.53), kind=kLoop, calls=%fused_computation.224 | loop fusion | bytes 630784 | tf_op jit(solution)/shard_map/transpose | solution.py:142
  141.1 4.0 %copy.63 = f32[22,14,16,16]{3,2,0,1:T(8,128)} copy(f32[22,14,16,16]{0,3,1,2:T(8,128)} %bitcast_bitcast_fusion) | data formatting | bytes 630784 | tf_op jit(solution)/shard_map/transpose | solution.py:142
  145.0 2.7 %reshape.50 = f32[22,14,256]{2,0,1:T(8,128)S(1)} reshape(f32[22,14,16,16]{3,2,0,1:T(8,128)} %copy.63) | data formatting | bytes 630784 | tf_op jit(solution)/shard_map/reshape | solution.py:142
  148.6 0.9 copy-done.12
  149.5 1.0 fusion.65
  152.2 1.3 copy.66
  153.5 2.3 %reshape.54 = f32[16,1,2048]{2,1,0:T(1,128)} reshape(f32[256,8,16]{2,1,0:T(8,128)} %bitcast.110) | data formatting | bytes 262144
  155.8 4.7 %all-to-all-start.1 = ((f32[16,1,2048]{2,1,0:T(1,128)}), f32[16,1,2048]{2,1,0:T(1,128)S(1)}, u32[]{:S(2)}, u32[]{:S(2)}) async-start(f32[16,1,2048]{2,1,0:T(1,128)} %reshape.54), calls=%async_computation.1 | async-start | bytes 262144 | tf_op jit(solution)/shard_map/all_to_all | solution.py:155
  160.5 3.8 %slice_add_fusion.23 = f32[32,32,256]{2,1,0:T(8,128)} fusion(f32[44,32,256]{2,1,0:T(8,128)} %slice.672, f32[44,32,256]{2,1,0:T(8,128)} %get-tuple-element.55, f32[44,32,256]{2,1,0:T(8,128)} %get-tuple-element.54, f32[44,32,256]{2,1,0:T(8,128)S(1)} %copy-done.5, f32[44,32,256]{2,1,0:T(8,128)S(1)} %copy-done.6, f32[44,32,256]{2,1,0:T(8,128)} %get-tuple-element.53), kind=kLoop, calls=%fused_computation.102 | loop fusion | flops 1835008 | bytes 7340032 | tf_op jit(solution)/shard_map/add | solution.py:48
  164.3 1.0 copy.69
  165.3 5.2 %all-to-all-done.1 = f32[16,1,2048]{2,1,0:T(1,128)S(1)} async-done(((f32[16,1,2048]{2,1,0:T(1,128)}), f32[16,1,2048]{2,1,0:T(1,128)S(1)}, u32[]{:S(2)}, u32[]{:S(2)}) %all-to-all-start.1) | async-done | bytes 131104 | tf_op jit(solution)/shard_map/all_to_all | solution.py:155
  170.5 1.0 reduce.1
  171.9 0.9 copy.68
  172.8 1.0 copy.70
  (82 shorter events, 18.2 us)
Async XLA Ops:
  0.6 1.7 copy-start
  0.6 1.8 %copy-start.1 = (f32[32,32,256]{2,1,0:T(8,128)S(1)}, f32[32,32,256]{2,1,0:T(8,128)}, u32[]{:S(2)}) copy-start(f32[32,32,256]{2,1,0:T(8,128)} %param.6) | copy-start | bytes 3145732
  2.5 6.4 %copy-start.13 = (f32[3,16,8,256]{3,2,1,0:T(8,128)S(1)}, f32[3,16,8,256]{3,2,1,0:T(8,128)}, u32[]{:S(2)}) copy-start(f32[3,16,8,256]{3,2,1,0:T(8,128)} %param.9) | copy-start | bytes 1179652
  2.6 15.9 %collective-permute-start.1 = (f32[3,10,32,256]{3,2,1,0:T(8,128)S(1)}, f32[3,10,32,256]{3,2,1,0:T(8,128)S(1)}, u32[]{:S(2)}, u32[]{:S(2)}) collective-permute-start(f32[3,10,32,256]{3,2,1,0:T(8,128)S(1)} %get-tuple-element.48), channel_id=1, source_target_pairs={{16,0},{32,16},{48,32},{64,48},{80,64},{96,80},{112,96},{128,112},... | collective-permute-start | bytes 2949128 | tf_op jit(solution)/shard_map/ppermute | solution.py:28
  7.0 17.5 %collective-permute-start = (f32[3,10,32,256]{3,2,1,0:T(8,128)S(1)}, f32[3,10,32,256]{3,2,1,0:T(8,128)S(1)}, u32[]{:S(2)}, u32[]{:S(2)}) collective-permute-start(f32[3,10,32,256]{3,2,1,0:T(8,128)S(1)} %get-tuple-element.47), channel_id=1, source_target_pairs={{0,16},{16,32},{32,48},{48,64},{64,80},{80,96},{96,112},{112,128},... | collective-permute-start | bytes 2949128 | tf_op jit(solution)/shard_map/ppermute | solution.py:25
  9.0 23.5 %copy-start.14 = (f32[3,16,8,256]{3,2,1,0:T(8,128)S(1)}, f32[3,16,8,256]{3,2,1,0:T(8,128)}, u32[]{:S(2)}) copy-start(f32[3,16,8,256]{3,2,1,0:T(8,128)} %param.10) | copy-start | bytes 1179652
  18.6 7.3 %copy-start.8 = (f32[3,10,32,256]{3,2,1,0:T(8,128)}, f32[3,10,32,256]{3,2,1,0:T(8,128)S(1)}, u32[]{:S(2)}) copy-start(f32[3,10,32,256]{3,2,1,0:T(8,128)S(1)} %collective-permute-done.1) | copy-start | bytes 2949124
  24.5 1.4 copy-start.10
  25.9 39.5 %collective-permute-start.3 = (f32[3,52,4,256]{3,2,1,0:T(4,128)}, f32[3,52,4,256]{3,2,1,0:T(4,128)}, u32[]{:S(2)}, u32[]{:S(2)}) collective-permute-start(f32[3,52,4,256]{3,2,1,0:T(4,128)} %get-tuple-element.46), channel_id=1, source_target_pairs={{1,0},{2,1},{3,2},{4,3},{5,4},{6,5},{7,6},{8,7},{9,8},{10,9},{11,1... | collective-permute-start | bytes 1916936 | tf_op jit(solution)/shard_map/ppermute | solution.py:28
  27.1 38.2 %collective-permute-start.2 = (f32[3,52,4,256]{3,2,1,0:T(4,128)}, f32[3,52,4,256]{3,2,1,0:T(4,128)}, u32[]{:S(2)}, u32[]{:S(2)}) collective-permute-start(f32[3,52,4,256]{3,2,1,0:T(4,128)} %get-tuple-element.45), channel_id=1, source_target_pairs={{0,1},{1,2},{2,3},{3,4},{4,5},{5,6},{6,7},{7,8},{8,9},{9,10},{10,1... | collective-permute-start | bytes 1916936 | tf_op jit(solution)/shard_map/ppermute | solution.py:25
  32.7 0.9 copy-start.2
  34.4 16.8 %collective-permute-start.5 = (f32[6,3,8,256]{3,1,2,0:T(4,128)}, f32[6,3,8,256]{3,1,2,0:T(4,128)S(1)}, u32[]{:S(2)}, u32[]{:S(2)}) collective-permute-start(f32[6,3,8,256]{3,1,2,0:T(4,128)} %get-tuple-element.61), channel_id=1, source_target_pairs={{16,0},{32,16},{48,32},{64,48},{80,64},{96,80},{112,96},{128,112},... | collective-permute-start | bytes 442376 | tf_op jit(solution)/shard_map/ppermute | solution.py:28
  36.3 20.3 %collective-permute-start.4 = (f32[6,3,8,256]{3,1,2,0:T(4,128)}, f32[6,3,8,256]{3,1,2,0:T(4,128)S(1)}, u32[]{:S(2)}, u32[]{:S(2)}) collective-permute-start(f32[6,3,8,256]{3,1,2,0:T(4,128)} %get-tuple-element.60), channel_id=1, source_target_pairs={{0,16},{16,32},{32,48},{48,64},{64,80},{80,96},{96,112},{112,128},... | collective-permute-start | bytes 442376 | tf_op jit(solution)/shard_map/ppermute | solution.py:25
  38.7 26.6 %copy-start.9 = (f32[3,10,32,256]{3,2,1,0:T(8,128)S(1)}, f32[3,10,32,256]{3,2,1,0:T(8,128)}, u32[]{:S(2)}) copy-start(f32[3,10,32,256]{3,2,1,0:T(8,128)} %copy-done.8) | copy-start | bytes 2949124
  38.7 26.6 %copy-start.11 = (f32[3,10,32,256]{3,2,1,0:T(8,128)S(1)}, f32[3,10,32,256]{3,2,1,0:T(8,128)}, u32[]{:S(2)}) copy-start(f32[3,10,32,256]{3,2,1,0:T(8,128)} %copy-done.10) | copy-start | bytes 2949124
  58.7 62.5 %collective-permute-start.7 = (f32[6,22,3,256]{3,1,2,0:T(8,128)}, f32[6,22,3,256]{3,1,2,0:T(8,128)}, u32[]{:S(2)}, u32[]{:S(2)}) collective-permute-start(f32[6,22,3,256]{3,1,2,0:T(8,128)} %get-tuple-element.57), channel_id=1, source_target_pairs={{1,0},{2,1},{3,2},{4,3},{5,4},{6,5},{7,6},{8,7},{9,8},{10,9},{11,1... | collective-permute-start | bytes 1216520 | tf_op jit(solution)/shard_map/ppermute | solution.py:28
  59.9 61.2 %collective-permute-start.6 = (f32[6,22,3,256]{3,1,2,0:T(8,128)}, f32[6,22,3,256]{3,1,2,0:T(8,128)}, u32[]{:S(2)}, u32[]{:S(2)}) collective-permute-start(f32[6,22,3,256]{3,1,2,0:T(8,128)} %get-tuple-element.56), channel_id=1, source_target_pairs={{0,1},{1,2},{2,3},{3,4},{4,5},{5,6},{6,7},{7,8},{8,9},{9,10},{10,1... | collective-permute-start | bytes 1216520 | tf_op jit(solution)/shard_map/ppermute | solution.py:25
  96.5 1.5 copy-start.15
  114.4 6.8 %copy-start.3 = (f32[6,16,8,256]{3,1,2,0:T(8,128)S(1)}, f32[6,16,8,256]{3,1,2,0:T(8,128)}, u32[]{:S(2)}) copy-start(f32[6,16,8,256]{3,1,2,0:T(8,128)} %copy-done.2) | copy-start | bytes 2359300
  116.9 14.9 %all-to-all-start = ((f32[16,1,4928]{2,1,0:T(1,128)}), f32[16,1,4928]{2,1,0:T(1,128)}, u32[]{:S(2)}, u32[]{:S(2)}) async-start(f32[16,1,4928]{2,1,0:T(1,128)} %reshape.52), calls=%async_computation | async-start | bytes 638976 | tf_op jit(solution)/shard_map/all_to_all | solution.py:141
  122.6 1.8 %copy-start.4 = (f32[46,34,256]{2,1,0:T(8,128)S(1)}, f32[46,34,256]{2,1,0:T(8,128)}, u32[]{:S(2)}) copy-start(f32[46,34,256]{2,1,0:T(8,128)} %get-tuple-element.35) | copy-start | bytes 4804612
  123.8 2.0 %copy-start.7 = (f32[44,32,256]{2,1,0:T(8,128)S(1)}, f32[44,32,256]{2,1,0:T(8,128)}, u32[]{:S(2)}) copy-start(f32[44,32,256]{2,1,0:T(8,128)} %get-tuple-element.32) | copy-start | bytes 4325380
  148.3 1.2 copy-start.12
  152.2 8.3 %copy-start.5 = (f32[44,32,256]{2,1,0:T(8,128)S(1)}, f32[44,32,256]{2,1,0:T(8,128)}, u32[]{:S(2)}) copy-start(f32[44,32,256]{2,1,0:T(8,128)} %get-tuple-element.51) | copy-start | bytes 4325380
  152.2 8.3 %copy-start.6 = (f32[44,32,256]{2,1,0:T(8,128)S(1)}, f32[44,32,256]{2,1,0:T(8,128)}, u32[]{:S(2)}) copy-start(f32[44,32,256]{2,1,0:T(8,128)} %get-tuple-element.52) | copy-start | bytes 4325380
  155.8 14.8 %all-to-all-start.1 = ((f32[16,1,2048]{2,1,0:T(1,128)}), f32[16,1,2048]{2,1,0:T(1,128)S(1)}, u32[]{:S(2)}, u32[]{:S(2)}) async-start(f32[16,1,2048]{2,1,0:T(1,128)} %reshape.54), calls=%async_computation.1 | async-start | bytes 262144 | tf_op jit(solution)/shard_map/all_to_all | solution.py:155

commit v5 on v1

--- a/solution.py
+++ b/solution.py
@@ -1,7 +1,11 @@
 import jax
 import jax.numpy as jnp
+import functools
+
 import numpy as np
 from jax import lax
+from jax.experimental import pallas as pl
+from jax.experimental.pallas import tpu as pltpu
 from jax.sharding import PartitionSpec as P
 
 STEPS = 4
@@ -15,6 +19,90 @@
 spring_term = 0.2
 first_weight = 0.5956
 second_weight = 2.695
+
+
+MESH = pl.DeviceIdType.MESH
+TILE = 8
+DIRS = [(sx, sy) for sx in (-1, 0, 1) for sy in (-1, 0, 1) if (sx, sy) != (0, 0)]
+
+
+def _src_window(side, size, width):
+    return {1: slice(size - width, size), -1: slice(0, width), 0: slice(0, size)}[side]
+
+
+def _dst_window(side, size, width):
+    return {1: slice(0, width), -1: slice(width + size, size + 2 * width), 0: slice(width, width + size)}[side]
+
+
+def halo_kernel(hx, nx, ny, blk_ref, out_ref, ext, send_sem, recv_sem):
+    c, x, y, z = blk_ref.shape
+    t = TILE
+    gx = lax.axis_index("gx")
+    gy = lax.axis_index("gy")
+
+    def exists(sx, sy):
+        return (gx + sx >= 0) & (gx + sx < nx) & (gy + sy >= 0) & (gy + sy < ny)
+
+    barrier = pltpu.get_barrier_semaphore()
+    for sx, sy in DIRS:
+        @pl.when(exists(sx, sy))
+        def _():
+            pl.semaphore_signal(barrier, inc=1, device_id=(gx + sx, gy + sy), device_id_type=MESH)
+    row = (gx + nx - 1) // nx + 1 + (2 * nx - 2 - gx) // nx
+    col = (gy + ny - 1) // ny + 1 + (2 * ny - 2 - gy) // ny
+    pl.semaphore_wait(barrier, row * col - 1)
+
+    copies = []
+    for k, (sx, sy) in enumerate(DIRS):
+        copy = pltpu.make_async_remote_copy(
+            src_ref=blk_ref.at[:, _src_window(sx, x, hx), _src_window(sy, y, t), :],
+            dst_ref=ext.at[:, _dst_window(sx, x, hx), _dst_window(sy, y, t), :],
+            send_sem=send_sem.at[k],
+            recv_sem=recv_sem.at[k],
+            device_id=(lax.rem(gx + sx + nx, nx), lax.rem(gy + sy + ny, ny)),
+            device_id_type=MESH,
+        )
+        copies.append(copy)
+
+        @pl.when(exists(sx, sy))
+        def _():
+            copy.start()
+
+    ext[:, hx:hx + x, t:t + y, :] = blk_ref[...]
+    for sx, sy in DIRS:
+        xs, ys = _dst_window(sx, x, hx), _dst_window(sy, y, t)
+
+        @pl.when(jnp.logical_not(exists(-sx, -sy)))
+        def _():
+            ext[:, xs, ys, :] = jnp.zeros((c, xs.stop - xs.start, ys.stop - ys.start, z), ext.dtype)
+
+    for (sx, sy), copy in zip(DIRS, copies):
+        @pl.when(exists(sx, sy))
+        def _():
+            copy.wait_send()
+
+        @pl.when(exists(-sx, -sy))
+        def _():
+            copy.wait_recv()
+    out_ref[...] = ext[...]
+
+
+def halo_exchange(block, hx, cid):
+    c, x, y, z = block.shape
+    nx, ny = lax.axis_size("gx"), lax.axis_size("gy")
+    shape = (c, x + 2 * hx, y + 2 * TILE, z)
+    return pl.pallas_call(
+        functools.partial(halo_kernel, hx, nx, ny),
+        out_shape=jax.ShapeDtypeStruct(shape, block.dtype),
+        in_specs=[pl.BlockSpec(memory_space=pltpu.VMEM)],
+        out_specs=pl.BlockSpec(memory_space=pltpu.VMEM),
+        scratch_shapes=[
+            pltpu.VMEM(shape, block.dtype),
+            pltpu.SemaphoreType.DMA((len(DIRS),)),
+            pltpu.SemaphoreType.DMA((len(DIRS),)),
+        ],
+        compiler_params=pltpu.CompilerParams(collective_id=cid, has_side_effects=True),
+    )(block)
 
 
 def padded_2(block, sides, width):
@@ -113,7 +201,7 @@
 def on_device(concentration, order_field, phase_labels, displacement, body_load):
     h = FINE_HALO
     fields = jnp.stack([concentration, order_field, mobility_of(phase_labels)])
-    fields = padded_2(fields, (("gx", 1), ("gy", 2)), h)
+    fields = halo_exchange(fields, h, 0)[:, :, TILE - h:TILE - h + fields.shape[2] + 2 * h]
     conc, order, mob = fields[0], fields[1], fields[2]
     for step in range(STEPS):
         conc, order, mob = advance(conc, order, mob, step == STEPS - 1)
@@ -124,7 +212,7 @@
 
     coarse = restrict_xzy(order)
     stiff = lax.all_to_all(coarse, "gy", split_axis=1, concat_axis=2, tiled=True)
-    stiff_pad = padded_2(stiff, (("gx", 0), ("gy", 1)), m)
+    stiff_pad = halo_exchange(stiff[None], m, 1)[0, :, TILE - m:TILE - m + stiff.shape[1] + 2 * m]
 
     faces, diag, center = face_terms(stiff_pad)
     for weight in (first_weight, second_weight):

time: 135 us -> 143 us (1.059); the launches traced: 133 us -> 143 us
  Pallas kernels: 0 us -> 47 us
  starting transfers between devices: 60.5 us -> 29.7 us
  waiting for transfers between devices: 22.5 us -> 9.01 us
  local copies, waits for them, and re-layouts: 17.9 us -> 24.2 us
    pallas_call x0 -> x2, Pallas kernels: none -> 47 us  [halo_exchange(): pl.pallas_call(functools.partial(halo_kernel, hx, nx, ny), out_shape=jax....]
    ppermute x6 -> x2, starting transfers between devices: 21.1 us -> 7.24 us  [padded_2(): lax.ppermute(lax.slice_in_dim(block, block.shape[dim] - width, None, axis...]
    ppermute x6 -> x2, waiting for transfers between devices: 10.5 us -> 0.01 us  [padded_2(): lax.ppermute(lax.slice_in_dim(block, block.shape[dim] - width, None, axis...]
    ppermute x6 -> x2, starting transfers between devices: 13.8 us -> 5.6 us  [padded_2(): lax.ppermute(lax.slice_in_dim(block, 0, width, axis=dim), axis, backward)]
    all_to_all x1, starting transfers between devices: 14.6 us -> 8.65 us  [on_device(): lax.all_to_all(coarse, 'gy', split_axis=1, concat_axis=2, tiled=True)]
    ppermute x6 -> x2, waiting for transfers between devices: 3.2 us -> 0.01 us  [padded_2(): lax.ppermute(lax.slice_in_dim(block, 0, width, axis=dim), axis, backward)]
    squeeze x1, local copies, waits for them, and re-layouts: 0.34 us -> 3.4 us  [on_device(): conc, order, mob = (fields[0], fields[1], fields[2])]
    all_to_all x1, starting transfers between devices: 11.1 us -> 8.2 us  [on_device(): lax.all_to_all(energy, 'gy', split_axis=2, concat_axis=1, tiled=True)]
  transfers between devices with their start and end apart: 14 -> 6, of which waited for: 7 -> 2; matrix products, arithmetic and copies ran while one was open for 26% -> 29% of each run, Pallas kernels for 0% -> 33%
where the time goes in v5:
time: 143 us
  Pallas kernels  47 us (33%)
  other arithmetic  31.1 us (22%)
  starting transfers between devices  29.7 us (21%)
  local copies, waits for them, and re-layouts  24.2 us (17%)
  waiting for transfers between devices  9.01 us (6%)
    pallas_call x2, Pallas kernels, halo_exchange(): pl.pallas_call(functools.partial(halo_kernel, hx, nx, ny), out_shape=jax....  47 us
    sub x4, other arithmetic, advance(): chem = conc_pad - order_pad * order_pad * (3.0 - 2.0 * order_pad)  16.6 us
    all_to_all x1, starting transfers between devices, on_device(): lax.all_to_all(coarse, 'gy', split_axis=1, concat_axis=2, tiled=True)  8.65 us
    all_to_all x1, starting transfers between devices, on_device(): lax.all_to_all(energy, 'gy', split_axis=2, concat_axis=1, tiled=True)  8.2 us
    all_to_all x1, waiting for transfers between devices, on_device(): lax.all_to_all(energy, 'gy', split_axis=2, concat_axis=1, tiled=True)  7.53 us
    ppermute x2, starting transfers between devices, padded_2(): lax.ppermute(lax.slice_in_dim(block, block.shape[dim] - width, None, axis...  7.24 us
    unnamed x17, local copies, waits for them, and re-layouts  7.21 us
    ppermute x2, starting transfers between devices, padded_2(): lax.ppermute(lax.slice_in_dim(block, 0, width, axis=dim), axis, backward)  5.6 us
  transfers between devices with their start and end apart: 6, of which 2 were waited for; matrix products, arithmetic and copies ran while one was open for 29% of the time, Pallas kernels for 33%

profile of v5, /device:TPU:2, one launch (start us, length us, event | category | flops | bytes accessed | tf_op | source)
XLA Modules:
  0.0 142.6 jit_solution(16189937066439612467)
XLA Ops:
  0.6 1.2 copy_dynamic-update-slice_fusion.1
  1.9 1.1 copy_dynamic-update-slice_fusion
  3.0 0.8 fusion.103
  3.8 4.3 %collective-permute-start.1 = (f32[6,3,8,256]{3,1,2,0:T(4,128)}, f32[6,3,8,256]{3,1,2,0:T(4,128)S(1)}, u32[]{:S(2)}, u32[]{:S(2)}) collective-permute-start(f32[6,3,8,256]{3,1,2,0:T(4,128)} %get-tuple-element.60), channel_id=1, source_target_pairs={{16,0},{32,16},{48,32},{64,48},{80,64},{96,80},{112,96},{128,112},... | collective-permute-start | bytes 442376 | tf_op jit(solution)/shard_map/ppermute | solution.py:116
  8.2 1.9 %collective-permute-start = (f32[6,3,8,256]{3,1,2,0:T(4,128)}, f32[6,3,8,256]{3,1,2,0:T(4,128)}, u32[]{:S(2)}, u32[]{:S(2)}) collective-permute-start(f32[6,3,8,256]{3,1,2,0:T(4,128)} %get-tuple-element.59), channel_id=1, source_target_pairs={{0,16},{16,32},{32,48},{48,64},{64,80},{80,96},{96,112},{112,128},... | collective-permute-start | bytes 442376 | tf_op jit(solution)/shard_map/ppermute | solution.py:113
  10.1 0.3 add_bitcast_fusion
  10.4 2.0 %pad_maximum_fusion.blk_ref = f32[3,32,32,256]{3,2,1,0:T(8,128)} fusion(f32[1,32,32,256]{3,2,1,0:T(8,128)S(1)} %add_bitcast_fusion, f32[1,32,32,256]{3,2,1,0:T(8,128)S(1)} %bitcast.45, f32[1,32,32,256]{3,2,1,0:T(8,128)S(1)} %bitcast.46), kind=kLoop, calls=%fused_computation | loop fusion | flops 1572864 | bytes 6291456 | tf_op jit(solution)/shard_map/stack | solution.py:203
  12.4 36.5 %shard_map.93 = f32[3,40,48,256]{3,2,1,0:T(8,128)} custom-call(f32[3,32,32,256]{3,2,1,0:T(8,128)} %pad_maximum_fusion.blk_ref), custom_call_target="tpu_custom_call" | custom-call | tf_op jit(solution)/shard_map/pallas_call | solution.py:94
  48.9 2.7 %multiply_subtract_fusion = f32[40,40,256]{2,1,0:T(8,128)S(1)} fusion(f32[3,40,48,256]{3,2,1,0:T(8,128)} %shard_map.93), kind=kLoop, calls=%fused_computation.18 | loop fusion | flops 2048000 | bytes 4915200 | tf_op jit(solution)/shard_map/sub | solution.py:131
  51.6 3.4 %slice_bitcast_fusion.1 = (f32[40,40,256]{2,1,0:T(8,128)S(1)}, f32[40,40,256]{2,1,0:T(8,128)S(1)}, f32[40,40,256]{2,1,0:T(8,128)S(1)}) fusion(f32[3,40,48,256]{3,2,1,0:T(8,128)} %shard_map.93), kind=kLoop, calls=%fused_computation.20 | loop fusion | bytes 9830400 | tf_op jit(solution)/shard_map/squeeze | solution.py:205
  55.0 4.5 %multiply_subtract_fusion.1 = (f32[38,38,256]{2,1,0:T(8,128)S(1)}, f32[38,38,256]{2,1,0:T(8,128)S(1)}, f32[38,38,256]{2,1,0:T(8,128)S(1)}) fusion(f32[40,40,256]{2,1,0:T(8,128)S(1)} %multiply_subtract_fusion, f32[40,40,256]{2,1,0:T(8,128)S(1)} %get-tuple-element.51, f32[40,40,256]{2,1,0:T(8,128)S(1)} %get-tuple-element.52, ...), kind=kLoop, calls=%fused_computation.42 | loop fusion | flops 13307904 | bytes 26390528 | tf_op jit(solution)/shard_map/sub | solution.py:131
  59.6 4.5 %multiply_subtract_fusion.2 = (f32[36,36,256]{2,1,0:T(8,128)S(1)}, f32[36,36,256]{2,1,0:T(8,128)S(1)}, f32[36,36,256]{2,1,0:T(8,128)S(1)}) fusion(f32[38,38,256]{2,1,0:T(8,128)S(1)} %get-tuple-element.47, f32[38,38,256]{2,1,0:T(8,128)S(1)} %get-tuple-element.48, f32[40,40,256]{2,1,0:T(8,128)S(1)} %get-tuple-element.52, f32[38,38,256]{2,1,0:T(8,128)S(1)} %get-tuple-element.49), kind=kLoop, calls=%fused_computation.63 | loop fusion | flops 11943936 | bytes 24788992 | tf_op jit(solution)/shard_map/sub | solution.py:131
  64.0 4.9 %multiply_subtract_fusion.3 = (f32[34,34,256]{2,1,0:T(8,128)S(1)}, f32[34,34,256]{2,1,0:T(8,128)S(1)}, f32[34,34,256]{2,1,0:T(8,128)}) fusion(f32[36,36,256]{2,1,0:T(8,128)S(1)} %get-tuple-element.44, f32[36,36,256]{2,1,0:T(8,128)S(1)} %get-tuple-element.45, f32[40,40,256]{2,1,0:T(8,128)S(1)} %get-tuple-element.52, f32[36,36,256]{2,1,0:T(8,128)S(1)} %get-tuple-element.46), kind=kLoop, calls=%fused_computation.84 | loop fusion | flops 10653696 | bytes 23212032 | tf_op jit(solution)/shard_map/sub | solution.py:131
  68.9 2.4 %bitcast_reduce_fusion = (f32[16,32,256]{2,1,0:T(8,128)S(1)}, f32[32,32,256]{2,1,0:T(8,128)}) fusion(f32[34,34,256]{2,1,0:T(8,128)S(1)} %get-tuple-element.41, f32[34,34,256]{2,1,0:T(8,128)S(1)} %get-tuple-element.42, f32[40,40,256]{2,1,0:T(8,128)S(1)} %get-tuple-element.52), kind=kLoop, calls=%fused_computation.107 | loop fusion | flops 5636096 | bytes 10305536 | tf_op jit(solution)/shard_map/reduce_sum | solution.py:156
  71.3 0.3 bitcast_reduce_fusion.1
  71.6 0.5 fusion.43
  72.1 0.5 copy.179
  72.6 1.0 reshape.38
  73.7 8.6 %all-to-all-start = ((f32[16,1,2048]{2,1,0:T(1,128)}), f32[16,1,2048]{2,1,0:T(1,128)S(1)}, u32[]{:S(2)}, u32[]{:S(2)}) async-start(f32[16,1,2048]{2,1,0:T(1,128)} %reshape.38), calls=%async_computation | async-start | bytes 262144 | tf_op jit(solution)/shard_map/all_to_all | solution.py:214
  82.3 2.0 %pad_maximum_fusion.4 = (f32[6,22,3,256]{3,1,2,0:T(8,128)}, f32[6,22,3,256]{3,1,2,0:T(8,128)}) fusion(f32[6,3,8,256]{3,1,2,0:T(4,128)S(1)} %collective-permute-done.1, f32[6,16,8,256]{3,1,2,0:T(8,128)S(1)} %copy_dynamic-update-slice_fusion, f32[6,3,8,256]{3,1,2,0:T(4,128)} %collective-permute-done), kind=kLoop, calls=%fused_computation.148 | loop fusion | flops 405504 | bytes 1892352 | tf_op jit(solution)/shard_map/slice | solution.py:114
  84.3 1.3 collective-permute-start.3
  85.6 5.3 %collective-permute-start.2 = (f32[6,22,3,256]{3,1,2,0:T(8,128)}, f32[6,22,3,256]{3,1,2,0:T(8,128)}, u32[]{:S(2)}, u32[]{:S(2)}) collective-permute-start(f32[6,22,3,256]{3,1,2,0:T(8,128)} %get-tuple-element.55), channel_id=1, source_target_pairs={{0,1},{1,2},{2,3},{3,4},{4,5},{5,6},{6,7},{7,8},{8,9},{9,10},{10,1... | collective-permute-start | bytes 1216520 | tf_op jit(solution)/shard_map/ppermute | solution.py:113
  90.9 1.5 %all-to-all-done = f32[16,1,2048]{2,1,0:T(1,128)S(1)} async-done(((f32[16,1,2048]{2,1,0:T(1,128)}), f32[16,1,2048]{2,1,0:T(1,128)S(1)}, u32[]{:S(2)}, u32[]{:S(2)}) %all-to-all-start) | async-done | bytes 131104 | tf_op jit(solution)/shard_map/all_to_all | solution.py:214
  92.4 0.6 broadcast.198
  93.0 0.9 reduce
  93.9 0.4 reshape.39
  94.3 1.6 %copy.181 = f32[16,8,16,16]{3,2,1,0:T(8,128)} copy(f32[16,8,16,16]{3,0,1,2:T(8,128)S(1)} %bitcast.42) | data formatting | bytes 262144 | tf_op jit(solution)/shard_map/all_to_all | solution.py:214
  95.8 2.3 %broadcast_in_dim.22.blk_ref = f32[1,16,8,256]{3,2,1,0:T(8,128)} reshape(f32[16,8,16,16]{3,2,1,0:T(8,128)} %copy.181) | data formatting | bytes 262144 | tf_op jit(solution)/shard_map/broadcast_in_dim | solution.py:215
  98.1 10.4 %shard_map.94 = f32[1,22,24,256]{3,2,1,0:T(8,128)} custom-call(f32[1,16,8,256]{3,2,1,0:T(8,128)} %broadcast_in_dim.22.blk_ref), custom_call_target="tpu_custom_call" | custom-call | tf_op jit(solution)/shard_map/pallas_call | solution.py:94
  108.5 1.1 slice_bitcast_fusion.3
  109.8 0.4 multiply_add_fusion
  113.1 1.5 %pad_maximum_fusion.1 = f32[6,22,14,256]{3,1,2,0:T(8,128)S(1)} fusion(f32[6,22,3,256]{3,1,2,0:T(8,128)} %collective-permute-done.3, f32[6,3,8,256]{3,1,2,0:T(4,128)S(1)} %collective-permute-done.1, f32[6,16,8,256]{3,1,2,0:T(8,128)S(1)} %copy_dynamic-update-slice_fusion, f32[6,3,8,256]{3,1,2,0:T(4,128)} %collective-permute-done, ...), kind=kLoop, calls=%fused_computation.17 | loop fusion | flops 1892352 | bytes 3784704 | tf_op jit(solution)/shard_map/concatenate | solution.py:117
  114.6 0.3 fusion.101
  114.9 0.9 fusion.67
  115.7 0.3 fusion.102
  116.0 0.7 fusion.78
  116.7 0.2 fusion.104
  116.9 0.4 fusion.84
  117.4 1.3 copy.208
  118.7 2.3 %reshape.40 = f32[16,1,2048]{2,1,0:T(1,128)} reshape(f32[256,8,16]{2,1,0:T(8,128)} %bitcast.41) | data formatting | bytes 262144
  121.0 8.2 %all-to-all-start.1 = ((f32[16,1,2048]{2,1,0:T(1,128)}), f32[16,1,2048]{2,1,0:T(1,128)S(1)}, u32[]{:S(2)}, u32[]{:S(2)}) async-start(f32[16,1,2048]{2,1,0:T(1,128)} %reshape.40), calls=%async_computation.1 | async-start | bytes 262144 | tf_op jit(solution)/shard_map/all_to_all | solution.py:228
  129.2 1.7 %fusion.48 = f32[32,32,256]{2,1,0:T(8,128)} fusion(f32[34,34,256]{2,1,0:T(8,128)S(1)} %get-tuple-element.41, f32[34,34,256]{2,1,0:T(8,128)S(1)} %copy-done), kind=kLoop, calls=%fused_computation.92 | loop fusion | flops 2359296 | bytes 8732672 | tf_op jit(solution)/shard_map/add | solution.py:136
  130.9 1.0 copy.211
  131.9 7.5 %all-to-all-done.1 = f32[16,1,2048]{2,1,0:T(1,128)S(1)} async-done(((f32[16,1,2048]{2,1,0:T(1,128)}), f32[16,1,2048]{2,1,0:T(1,128)S(1)}, u32[]{:S(2)}, u32[]{:S(2)}) %all-to-all-start.1) | async-done | bytes 131104 | tf_op jit(solution)/shard_map/all_to_all | solution.py:228
  139.4 0.9 reduce.1
  140.4 0.4 reshape.41
  140.7 0.9 copy.210
  141.7 1.0 copy.212
  (53 shorter events, 2.8 us)
Async XLA Ops:
  0.6 9.5 %copy-start.1 = (s32[32,32,256]{2,1,0:T(8,128)S(1)}, s32[32,32,256]{2,1,0:T(8,128)}, u32[]{:S(2)}) copy-start(s32[32,32,256]{2,1,0:T(8,128)} %param.8) | copy-start | bytes 3145732
  3.0 7.4 %copy-start.2 = (f32[32,32,256]{2,1,0:T(8,128)S(1)}, f32[32,32,256]{2,1,0:T(8,128)}, u32[]{:S(2)}) copy-start(f32[32,32,256]{2,1,0:T(8,128)} %param.7) | copy-start | bytes 3145732
  3.0 7.4 %copy-start.3 = (f32[32,32,256]{2,1,0:T(8,128)S(1)}, f32[32,32,256]{2,1,0:T(8,128)}, u32[]{:S(2)}) copy-start(f32[32,32,256]{2,1,0:T(8,128)} %param.6) | copy-start | bytes 3145732
  3.8 78.5 %collective-permute-start.1 = (f32[6,3,8,256]{3,1,2,0:T(4,128)}, f32[6,3,8,256]{3,1,2,0:T(4,128)S(1)}, u32[]{:S(2)}, u32[]{:S(2)}) collective-permute-start(f32[6,3,8,256]{3,1,2,0:T(4,128)} %get-tuple-element.60), channel_id=1, source_target_pairs={{16,0},{32,16},{48,32},{64,48},{80,64},{96,80},{112,96},{128,112},... | collective-permute-start | bytes 442376 | tf_op jit(solution)/shard_map/ppermute | solution.py:116
  8.2 74.2 %collective-permute-start = (f32[6,3,8,256]{3,1,2,0:T(4,128)}, f32[6,3,8,256]{3,1,2,0:T(4,128)}, u32[]{:S(2)}, u32[]{:S(2)}) collective-permute-start(f32[6,3,8,256]{3,1,2,0:T(4,128)} %get-tuple-element.59), channel_id=1, source_target_pairs={{0,16},{16,32},{32,48},{48,64},{64,80},{80,96},{96,112},{112,128},... | collective-permute-start | bytes 442376 | tf_op jit(solution)/shard_map/ppermute | solution.py:113
  68.9 2.7 %copy-start.4 = (f32[256,128,1]{1,0,2:T(8,128)S(1)}, f32[256,128,1]{1,0,2:T(8,128)}, u32[]{:S(2)}) copy-start(f32[256,128,1]{1,0,2:T(8,128)} %constant.99) | copy-start | bytes 393220
  73.7 18.7 %all-to-all-start = ((f32[16,1,2048]{2,1,0:T(1,128)}), f32[16,1,2048]{2,1,0:T(1,128)S(1)}, u32[]{:S(2)}, u32[]{:S(2)}) async-start(f32[16,1,2048]{2,1,0:T(1,128)} %reshape.38), calls=%async_computation | async-start | bytes 262144 | tf_op jit(solution)/shard_map/all_to_all | solution.py:214
  84.3 28.7 %collective-permute-start.3 = (f32[6,22,3,256]{3,1,2,0:T(8,128)}, f32[6,22,3,256]{3,1,2,0:T(8,128)}, u32[]{:S(2)}, u32[]{:S(2)}) collective-permute-start(f32[6,22,3,256]{3,1,2,0:T(8,128)} %get-tuple-element.56), channel_id=1, source_target_pairs={{1,0},{2,1},{3,2},{4,3},{5,4},{6,5},{7,6},{8,7},{9,8},{10,9},{11,1... | collective-permute-start | bytes 1216520 | tf_op jit(solution)/shard_map/ppermute | solution.py:116
  85.6 27.5 %collective-permute-start.2 = (f32[6,22,3,256]{3,1,2,0:T(8,128)}, f32[6,22,3,256]{3,1,2,0:T(8,128)}, u32[]{:S(2)}, u32[]{:S(2)}) collective-permute-start(f32[6,22,3,256]{3,1,2,0:T(8,128)} %get-tuple-element.55), channel_id=1, source_target_pairs={{0,1},{1,2},{2,3},{3,4},{4,5},{5,6},{6,7},{7,8},{8,9},{9,10},{10,1... | collective-permute-start | bytes 1216520 | tf_op jit(solution)/shard_map/ppermute | solution.py:113
  117.4 11.8 %copy-start = (f32[34,34,256]{2,1,0:T(8,128)S(1)}, f32[34,34,256]{2,1,0:T(8,128)}, u32[]{:S(2)}) copy-start(f32[34,34,256]{2,1,0:T(8,128)} %get-tuple-element.43) | copy-start | bytes 3551236
  121.0 18.5 %all-to-all-start.1 = ((f32[16,1,2048]{2,1,0:T(1,128)}), f32[16,1,2048]{2,1,0:T(1,128)S(1)}, u32[]{:S(2)}, u32[]{:S(2)}) async-start(f32[16,1,2048]{2,1,0:T(1,128)} %reshape.40), calls=%async_computation.1 | async-start | bytes 262144 | tf_op jit(solution)/shard_map/all_to_all | solution.py:228

commit v6 on v5

--- a/solution.py
+++ b/solution.py
@@ -201,7 +201,7 @@
 def on_device(concentration, order_field, phase_labels, displacement, body_load):
     h = FINE_HALO
     fields = jnp.stack([concentration, order_field, mobility_of(phase_labels)])
-    fields = halo_exchange(fields, h, 0)[:, :, TILE - h:TILE - h + fields.shape[2] + 2 * h]
+    fields = padded_2(fields, (("gx", 1), ("gy", 2)), h)
     conc, order, mob = fields[0], fields[1], fields[2]
     for step in range(STEPS):
         conc, order, mob = advance(conc, order, mob, step == STEPS - 1)
@@ -212,7 +212,7 @@
 
     coarse = restrict_xzy(order)
     stiff = lax.all_to_all(coarse, "gy", split_axis=1, concat_axis=2, tiled=True)
-    stiff_pad = halo_exchange(stiff[None], m, 1)[0, :, TILE - m:TILE - m + stiff.shape[1] + 2 * m]
+    stiff_pad = halo_exchange(stiff[None], m, 0)[0, :, TILE - m:TILE - m + stiff.shape[1] + 2 * m]
 
     faces, diag, center = face_terms(stiff_pad)
     for weight in (first_weight, second_weight):

time: 143 us -> 147 us (1.028)
  Pallas kernels: 47 us -> 11.1 us
  waiting for transfers between devices: 9.01 us -> 32.2 us
  starting transfers between devices: 29.7 us -> 45.2 us
  other arithmetic: 31.1 us -> 28.1 us
  local copies, waits for them, and re-layouts: 24.2 us -> 26.9 us
    pallas_call x2 -> x1, Pallas kernels: 47 us -> 11.1 us  [halo_exchange(): pl.pallas_call(functools.partial(halo_kernel, hx, nx, ny), out_shape=jax....]
    ppermute x2 -> x4, waiting for transfers between devices: 0.01 us -> 8.3 us  [padded_2(): lax.ppermute(lax.slice_in_dim(block, block.shape[dim] - width, None, axis...]
    ppermute x2 -> x4, waiting for transfers between devices: 0.01 us -> 7.71 us  [padded_2(): lax.ppermute(lax.slice_in_dim(block, 0, width, axis=dim), axis, backward)]
    ppermute x2 -> x4, starting transfers between devices: 5.6 us -> 12.8 us  [padded_2(): lax.ppermute(lax.slice_in_dim(block, 0, width, axis=dim), axis, backward)]
    all_to_all x1, waiting for transfers between devices: 1.47 us -> 8.6 us  [on_device(): lax.all_to_all(coarse, 'gy', split_axis=1, concat_axis=2, tiled=True)]
    all_to_all x1, starting transfers between devices: 8.65 us -> 15.5 us  [on_device(): lax.all_to_all(coarse, 'gy', split_axis=1, concat_axis=2, tiled=True)]
    ppermute x2 -> x4, starting transfers between devices: 7.24 us -> 13 us  [padded_2(): lax.ppermute(lax.slice_in_dim(block, block.shape[dim] - width, None, axis...]
    all_to_all x1, starting transfers between devices: 8.2 us -> 3.92 us  [on_device(): lax.all_to_all(energy, 'gy', split_axis=2, concat_axis=1, tiled=True)]
  transfers between devices with their start and end apart: 6 -> 10, of which waited for: 2 -> 8; matrix products, arithmetic and copies ran while one was open for 29% -> 4% of each run, Pallas kernels for 33% -> 0%
where the time goes in v6:
time: 147 us; the launch traced here: 146 us
  starting transfers between devices  45.2 us (31%)
  waiting for transfers between devices  32.2 us (22%)
  other arithmetic  28.1 us (19%)
  local copies, waits for them, and re-layouts  26.9 us (18%)
  Pallas kernels  11.1 us (8%)
    all_to_all x1, starting transfers between devices, on_device(): lax.all_to_all(coarse, 'gy', split_axis=1, concat_axis=2, tiled=True)  15.5 us
    sub x4, other arithmetic, advance(): chem = conc_pad - order_pad * order_pad * (3.0 - 2.0 * order_pad)  14.1 us
    ppermute x4, starting transfers between devices, padded_2(): lax.ppermute(lax.slice_in_dim(block, block.shape[dim] - width, None, axis...  13 us
    ppermute x4, starting transfers between devices, padded_2(): lax.ppermute(lax.slice_in_dim(block, 0, width, axis=dim), axis, backward)  12.8 us
    pallas_call x1, Pallas kernels, halo_exchange(): pl.pallas_call(functools.partial(halo_kernel, hx, nx, ny), out_shape=jax....  11.1 us
    unnamed x23, local copies, waits for them, and re-layouts  10.5 us
    all_to_all x1, waiting for transfers between devices, on_device(): lax.all_to_all(coarse, 'gy', split_axis=1, concat_axis=2, tiled=True)  8.6 us
    ppermute x4, waiting for transfers between devices, padded_2(): lax.ppermute(lax.slice_in_dim(block, block.shape[dim] - width, None, axis...  8.3 us
  transfers between devices with their start and end apart: 10, of which 8 were waited for; matrix products, arithmetic and copies ran while one was open for 4% of the time, Pallas kernels for 0%

profile of v6, /device:TPU:2, one launch (start us, length us, event | category | flops | bytes accessed | tf_op | source)
XLA Modules:
  0.0 145.8 jit_solution(9587200833309490209)
XLA Ops:
  0.7 1.6 %add_bitcast_fusion = f32[1,32,32,256]{3,2,1,0:T(8,128)S(1)} fusion(s32[32,32,256]{2,1,0:T(8,128)} %param.8), kind=kLoop, calls=%fused_computation.108 | loop fusion | flops 2097152 | bytes 2097152 | tf_op jit(solution)/shard_map/stack | solution.py:203
  2.6 4.5 %collective-permute-start.1 = (f32[3,4,32,256]{3,2,1,0:T(8,128)S(1)}, f32[3,4,32,256]{3,2,1,0:T(8,128)S(1)}, u32[]{:S(2)}, u32[]{:S(2)}) collective-permute-start(f32[3,4,32,256]{3,2,1,0:T(8,128)S(1)} %get-tuple-element.56), channel_id=1, source_target_pairs={{16,0},{32,16},{48,32},{64,48},{80,64},{96,80},{112,96},{128,112},... | collective-permute-start | bytes 1179656 | tf_op jit(solution)/shard_map/ppermute | solution.py:116
  7.0 1.9 %collective-permute-start = (f32[3,4,32,256]{3,2,1,0:T(8,128)S(1)}, f32[3,4,32,256]{3,2,1,0:T(8,128)S(1)}, u32[]{:S(2)}, u32[]{:S(2)}) collective-permute-start(f32[3,4,32,256]{3,2,1,0:T(8,128)S(1)} %get-tuple-element.55), channel_id=1, source_target_pairs={{0,16},{16,32},{32,48},{48,64},{64,80},{80,96},{96,112},{112,128},... | collective-permute-start | bytes 1179656 | tf_op jit(solution)/shard_map/ppermute | solution.py:113
  9.3 5.8 %collective-permute-start.5 = (f32[6,3,8,256]{3,1,2,0:T(4,128)S(1)}, f32[6,3,8,256]{3,1,2,0:T(4,128)S(1)}, u32[]{:S(2)}, u32[]{:S(2)}) collective-permute-start(f32[6,3,8,256]{3,1,2,0:T(4,128)S(1)} %get-tuple-element.64), channel_id=1, source_target_pairs={{16,0},{32,16},{48,32},{64,48},{80,64},{96,80},{112,96},{128,112},... | collective-permute-start | bytes 442376 | tf_op jit(solution)/shard_map/ppermute | solution.py:116
  15.1 1.9 %collective-permute-start.4 = (f32[6,3,8,256]{3,1,2,0:T(4,128)S(1)}, f32[6,3,8,256]{3,1,2,0:T(4,128)S(1)}, u32[]{:S(2)}, u32[]{:S(2)}) collective-permute-start(f32[6,3,8,256]{3,1,2,0:T(4,128)S(1)} %get-tuple-element.63), channel_id=1, source_target_pairs={{0,16},{16,32},{32,48},{48,64},{64,80},{80,96},{96,112},{112,128},... | collective-permute-start | bytes 442376 | tf_op jit(solution)/shard_map/ppermute | solution.py:113
  17.0 1.2 collective-permute-done.5
  18.2 5.9 %collective-permute-done.4 = f32[6,3,8,256]{3,1,2,0:T(4,128)S(1)} collective-permute-done((f32[6,3,8,256]{3,1,2,0:T(4,128)S(1)}, f32[6,3,8,256]{3,1,2,0:T(4,128)S(1)}, u32[]{:S(2)}, u32[]{:S(2)}) %collective-permute-start.4) | collective-permute-done | bytes 147488 | tf_op jit(solution)/shard_map/ppermute | solution.py:113
  24.3 1.3 collective-permute-start.7
  25.6 4.6 %collective-permute-start.6 = (f32[6,22,3,256]{3,1,2,0:T(8,128)S(1)}, f32[6,22,3,256]{3,1,2,0:T(8,128)S(1)}, u32[]{:S(2)}, u32[]{:S(2)}) collective-permute-start(f32[6,22,3,256]{3,1,2,0:T(8,128)S(1)} %get-tuple-element.59), channel_id=1, source_target_pairs={{0,1},{1,2},{2,3},{3,4},{4,5},{5,6},{6,7},{7,8},{8,9},{9,10},{10,1... | collective-permute-start | bytes 1216520 | tf_op jit(solution)/shard_map/ppermute | solution.py:113
  30.4 1.3 collective-permute-start.3
  31.7 4.6 %collective-permute-start.2 = (f32[3,40,4,256]{3,2,1,0:T(4,128)S(1)}, f32[3,40,4,256]{3,2,1,0:T(4,128)S(1)}, u32[]{:S(2)}, u32[]{:S(2)}) collective-permute-start(f32[3,40,4,256]{3,2,1,0:T(4,128)S(1)} %get-tuple-element.53), channel_id=1, source_target_pairs={{0,1},{1,2},{2,3},{3,4},{4,5},{5,6},{6,7},{7,8},{8,9},{9,10},{10,1... | collective-permute-start | bytes 1474568 | tf_op jit(solution)/shard_map/ppermute | solution.py:113
  36.3 2.6 %collective-permute-done.7 = f32[6,22,3,256]{3,1,2,0:T(8,128)S(1)} collective-permute-done((f32[6,22,3,256]{3,1,2,0:T(8,128)S(1)}, f32[6,22,3,256]{3,1,2,0:T(8,128)S(1)}, u32[]{:S(2)}, u32[]{:S(2)}) %collective-permute-start.7) | collective-permute-done | bytes 405536 | tf_op jit(solution)/shard_map/ppermute | solution.py:116
  38.9 1.2 collective-permute-done.6
  40.4 3.8 %collective-permute-done.3 = f32[3,40,4,256]{3,2,1,0:T(4,128)S(1)} collective-permute-done((f32[3,40,4,256]{3,2,1,0:T(4,128)S(1)}, f32[3,40,4,256]{3,2,1,0:T(4,128)S(1)}, u32[]{:S(2)}, u32[]{:S(2)}) %collective-permute-start.3) | collective-permute-done | bytes 491552 | tf_op jit(solution)/shard_map/ppermute | solution.py:116
  44.2 1.2 collective-permute-done.2
  45.4 1.0 pad_maximum_fusion
  47.0 4.5 %multiply_subtract_fusion.1 = (f32[38,38,256]{2,1,0:T(8,128)S(1)}, f32[38,38,256]{2,1,0:T(8,128)S(1)}, f32[38,38,256]{2,1,0:T(8,128)S(1)}) fusion(f32[40,40,256]{2,1,0:T(8,128)S(1)} %multiply_subtract_fusion, f32[40,40,256]{2,1,0:T(8,128)S(1)} %get-tuple-element.51, f32[40,40,256]{2,1,0:T(8,128)S(1)} %get-tuple-element.52, ...), kind=kLoop, calls=%fused_computation.42 | loop fusion | flops 13307904 | bytes 26390528 | tf_op jit(solution)/shard_map/sub | solution.py:131
  51.6 4.5 %multiply_subtract_fusion.2 = (f32[36,36,256]{2,1,0:T(8,128)S(1)}, f32[36,36,256]{2,1,0:T(8,128)S(1)}, f32[36,36,256]{2,1,0:T(8,128)S(1)}) fusion(f32[38,38,256]{2,1,0:T(8,128)S(1)} %get-tuple-element.47, f32[38,38,256]{2,1,0:T(8,128)S(1)} %get-tuple-element.48, f32[40,40,256]{2,1,0:T(8,128)S(1)} %get-tuple-element.52, f32[38,38,256]{2,1,0:T(8,128)S(1)} %get-tuple-element.49), kind=kLoop, calls=%fused_computation.63 | loop fusion | flops 11943936 | bytes 24788992 | tf_op jit(solution)/shard_map/sub | solution.py:131
  56.1 4.9 %multiply_subtract_fusion.3 = (f32[34,34,256]{2,1,0:T(8,128)S(1)}, f32[34,34,256]{2,1,0:T(8,128)S(1)}, f32[34,34,256]{2,1,0:T(8,128)}) fusion(f32[36,36,256]{2,1,0:T(8,128)S(1)} %get-tuple-element.44, f32[36,36,256]{2,1,0:T(8,128)S(1)} %get-tuple-element.45, f32[40,40,256]{2,1,0:T(8,128)S(1)} %get-tuple-element.52, f32[36,36,256]{2,1,0:T(8,128)S(1)} %get-tuple-element.46), kind=kLoop, calls=%fused_computation.84 | loop fusion | flops 10653696 | bytes 23212032 | tf_op jit(solution)/shard_map/sub | solution.py:131
  60.9 2.4 %bitcast_reduce_fusion = (f32[16,32,256]{2,1,0:T(8,128)S(1)}, f32[32,32,256]{2,1,0:T(8,128)}) fusion(f32[34,34,256]{2,1,0:T(8,128)S(1)} %get-tuple-element.41, f32[34,34,256]{2,1,0:T(8,128)S(1)} %get-tuple-element.42, f32[40,40,256]{2,1,0:T(8,128)S(1)} %get-tuple-element.52), kind=kLoop, calls=%fused_computation.107 | loop fusion | flops 5636096 | bytes 10305536 | tf_op jit(solution)/shard_map/reduce_sum | solution.py:156
  63.6 1.1 fusion.43
  64.8 2.3 %copy.179 = f32[16,128,16]{2,0,1:T(8,128)} copy(f32[16,128,16]{1,2,0:T(8,128)} %fusion.43) | data formatting | bytes 262144 | tf_op jit(solution)/shard_map/add | solution.py:160
  67.0 2.3 %reshape.38 = f32[16,1,2048]{2,1,0:T(1,128)} reshape(f32[128,16,16]{2,1,0:T(8,128)} %bitcast.46) | data formatting | bytes 262144
  69.3 15.5 %all-to-all-start = ((f32[16,1,2048]{2,1,0:T(1,128)}), f32[16,1,2048]{2,1,0:T(1,128)}, u32[]{:S(2)}, u32[]{:S(2)}) async-start(f32[16,1,2048]{2,1,0:T(1,128)} %reshape.38), calls=%async_computation | async-start | bytes 262144 | tf_op jit(solution)/shard_map/all_to_all | solution.py:214
  84.8 1.5 %fusion.101 = (f32[3,20,12,255]{3,1,2,0:T(8,128)}, f32[3,20,12,255]{3,1,2,0:T(8,128)}) fusion(f32[6,22,14,256]{3,1,2,0:T(8,128)S(1)} %pad_maximum_fusion.1), kind=kLoop, calls=%fused_computation.185 | loop fusion | bytes 2937600 | tf_op jit(solution)/shard_map/slice | solution.py:165
  86.3 8.6 %all-to-all-done = f32[16,1,2048]{2,1,0:T(1,128)} async-done(((f32[16,1,2048]{2,1,0:T(1,128)}), f32[16,1,2048]{2,1,0:T(1,128)}, u32[]{:S(2)}, u32[]{:S(2)}) %all-to-all-start) | async-done | bytes 131104 | tf_op jit(solution)/shard_map/all_to_all | solution.py:214
  94.9 0.6 broadcast.198
  95.5 2.5 %reduce = f32[16,2048]{1,0:T(8,128)} reduce(f32[16,1,2048]{2,1,0:T(1,128)} %all-to-all-done, f32[]{:T(128)} %broadcast.198), dimensions={1}, to_apply=%all_to_all.24.reduce_sub_computation | reduce | bytes 262148 | tf_op jit(solution)/shard_map/all_to_all | solution.py:214
  98.0 2.2 %reshape.39 = f32[128,16,16]{2,1,0:T(8,128)} reshape(f32[16,2048]{1,0:T(8,128)} %reduce) | data formatting | bytes 262144
  100.3 2.8 %copy.181 = f32[16,8,16,16]{3,2,1,0:T(8,128)} copy(f32[16,8,16,16]{3,0,1,2:T(8,128)} %bitcast.48) | data formatting | bytes 262144 | tf_op jit(solution)/shard_map/all_to_all | solution.py:214
  103.1 2.3 %broadcast_in_dim.22.blk_ref = f32[1,16,8,256]{3,2,1,0:T(8,128)} reshape(f32[16,8,16,16]{3,2,1,0:T(8,128)} %copy.181) | data formatting | bytes 262144 | tf_op jit(solution)/shard_map/broadcast_in_dim | solution.py:215
  105.3 11.1 %shard_map.93 = f32[1,22,24,256]{3,2,1,0:T(8,128)} custom-call(f32[1,16,8,256]{3,2,1,0:T(8,128)} %broadcast_in_dim.22.blk_ref), custom_call_target="tpu_custom_call" | custom-call | tf_op jit(solution)/shard_map/pallas_call | solution.py:94
  116.4 1.1 slice_bitcast_fusion.3
  117.7 0.4 multiply_add_fusion
  119.7 0.8 copy-done.3
  120.9 1.0 fusion.67
  123.0 0.8 fusion.78
  124.3 0.4 fusion.84
  124.7 1.3 copy.208
  126.0 2.3 %reshape.40 = f32[16,1,2048]{2,1,0:T(1,128)} reshape(f32[256,8,16]{2,1,0:T(8,128)} %bitcast.47) | data formatting | bytes 262144
  128.3 3.9 %all-to-all-start.1 = ((f32[16,1,2048]{2,1,0:T(1,128)}), f32[16,1,2048]{2,1,0:T(1,128)S(1)}, u32[]{:S(2)}, u32[]{:S(2)}) async-start(f32[16,1,2048]{2,1,0:T(1,128)} %reshape.40), calls=%async_computation.1 | async-start | bytes 262144 | tf_op jit(solution)/shard_map/all_to_all | solution.py:228
  132.2 1.7 %fusion.48 = f32[32,32,256]{2,1,0:T(8,128)} fusion(f32[34,34,256]{2,1,0:T(8,128)S(1)} %get-tuple-element.41, f32[34,34,256]{2,1,0:T(8,128)S(1)} %copy-done.2), kind=kLoop, calls=%fused_computation.92 | loop fusion | flops 2359296 | bytes 8732672 | tf_op jit(solution)/shard_map/add | solution.py:136
  134.0 1.0 copy.211
  135.0 7.5 %all-to-all-done.1 = f32[16,1,2048]{2,1,0:T(1,128)S(1)} async-done(((f32[16,1,2048]{2,1,0:T(1,128)}), f32[16,1,2048]{2,1,0:T(1,128)S(1)}, u32[]{:S(2)}, u32[]{:S(2)}) %all-to-all-start.1) | async-done | bytes 131104 | tf_op jit(solution)/shard_map/all_to_all | solution.py:228
  142.5 1.0 reduce.1
  143.5 0.4 reshape.41
  143.9 0.9 copy.210
  144.8 1.0 copy.212
  (68 shorter events, 5.5 us)
Async XLA Ops:
  0.6 1.7 %copy-start = (f32[32,32,256]{2,1,0:T(8,128)S(1)}, f32[32,32,256]{2,1,0:T(8,128)}, u32[]{:S(2)}) copy-start(f32[32,32,256]{2,1,0:T(8,128)} %param.7) | copy-start | bytes 3145732
  0.6 1.8 %copy-start.1 = (f32[32,32,256]{2,1,0:T(8,128)S(1)}, f32[32,32,256]{2,1,0:T(8,128)}, u32[]{:S(2)}) copy-start(f32[32,32,256]{2,1,0:T(8,128)} %param.6) | copy-start | bytes 3145732
  2.5 6.5 %copy-start.5 = (f32[3,16,8,256]{3,2,1,0:T(8,128)S(1)}, f32[3,16,8,256]{3,2,1,0:T(8,128)}, u32[]{:S(2)}) copy-start(f32[3,16,8,256]{3,2,1,0:T(8,128)} %param.9) | copy-start | bytes 1179652
  2.5 6.6 %copy-start.6 = (f32[3,16,8,256]{3,2,1,0:T(8,128)S(1)}, f32[3,16,8,256]{3,2,1,0:T(8,128)}, u32[]{:S(2)}) copy-start(f32[3,16,8,256]{3,2,1,0:T(8,128)} %param.10) | copy-start | bytes 1179652
  2.6 27.6 %collective-permute-start.1 = (f32[3,4,32,256]{3,2,1,0:T(8,128)S(1)}, f32[3,4,32,256]{3,2,1,0:T(8,128)S(1)}, u32[]{:S(2)}, u32[]{:S(2)}) collective-permute-start(f32[3,4,32,256]{3,2,1,0:T(8,128)S(1)} %get-tuple-element.56), channel_id=1, source_target_pairs={{16,0},{32,16},{48,32},{64,48},{80,64},{96,80},{112,96},{128,112},... | collective-permute-start | bytes 1179656 | tf_op jit(solution)/shard_map/ppermute | solution.py:116
  7.0 23.2 %collective-permute-start = (f32[3,4,32,256]{3,2,1,0:T(8,128)S(1)}, f32[3,4,32,256]{3,2,1,0:T(8,128)S(1)}, u32[]{:S(2)}, u32[]{:S(2)}) collective-permute-start(f32[3,4,32,256]{3,2,1,0:T(8,128)S(1)} %get-tuple-element.55), channel_id=1, source_target_pairs={{0,16},{16,32},{32,48},{48,64},{64,80},{80,96},{96,112},{112,128},... | collective-permute-start | bytes 1179656 | tf_op jit(solution)/shard_map/ppermute | solution.py:113
  9.3 8.9 %collective-permute-start.5 = (f32[6,3,8,256]{3,1,2,0:T(4,128)S(1)}, f32[6,3,8,256]{3,1,2,0:T(4,128)S(1)}, u32[]{:S(2)}, u32[]{:S(2)}) collective-permute-start(f32[6,3,8,256]{3,1,2,0:T(4,128)S(1)} %get-tuple-element.64), channel_id=1, source_target_pairs={{16,0},{32,16},{48,32},{64,48},{80,64},{96,80},{112,96},{128,112},... | collective-permute-start | bytes 442376 | tf_op jit(solution)/shard_map/ppermute | solution.py:116
  15.1 9.1 %collective-permute-start.4 = (f32[6,3,8,256]{3,1,2,0:T(4,128)S(1)}, f32[6,3,8,256]{3,1,2,0:T(4,128)S(1)}, u32[]{:S(2)}, u32[]{:S(2)}) collective-permute-start(f32[6,3,8,256]{3,1,2,0:T(4,128)S(1)} %get-tuple-element.63), channel_id=1, source_target_pairs={{0,16},{16,32},{32,48},{48,64},{64,80},{80,96},{96,112},{112,128},... | collective-permute-start | bytes 442376 | tf_op jit(solution)/shard_map/ppermute | solution.py:113
  24.3 14.6 %collective-permute-start.7 = (f32[6,22,3,256]{3,1,2,0:T(8,128)S(1)}, f32[6,22,3,256]{3,1,2,0:T(8,128)S(1)}, u32[]{:S(2)}, u32[]{:S(2)}) collective-permute-start(f32[6,22,3,256]{3,1,2,0:T(8,128)S(1)} %get-tuple-element.60), channel_id=1, source_target_pairs={{1,0},{2,1},{3,2},{4,3},{5,4},{6,5},{7,6},{8,7},{9,8},{10,9},{11,1... | collective-permute-start | bytes 1216520 | tf_op jit(solution)/shard_map/ppermute | solution.py:116
  25.6 14.5 %collective-permute-start.6 = (f32[6,22,3,256]{3,1,2,0:T(8,128)S(1)}, f32[6,22,3,256]{3,1,2,0:T(8,128)S(1)}, u32[]{:S(2)}, u32[]{:S(2)}) collective-permute-start(f32[6,22,3,256]{3,1,2,0:T(8,128)S(1)} %get-tuple-element.59), channel_id=1, source_target_pairs={{0,1},{1,2},{2,3},{3,4},{4,5},{5,6},{6,7},{7,8},{8,9},{9,10},{10,1... | collective-permute-start | bytes 1216520 | tf_op jit(solution)/shard_map/ppermute | solution.py:113
  30.4 13.8 %collective-permute-start.3 = (f32[3,40,4,256]{3,2,1,0:T(4,128)S(1)}, f32[3,40,4,256]{3,2,1,0:T(4,128)S(1)}, u32[]{:S(2)}, u32[]{:S(2)}) collective-permute-start(f32[3,40,4,256]{3,2,1,0:T(4,128)S(1)} %get-tuple-element.54), channel_id=1, source_target_pairs={{1,0},{2,1},{3,2},{4,3},{5,4},{6,5},{7,6},{8,7},{9,8},{10,9},{11,1... | collective-permute-start | bytes 1474568 | tf_op jit(solution)/shard_map/ppermute | solution.py:116
  31.7 13.7 %collective-permute-start.2 = (f32[3,40,4,256]{3,2,1,0:T(4,128)S(1)}, f32[3,40,4,256]{3,2,1,0:T(4,128)S(1)}, u32[]{:S(2)}, u32[]{:S(2)}) collective-permute-start(f32[3,40,4,256]{3,2,1,0:T(4,128)S(1)} %get-tuple-element.53), channel_id=1, source_target_pairs={{0,1},{1,2},{2,3},{3,4},{4,5},{5,6},{6,7},{7,8},{8,9},{9,10},{10,1... | collective-permute-start | bytes 1474568 | tf_op jit(solution)/shard_map/ppermute | solution.py:113
  60.9 2.7 %copy-start.7 = (f32[256,128,1]{1,0,2:T(8,128)S(1)}, f32[256,128,1]{1,0,2:T(8,128)}, u32[]{:S(2)}) copy-start(f32[256,128,1]{1,0,2:T(8,128)} %constant.99) | copy-start | bytes 393220
  69.3 25.6 %all-to-all-start = ((f32[16,1,2048]{2,1,0:T(1,128)}), f32[16,1,2048]{2,1,0:T(1,128)}, u32[]{:S(2)}, u32[]{:S(2)}) async-start(f32[16,1,2048]{2,1,0:T(1,128)} %reshape.38), calls=%async_computation | async-start | bytes 262144 | tf_op jit(solution)/shard_map/all_to_all | solution.py:214
  119.4 1.2 copy-start.3
  119.4 1.4 copy-start.4
  124.7 7.5 %copy-start.2 = (f32[34,34,256]{2,1,0:T(8,128)S(1)}, f32[34,34,256]{2,1,0:T(8,128)}, u32[]{:S(2)}) copy-start(f32[34,34,256]{2,1,0:T(8,128)} %get-tuple-element.43) | copy-start | bytes 3551236
  128.3 14.2 %all-to-all-start.1 = ((f32[16,1,2048]{2,1,0:T(1,128)}), f32[16,1,2048]{2,1,0:T(1,128)S(1)}, u32[]{:S(2)}, u32[]{:S(2)}) async-start(f32[16,1,2048]{2,1,0:T(1,128)} %reshape.40), calls=%async_computation.1 | async-start | bytes 262144 | tf_op jit(solution)/shard_map/all_to_all | solution.py:228

commit v7 on v6

--- a/solution.py
+++ b/solution.py
@@ -207,7 +207,8 @@
         conc, order, mob = advance(conc, order, mob, step == STEPS - 1)
 
     m = MECH_HALO
-    ub = padded_2(jnp.concatenate([displacement, body_load]), (("gx", 1), ("gy", 2)), m)
+    order, ub = lax.optimization_barrier((order, jnp.concatenate([displacement, body_load])))
+    ub = padded_2(ub, (("gx", 1), ("gy", 2)), m)
     disp, load = ub[:3], ub[3:]
 
     coarse = restrict_xzy(order)

time: 147 us -> 131 us (0.89)
  local copies, waits for them, and re-layouts: 26.9 us -> 14.3 us
  Pallas kernels: 11.1 us -> 17.6 us
  waiting for transfers between devices: 32.2 us -> 26.7 us
  starting transfers between devices: 45.2 us -> 43.4 us
    pallas_call x1, Pallas kernels: 11.1 us -> 17.6 us  [halo_exchange(): pl.pallas_call(functools.partial(halo_kernel, hx, nx, ny), out_shape=jax....]
    all_to_all x1, waiting for transfers between devices: 8.6 us -> 2.36 us  [on_device(): lax.all_to_all(coarse, 'gy', split_axis=1, concat_axis=2, tiled=True)]
    unnamed x23 -> x24, local copies, waits for them, and re-layouts: 10.5 us -> 5.46 us
    reduce_sum x1, other arithmetic: 2.4 us -> 0.1 us  [restrict_xzy(): sq = sq.reshape(sx // 2, 2, sy, sz).sum(axis=1)]
    all_to_all x2, local copies, waits for them, and re-layouts: 3.38 us -> 1.12 us  [on_device(): lax.all_to_all(coarse, 'gy', split_axis=1, concat_axis=2, tiled=True)]
    all_to_all x1, starting transfers between devices: 15.5 us -> 13.3 us  [on_device(): lax.all_to_all(coarse, 'gy', split_axis=1, concat_axis=2, tiled=True)]
    add x1, other arithmetic: 1.75 us -> 3.64 us  [advance(): order_in + mobility * (rate_order * fine_laplace(order_pad) - well_height...]
    add x1, local copies, waits for them, and re-layouts: 2.27 us -> 0.48 us  [restrict_xzy(): return 0.1 + 0.125 * summed]
  transfers between devices with their start and end apart: 10 -> 10, of which waited for: 8 -> 6; matrix products, arithmetic and copies ran while one was open for 4% -> 9% of each run, Pallas kernels for 0% -> 13%
where the time goes in v7:
time: 131 us
  starting transfers between devices  43.4 us (33%)
  other arithmetic  27.1 us (21%)
  waiting for transfers between devices  26.7 us (20%)
  Pallas kernels  17.6 us (13%)
  local copies, waits for them, and re-layouts  14.3 us (11%)
  between operations  1.36 us (1%)
    pallas_call x1, Pallas kernels, halo_exchange(): pl.pallas_call(functools.partial(halo_kernel, hx, nx, ny), out_shape=jax....  17.6 us
    ppermute x4, starting transfers between devices, padded_2(): lax.ppermute(lax.slice_in_dim(block, block.shape[dim] - width, None, axis...  13.9 us
    all_to_all x1, starting transfers between devices, on_device(): lax.all_to_all(coarse, 'gy', split_axis=1, concat_axis=2, tiled=True)  13.3 us
    sub x4, other arithmetic, advance(): chem = conc_pad - order_pad * order_pad * (3.0 - 2.0 * order_pad)  13.3 us
    ppermute x4, starting transfers between devices, padded_2(): lax.ppermute(lax.slice_in_dim(block, 0, width, axis=dim), axis, backward)  12.5 us
    all_to_all x1, waiting for transfers between devices, on_device(): lax.all_to_all(energy, 'gy', split_axis=2, concat_axis=1, tiled=True)  9.1 us
    ppermute x4, waiting for transfers between devices, padded_2(): lax.ppermute(lax.slice_in_dim(block, 0, width, axis=dim), axis, backward)  7.66 us
    ppermute x4, waiting for transfers between devices, padded_2(): lax.ppermute(lax.slice_in_dim(block, block.shape[dim] - width, None, axis...  7.55 us
  transfers between devices with their start and end apart: 10, of which 6 were waited for; matrix products, arithmetic and copies ran while one was open for 9% of the time, Pallas kernels for 13%

profile of v7, /device:TPU:2, one launch (start us, length us, event | category | flops | bytes accessed | tf_op | source)
XLA Modules:
  0.0 130.9 jit_solution(4578398992570268889)
XLA Ops:
  0.7 1.6 %add_bitcast_fusion = f32[1,32,32,256]{3,2,1,0:T(8,128)S(1)} fusion(s32[32,32,256]{2,1,0:T(8,128)} %param.8), kind=kLoop, calls=%fused_computation.108 | loop fusion | flops 2097152 | bytes 2097152 | tf_op jit(solution)/shard_map/stack | solution.py:203
  2.6 4.3 %collective-permute-start.1 = (f32[3,4,32,256]{3,2,1,0:T(8,128)S(1)}, f32[3,4,32,256]{3,2,1,0:T(8,128)S(1)}, u32[]{:S(2)}, u32[]{:S(2)}) collective-permute-start(f32[3,4,32,256]{3,2,1,0:T(8,128)S(1)} %get-tuple-element.58), channel_id=1, source_target_pairs={{16,0},{32,16},{48,32},{64,48},{80,64},{96,80},{112,96},{128,112},... | collective-permute-start | bytes 1179656 | tf_op jit(solution)/shard_map/ppermute | solution.py:116
  6.9 2.1 %collective-permute-start = (f32[3,4,32,256]{3,2,1,0:T(8,128)S(1)}, f32[3,4,32,256]{3,2,1,0:T(8,128)S(1)}, u32[]{:S(2)}, u32[]{:S(2)}) collective-permute-start(f32[3,4,32,256]{3,2,1,0:T(8,128)S(1)} %get-tuple-element.57), channel_id=1, source_target_pairs={{0,16},{16,32},{32,48},{48,64},{64,80},{80,96},{96,112},{112,128},... | collective-permute-start | bytes 1179656 | tf_op jit(solution)/shard_map/ppermute | solution.py:113
  9.0 3.2 %collective-permute-done.1 = f32[3,4,32,256]{3,2,1,0:T(8,128)S(1)} collective-permute-done((f32[3,4,32,256]{3,2,1,0:T(8,128)S(1)}, f32[3,4,32,256]{3,2,1,0:T(8,128)S(1)}, u32[]{:S(2)}, u32[]{:S(2)}) %collective-permute-start.1) | collective-permute-done | bytes 393248 | tf_op jit(solution)/shard_map/ppermute | solution.py:116
  12.2 6.1 %collective-permute-done = f32[3,4,32,256]{3,2,1,0:T(8,128)S(1)} collective-permute-done((f32[3,4,32,256]{3,2,1,0:T(8,128)S(1)}, f32[3,4,32,256]{3,2,1,0:T(8,128)S(1)}, u32[]{:S(2)}, u32[]{:S(2)}) %collective-permute-start) | collective-permute-done | bytes 393248 | tf_op jit(solution)/shard_map/ppermute | solution.py:113
  18.4 1.3 collective-permute-start.3
  19.7 4.6 %collective-permute-start.2 = (f32[3,40,4,256]{3,2,1,0:T(4,128)S(1)}, f32[3,40,4,256]{3,2,1,0:T(4,128)S(1)}, u32[]{:S(2)}, u32[]{:S(2)}) collective-permute-start(f32[3,40,4,256]{3,2,1,0:T(4,128)S(1)} %get-tuple-element.55), channel_id=1, source_target_pairs={{0,1},{1,2},{2,3},{3,4},{4,5},{5,6},{6,7},{7,8},{8,9},{9,10},{10,1... | collective-permute-start | bytes 1474568 | tf_op jit(solution)/shard_map/ppermute | solution.py:113
  24.7 4.5 %collective-permute-done.3 = f32[3,40,4,256]{3,2,1,0:T(4,128)S(1)} collective-permute-done((f32[3,40,4,256]{3,2,1,0:T(4,128)S(1)}, f32[3,40,4,256]{3,2,1,0:T(4,128)S(1)}, u32[]{:S(2)}, u32[]{:S(2)}) %collective-permute-start.3) | collective-permute-done | bytes 491552 | tf_op jit(solution)/shard_map/ppermute | solution.py:116
  29.2 1.5 %collective-permute-done.2 = f32[3,40,4,256]{3,2,1,0:T(4,128)S(1)} collective-permute-done((f32[3,40,4,256]{3,2,1,0:T(4,128)S(1)}, f32[3,40,4,256]{3,2,1,0:T(4,128)S(1)}, u32[]{:S(2)}, u32[]{:S(2)}) %collective-permute-start.2) | collective-permute-done | bytes 491552 | tf_op jit(solution)/shard_map/ppermute | solution.py:113
  30.6 1.0 pad_maximum_fusion
  31.9 0.3 slice_bitcast_fusion.1
  32.3 4.5 %multiply_subtract_fusion.1 = (f32[38,38,256]{2,1,0:T(8,128)S(1)}, f32[38,38,256]{2,1,0:T(8,128)S(1)}, f32[38,38,256]{2,1,0:T(8,128)S(1)}) fusion(f32[40,40,256]{2,1,0:T(8,128)S(1)} %multiply_subtract_fusion, f32[40,40,256]{2,1,0:T(8,128)S(1)} %get-tuple-element.53, f32[40,40,256]{2,1,0:T(8,128)S(1)} %get-tuple-element.54, ...), kind=kLoop, calls=%fused_computation.42 | loop fusion | flops 13307904 | bytes 26390528 | tf_op jit(solution)/shard_map/sub | solution.py:131
  36.8 4.5 %multiply_subtract_fusion.2 = (f32[36,36,256]{2,1,0:T(8,128)S(1)}, f32[36,36,256]{2,1,0:T(8,128)S(1)}, f32[36,36,256]{2,1,0:T(8,128)S(1)}) fusion(f32[38,38,256]{2,1,0:T(8,128)S(1)} %get-tuple-element.49, f32[38,38,256]{2,1,0:T(8,128)S(1)} %get-tuple-element.50, f32[40,40,256]{2,1,0:T(8,128)S(1)} %get-tuple-element.54, f32[38,38,256]{2,1,0:T(8,128)S(1)} %get-tuple-element.51), kind=kLoop, calls=%fused_computation.63 | loop fusion | flops 11943936 | bytes 24788992 | tf_op jit(solution)/shard_map/sub | solution.py:131
  41.3 4.0 %multiply_subtract_fusion.3 = (f32[34,34,256]{2,1,0:T(8,128)S(1)}, f32[34,34,256]{2,1,0:T(8,128)S(1)}, f32[34,34,256]{2,1,0:T(8,128)S(1)}) fusion(f32[36,36,256]{2,1,0:T(8,128)S(1)} %get-tuple-element.46, f32[36,36,256]{2,1,0:T(8,128)S(1)} %get-tuple-element.47, f32[40,40,256]{2,1,0:T(8,128)S(1)} %get-tuple-element.54, f32[36,36,256]{2,1,0:T(8,128)S(1)} %get-tuple-element.48), kind=kLoop, calls=%fused_computation.84 | loop fusion | flops 10653696 | bytes 23212032 | tf_op jit(solution)/shard_map/sub | solution.py:131
  45.3 3.6 %fusion.56 = (f32[32,32,256]{2,1,0:T(8,128)S(1)}, f32[32,32,256]{2,1,0:T(8,128)}) fusion(f32[34,34,256]{2,1,0:T(8,128)S(1)} %get-tuple-element.44, f32[40,40,256]{2,1,0:T(8,128)S(1)} %get-tuple-element.54, f32[34,34,256]{2,1,0:T(8,128)S(1)} %get-tuple-element.43, f32[34,34,256]{2,1,0:T(8,128)S(1)} %get-tuple-element.45), kind=kLoop, calls=%fused_computation.100 | loop fusion | flops 7602176 | bytes 17465344 | tf_op jit(solution)/shard_map/add | solution.py:139
  49.0 5.6 %collective-permute-start.5 = (f32[6,3,8,256]{3,1,2,0:T(4,128)S(1)}, f32[6,3,8,256]{3,1,2,0:T(4,128)S(1)}, u32[]{:S(2)}, u32[]{:S(2)}) collective-permute-start(f32[6,3,8,256]{3,1,2,0:T(4,128)S(1)} %get-tuple-element.68), channel_id=1, source_target_pairs={{16,0},{32,16},{48,32},{64,48},{80,64},{96,80},{112,96},{128,112},... | collective-permute-start | bytes 442376 | tf_op jit(solution)/shard_map/ppermute | solution.py:116
  54.6 1.9 %collective-permute-start.4 = (f32[6,3,8,256]{3,1,2,0:T(4,128)S(1)}, f32[6,3,8,256]{3,1,2,0:T(4,128)S(1)}, u32[]{:S(2)}, u32[]{:S(2)}) collective-permute-start(f32[6,3,8,256]{3,1,2,0:T(4,128)S(1)} %get-tuple-element.67), channel_id=1, source_target_pairs={{0,16},{16,32},{32,48},{48,64},{64,80},{80,96},{96,112},{112,128},... | collective-permute-start | bytes 442376 | tf_op jit(solution)/shard_map/ppermute | solution.py:113
  56.6 0.3 bitcast_reduce_fusion.1
  57.0 0.5 fusion.43
  57.4 0.5 copy.181
  57.9 1.0 reshape.38
  59.0 13.3 %all-to-all-start = ((f32[16,1,2048]{2,1,0:T(1,128)}), f32[16,1,2048]{2,1,0:T(1,128)S(1)}, u32[]{:S(2)}, u32[]{:S(2)}) async-start(f32[16,1,2048]{2,1,0:T(1,128)} %reshape.38), calls=%async_computation | async-start | bytes 262144 | tf_op jit(solution)/shard_map/all_to_all | solution.py:215
  72.3 1.1 pad_maximum_fusion.10
  73.4 1.3 collective-permute-start.7
  74.7 5.3 %collective-permute-start.6 = (f32[6,22,3,256]{3,1,2,0:T(8,128)}, f32[6,22,3,256]{3,1,2,0:T(8,128)}, u32[]{:S(2)}, u32[]{:S(2)}) collective-permute-start(f32[6,22,3,256]{3,1,2,0:T(8,128)} %get-tuple-element.63), channel_id=1, source_target_pairs={{0,1},{1,2},{2,3},{3,4},{4,5},{5,6},{6,7},{7,8},{8,9},{9,10},{10,1... | collective-permute-start | bytes 1216520 | tf_op jit(solution)/shard_map/ppermute | solution.py:113
  80.0 2.4 %all-to-all-done = f32[16,1,2048]{2,1,0:T(1,128)S(1)} async-done(((f32[16,1,2048]{2,1,0:T(1,128)}), f32[16,1,2048]{2,1,0:T(1,128)S(1)}, u32[]{:S(2)}, u32[]{:S(2)}) %all-to-all-start) | async-done | bytes 131104 | tf_op jit(solution)/shard_map/all_to_all | solution.py:215
  82.4 0.5 broadcast.193
  82.9 0.9 reduce
  83.8 0.4 reshape.39
  84.1 0.6 copy.183
  84.7 1.1 broadcast_in_dim.22.blk_ref
  85.8 17.6 %shard_map.93 = f32[1,22,24,256]{3,2,1,0:T(8,128)} custom-call(f32[1,16,8,256]{3,2,1,0:T(8,128)} %broadcast_in_dim.22.blk_ref), custom_call_target="tpu_custom_call" | custom-call | tf_op jit(solution)/shard_map/pallas_call | solution.py:94
  103.4 1.1 slice_bitcast_fusion.3
  104.6 0.4 multiply_add_fusion
  108.1 1.4 %pad_maximum_fusion.1 = f32[6,22,14,256]{3,1,2,0:T(8,128)S(1)} fusion(f32[6,22,3,256]{3,1,2,0:T(8,128)} %collective-permute-done.7, f32[6,3,8,256]{3,1,2,0:T(4,128)S(1)} %collective-permute-done.5, f32[6,16,8,256]{3,1,2,0:T(8,128)S(1)} %pad_maximum_fusion.2, f32[6,3,8,256]{3,1,2,0:T(4,128)S(1)} %copy-done.4, f32[6,22,3,256]{3,1,2,0:T(8,128)} %collective-permute-done.6), kind=kLoop, calls=%fused_computation.17 | loop fusion | flops 1892352 | bytes 3784704 | tf_op jit(solution)/shard_map/concatenate | solution.py:117
  109.5 0.3 fusion.100
  109.9 0.8 fusion.67
  111.0 0.8 fusion.78
  112.0 0.4 fusion.84
  112.4 0.4 copy.208
  112.8 1.0 reshape.40
  113.9 3.8 %all-to-all-start.1 = ((f32[16,1,2048]{2,1,0:T(1,128)}), f32[16,1,2048]{2,1,0:T(1,128)S(1)}, u32[]{:S(2)}, u32[]{:S(2)}) async-start(f32[16,1,2048]{2,1,0:T(1,128)} %reshape.40), calls=%async_computation.1 | async-start | bytes 262144 | tf_op jit(solution)/shard_map/all_to_all | solution.py:229
  117.7 1.0 copy.211
  118.6 9.1 %all-to-all-done.1 = f32[16,1,2048]{2,1,0:T(1,128)S(1)} async-done(((f32[16,1,2048]{2,1,0:T(1,128)}), f32[16,1,2048]{2,1,0:T(1,128)S(1)}, u32[]{:S(2)}, u32[]{:S(2)}) %all-to-all-start.1) | async-done | bytes 131104 | tf_op jit(solution)/shard_map/all_to_all | solution.py:229
  127.7 0.9 reduce.1
  128.6 0.4 reshape.41
  129.0 0.9 copy.210
  129.9 1.0 copy.212
  (69 shorter events, 4.7 us)
Async XLA Ops:
  0.6 1.7 %copy-start = (f32[32,32,256]{2,1,0:T(8,128)S(1)}, f32[32,32,256]{2,1,0:T(8,128)}, u32[]{:S(2)}) copy-start(f32[32,32,256]{2,1,0:T(8,128)} %param.7) | copy-start | bytes 3145732
  0.6 1.8 %copy-start.1 = (f32[32,32,256]{2,1,0:T(8,128)S(1)}, f32[32,32,256]{2,1,0:T(8,128)}, u32[]{:S(2)}) copy-start(f32[32,32,256]{2,1,0:T(8,128)} %param.6) | copy-start | bytes 3145732
  2.6 9.6 %collective-permute-start.1 = (f32[3,4,32,256]{3,2,1,0:T(8,128)S(1)}, f32[3,4,32,256]{3,2,1,0:T(8,128)S(1)}, u32[]{:S(2)}, u32[]{:S(2)}) collective-permute-start(f32[3,4,32,256]{3,2,1,0:T(8,128)S(1)} %get-tuple-element.58), channel_id=1, source_target_pairs={{16,0},{32,16},{48,32},{64,48},{80,64},{96,80},{112,96},{128,112},... | collective-permute-start | bytes 1179656 | tf_op jit(solution)/shard_map/ppermute | solution.py:116
  6.9 17.4 %copy-start.5 = (f32[3,16,8,256]{3,2,1,0:T(8,128)S(1)}, f32[3,16,8,256]{3,2,1,0:T(8,128)}, u32[]{:S(2)}) copy-start(f32[3,16,8,256]{3,2,1,0:T(8,128)} %param.10) | copy-start | bytes 1179652
  6.9 17.6 %copy-start.6 = (f32[3,16,8,256]{3,2,1,0:T(8,128)S(1)}, f32[3,16,8,256]{3,2,1,0:T(8,128)}, u32[]{:S(2)}) copy-start(f32[3,16,8,256]{3,2,1,0:T(8,128)} %param.9) | copy-start | bytes 1179652
  6.9 11.3 %collective-permute-start = (f32[3,4,32,256]{3,2,1,0:T(8,128)S(1)}, f32[3,4,32,256]{3,2,1,0:T(8,128)S(1)}, u32[]{:S(2)}, u32[]{:S(2)}) collective-permute-start(f32[3,4,32,256]{3,2,1,0:T(8,128)S(1)} %get-tuple-element.57), channel_id=1, source_target_pairs={{0,16},{16,32},{32,48},{48,64},{64,80},{80,96},{96,112},{112,128},... | collective-permute-start | bytes 1179656 | tf_op jit(solution)/shard_map/ppermute | solution.py:113
  18.4 10.7 %collective-permute-start.3 = (f32[3,40,4,256]{3,2,1,0:T(4,128)S(1)}, f32[3,40,4,256]{3,2,1,0:T(4,128)S(1)}, u32[]{:S(2)}, u32[]{:S(2)}) collective-permute-start(f32[3,40,4,256]{3,2,1,0:T(4,128)S(1)} %get-tuple-element.56), channel_id=1, source_target_pairs={{1,0},{2,1},{3,2},{4,3},{5,4},{6,5},{7,6},{8,7},{9,8},{10,9},{11,1... | collective-permute-start | bytes 1474568 | tf_op jit(solution)/shard_map/ppermute | solution.py:116
  19.7 10.9 %collective-permute-start.2 = (f32[3,40,4,256]{3,2,1,0:T(4,128)S(1)}, f32[3,40,4,256]{3,2,1,0:T(4,128)S(1)}, u32[]{:S(2)}, u32[]{:S(2)}) collective-permute-start(f32[3,40,4,256]{3,2,1,0:T(4,128)S(1)} %get-tuple-element.55), channel_id=1, source_target_pairs={{0,1},{1,2},{2,3},{3,4},{4,5},{5,6},{6,7},{7,8},{8,9},{9,10},{10,1... | collective-permute-start | bytes 1474568 | tf_op jit(solution)/shard_map/ppermute | solution.py:113
  48.9 8.0 %copy-start.2 = (f32[32,32,256]{2,1,0:T(8,128)}, f32[32,32,256]{2,1,0:T(8,128)S(1)}, u32[]{:S(2)}) copy-start(f32[32,32,256]{2,1,0:T(8,128)S(1)} %get-tuple-element.33) | copy-start | bytes 3145732
  48.9 8.0 %copy-start.7 = (f32[256,128,1]{1,0,2:T(8,128)S(1)}, f32[256,128,1]{1,0,2:T(8,128)}, u32[]{:S(2)}) copy-start(f32[256,128,1]{1,0,2:T(8,128)} %constant.99) | copy-start | bytes 393220
  49.0 23.3 %collective-permute-start.5 = (f32[6,3,8,256]{3,1,2,0:T(4,128)S(1)}, f32[6,3,8,256]{3,1,2,0:T(4,128)S(1)}, u32[]{:S(2)}, u32[]{:S(2)}) collective-permute-start(f32[6,3,8,256]{3,1,2,0:T(4,128)S(1)} %get-tuple-element.68), channel_id=1, source_target_pairs={{16,0},{32,16},{48,32},{64,48},{80,64},{96,80},{112,96},{128,112},... | collective-permute-start | bytes 442376 | tf_op jit(solution)/shard_map/ppermute | solution.py:116
  54.6 17.7 %collective-permute-start.4 = (f32[6,3,8,256]{3,1,2,0:T(4,128)S(1)}, f32[6,3,8,256]{3,1,2,0:T(4,128)S(1)}, u32[]{:S(2)}, u32[]{:S(2)}) collective-permute-start(f32[6,3,8,256]{3,1,2,0:T(4,128)S(1)} %get-tuple-element.67), channel_id=1, source_target_pairs={{0,16},{16,32},{32,48},{48,64},{64,80},{80,96},{96,112},{112,128},... | collective-permute-start | bytes 442376 | tf_op jit(solution)/shard_map/ppermute | solution.py:113
  59.0 23.4 %all-to-all-start = ((f32[16,1,2048]{2,1,0:T(1,128)}), f32[16,1,2048]{2,1,0:T(1,128)S(1)}, u32[]{:S(2)}, u32[]{:S(2)}) async-start(f32[16,1,2048]{2,1,0:T(1,128)} %reshape.38), calls=%async_computation | async-start | bytes 262144 | tf_op jit(solution)/shard_map/all_to_all | solution.py:215
  72.3 11.8 %copy-start.3 = (f32[6,3,8,256]{3,1,2,0:T(4,128)}, f32[6,3,8,256]{3,1,2,0:T(4,128)S(1)}, u32[]{:S(2)}) copy-start(f32[6,3,8,256]{3,1,2,0:T(4,128)S(1)} %collective-permute-done.4) | copy-start | bytes 442372
  73.4 34.5 %collective-permute-start.7 = (f32[6,22,3,256]{3,1,2,0:T(8,128)}, f32[6,22,3,256]{3,1,2,0:T(8,128)}, u32[]{:S(2)}, u32[]{:S(2)}) collective-permute-start(f32[6,22,3,256]{3,1,2,0:T(8,128)} %get-tuple-element.64), channel_id=1, source_target_pairs={{1,0},{2,1},{3,2},{4,3},{5,4},{6,5},{7,6},{8,7},{9,8},{10,9},{11,1... | collective-permute-start | bytes 1216520 | tf_op jit(solution)/shard_map/ppermute | solution.py:116
  74.7 33.2 %collective-permute-start.6 = (f32[6,22,3,256]{3,1,2,0:T(8,128)}, f32[6,22,3,256]{3,1,2,0:T(8,128)}, u32[]{:S(2)}, u32[]{:S(2)}) collective-permute-start(f32[6,22,3,256]{3,1,2,0:T(8,128)} %get-tuple-element.63), channel_id=1, source_target_pairs={{0,1},{1,2},{2,3},{3,4},{4,5},{5,6},{6,7},{7,8},{8,9},{9,10},{10,1... | collective-permute-start | bytes 1216520 | tf_op jit(solution)/shard_map/ppermute | solution.py:113
  107.2 0.9 copy-start.4
  113.9 13.9 %all-to-all-start.1 = ((f32[16,1,2048]{2,1,0:T(1,128)}), f32[16,1,2048]{2,1,0:T(1,128)S(1)}, u32[]{:S(2)}, u32[]{:S(2)}) async-start(f32[16,1,2048]{2,1,0:T(1,128)} %reshape.40), calls=%async_computation.1 | async-start | bytes 262144 | tf_op jit(solution)/shard_map/all_to_all | solution.py:229

commit v8 on v6

--- a/solution.py
+++ b/solution.py
@@ -103,6 +103,36 @@
         ],
         compiler_params=pltpu.CompilerParams(collective_id=cid, has_side_effects=True),
     )(block)
+
+
+def padded_many(blocks, rounds):
+    blocks = list(blocks)
+    for axis, specs in rounds:
+        count = lax.axis_size(axis)
+        forward = [(i, i + 1) for i in range(count - 1)]
+        backward = [(target, source) for source, target in forward]
+        highs, lows = [], []
+        for block, (dim, width) in zip(blocks, specs):
+            highs.append(lax.slice_in_dim(block, block.shape[dim] - width, None, axis=dim))
+            lows.append(lax.slice_in_dim(block, 0, width, axis=dim))
+        lane = blocks[0].shape[-1]
+
+        def pack(parts):
+            return jnp.concatenate([p.reshape(-1, lane) for p in parts])
+
+        def unpack(flat, like):
+            out, at = [], 0
+            for p in like:
+                rows = p.size // lane
+                out.append(flat[at:at + rows].reshape(p.shape))
+                at += rows
+            return out
+
+        got_low = unpack(lax.ppermute(pack(highs), axis, forward), highs)
+        got_high = unpack(lax.ppermute(pack(lows), axis, backward), lows)
+        blocks = [jnp.concatenate([lo, b, hi], axis=dim)
+                  for b, lo, hi, (dim, _) in zip(blocks, got_low, got_high, specs)]
+    return blocks
 
 
 def padded_2(block, sides, width):
@@ -201,13 +231,15 @@
 def on_device(concentration, order_field, phase_labels, displacement, body_load):
     h = FINE_HALO
     fields = jnp.stack([concentration, order_field, mobility_of(phase_labels)])
-    fields = padded_2(fields, (("gx", 1), ("gy", 2)), h)
+    m = MECH_HALO
+    fields, ub = padded_many(
+        [fields, jnp.concatenate([displacement, body_load])],
+        [("gx", [(1, h), (1, m)]), ("gy", [(2, h), (2, m)])],
+    )
     conc, order, mob = fields[0], fields[1], fields[2]
     for step in range(STEPS):
         conc, order, mob = advance(conc, order, mob, step == STEPS - 1)
 
-    m = MECH_HALO
-    ub = padded_2(jnp.concatenate([displacement, body_load]), (("gx", 1), ("gy", 2)), m)
     disp, load = ub[:3], ub[3:]
 
     coarse = restrict_xzy(order)

time: 147 us -> 164 us (1.12)
  local copies, waits for them, and re-layouts: 26.9 us -> 46.6 us
  starting transfers between devices: 45.2 us -> 30.9 us
  other arithmetic: 28.1 us -> 37.9 us
  waiting for transfers between devices: 32.2 us -> 35.2 us
    reshape x0 -> x8, local copies, waits for them, and re-layouts: none -> 13.9 us  [the longest x4 8.04 us: pack(): return jnp.concatenate([p.reshape(-1, lane) for p in parts])]
    ppermute x8 -> x4, starting transfers between devices: 25.8 us -> 13.9 us  [the longest x2 7.21 us: padded_many(): got_high = unpack(lax.ppermute(pack(lows), axis, backward), lows)]
    slice x1 -> x10, local copies, waits for them, and re-layouts: 0.07 us -> 8.87 us  [the longest x8 7.69 us: unpack(): out.append(flat[at:at + rows].reshape(p.shape))]
    concatenate x2 -> x7, other arithmetic: 1.28 us -> 9.74 us  [the longest x3 5.4 us: padded_many(): jnp.concatenate([lo, b, hi], axis=dim)]
    ppermute x8 -> x4, waiting for transfers between devices: 16 us -> 24.4 us  [the longest x2 16 us: padded_many(): got_low = unpack(lax.ppermute(pack(highs), axis, forward), highs)]
    all_to_all x1, starting transfers between devices: 15.5 us -> 9.14 us  [on_device(): lax.all_to_all(coarse, 'gy', split_axis=1, concat_axis=2, tiled=True)]
    all_to_all x1, waiting for transfers between devices: 8.6 us -> 2.52 us  [on_device(): lax.all_to_all(coarse, 'gy', split_axis=1, concat_axis=2, tiled=True)]
    all_to_all x1, starting transfers between devices: 3.92 us -> 7.87 us  [on_device(): lax.all_to_all(energy, 'gy', split_axis=2, concat_axis=1, tiled=True)]
  transfers between devices with their start and end apart: 10 -> 6, of which waited for: 8 -> 6; matrix products, arithmetic and copies ran while one was open for 4% -> 12% of each run, Pallas kernels for 0% -> 0%
where the time goes in v8:
time: 164 us; the launch traced here: 163 us
  local copies, waits for them, and re-layouts  46.6 us (28%)
  other arithmetic  37.9 us (23%)
  waiting for transfers between devices  35.2 us (21%)
  starting transfers between devices  30.9 us (19%)
  Pallas kernels  10.9 us (7%)
    ppermute x2, waiting for transfers between devices, padded_many(): got_low = unpack(lax.ppermute(pack(highs), axis, forward), highs)  16 us
    sub x4, other arithmetic, advance(): chem = conc_pad - order_pad * order_pad * (3.0 - 2.0 * order_pad)  14.1 us
    unnamed x34, local copies, waits for them, and re-layouts  11.5 us
    pallas_call x1, Pallas kernels, halo_exchange(): pl.pallas_call(functools.partial(halo_kernel, hx, nx, ny), out_shape=jax....  10.9 us
    all_to_all x1, starting transfers between devices, on_device(): lax.all_to_all(coarse, 'gy', split_axis=1, concat_axis=2, tiled=True)  9.14 us
    ppermute x2, waiting for transfers between devices, padded_many(): got_high = unpack(lax.ppermute(pack(lows), axis, backward), lows)  8.39 us
    all_to_all x1, waiting for transfers between devices, on_device(): lax.all_to_all(energy, 'gy', split_axis=2, concat_axis=1, tiled=True)  8.32 us
    reshape x4, local copies, waits for them, and re-layouts, pack(): return jnp.concatenate([p.reshape(-1, lane) for p in parts])  8.04 us
  transfers between devices with their start and end apart: 6, of which 6 were waited for; matrix products, arithmetic and copies ran while one was open for 12% of the time, Pallas kernels for 0%

profile of v8, /device:TPU:2, one launch (start us, length us, event | category | flops | bytes accessed | tf_op | source)
XLA Modules:
  0.0 163.0 jit_solution(8422220449680030118)
XLA Ops:
  0.7 1.6 add_bitcast_fusion
  4.2 1.9 %collective-permute-start = (f32[528,256]{1,0:T(8,128)S(1)}, f32[528,256]{1,0:T(8,128)S(1)}, u32[]{:S(2)}, u32[]{:S(2)}) collective-permute-start(f32[528,256]{1,0:T(8,128)S(1)} %pad_maximum_fusion.5), channel_id=1, source_target_pairs={{0,16},{16,32},{32,48},{48,64},{64,80},{80,96},{96,112},{112,128},... | collective-permute-start | bytes 1622024 | tf_op jit(solution)/shard_map/ppermute | solution.py:131
  6.1 5.8 %collective-permute-start.1 = (f32[528,256]{1,0:T(8,128)S(1)}, f32[528,256]{1,0:T(8,128)S(1)}, u32[]{:S(2)}, u32[]{:S(2)}) collective-permute-start(f32[528,256]{1,0:T(8,128)S(1)} %pad_maximum_fusion.6), channel_id=1, source_target_pairs={{16,0},{32,16},{48,32},{64,48},{80,64},{96,80},{112,96},{128,112},... | collective-permute-start | bytes 1622024 | tf_op jit(solution)/shard_map/ppermute | solution.py:132
  11.9 5.1 %collective-permute-done = f32[528,256]{1,0:T(8,128)S(1)} collective-permute-done((f32[528,256]{1,0:T(8,128)S(1)}, f32[528,256]{1,0:T(8,128)S(1)}, u32[]{:S(2)}, u32[]{:S(2)}) %collective-permute-start) | collective-permute-done | bytes 540704 | tf_op jit(solution)/shard_map/ppermute | solution.py:131
  17.7 1.0 collective-permute-done.1
  19.6 1.1 pad_maximum_fusion.11
  20.7 2.0 %reshape.89 = f32[480,256]{1,0:T(8,128)} reshape(f32[3,40,4,256]{3,2,1,0:T(4,128)} %get-tuple-element.51) | data formatting | bytes 983040 | tf_op jit(solution)/shard_map/reshape | solution.py:121
  24.7 1.3 pad_maximum_fusion.2
  25.9 1.2 fusion.102
  27.1 2.0 %reshape.92 = f32[396,256]{1,0:T(8,128)} reshape(f32[6,22,3,256]{3,2,1,0:T(4,128)} %get-tuple-element.57) | data formatting | bytes 811008 | tf_op jit(solution)/shard_map/reshape | solution.py:121
  29.1 2.1 %pad_maximum_fusion.3 = f32[876,256]{1,0:T(8,128)} fusion(f32[396,256]{1,0:T(8,128)} %reshape.92, f32[480,256]{1,0:T(8,128)} %reshape.89), kind=kLoop, calls=%fused_computation.125 | loop fusion | flops 224256 | bytes 1794048 | tf_op jit(solution)/shard_map/concatenate | solution.py:121
  31.3 4.7 %collective-permute-start.2 = (f32[876,256]{1,0:T(8,128)}, f32[876,256]{1,0:T(8,128)}, u32[]{:S(2)}, u32[]{:S(2)}) collective-permute-start(f32[876,256]{1,0:T(8,128)} %pad_maximum_fusion.3), channel_id=1, source_target_pairs={{0,1},{1,2},{2,3},{3,4},{4,5},{5,6},{6,7},{7,8},{8,9},{9,10},{10,1... | collective-permute-start | bytes 2691080 | tf_op jit(solution)/shard_map/ppermute | solution.py:131
  36.0 2.0 %reshape.94 = f32[480,256]{1,0:T(8,128)} reshape(f32[3,40,4,256]{3,2,1,0:T(4,128)} %get-tuple-element.52) | data formatting | bytes 983040 | tf_op jit(solution)/shard_map/reshape | solution.py:121
  38.0 2.0 %reshape.95 = f32[396,256]{1,0:T(8,128)} reshape(f32[6,22,3,256]{3,2,1,0:T(4,128)} %get-tuple-element.58) | data formatting | bytes 811008 | tf_op jit(solution)/shard_map/reshape | solution.py:121
  40.0 2.1 %pad_maximum_fusion.4 = f32[876,256]{1,0:T(8,128)} fusion(f32[396,256]{1,0:T(8,128)} %reshape.95, f32[480,256]{1,0:T(8,128)} %reshape.94), kind=kLoop, calls=%fused_computation.126 | loop fusion | flops 224256 | bytes 1794048 | tf_op jit(solution)/shard_map/concatenate | solution.py:121
  42.2 1.5 collective-permute-start.3
  43.6 10.9 %collective-permute-done.2 = f32[876,256]{1,0:T(8,128)} collective-permute-done((f32[876,256]{1,0:T(8,128)}, f32[876,256]{1,0:T(8,128)}, u32[]{:S(2)}, u32[]{:S(2)}) %collective-permute-start.2) | collective-permute-done | bytes 897056 | tf_op jit(solution)/shard_map/ppermute | solution.py:131
  54.6 1.8 %slice.595 = f32[480,256]{1,0:T(8,128)} slice(f32[876,256]{1,0:T(8,128)} %collective-permute-done.2), slice={[0:480], [0:256]} | slice | bytes 983040 | tf_op jit(solution)/shard_map/slice | solution.py:127
  56.4 1.9 %reshape.93 = f32[3,40,4,256]{3,2,1,0:T(4,128)} reshape(f32[480,256]{1,0:T(8,128)} %slice.595) | data formatting | bytes 983040 | tf_op jit(solution)/shard_map/reshape | solution.py:127
  58.3 7.4 %collective-permute-done.3 = f32[876,256]{1,0:T(8,128)} collective-permute-done((f32[876,256]{1,0:T(8,128)}, f32[876,256]{1,0:T(8,128)}, u32[]{:S(2)}, u32[]{:S(2)}) %collective-permute-start.3) | collective-permute-done | bytes 897056 | tf_op jit(solution)/shard_map/ppermute | solution.py:132
  65.7 1.8 %slice.597 = f32[480,256]{1,0:T(8,128)} slice(f32[876,256]{1,0:T(8,128)} %collective-permute-done.3), slice={[0:480], [0:256]} | slice | bytes 983040 | tf_op jit(solution)/shard_map/slice | solution.py:127
  67.6 1.9 %reshape.96 = f32[3,40,4,256]{3,2,1,0:T(4,128)} reshape(f32[480,256]{1,0:T(8,128)} %slice.597) | data formatting | bytes 983040 | tf_op jit(solution)/shard_map/reshape | solution.py:127
  69.5 2.2 %pad_maximum_fusion = f32[3,40,40,256]{3,2,1,0:T(8,128)S(1)} fusion(f32[3,40,4,256]{3,2,1,0:T(4,128)} %reshape.96, f32[3,4,32,256]{3,2,1,0:T(8,128)} %bitcast.62, f32[1,32,32,256]{3,2,1,0:T(8,128)S(1)} %add_bitcast_fusion, f32[1,32,32,256]{3,2,1,0:T(8,128)S(1)} %bitcast.50, f32[1,32,32,256]{3,2,1,0:T(8,128)S(1)} %bitcast.53, f32[3,4,32,256]{3,2,1,0:T(8,128)S(1)} %bitcast.60, ...), kind=kLoop, calls=%fused_computation | loop fusion | flops 7372800 | bytes 9830400 | tf_op jit(solution)/shard_map/concatenate | solution.py:133
  72.3 4.5 %multiply_subtract_fusion.1 = (f32[38,38,256]{2,1,0:T(8,128)S(1)}, f32[38,38,256]{2,1,0:T(8,128)S(1)}, f32[38,38,256]{2,1,0:T(8,128)S(1)}) fusion(f32[40,40,256]{2,1,0:T(8,128)S(1)} %multiply_subtract_fusion, f32[40,40,256]{2,1,0:T(8,128)S(1)} %get-tuple-element.49, f32[40,40,256]{2,1,0:T(8,128)S(1)} %get-tuple-element.50, ...), kind=kLoop, calls=%fused_computation.42 | loop fusion | flops 13307904 | bytes 26390528 | tf_op jit(solution)/shard_map/sub | solution.py:161
  76.9 4.5 %multiply_subtract_fusion.2 = (f32[36,36,256]{2,1,0:T(8,128)S(1)}, f32[36,36,256]{2,1,0:T(8,128)S(1)}, f32[36,36,256]{2,1,0:T(8,128)S(1)}) fusion(f32[38,38,256]{2,1,0:T(8,128)S(1)} %get-tuple-element.45, f32[38,38,256]{2,1,0:T(8,128)S(1)} %get-tuple-element.46, f32[40,40,256]{2,1,0:T(8,128)S(1)} %get-tuple-element.50, f32[38,38,256]{2,1,0:T(8,128)S(1)} %get-tuple-element.47), kind=kLoop, calls=%fused_computation.63 | loop fusion | flops 11943936 | bytes 24788992 | tf_op jit(solution)/shard_map/sub | solution.py:161
  81.4 4.9 %multiply_subtract_fusion.3 = (f32[34,34,256]{2,1,0:T(8,128)S(1)}, f32[34,34,256]{2,1,0:T(8,128)S(1)}, f32[34,34,256]{2,1,0:T(8,128)}) fusion(f32[36,36,256]{2,1,0:T(8,128)S(1)} %get-tuple-element.42, f32[36,36,256]{2,1,0:T(8,128)S(1)} %get-tuple-element.43, f32[40,40,256]{2,1,0:T(8,128)S(1)} %get-tuple-element.50, f32[36,36,256]{2,1,0:T(8,128)S(1)} %get-tuple-element.44), kind=kLoop, calls=%fused_computation.84 | loop fusion | flops 10653696 | bytes 23212032 | tf_op jit(solution)/shard_map/sub | solution.py:161
  86.2 2.4 %bitcast_reduce_fusion = (f32[16,32,256]{2,1,0:T(8,128)S(1)}, f32[32,32,256]{2,1,0:T(8,128)}) fusion(f32[34,34,256]{2,1,0:T(8,128)S(1)} %get-tuple-element.39, f32[34,34,256]{2,1,0:T(8,128)S(1)} %get-tuple-element.40, f32[40,40,256]{2,1,0:T(8,128)S(1)} %get-tuple-element.50), kind=kLoop, calls=%fused_computation.108 | loop fusion | flops 5636096 | bytes 10305536 | tf_op jit(solution)/shard_map/reduce_sum | solution.py:186
  89.9 1.0 reshape.102
  91.0 9.1 %all-to-all-start = ((f32[16,1,2048]{2,1,0:T(1,128)}), f32[16,1,2048]{2,1,0:T(1,128)}, u32[]{:S(2)}, u32[]{:S(2)}) async-start(f32[16,1,2048]{2,1,0:T(1,128)} %reshape.102), calls=%async_computation | async-start | bytes 262144 | tf_op jit(solution)/shard_map/all_to_all | solution.py:246
  100.1 1.0 slice.651
  101.1 1.0 reshape.99
  102.1 1.0 slice.652
  104.1 1.9 %pad_maximum_fusion.1 = f32[6,22,14,256]{3,2,1,0:T(8,128)S(1)} fusion(f32[6,22,3,256]{3,2,1,0:T(4,128)} %reshape.100, f32[6,3,8,256]{3,2,1,0:T(8,128)} %bitcast.66, f32[6,16,8,256]{3,2,1,0:T(8,128)} %copy-done.2, f32[6,3,8,256]{3,2,1,0:T(8,128)} %bitcast.68, f32[6,22,3,256]{3,2,1,0:T(4,128)} %reshape.99), kind=kLoop, calls=%fused_computation.17 | loop fusion | flops 1892352 | bytes 3784704 | tf_op jit(solution)/shard_map/concatenate | solution.py:133
  106.0 1.7 %fusion.101 = (f32[3,20,12,255]{3,2,1,0:T(8,128)}, f32[3,20,12,255]{3,2,1,0:T(8,128)}) fusion(f32[6,22,14,256]{3,2,1,0:T(8,128)S(1)} %pad_maximum_fusion.1), kind=kLoop, calls=%fused_computation.187 | loop fusion | bytes 2937600 | tf_op jit(solution)/shard_map/slice | solution.py:195
  107.7 2.5 %all-to-all-done = f32[16,1,2048]{2,1,0:T(1,128)} async-done(((f32[16,1,2048]{2,1,0:T(1,128)}), f32[16,1,2048]{2,1,0:T(1,128)}, u32[]{:S(2)}, u32[]{:S(2)}) %all-to-all-start) | async-done | bytes 131104 | tf_op jit(solution)/shard_map/all_to_all | solution.py:246
  110.7 2.4 %reduce = f32[16,2048]{1,0:T(8,128)} reduce(f32[16,1,2048]{2,1,0:T(1,128)} %all-to-all-done, f32[]{:T(128)} %broadcast.198), dimensions={1}, to_apply=%all_to_all.24.reduce_sub_computation | reduce | bytes 262148 | tf_op jit(solution)/shard_map/all_to_all | solution.py:246
  113.1 2.2 %reshape.103 = f32[128,16,16]{2,1,0:T(8,128)} reshape(f32[16,2048]{1,0:T(8,128)} %reduce) | data formatting | bytes 262144
  115.4 2.8 %copy.47 = f32[16,8,16,16]{3,2,1,0:T(8,128)} copy(f32[16,8,16,16]{3,0,1,2:T(8,128)} %bitcast.56) | data formatting | bytes 262144 | tf_op jit(solution)/shard_map/all_to_all | solution.py:246
  118.2 2.3 %broadcast_in_dim.22.blk_ref = f32[1,16,8,256]{3,2,1,0:T(8,128)} reshape(f32[16,8,16,16]{3,2,1,0:T(8,128)} %copy.47) | data formatting | bytes 262144 | tf_op jit(solution)/shard_map/broadcast_in_dim | solution.py:247
  120.4 10.9 %shard_map.93 = f32[1,22,24,256]{3,2,1,0:T(8,128)} custom-call(f32[1,16,8,256]{3,2,1,0:T(8,128)} %broadcast_in_dim.22.blk_ref), custom_call_target="tpu_custom_call" | custom-call | tf_op jit(solution)/shard_map/pallas_call | solution.py:94
  131.3 1.1 slice_bitcast_fusion.3
  134.8 1.0 fusion.67
  137.2 1.1 fusion.84
  138.3 1.3 copy.48
  139.7 2.3 %reshape.104 = f32[16,1,2048]{2,1,0:T(1,128)} reshape(f32[256,8,16]{2,1,0:T(8,128)} %bitcast.55) | data formatting | bytes 262144
  141.9 7.9 %all-to-all-start.1 = ((f32[16,1,2048]{2,1,0:T(1,128)}), f32[16,1,2048]{2,1,0:T(1,128)S(1)}, u32[]{:S(2)}, u32[]{:S(2)}) async-start(f32[16,1,2048]{2,1,0:T(1,128)} %reshape.104), calls=%async_computation.1 | async-start | bytes 262144 | tf_op jit(solution)/shard_map/all_to_all | solution.py:260
  149.8 1.7 %fusion.48 = f32[32,32,256]{2,1,0:T(8,128)} fusion(f32[34,34,256]{2,1,0:T(8,128)S(1)} %get-tuple-element.39, f32[34,34,256]{2,1,0:T(8,128)S(1)} %copy-done.3), kind=kLoop, calls=%fused_computation.93 | loop fusion | flops 2359296 | bytes 8732672 | tf_op jit(solution)/shard_map/add | solution.py:166
  151.6 8.3 %all-to-all-done.1 = f32[16,1,2048]{2,1,0:T(1,128)S(1)} async-done(((f32[16,1,2048]{2,1,0:T(1,128)}), f32[16,1,2048]{2,1,0:T(1,128)S(1)}, u32[]{:S(2)}, u32[]{:S(2)}) %all-to-all-start.1) | async-done | bytes 131104 | tf_op jit(solution)/shard_map/all_to_all | solution.py:260
  (70 shorter events, 15.5 us)
Async XLA Ops:
  0.6 1.6 copy-start.11
  0.6 1.7 %copy-start.12 = (f32[3,16,8,256]{3,2,1,0:T(8,128)S(1)}, f32[3,16,8,256]{3,2,1,0:T(8,128)}, u32[]{:S(2)}) copy-start(f32[3,16,8,256]{3,2,1,0:T(8,128)} %param.10) | copy-start | bytes 1179652
  2.2 1.5 copy-start
  2.2 1.8 %copy-start.1 = (f32[32,32,256]{2,1,0:T(8,128)S(1)}, f32[32,32,256]{2,1,0:T(8,128)}, u32[]{:S(2)}) copy-start(f32[32,32,256]{2,1,0:T(8,128)} %param.6) | copy-start | bytes 3145732
  2.3 0.9 copy-start.2
  4.2 12.8 %collective-permute-start = (f32[528,256]{1,0:T(8,128)S(1)}, f32[528,256]{1,0:T(8,128)S(1)}, u32[]{:S(2)}, u32[]{:S(2)}) collective-permute-start(f32[528,256]{1,0:T(8,128)S(1)} %pad_maximum_fusion.5), channel_id=1, source_target_pairs={{0,16},{16,32},{32,48},{48,64},{64,80},{80,96},{96,112},{112,128},... | collective-permute-start | bytes 1622024 | tf_op jit(solution)/shard_map/ppermute | solution.py:131
  6.1 12.6 %collective-permute-start.1 = (f32[528,256]{1,0:T(8,128)S(1)}, f32[528,256]{1,0:T(8,128)S(1)}, u32[]{:S(2)}, u32[]{:S(2)}) collective-permute-start(f32[528,256]{1,0:T(8,128)S(1)} %pad_maximum_fusion.6), channel_id=1, source_target_pairs={{16,0},{32,16},{48,32},{64,48},{80,64},{96,80},{112,96},{128,112},... | collective-permute-start | bytes 1622024 | tf_op jit(solution)/shard_map/ppermute | solution.py:132
  16.9 0.8 copy-start.9
  18.7 0.8 copy-start.10
  19.6 1.2 copy-start.6
  23.7 3.5 %copy-start.7 = (f32[144,256]{1,0:T(8,128)}, f32[144,256]{1,0:T(8,128)S(1)}, u32[]{:S(2)}) copy-start(f32[144,256]{1,0:T(8,128)S(1)} %slice.593) | copy-start | bytes 442372
  24.6 2.5 %copy-start.8 = (f32[144,256]{1,0:T(8,128)}, f32[144,256]{1,0:T(8,128)S(1)}, u32[]{:S(2)}) copy-start(f32[144,256]{1,0:T(8,128)S(1)} %slice.592) | copy-start | bytes 442372
  31.3 23.3 %collective-permute-start.2 = (f32[876,256]{1,0:T(8,128)}, f32[876,256]{1,0:T(8,128)}, u32[]{:S(2)}, u32[]{:S(2)}) collective-permute-start(f32[876,256]{1,0:T(8,128)} %pad_maximum_fusion.3), channel_id=1, source_target_pairs={{0,1},{1,2},{2,3},{3,4},{4,5},{5,6},{6,7},{7,8},{8,9},{9,10},{10,1... | collective-permute-start | bytes 2691080 | tf_op jit(solution)/shard_map/ppermute | solution.py:131
  42.2 23.6 %collective-permute-start.3 = (f32[876,256]{1,0:T(8,128)}, f32[876,256]{1,0:T(8,128)}, u32[]{:S(2)}, u32[]{:S(2)}) collective-permute-start(f32[876,256]{1,0:T(8,128)} %pad_maximum_fusion.4), channel_id=1, source_target_pairs={{1,0},{2,1},{3,2},{4,3},{5,4},{6,5},{7,6},{8,7},{9,8},{10,9},{11,1... | collective-permute-start | bytes 2691080 | tf_op jit(solution)/shard_map/ppermute | solution.py:132
  86.2 2.7 %copy-start.13 = (f32[256,128,1]{1,0,2:T(8,128)S(1)}, f32[256,128,1]{1,0,2:T(8,128)}, u32[]{:S(2)}) copy-start(f32[256,128,1]{1,0,2:T(8,128)} %constant.99) | copy-start | bytes 393220
  91.0 19.3 %all-to-all-start = ((f32[16,1,2048]{2,1,0:T(1,128)}), f32[16,1,2048]{2,1,0:T(1,128)}, u32[]{:S(2)}, u32[]{:S(2)}) async-start(f32[16,1,2048]{2,1,0:T(1,128)} %reshape.102), calls=%async_computation | async-start | bytes 262144 | tf_op jit(solution)/shard_map/all_to_all | solution.py:246
  133.2 1.2 copy-start.4
  133.3 1.5 copy-start.5
  138.3 11.5 %copy-start.3 = (f32[34,34,256]{2,1,0:T(8,128)S(1)}, f32[34,34,256]{2,1,0:T(8,128)}, u32[]{:S(2)}) copy-start(f32[34,34,256]{2,1,0:T(8,128)} %get-tuple-element.41) | copy-start | bytes 3551236
  141.9 18.0 %all-to-all-start.1 = ((f32[16,1,2048]{2,1,0:T(1,128)}), f32[16,1,2048]{2,1,0:T(1,128)S(1)}, u32[]{:S(2)}, u32[]{:S(2)}) async-start(f32[16,1,2048]{2,1,0:T(1,128)} %reshape.104), calls=%async_computation.1 | async-start | bytes 262144 | tf_op jit(solution)/shard_map/all_to_all | solution.py:260

commit v9 on v6

--- a/solution.py
+++ b/solution.py
@@ -201,13 +201,17 @@
 def on_device(concentration, order_field, phase_labels, displacement, body_load):
     h = FINE_HALO
     fields = jnp.stack([concentration, order_field, mobility_of(phase_labels)])
-    fields = padded_2(fields, (("gx", 1), ("gy", 2)), h)
+    m = MECH_HALO
+    fields = padded_2(fields, (("gx", 1),), h)
+    fields, ub = lax.optimization_barrier((fields, jnp.concatenate([displacement, body_load])))
+    ub = padded_2(ub, (("gx", 1),), m)
+    fields = padded_2(fields, (("gy", 2),), h)
     conc, order, mob = fields[0], fields[1], fields[2]
     for step in range(STEPS):
         conc, order, mob = advance(conc, order, mob, step == STEPS - 1)
 
-    m = MECH_HALO
-    ub = padded_2(jnp.concatenate([displacement, body_load]), (("gx", 1), ("gy", 2)), m)
+    order, ub = lax.optimization_barrier((order, ub))
+    ub = padded_2(ub, (("gy", 2),), m)
     disp, load = ub[:3], ub[3:]
 
     coarse = restrict_xzy(order)

time: 147 us -> 129 us (0.88)
  starting transfers between devices: 45.2 us -> 34.3 us
  local copies, waits for them, and re-layouts: 26.9 us -> 18.1 us
  waiting for transfers between devices: 32.2 us -> 38.3 us
  other arithmetic: 28.1 us -> 25.1 us
    all_to_all x1, starting transfers between devices: 15.5 us -> 3.51 us  [on_device(): lax.all_to_all(coarse, 'gy', split_axis=1, concat_axis=2, tiled=True)]
    ppermute x4, waiting for transfers between devices: 7.71 us -> 14.3 us  [padded_2(): lax.ppermute(lax.slice_in_dim(block, 0, width, axis=dim), axis, backward)]
    all_to_all x1, waiting for transfers between devices: 8.6 us -> 3.07 us  [on_device(): lax.all_to_all(coarse, 'gy', split_axis=1, concat_axis=2, tiled=True)]
    all_to_all x1, starting transfers between devices: 3.92 us -> 8.3 us  [on_device(): lax.all_to_all(energy, 'gy', split_axis=2, concat_axis=1, tiled=True)]
    ppermute x4, starting transfers between devices: 12.8 us -> 9.14 us  [padded_2(): lax.ppermute(lax.slice_in_dim(block, 0, width, axis=dim), axis, backward)]
    unnamed x23 -> x22, local copies, waits for them, and re-layouts: 10.5 us -> 6.98 us
    ppermute x4, waiting for transfers between devices: 8.3 us -> 11.6 us  [padded_2(): lax.ppermute(lax.slice_in_dim(block, block.shape[dim] - width, None, axis...]
    reduce_sum x1, other arithmetic: 2.4 us -> 0.09 us  [restrict_xzy(): sq = sq.reshape(sx // 2, 2, sy, sz).sum(axis=1)]
  transfers between devices with their start and end apart: 10 -> 10, of which waited for: 8 -> 6; matrix products, arithmetic and copies ran while one was open for 4% -> 9% of each run, Pallas kernels for 0% -> 8%
where the time goes in v9:
time: 129 us; the launch traced here: 128 us
  waiting for transfers between devices  38.3 us (30%)
  starting transfers between devices  34.3 us (27%)
  other arithmetic  25.1 us (19%)
  local copies, waits for them, and re-layouts  18.1 us (14%)
  Pallas kernels  10.5 us (8%)
  between operations  1.35 us (1%)
    ppermute x4, waiting for transfers between devices, padded_2(): lax.ppermute(lax.slice_in_dim(block, 0, width, axis=dim), axis, backward)  14.3 us
    ppermute x4, starting transfers between devices, padded_2(): lax.ppermute(lax.slice_in_dim(block, block.shape[dim] - width, None, axis...  13.4 us
    sub x4, other arithmetic, advance(): chem = conc_pad - order_pad * order_pad * (3.0 - 2.0 * order_pad)  13.3 us
    ppermute x4, waiting for transfers between devices, padded_2(): lax.ppermute(lax.slice_in_dim(block, block.shape[dim] - width, None, axis...  11.6 us
    pallas_call x1, Pallas kernels, halo_exchange(): pl.pallas_call(functools.partial(halo_kernel, hx, nx, ny), out_shape=jax....  10.5 us
    all_to_all x1, waiting for transfers between devices, on_device(): lax.all_to_all(energy, 'gy', split_axis=2, concat_axis=1, tiled=True)  9.27 us
    ppermute x4, starting transfers between devices, padded_2(): lax.ppermute(lax.slice_in_dim(block, 0, width, axis=dim), axis, backward)  9.14 us
    all_to_all x1, starting transfers between devices, on_device(): lax.all_to_all(energy, 'gy', split_axis=2, concat_axis=1, tiled=True)  8.3 us
  transfers between devices with their start and end apart: 10, of which 6 were waited for; matrix products, arithmetic and copies ran while one was open for 9% of the time, Pallas kernels for 8%

profile of v9, /device:TPU:2, one launch (start us, length us, event | category | flops | bytes accessed | tf_op | source)
XLA Modules:
  0.0 128.1 jit_solution(7061218044795486809)
XLA Ops:
  0.7 1.6 %add_bitcast_fusion = f32[1,32,32,256]{3,2,1,0:T(8,128)S(1)} fusion(s32[32,32,256]{2,1,0:T(8,128)} %param.8), kind=kLoop, calls=%fused_computation.109 | loop fusion | flops 2097152 | bytes 2097152 | tf_op jit(solution)/shard_map/stack | solution.py:203
  2.6 4.5 %collective-permute-start.1 = (f32[3,4,32,256]{3,2,1,0:T(8,128)S(1)}, f32[3,4,32,256]{3,2,1,0:T(8,128)S(1)}, u32[]{:S(2)}, u32[]{:S(2)}) collective-permute-start(f32[3,4,32,256]{3,2,1,0:T(8,128)S(1)} %get-tuple-element.62), channel_id=1, source_target_pairs={{16,0},{32,16},{48,32},{64,48},{80,64},{96,80},{112,96},{128,112},... | collective-permute-start | bytes 1179656 | tf_op jit(solution)/shard_map/ppermute | solution.py:116
  7.0 1.9 %collective-permute-start = (f32[3,4,32,256]{3,2,1,0:T(8,128)S(1)}, f32[3,4,32,256]{3,2,1,0:T(8,128)S(1)}, u32[]{:S(2)}, u32[]{:S(2)}) collective-permute-start(f32[3,4,32,256]{3,2,1,0:T(8,128)S(1)} %get-tuple-element.61), channel_id=1, source_target_pairs={{0,16},{16,32},{32,48},{48,64},{64,80},{80,96},{96,112},{112,128},... | collective-permute-start | bytes 1179656 | tf_op jit(solution)/shard_map/ppermute | solution.py:113
  9.3 3.0 %collective-permute-done.1 = f32[3,4,32,256]{3,2,1,0:T(8,128)S(1)} collective-permute-done((f32[3,4,32,256]{3,2,1,0:T(8,128)S(1)}, f32[3,4,32,256]{3,2,1,0:T(8,128)S(1)}, u32[]{:S(2)}, u32[]{:S(2)}) %collective-permute-start.1) | collective-permute-done | bytes 393248 | tf_op jit(solution)/shard_map/ppermute | solution.py:116
  12.3 5.9 %collective-permute-done = f32[3,4,32,256]{3,2,1,0:T(8,128)S(1)} collective-permute-done((f32[3,4,32,256]{3,2,1,0:T(8,128)S(1)}, f32[3,4,32,256]{3,2,1,0:T(8,128)S(1)}, u32[]{:S(2)}, u32[]{:S(2)}) %collective-permute-start) | collective-permute-done | bytes 393248 | tf_op jit(solution)/shard_map/ppermute | solution.py:113
  18.2 0.4 pad_maximum_fusion.1
  18.8 1.3 %collective-permute-start.3 = (f32[3,40,4,256]{3,2,1,0:T(4,128)S(1)}, f32[3,40,4,256]{3,2,1,0:T(4,128)S(1)}, u32[]{:S(2)}, u32[]{:S(2)}) collective-permute-start(f32[3,40,4,256]{3,2,1,0:T(4,128)S(1)} %get-tuple-element.60), channel_id=1, source_target_pairs={{1,0},{2,1},{3,2},{4,3},{5,4},{6,5},{7,6},{8,7},{9,8},{10,9},{11,1... | collective-permute-start | bytes 1474568 | tf_op jit(solution)/shard_map/ppermute | solution.py:116
  20.1 4.6 %collective-permute-start.2 = (f32[3,40,4,256]{3,2,1,0:T(4,128)S(1)}, f32[3,40,4,256]{3,2,1,0:T(4,128)S(1)}, u32[]{:S(2)}, u32[]{:S(2)}) collective-permute-start(f32[3,40,4,256]{3,2,1,0:T(4,128)S(1)} %get-tuple-element.59), channel_id=1, source_target_pairs={{0,1},{1,2},{2,3},{3,4},{4,5},{5,6},{6,7},{7,8},{8,9},{9,10},{10,1... | collective-permute-start | bytes 1474568 | tf_op jit(solution)/shard_map/ppermute | solution.py:113
  24.8 1.9 %collective-permute-start.5 = (f32[6,3,8,256]{3,1,2,0:T(4,128)S(1)}, f32[6,3,8,256]{3,1,2,0:T(4,128)S(1)}, u32[]{:S(2)}, u32[]{:S(2)}) collective-permute-start(f32[6,3,8,256]{3,1,2,0:T(4,128)S(1)} %get-tuple-element.72), channel_id=1, source_target_pairs={{16,0},{32,16},{48,32},{64,48},{80,64},{96,80},{112,96},{128,112},... | collective-permute-start | bytes 442376 | tf_op jit(solution)/shard_map/ppermute | solution.py:116
  26.7 2.4 %collective-permute-start.4 = (f32[6,3,8,256]{3,1,2,0:T(4,128)S(1)}, f32[6,3,8,256]{3,1,2,0:T(4,128)S(1)}, u32[]{:S(2)}, u32[]{:S(2)}) collective-permute-start(f32[6,3,8,256]{3,1,2,0:T(4,128)S(1)} %get-tuple-element.71), channel_id=1, source_target_pairs={{0,16},{16,32},{32,48},{48,64},{64,80},{80,96},{96,112},{112,128},... | collective-permute-start | bytes 442376 | tf_op jit(solution)/shard_map/ppermute | solution.py:113
  29.1 11.3 %collective-permute-done.5 = f32[6,3,8,256]{3,1,2,0:T(4,128)S(1)} collective-permute-done((f32[6,3,8,256]{3,1,2,0:T(4,128)S(1)}, f32[6,3,8,256]{3,1,2,0:T(4,128)S(1)}, u32[]{:S(2)}, u32[]{:S(2)}) %collective-permute-start.5) | collective-permute-done | bytes 147488 | tf_op jit(solution)/shard_map/ppermute | solution.py:116
  40.5 5.7 %collective-permute-done.4 = f32[6,3,8,256]{3,1,2,0:T(4,128)S(1)} collective-permute-done((f32[6,3,8,256]{3,1,2,0:T(4,128)S(1)}, f32[6,3,8,256]{3,1,2,0:T(4,128)S(1)}, u32[]{:S(2)}, u32[]{:S(2)}) %collective-permute-start.4) | collective-permute-done | bytes 147488 | tf_op jit(solution)/shard_map/ppermute | solution.py:113
  46.4 0.9 pad_maximum_fusion
  47.9 4.5 %multiply_subtract_fusion.1 = (f32[38,38,256]{2,1,0:T(8,128)S(1)}, f32[38,38,256]{2,1,0:T(8,128)S(1)}, f32[38,38,256]{2,1,0:T(8,128)S(1)}) fusion(f32[40,40,256]{2,1,0:T(8,128)S(1)} %multiply_subtract_fusion, f32[40,40,256]{2,1,0:T(8,128)S(1)} %get-tuple-element.57, f32[40,40,256]{2,1,0:T(8,128)S(1)} %get-tuple-element.58, ...), kind=kLoop, calls=%fused_computation.42 | loop fusion | flops 13307904 | bytes 26390528 | tf_op jit(solution)/shard_map/sub | solution.py:131
  52.4 4.5 %multiply_subtract_fusion.2 = (f32[36,36,256]{2,1,0:T(8,128)S(1)}, f32[36,36,256]{2,1,0:T(8,128)S(1)}, f32[36,36,256]{2,1,0:T(8,128)S(1)}) fusion(f32[38,38,256]{2,1,0:T(8,128)S(1)} %get-tuple-element.53, f32[38,38,256]{2,1,0:T(8,128)S(1)} %get-tuple-element.54, f32[40,40,256]{2,1,0:T(8,128)S(1)} %get-tuple-element.58, f32[38,38,256]{2,1,0:T(8,128)S(1)} %get-tuple-element.55), kind=kLoop, calls=%fused_computation.63 | loop fusion | flops 11943936 | bytes 24788992 | tf_op jit(solution)/shard_map/sub | solution.py:131
  56.9 4.0 %multiply_subtract_fusion.3 = (f32[34,34,256]{2,1,0:T(8,128)S(1)}, f32[34,34,256]{2,1,0:T(8,128)S(1)}, f32[34,34,256]{2,1,0:T(8,128)S(1)}) fusion(f32[36,36,256]{2,1,0:T(8,128)S(1)} %get-tuple-element.50, f32[36,36,256]{2,1,0:T(8,128)S(1)} %get-tuple-element.51, f32[40,40,256]{2,1,0:T(8,128)S(1)} %get-tuple-element.58, f32[36,36,256]{2,1,0:T(8,128)S(1)} %get-tuple-element.52), kind=kLoop, calls=%fused_computation.84 | loop fusion | flops 10653696 | bytes 23212032 | tf_op jit(solution)/shard_map/sub | solution.py:131
  60.9 3.8 %fusion.56 = (f32[32,32,256]{2,1,0:T(8,128)S(1)}, f32[32,32,256]{2,1,0:T(8,128)}) fusion(f32[34,34,256]{2,1,0:T(8,128)S(1)} %get-tuple-element.48, f32[40,40,256]{2,1,0:T(8,128)S(1)} %get-tuple-element.58, f32[34,34,256]{2,1,0:T(8,128)S(1)} %get-tuple-element.47, f32[34,34,256]{2,1,0:T(8,128)S(1)} %get-tuple-element.49), kind=kLoop, calls=%fused_computation.101 | loop fusion | flops 7602176 | bytes 17465344 | tf_op jit(solution)/shard_map/add | solution.py:139
  65.1 0.6 copy-done.5
  65.8 0.5 fusion.43
  66.2 0.5 copy.181
  66.7 1.0 reshape.38
  67.8 3.5 %all-to-all-start = ((f32[16,1,2048]{2,1,0:T(1,128)}), f32[16,1,2048]{2,1,0:T(1,128)S(1)}, u32[]{:S(2)}, u32[]{:S(2)}) async-start(f32[16,1,2048]{2,1,0:T(1,128)} %reshape.38), calls=%async_computation | async-start | bytes 262144 | tf_op jit(solution)/shard_map/all_to_all | solution.py:218
  71.3 1.0 fusion.102
  72.3 4.5 %collective-permute-start.6 = (f32[6,22,3,256]{3,1,2,0:T(8,128)}, f32[6,22,3,256]{3,1,2,0:T(8,128)}, u32[]{:S(2)}, u32[]{:S(2)}) collective-permute-start(f32[6,22,3,256]{3,1,2,0:T(8,128)} %get-tuple-element.68), channel_id=1, source_target_pairs={{0,1},{1,2},{2,3},{3,4},{4,5},{5,6},{6,7},{7,8},{8,9},{9,10},{10,1... | collective-permute-start | bytes 1216520 | tf_op jit(solution)/shard_map/ppermute | solution.py:113
  76.8 1.5 %collective-permute-start.7 = (f32[6,22,3,256]{3,1,2,0:T(8,128)}, f32[6,22,3,256]{3,1,2,0:T(8,128)}, u32[]{:S(2)}, u32[]{:S(2)}) collective-permute-start(f32[6,22,3,256]{3,1,2,0:T(8,128)} %get-tuple-element.67), channel_id=1, source_target_pairs={{1,0},{2,1},{3,2},{4,3},{5,4},{6,5},{7,6},{8,7},{9,8},{10,9},{11,1... | collective-permute-start | bytes 1216520 | tf_op jit(solution)/shard_map/ppermute | solution.py:116
  78.3 3.1 %all-to-all-done = f32[16,1,2048]{2,1,0:T(1,128)S(1)} async-done(((f32[16,1,2048]{2,1,0:T(1,128)}), f32[16,1,2048]{2,1,0:T(1,128)S(1)}, u32[]{:S(2)}, u32[]{:S(2)}) %all-to-all-start) | async-done | bytes 131104 | tf_op jit(solution)/shard_map/all_to_all | solution.py:218
  81.3 0.5 broadcast.193
  81.9 0.9 reduce
  82.8 0.4 reshape.39
  83.2 0.6 copy.183
  83.8 1.1 broadcast_in_dim.22.blk_ref
  84.8 10.5 %shard_map.93 = f32[1,22,24,256]{3,2,1,0:T(8,128)} custom-call(f32[1,16,8,256]{3,2,1,0:T(8,128)} %broadcast_in_dim.22.blk_ref), custom_call_target="tpu_custom_call" | custom-call | tf_op jit(solution)/shard_map/pallas_call | solution.py:94
  95.4 1.1 slice_bitcast_fusion.3
  96.6 0.4 multiply_add_fusion
  99.9 1.0 constant_dynamic-update-slice_fusion.2
  101.1 1.0 constant_dynamic-update-slice_fusion
  102.5 0.8 fusion.67
  103.6 0.7 fusion.78
  104.5 0.4 fusion.84
  104.9 0.4 copy.208
  105.4 1.0 reshape.40
  106.4 8.3 %all-to-all-start.1 = ((f32[16,1,2048]{2,1,0:T(1,128)}), f32[16,1,2048]{2,1,0:T(1,128)S(1)}, u32[]{:S(2)}, u32[]{:S(2)}) async-start(f32[16,1,2048]{2,1,0:T(1,128)} %reshape.40), calls=%async_computation.1 | async-start | bytes 262144 | tf_op jit(solution)/shard_map/all_to_all | solution.py:232
  114.7 1.0 copy.211
  115.7 9.3 %all-to-all-done.1 = f32[16,1,2048]{2,1,0:T(1,128)S(1)} async-done(((f32[16,1,2048]{2,1,0:T(1,128)}), f32[16,1,2048]{2,1,0:T(1,128)S(1)}, u32[]{:S(2)}, u32[]{:S(2)}) %all-to-all-start.1) | async-done | bytes 131104 | tf_op jit(solution)/shard_map/all_to_all | solution.py:232
  124.9 0.9 reduce.1
  125.9 0.4 reshape.41
  126.2 0.9 copy.210
  127.2 1.0 copy.212
  (69 shorter events, 5.6 us)
Async XLA Ops:
  0.6 1.7 %copy-start.1 = (f32[32,32,256]{2,1,0:T(8,128)S(1)}, f32[32,32,256]{2,1,0:T(8,128)}, u32[]{:S(2)}) copy-start(f32[32,32,256]{2,1,0:T(8,128)} %param.7) | copy-start | bytes 3145732
  0.6 1.8 %copy-start.2 = (f32[32,32,256]{2,1,0:T(8,128)S(1)}, f32[32,32,256]{2,1,0:T(8,128)}, u32[]{:S(2)}) copy-start(f32[32,32,256]{2,1,0:T(8,128)} %param.6) | copy-start | bytes 3145732
  2.5 6.5 %copy-start.3 = (f32[3,16,8,256]{3,2,1,0:T(8,128)S(1)}, f32[3,16,8,256]{3,2,1,0:T(8,128)}, u32[]{:S(2)}) copy-start(f32[3,16,8,256]{3,2,1,0:T(8,128)} %param.10) | copy-start | bytes 1179652
  2.5 6.6 %copy-start.4 = (f32[3,16,8,256]{3,2,1,0:T(8,128)S(1)}, f32[3,16,8,256]{3,2,1,0:T(8,128)}, u32[]{:S(2)}) copy-start(f32[3,16,8,256]{3,2,1,0:T(8,128)} %param.9) | copy-start | bytes 1179652
  2.6 9.7 %collective-permute-start.1 = (f32[3,4,32,256]{3,2,1,0:T(8,128)S(1)}, f32[3,4,32,256]{3,2,1,0:T(8,128)S(1)}, u32[]{:S(2)}, u32[]{:S(2)}) collective-permute-start(f32[3,4,32,256]{3,2,1,0:T(8,128)S(1)} %get-tuple-element.62), channel_id=1, source_target_pairs={{16,0},{32,16},{48,32},{64,48},{80,64},{96,80},{112,96},{128,112},... | collective-permute-start | bytes 1179656 | tf_op jit(solution)/shard_map/ppermute | solution.py:116
  7.0 11.2 %collective-permute-start = (f32[3,4,32,256]{3,2,1,0:T(8,128)S(1)}, f32[3,4,32,256]{3,2,1,0:T(8,128)S(1)}, u32[]{:S(2)}, u32[]{:S(2)}) collective-permute-start(f32[3,4,32,256]{3,2,1,0:T(8,128)S(1)} %get-tuple-element.61), channel_id=1, source_target_pairs={{0,16},{16,32},{32,48},{48,64},{64,80},{80,96},{96,112},{112,128},... | collective-permute-start | bytes 1179656 | tf_op jit(solution)/shard_map/ppermute | solution.py:113
  18.8 27.5 %collective-permute-start.3 = (f32[3,40,4,256]{3,2,1,0:T(4,128)S(1)}, f32[3,40,4,256]{3,2,1,0:T(4,128)S(1)}, u32[]{:S(2)}, u32[]{:S(2)}) collective-permute-start(f32[3,40,4,256]{3,2,1,0:T(4,128)S(1)} %get-tuple-element.60), channel_id=1, source_target_pairs={{1,0},{2,1},{3,2},{4,3},{5,4},{6,5},{7,6},{8,7},{9,8},{10,9},{11,1... | collective-permute-start | bytes 1474568 | tf_op jit(solution)/shard_map/ppermute | solution.py:116
  20.1 26.2 %collective-permute-start.2 = (f32[3,40,4,256]{3,2,1,0:T(4,128)S(1)}, f32[3,40,4,256]{3,2,1,0:T(4,128)S(1)}, u32[]{:S(2)}, u32[]{:S(2)}) collective-permute-start(f32[3,40,4,256]{3,2,1,0:T(4,128)S(1)} %get-tuple-element.59), channel_id=1, source_target_pairs={{0,1},{1,2},{2,3},{3,4},{4,5},{5,6},{6,7},{7,8},{8,9},{9,10},{10,1... | collective-permute-start | bytes 1474568 | tf_op jit(solution)/shard_map/ppermute | solution.py:113
  24.8 15.7 %collective-permute-start.5 = (f32[6,3,8,256]{3,1,2,0:T(4,128)S(1)}, f32[6,3,8,256]{3,1,2,0:T(4,128)S(1)}, u32[]{:S(2)}, u32[]{:S(2)}) collective-permute-start(f32[6,3,8,256]{3,1,2,0:T(4,128)S(1)} %get-tuple-element.72), channel_id=1, source_target_pairs={{16,0},{32,16},{48,32},{64,48},{80,64},{96,80},{112,96},{128,112},... | collective-permute-start | bytes 442376 | tf_op jit(solution)/shard_map/ppermute | solution.py:116
  26.7 19.4 %collective-permute-start.4 = (f32[6,3,8,256]{3,1,2,0:T(4,128)S(1)}, f32[6,3,8,256]{3,1,2,0:T(4,128)S(1)}, u32[]{:S(2)}, u32[]{:S(2)}) collective-permute-start(f32[6,3,8,256]{3,1,2,0:T(4,128)S(1)} %get-tuple-element.71), channel_id=1, source_target_pairs={{0,16},{16,32},{32,48},{48,64},{64,80},{80,96},{96,112},{112,128},... | collective-permute-start | bytes 442376 | tf_op jit(solution)/shard_map/ppermute | solution.py:113
  64.7 2.0 %copy-start = (f32[32,32,256]{2,1,0:T(8,128)}, f32[32,32,256]{2,1,0:T(8,128)S(1)}, u32[]{:S(2)}) copy-start(f32[32,32,256]{2,1,0:T(8,128)S(1)} %get-tuple-element.37) | copy-start | bytes 3145732
  64.7 1.0 copy-start.5
  67.8 13.6 %all-to-all-start = ((f32[16,1,2048]{2,1,0:T(1,128)}), f32[16,1,2048]{2,1,0:T(1,128)S(1)}, u32[]{:S(2)}, u32[]{:S(2)}) async-start(f32[16,1,2048]{2,1,0:T(1,128)} %reshape.38), calls=%async_computation | async-start | bytes 262144 | tf_op jit(solution)/shard_map/all_to_all | solution.py:218
  72.3 27.6 %collective-permute-start.6 = (f32[6,22,3,256]{3,1,2,0:T(8,128)}, f32[6,22,3,256]{3,1,2,0:T(8,128)}, u32[]{:S(2)}, u32[]{:S(2)}) collective-permute-start(f32[6,22,3,256]{3,1,2,0:T(8,128)} %get-tuple-element.68), channel_id=1, source_target_pairs={{0,1},{1,2},{2,3},{3,4},{4,5},{5,6},{6,7},{7,8},{8,9},{9,10},{10,1... | collective-permute-start | bytes 1216520 | tf_op jit(solution)/shard_map/ppermute | solution.py:113
  76.8 24.3 %collective-permute-start.7 = (f32[6,22,3,256]{3,1,2,0:T(8,128)}, f32[6,22,3,256]{3,1,2,0:T(8,128)}, u32[]{:S(2)}, u32[]{:S(2)}) collective-permute-start(f32[6,22,3,256]{3,1,2,0:T(8,128)} %get-tuple-element.67), channel_id=1, source_target_pairs={{1,0},{2,1},{3,2},{4,3},{5,4},{6,5},{7,6},{8,7},{9,8},{10,9},{11,1... | collective-permute-start | bytes 1216520 | tf_op jit(solution)/shard_map/ppermute | solution.py:116
  106.4 18.6 %all-to-all-start.1 = ((f32[16,1,2048]{2,1,0:T(1,128)}), f32[16,1,2048]{2,1,0:T(1,128)S(1)}, u32[]{:S(2)}, u32[]{:S(2)}) async-start(f32[16,1,2048]{2,1,0:T(1,128)} %reshape.40), calls=%async_computation.1 | async-start | bytes 262144 | tf_op jit(solution)/shard_map/all_to_all | solution.py:232

commit v10 on v9

--- a/solution.py
+++ b/solution.py
@@ -103,6 +103,81 @@
         ],
         compiler_params=pltpu.CompilerParams(collective_id=cid, has_side_effects=True),
     )(block)
+
+
+def _rolls(v):
+    lane = lax.broadcasted_iota(jnp.int32, v.shape, 1)
+    last = v.shape[1] - 1
+    return (pltpu.roll(v, v.shape[0] - 1, 0), pltpu.roll(v, 1, 0),
+            jnp.where(lane == last, 0.0, pltpu.roll(v, last, 1)), jnp.where(lane == 0, 0.0, pltpu.roll(v, 1, 1)))
+
+
+def mech_kernel(zoff, s_ref, ub_ref, disp_out, energy_out, u1, u2):
+    _, nxe, nz, _ = ub_ref.shape
+    bx, bz = disp_out.shape[1], disp_out.shape[2]
+    m = (nxe - bx) // 2
+    lo = (nz - bz) // 2
+
+    def faces_at(i):
+        c = s_ref[i, pl.ds(zoff, nz), :]
+        xp = s_ref[i + 1, pl.ds(zoff, nz), :]
+        xm = s_ref[i - 1, pl.ds(zoff, nz), :]
+        zp, zm, yp, ym = _rolls(c)
+        faces = [0.5 * (c + o) for o in (xp, xm, zp, zm, yp, ym)]
+        diag = faces[0] + faces[1] + faces[2] + faces[3] + faces[4] + faces[5] + spring_term * c
+        return c, faces, diag
+
+    def sweep(src, dst, weight, i):
+        c, faces, diag = faces_at(i)
+        for k in range(3):
+            u = src[k, i]
+            others = (src[k, i + 1], src[k, i - 1]) + _rolls(u)
+            result = diag * u
+            for face, other in zip(faces, others):
+                result = result - face * other
+            new = u + weight * (ub_ref[3 + k, i] - result) / diag
+            dst[k, i] = jnp.where(c > 0, new, 0.0)
+
+    def first(i, carry):
+        sweep(ub_ref, u1, first_weight, i)
+        return carry
+
+    def second(i, carry):
+        sweep(u1, u2, second_weight, i)
+        return carry
+
+    lax.fori_loop(1, nxe - 1, first, 0)
+    lax.fori_loop(2, nxe - 2, second, 0)
+
+    def energy_row(i, carry):
+        _, faces, _ = faces_at(i)
+        parts = []
+        for k in range(3):
+            u = u2[k, i]
+            others = (u2[k, i + 1], u2[k, i - 1]) + _rolls(u)
+            total = jnp.zeros(u.shape, jnp.float32)
+            for face, other in zip(faces, others):
+                diff = u - other
+                total = total + face * diff * diff
+            parts.append(total)
+        u1[0, i] = 0.25 * (parts[0] + parts[1] + parts[2])
+        return carry
+
+    lax.fori_loop(m, m + bx, energy_row, 0)
+    energy_out[...] = u1[0, pl.ds(m, bx), pl.ds(lo, bz), :]
+    disp_out[...] = u2[:, pl.ds(m, bx), pl.ds(lo, bz), :]
+
+
+def mechanics(stiff_ext, ub, zoff, bx, bz):
+    _, nxe, nz, ny = ub.shape
+    return pl.pallas_call(
+        functools.partial(mech_kernel, zoff),
+        out_shape=(jax.ShapeDtypeStruct((3, bx, bz, ny), jnp.float32),
+                   jax.ShapeDtypeStruct((bx, bz, ny), jnp.float32)),
+        in_specs=[pl.BlockSpec(memory_space=pltpu.VMEM)] * 2,
+        out_specs=(pl.BlockSpec(memory_space=pltpu.VMEM), pl.BlockSpec(memory_space=pltpu.VMEM)),
+        scratch_shapes=[pltpu.VMEM((3, nxe, nz, ny), jnp.float32), pltpu.VMEM((3, nxe, nz, ny), jnp.float32)],
+    )(stiff_ext, ub)
 
 
 def padded_2(block, sides, width):
@@ -211,24 +286,14 @@
         conc, order, mob = advance(conc, order, mob, step == STEPS - 1)
 
     order, ub = lax.optimization_barrier((order, ub))
-    ub = padded_2(ub, (("gy", 2),), m)
+    ub = padded_2(ub, (("gy", 2),), m + 1)
     disp, load = ub[:3], ub[3:]
 
     coarse = restrict_xzy(order)
     stiff = lax.all_to_all(coarse, "gy", split_axis=1, concat_axis=2, tiled=True)
-    stiff_pad = halo_exchange(stiff[None], m, 0)[0, :, TILE - m:TILE - m + stiff.shape[1] + 2 * m]
-
-    faces, diag, center = face_terms(stiff_pad)
-    for weight in (first_weight, second_weight):
-        load = load[:, 1:-1, 1:-1]
-        result, u_c = apply_op(disp, faces, diag)
-        new = u_c + weight * (load - result) / diag
-        disp = jnp.where(center > 0, new, 0.0)
-        faces = [f[1:-1, 1:-1] for f in faces]
-        diag = diag[1:-1, 1:-1]
-        center = center[1:-1, 1:-1]
-    energy = strain_energy(disp, faces)
-    disp = disp[:, 1:-1, 1:-1]
+    stiff_ext = halo_exchange(stiff[None], m, 0)[0]
+    bx, bz = stiff.shape[0], stiff.shape[1]
+    disp, energy = mechanics(stiff_ext, ub, TILE - (m + 1), bx, bz)
     tiles = lax.all_to_all(energy, "gy", split_axis=2, concat_axis=1, tiled=True)
     return (conc, order, disp, jnp.transpose(tiles, (0, 2, 1)))
 

time: 129 us -> 132 us (1.023)
  blocking collectives: 0 us -> 35.8 us
  waiting for transfers between devices: 38.3 us -> 14 us
  Pallas kernels: 10.5 us -> 21.6 us
  starting transfers between devices: 34.3 us -> 24.3 us
  local copies, waits for them, and re-layouts: 18.1 us -> 9.39 us
    all_to_all x0 -> x2, blocking collectives: none -> 35.8 us  [the longest x1 21.3 us: on_device(): lax.all_to_all(coarse, 'gy', split_axis=1, concat_axis=2, tiled=True)]
    ppermute x4, waiting for transfers between devices: 14.3 us -> 1.76 us  [padded_2(): lax.ppermute(lax.slice_in_dim(block, 0, width, axis=dim), axis, backward)]
    all_to_all x2 -> x0, waiting for transfers between devices: 12.3 us -> none  [the longest x1 9.27 us: on_device(): lax.all_to_all(energy, 'gy', split_axis=2, concat_axis=1, tiled=True)]
    all_to_all x2 -> x0, starting transfers between devices: 11.8 us -> none  [the longest x1 8.3 us: on_device(): lax.all_to_all(energy, 'gy', split_axis=2, concat_axis=1, tiled=True)]
    pallas_call x0 -> x1, Pallas kernels: none -> 10.3 us  [mechanics(): pl.pallas_call(functools.partial(mech_kernel, zoff), out_shape=(jax.Shape...]
    ppermute x4, starting transfers between devices: 9.14 us -> 14.3 us  [padded_2(): lax.ppermute(lax.slice_in_dim(block, 0, width, axis=dim), axis, backward)]
    unnamed x22 -> x17, local copies, waits for them, and re-layouts: 6.98 us -> 2.66 us
    ppermute x4, starting transfers between devices: 13.4 us -> 10 us  [padded_2(): lax.ppermute(lax.slice_in_dim(block, block.shape[dim] - width, None, axis...]
  transfers between devices with their start and end apart: 10 -> 8, of which waited for: 6 -> 3; matrix products, arithmetic and copies ran while one was open for 9% -> 4% of each run, Pallas kernels for 8% -> 9%
where the time goes in v10:
time: 132 us
  blocking collectives  35.8 us (27%)
  other arithmetic  25.3 us (19%)
  starting transfers between devices  24.3 us (18%)
  Pallas kernels  21.6 us (16%)
  waiting for transfers between devices  14 us (11%)
  local copies, waits for them, and re-layouts  9.39 us (7%)
    all_to_all x1, blocking collectives, on_device(): lax.all_to_all(coarse, 'gy', split_axis=1, concat_axis=2, tiled=True)  21.3 us
    all_to_all x1, blocking collectives, on_device(): lax.all_to_all(energy, 'gy', split_axis=2, concat_axis=1, tiled=True)  14.5 us
    ppermute x4, starting transfers between devices, padded_2(): lax.ppermute(lax.slice_in_dim(block, 0, width, axis=dim), axis, backward)  14.3 us
    sub x4, other arithmetic, advance(): chem = conc_pad - order_pad * order_pad * (3.0 - 2.0 * order_pad)  13.3 us
    ppermute x4, waiting for transfers between devices, padded_2(): lax.ppermute(lax.slice_in_dim(block, block.shape[dim] - width, None, axis...  12.3 us
    pallas_call x1, Pallas kernels, halo_exchange(): pl.pallas_call(functools.partial(halo_kernel, hx, nx, ny), out_shape=jax....  11.3 us
    pallas_call x1, Pallas kernels, mechanics(): pl.pallas_call(functools.partial(mech_kernel, zoff), out_shape=(jax.Shape...  10.3 us
    ppermute x4, starting transfers between devices, padded_2(): lax.ppermute(lax.slice_in_dim(block, block.shape[dim] - width, None, axis...  10 us
  transfers between devices with their start and end apart: 8, of which 3 were waited for; matrix products, arithmetic and copies ran while one was open for 4% of the time, Pallas kernels for 9%

profile of v10, /device:TPU:2, one launch (start us, length us, event | category | flops | bytes accessed | tf_op | source)
XLA Modules:
  0.0 131.9 jit_solution(1488445095951903514)
XLA Ops:
  0.7 1.6 %add_bitcast_fusion = f32[1,32,32,256]{3,2,1,0:T(8,128)S(1)} fusion(s32[32,32,256]{2,1,0:T(8,128)} %param.8), kind=kLoop, calls=%fused_computation.110 | loop fusion | flops 2097152 | bytes 2097152 | tf_op jit(solution)/shard_map/stack | solution.py:278
  2.3 0.2 copy-done.1
  2.5 0.1 pad_maximum_fusion.7
  2.6 2.1 %collective-permute-start = (f32[3,4,32,256]{3,2,1,0:T(8,128)S(1)}, f32[3,4,32,256]{3,2,1,0:T(8,128)S(1)}, u32[]{:S(2)}, u32[]{:S(2)}) collective-permute-start(f32[3,4,32,256]{3,2,1,0:T(8,128)S(1)} %get-tuple-element.54), channel_id=1, source_target_pairs={{0,16},{16,32},{32,48},{48,64},{64,80},{80,96},{96,112},{112,128},... | collective-permute-start | bytes 1179656 | tf_op jit(solution)/shard_map/ppermute | solution.py:188
  4.6 5.8 %collective-permute-start.1 = (f32[3,4,32,256]{3,2,1,0:T(8,128)S(1)}, f32[3,4,32,256]{3,2,1,0:T(8,128)S(1)}, u32[]{:S(2)}, u32[]{:S(2)}) collective-permute-start(f32[3,4,32,256]{3,2,1,0:T(8,128)S(1)} %get-tuple-element.55), channel_id=1, source_target_pairs={{16,0},{32,16},{48,32},{64,48},{80,64},{96,80},{112,96},{128,112},... | collective-permute-start | bytes 1179656 | tf_op jit(solution)/shard_map/ppermute | solution.py:191
  10.4 0.1 pad_maximum_fusion.4
  10.5 3.4 %collective-permute-done = f32[3,4,32,256]{3,2,1,0:T(8,128)S(1)} collective-permute-done((f32[3,4,32,256]{3,2,1,0:T(8,128)S(1)}, f32[3,4,32,256]{3,2,1,0:T(8,128)S(1)}, u32[]{:S(2)}, u32[]{:S(2)}) %collective-permute-start) | collective-permute-done | bytes 393248 | tf_op jit(solution)/shard_map/ppermute | solution.py:188
  13.9 1.8 %collective-permute-done.1 = f32[3,4,32,256]{3,2,1,0:T(8,128)S(1)} collective-permute-done((f32[3,4,32,256]{3,2,1,0:T(8,128)S(1)}, f32[3,4,32,256]{3,2,1,0:T(8,128)S(1)}, u32[]{:S(2)}, u32[]{:S(2)}) %collective-permute-start.1) | collective-permute-done | bytes 393248 | tf_op jit(solution)/shard_map/ppermute | solution.py:191
  15.7 0.4 pad_maximum_fusion.1
  16.1 0.2 fusion.64
  16.2 3.9 %collective-permute-start.2 = (f32[3,40,4,256]{3,2,1,0:T(4,128)S(1)}, f32[3,40,4,256]{3,2,1,0:T(4,128)S(1)}, u32[]{:S(2)}, u32[]{:S(2)}) collective-permute-start(f32[3,40,4,256]{3,2,1,0:T(4,128)S(1)} %get-tuple-element.52), channel_id=1, source_target_pairs={{0,1},{1,2},{2,3},{3,4},{4,5},{5,6},{6,7},{7,8},{8,9},{9,10},{10,1... | collective-permute-start | bytes 1474568 | tf_op jit(solution)/shard_map/ppermute | solution.py:188
  20.1 1.3 collective-permute-start.3
  21.4 1.9 %collective-permute-start.4 = (f32[6,3,8,256]{3,2,1,0:T(8,128)S(1)}, f32[6,3,8,256]{3,2,1,0:T(8,128)S(1)}, u32[]{:S(2)}, u32[]{:S(2)}) collective-permute-start(f32[6,3,8,256]{3,2,1,0:T(8,128)S(1)} %get-tuple-element.60), channel_id=1, source_target_pairs={{0,16},{16,32},{32,48},{48,64},{64,80},{80,96},{96,112},{112,128},... | collective-permute-start | bytes 442376 | tf_op jit(solution)/shard_map/ppermute | solution.py:188
  23.4 5.8 %collective-permute-start.5 = (f32[6,3,8,256]{3,2,1,0:T(8,128)S(1)}, f32[6,3,8,256]{3,2,1,0:T(8,128)S(1)}, u32[]{:S(2)}, u32[]{:S(2)}) collective-permute-start(f32[6,3,8,256]{3,2,1,0:T(8,128)S(1)} %get-tuple-element.61), channel_id=1, source_target_pairs={{16,0},{32,16},{48,32},{64,48},{80,64},{96,80},{112,96},{128,112},... | collective-permute-start | bytes 442376 | tf_op jit(solution)/shard_map/ppermute | solution.py:191
  29.1 8.8 %collective-permute-done.4 = f32[6,3,8,256]{3,2,1,0:T(8,128)S(1)} collective-permute-done((f32[6,3,8,256]{3,2,1,0:T(8,128)S(1)}, f32[6,3,8,256]{3,2,1,0:T(8,128)S(1)}, u32[]{:S(2)}, u32[]{:S(2)}) %collective-permute-start.4) | collective-permute-done | bytes 147488 | tf_op jit(solution)/shard_map/ppermute | solution.py:188
  38.0 0.1 pad_maximum_fusion.3
  38.1 0.0 collective-permute-done.3
  38.1 0.9 pad_maximum_fusion
  39.0 0.3 slice_bitcast_fusion.1
  39.3 0.3 multiply_subtract_fusion
  39.6 4.5 %multiply_subtract_fusion.1 = (f32[38,38,256]{2,1,0:T(8,128)S(1)}, f32[38,38,256]{2,1,0:T(8,128)S(1)}, f32[38,38,256]{2,1,0:T(8,128)S(1)}) fusion(f32[40,40,256]{2,1,0:T(8,128)S(1)} %multiply_subtract_fusion, f32[40,40,256]{2,1,0:T(8,128)S(1)} %get-tuple-element.50, f32[40,40,256]{2,1,0:T(8,128)S(1)} %get-tuple-element.51, ...), kind=kLoop, calls=%fused_computation.43 | loop fusion | flops 13307904 | bytes 26390528 | tf_op jit(solution)/shard_map/sub | solution.py:206
  44.2 4.5 %multiply_subtract_fusion.2 = (f32[36,36,256]{2,1,0:T(8,128)S(1)}, f32[36,36,256]{2,1,0:T(8,128)S(1)}, f32[36,36,256]{2,1,0:T(8,128)S(1)}) fusion(f32[38,38,256]{2,1,0:T(8,128)S(1)} %get-tuple-element.46, f32[38,38,256]{2,1,0:T(8,128)S(1)} %get-tuple-element.47, f32[40,40,256]{2,1,0:T(8,128)S(1)} %get-tuple-element.51, f32[38,38,256]{2,1,0:T(8,128)S(1)} %get-tuple-element.48), kind=kLoop, calls=%fused_computation.64 | loop fusion | flops 11943936 | bytes 24788992 | tf_op jit(solution)/shard_map/sub | solution.py:206
  48.6 4.0 %multiply_subtract_fusion.3 = (f32[34,34,256]{2,1,0:T(8,128)S(1)}, f32[34,34,256]{2,1,0:T(8,128)S(1)}, f32[34,34,256]{2,1,0:T(8,128)S(1)}) fusion(f32[36,36,256]{2,1,0:T(8,128)S(1)} %get-tuple-element.43, f32[36,36,256]{2,1,0:T(8,128)S(1)} %get-tuple-element.44, f32[40,40,256]{2,1,0:T(8,128)S(1)} %get-tuple-element.51, f32[36,36,256]{2,1,0:T(8,128)S(1)} %get-tuple-element.45), kind=kLoop, calls=%fused_computation.85 | loop fusion | flops 10653696 | bytes 23212032 | tf_op jit(solution)/shard_map/sub | solution.py:206
  52.7 3.8 %fusion.56 = (f32[32,32,256]{2,1,0:T(8,128)S(1)}, f32[32,32,256]{2,1,0:T(8,128)}) fusion(f32[34,34,256]{2,1,0:T(8,128)S(1)} %get-tuple-element.41, f32[40,40,256]{2,1,0:T(8,128)S(1)} %get-tuple-element.51, f32[34,34,256]{2,1,0:T(8,128)S(1)} %get-tuple-element.40, f32[34,34,256]{2,1,0:T(8,128)S(1)} %get-tuple-element.42), kind=kLoop, calls=%fused_computation.102 | loop fusion | flops 7602176 | bytes 17465344 | tf_op jit(solution)/shard_map/add | solution.py:214
  56.5 1.3 fusion.65
  57.8 2.2 %collective-permute-start.6 = (f32[6,22,4,256]{3,2,1,0:T(4,128)}, f32[6,22,4,256]{3,2,1,0:T(4,128)}, u32[]{:S(2)}, u32[]{:S(2)}) collective-permute-start(f32[6,22,4,256]{3,2,1,0:T(4,128)} %get-tuple-element.58), channel_id=1, source_target_pairs={{0,1},{1,2},{2,3},{3,4},{4,5},{5,6},{6,7},{7,8},{8,9},{9,10},{10,1... | collective-permute-start | bytes 1622024 | tf_op jit(solution)/shard_map/ppermute | solution.py:188
  60.0 1.5 %collective-permute-start.7 = (f32[6,22,4,256]{3,2,1,0:T(4,128)}, f32[6,22,4,256]{3,2,1,0:T(4,128)}, u32[]{:S(2)}, u32[]{:S(2)}) collective-permute-start(f32[6,22,4,256]{3,2,1,0:T(4,128)} %get-tuple-element.59), channel_id=1, source_target_pairs={{1,0},{2,1},{3,2},{4,3},{5,4},{6,5},{7,6},{8,7},{9,8},{10,9},{11,1... | collective-permute-start | bytes 1622024 | tf_op jit(solution)/shard_map/ppermute | solution.py:191
  61.5 0.1 bitcast_reduce_fusion
  61.6 0.3 bitcast_reduce_fusion.1
  61.9 0.5 fusion.43
  62.4 0.5 copy.43
  62.9 0.4 reshape.18
  63.3 21.3 %all_to_all.33 = f32[16,1,2048]{2,1,0:T(1,128)S(1)} all-to-all(f32[16,1,2048]{2,1,0:T(1,128)S(1)} %reshape.18), channel_id=1, replica_groups=mesh['gx'=16,'gy'=16] {'gy'}, dimensions={0} | all-to-all | bytes 262144 | tf_op jit(solution)/shard_map/all_to_all | solution.py:293
  84.6 0.5 broadcast.141
  85.1 0.9 reduce
  86.0 0.4 reshape.19
  86.3 0.6 copy.45
  86.9 1.1 broadcast_in_dim.9.blk_ref
  88.0 11.3 %shard_map.93 = f32[1,22,24,256]{3,2,1,0:T(8,128)} custom-call(f32[1,16,8,256]{3,2,1,0:T(8,128)} %broadcast_in_dim.9.blk_ref), custom_call_target="tpu_custom_call" | custom-call | tf_op jit(solution)/shard_map/pallas_call | solution.py:94
  99.3 3.0 %pad_maximum_fusion.2.ub_ref = f32[6,22,16,256]{3,2,1,0:T(8,128)} fusion(f32[6,22,4,256]{3,2,1,0:T(4,128)} %collective-permute-done.7, f32[6,22,8,256]{3,2,1,0:T(8,128)S(1)} %pad_maximum_fusion.3, f32[6,22,4,256]{3,2,1,0:T(4,128)} %collective-permute-done.6), kind=kLoop, calls=%fused_computation.18 | loop fusion | flops 1081344 | bytes 4325376 | tf_op jit(solution)/shard_map/concatenate | solution.py:192
  102.2 10.3 %shard_map.94 = (f32[3,16,8,256]{3,2,1,0:T(8,128)}, f32[16,8,256]{2,1,0:T(8,128)}) custom-call(f32[22,24,256]{2,1,0:T(8,128)} %bitcast.47, f32[6,22,16,256]{3,2,1,0:T(8,128)} %pad_maximum_fusion.2.ub_ref), custom_call_target="tpu_custom_call" | custom-call | tf_op jit(solution)/shard_map/pallas_call | solution.py:173
  112.6 1.3 %copy.46 = f32[16,8,256]{0,1,2:T(8,128)S(1)} copy(f32[16,8,256]{2,1,0:T(8,128)} %get-tuple-element.15) | data formatting | bytes 262144 | tf_op jit(solution)/shard_map/pallas_call | solution.py:173
  113.9 0.4 reshape.20
  114.3 14.5 %all_to_all.34 = f32[16,1,2048]{2,1,0:T(1,128)S(1)} all-to-all(f32[16,1,2048]{2,1,0:T(1,128)S(1)} %reshape.20), channel_id=1, replica_groups=mesh['gx'=16,'gy'=16] {'gy'}, dimensions={0} | all-to-all | bytes 262144 | tf_op jit(solution)/shard_map/all_to_all | solution.py:297
  128.8 0.9 reduce.1
  129.6 0.4 reshape.21
  130.0 0.9 copy.47
  130.9 1.0 copy.48
  (16 shorter events, 0.1 us)
Async XLA Ops:
  0.6 1.7 %copy-start.2 = (f32[32,32,256]{2,1,0:T(8,128)S(1)}, f32[32,32,256]{2,1,0:T(8,128)}, u32[]{:S(2)}) copy-start(f32[32,32,256]{2,1,0:T(8,128)} %param.6) | copy-start | bytes 3145732
  0.6 1.8 %copy-start.1 = (f32[32,32,256]{2,1,0:T(8,128)S(1)}, f32[32,32,256]{2,1,0:T(8,128)}, u32[]{:S(2)}) copy-start(f32[32,32,256]{2,1,0:T(8,128)} %param.7) | copy-start | bytes 3145732
  2.5 7.9 %copy-start.3 = (f32[3,16,8,256]{3,2,1,0:T(8,128)S(1)}, f32[3,16,8,256]{3,2,1,0:T(8,128)}, u32[]{:S(2)}) copy-start(f32[3,16,8,256]{3,2,1,0:T(8,128)} %param.10) | copy-start | bytes 1179652
  2.5 7.9 %copy-start.4 = (f32[3,16,8,256]{3,2,1,0:T(8,128)S(1)}, f32[3,16,8,256]{3,2,1,0:T(8,128)}, u32[]{:S(2)}) copy-start(f32[3,16,8,256]{3,2,1,0:T(8,128)} %param.9) | copy-start | bytes 1179652
  2.6 11.3 %collective-permute-start = (f32[3,4,32,256]{3,2,1,0:T(8,128)S(1)}, f32[3,4,32,256]{3,2,1,0:T(8,128)S(1)}, u32[]{:S(2)}, u32[]{:S(2)}) collective-permute-start(f32[3,4,32,256]{3,2,1,0:T(8,128)S(1)} %get-tuple-element.54), channel_id=1, source_target_pairs={{0,16},{16,32},{32,48},{48,64},{64,80},{80,96},{96,112},{112,128},... | collective-permute-start | bytes 1179656 | tf_op jit(solution)/shard_map/ppermute | solution.py:188
  4.6 11.0 %collective-permute-start.1 = (f32[3,4,32,256]{3,2,1,0:T(8,128)S(1)}, f32[3,4,32,256]{3,2,1,0:T(8,128)S(1)}, u32[]{:S(2)}, u32[]{:S(2)}) collective-permute-start(f32[3,4,32,256]{3,2,1,0:T(8,128)S(1)} %get-tuple-element.55), channel_id=1, source_target_pairs={{16,0},{32,16},{48,32},{64,48},{80,64},{96,80},{112,96},{128,112},... | collective-permute-start | bytes 1179656 | tf_op jit(solution)/shard_map/ppermute | solution.py:191
  16.2 21.8 %collective-permute-start.2 = (f32[3,40,4,256]{3,2,1,0:T(4,128)S(1)}, f32[3,40,4,256]{3,2,1,0:T(4,128)S(1)}, u32[]{:S(2)}, u32[]{:S(2)}) collective-permute-start(f32[3,40,4,256]{3,2,1,0:T(4,128)S(1)} %get-tuple-element.52), channel_id=1, source_target_pairs={{0,1},{1,2},{2,3},{3,4},{4,5},{5,6},{6,7},{7,8},{8,9},{9,10},{10,1... | collective-permute-start | bytes 1474568 | tf_op jit(solution)/shard_map/ppermute | solution.py:188
  20.1 18.0 %collective-permute-start.3 = (f32[3,40,4,256]{3,2,1,0:T(4,128)S(1)}, f32[3,40,4,256]{3,2,1,0:T(4,128)S(1)}, u32[]{:S(2)}, u32[]{:S(2)}) collective-permute-start(f32[3,40,4,256]{3,2,1,0:T(4,128)S(1)} %get-tuple-element.53), channel_id=1, source_target_pairs={{1,0},{2,1},{3,2},{4,3},{5,4},{6,5},{7,6},{8,7},{9,8},{10,9},{11,1... | collective-permute-start | bytes 1474568 | tf_op jit(solution)/shard_map/ppermute | solution.py:191
  21.4 16.5 %collective-permute-start.4 = (f32[6,3,8,256]{3,2,1,0:T(8,128)S(1)}, f32[6,3,8,256]{3,2,1,0:T(8,128)S(1)}, u32[]{:S(2)}, u32[]{:S(2)}) collective-permute-start(f32[6,3,8,256]{3,2,1,0:T(8,128)S(1)} %get-tuple-element.60), channel_id=1, source_target_pairs={{0,16},{16,32},{32,48},{48,64},{64,80},{80,96},{96,112},{112,128},... | collective-permute-start | bytes 442376 | tf_op jit(solution)/shard_map/ppermute | solution.py:188
  23.4 14.6 %collective-permute-start.5 = (f32[6,3,8,256]{3,2,1,0:T(8,128)S(1)}, f32[6,3,8,256]{3,2,1,0:T(8,128)S(1)}, u32[]{:S(2)}, u32[]{:S(2)}) collective-permute-start(f32[6,3,8,256]{3,2,1,0:T(8,128)S(1)} %get-tuple-element.61), channel_id=1, source_target_pairs={{16,0},{32,16},{48,32},{64,48},{80,64},{96,80},{112,96},{128,112},... | collective-permute-start | bytes 442376 | tf_op jit(solution)/shard_map/ppermute | solution.py:191
  56.5 5.1 %copy-start = (f32[32,32,256]{2,1,0:T(8,128)}, f32[32,32,256]{2,1,0:T(8,128)S(1)}, u32[]{:S(2)}) copy-start(f32[32,32,256]{2,1,0:T(8,128)S(1)} %get-tuple-element.37) | copy-start | bytes 3145732
  57.8 4.1 %copy-start.5 = (f32[256,128,1]{1,0,2:T(8,128)S(1)}, f32[256,128,1]{1,0,2:T(8,128)}, u32[]{:S(2)}) copy-start(f32[256,128,1]{1,0,2:T(8,128)} %constant.36) | copy-start | bytes 393220
  57.8 41.5 %collective-permute-start.6 = (f32[6,22,4,256]{3,2,1,0:T(4,128)}, f32[6,22,4,256]{3,2,1,0:T(4,128)}, u32[]{:S(2)}, u32[]{:S(2)}) collective-permute-start(f32[6,22,4,256]{3,2,1,0:T(4,128)} %get-tuple-element.58), channel_id=1, source_target_pairs={{0,1},{1,2},{2,3},{3,4},{4,5},{5,6},{6,7},{7,8},{8,9},{9,10},{10,1... | collective-permute-start | bytes 1622024 | tf_op jit(solution)/shard_map/ppermute | solution.py:188
  60.0 39.3 %collective-permute-start.7 = (f32[6,22,4,256]{3,2,1,0:T(4,128)}, f32[6,22,4,256]{3,2,1,0:T(4,128)}, u32[]{:S(2)}, u32[]{:S(2)}) collective-permute-start(f32[6,22,4,256]{3,2,1,0:T(4,128)} %get-tuple-element.59), channel_id=1, source_target_pairs={{1,0},{2,1},{3,2},{4,3},{5,4},{6,5},{7,6},{8,7},{9,8},{10,9},{11,1... | collective-permute-start | bytes 1622024 | tf_op jit(solution)/shard_map/ppermute | solution.py:191

commit v11 on v10

--- a/solution.py
+++ b/solution.py
@@ -112,29 +112,39 @@
             jnp.where(lane == last, 0.0, pltpu.roll(v, last, 1)), jnp.where(lane == 0, 0.0, pltpu.roll(v, 1, 1)))
 
 
-def mech_kernel(zoff, s_ref, ub_ref, disp_out, energy_out, u1, u2):
+def mech_kernel(zoff, s_ref, ub_ref, disp_out, energy_out, u1, u2, fc):
     _, nxe, nz, _ = ub_ref.shape
     bx, bz = disp_out.shape[1], disp_out.shape[2]
     m = (nxe - bx) // 2
     lo = (nz - bz) // 2
 
-    def faces_at(i):
-        c = s_ref[i, pl.ds(zoff, nz), :]
-        xp = s_ref[i + 1, pl.ds(zoff, nz), :]
-        xm = s_ref[i - 1, pl.ds(zoff, nz), :]
+    def align(i, carry):
+        fc[7, i] = s_ref[i, pl.ds(zoff, nz), :]
+        return carry
+
+    lax.fori_loop(0, nxe, align, 0)
+
+    def faces_row(i, carry):
+        c = fc[7, i]
         zp, zm, yp, ym = _rolls(c)
-        faces = [0.5 * (c + o) for o in (xp, xm, zp, zm, yp, ym)]
-        diag = faces[0] + faces[1] + faces[2] + faces[3] + faces[4] + faces[5] + spring_term * c
-        return c, faces, diag
+        diag = None
+        for f, o in enumerate((fc[7, i + 1], fc[7, i - 1], zp, zm, yp, ym)):
+            face = 0.5 * (c + o)
+            fc[f, i] = face
+            diag = face if diag is None else diag + face
+        fc[6, i] = diag + spring_term * c
+        return carry
+
+    lax.fori_loop(1, nxe - 1, faces_row, 0)
 
     def sweep(src, dst, weight, i):
-        c, faces, diag = faces_at(i)
+        c, diag = fc[7, i], fc[6, i]
         for k in range(3):
             u = src[k, i]
             others = (src[k, i + 1], src[k, i - 1]) + _rolls(u)
             result = diag * u
-            for face, other in zip(faces, others):
-                result = result - face * other
+            for f, other in enumerate(others):
+                result = result - fc[f, i] * other
             new = u + weight * (ub_ref[3 + k, i] - result) / diag
             dst[k, i] = jnp.where(c > 0, new, 0.0)
 
@@ -150,15 +160,14 @@
     lax.fori_loop(2, nxe - 2, second, 0)
 
     def energy_row(i, carry):
-        _, faces, _ = faces_at(i)
         parts = []
         for k in range(3):
             u = u2[k, i]
             others = (u2[k, i + 1], u2[k, i - 1]) + _rolls(u)
             total = jnp.zeros(u.shape, jnp.float32)
-            for face, other in zip(faces, others):
+            for f, other in enumerate(others):
                 diff = u - other
-                total = total + face * diff * diff
+                total = total + fc[f, i] * diff * diff
             parts.append(total)
         u1[0, i] = 0.25 * (parts[0] + parts[1] + parts[2])
         return carry
@@ -176,7 +185,8 @@
                    jax.ShapeDtypeStruct((bx, bz, ny), jnp.float32)),
         in_specs=[pl.BlockSpec(memory_space=pltpu.VMEM)] * 2,
         out_specs=(pl.BlockSpec(memory_space=pltpu.VMEM), pl.BlockSpec(memory_space=pltpu.VMEM)),
-        scratch_shapes=[pltpu.VMEM((3, nxe, nz, ny), jnp.float32), pltpu.VMEM((3, nxe, nz, ny), jnp.float32)],
+        scratch_shapes=[pltpu.VMEM((3, nxe, nz, ny), jnp.float32), pltpu.VMEM((3, nxe, nz, ny), jnp.float32),
+                        pltpu.VMEM((8, nxe, nz, ny), jnp.float32)],
     )(stiff_ext, ub)
 
 

time: 132 us -> 132 us (level)
  no operation moved by 1% of the time
where the time goes in v11:
time: 132 us; the launch traced here: 131 us
  blocking collectives  35.8 us (27%)
  other arithmetic  25.3 us (19%)
  starting transfers between devices  24.3 us (18%)
  Pallas kernels  21.2 us (16%)
  waiting for transfers between devices  14 us (11%)
  local copies, waits for them, and re-layouts  9.39 us (7%)
    all_to_all x1, blocking collectives, on_device(): lax.all_to_all(coarse, 'gy', split_axis=1, concat_axis=2, tiled=True)  21.3 us
    all_to_all x1, blocking collectives, on_device(): lax.all_to_all(energy, 'gy', split_axis=2, concat_axis=1, tiled=True)  14.5 us
    ppermute x4, starting transfers between devices, padded_2(): lax.ppermute(lax.slice_in_dim(block, 0, width, axis=dim), axis, backward)  14.3 us
    sub x4, other arithmetic, advance(): chem = conc_pad - order_pad * order_pad * (3.0 - 2.0 * order_pad)  13.3 us
    ppermute x4, waiting for transfers between devices, padded_2(): lax.ppermute(lax.slice_in_dim(block, block.shape[dim] - width, None, axis...  12.3 us
    pallas_call x1, Pallas kernels, halo_exchange(): pl.pallas_call(functools.partial(halo_kernel, hx, nx, ny), out_shape=jax....  11.3 us
    ppermute x4, starting transfers between devices, padded_2(): lax.ppermute(lax.slice_in_dim(block, block.shape[dim] - width, None, axis...  10 us
    pallas_call x1, Pallas kernels, mechanics(): pl.pallas_call(functools.partial(mech_kernel, zoff), out_shape=(jax.Shape...  9.92 us
  transfers between devices with their start and end apart: 8, of which 3 were waited for; matrix products, arithmetic and copies ran while one was open for 4% of the time, Pallas kernels for 9%

profile of v11, /device:TPU:2, one launch (start us, length us, event | category | flops | bytes accessed | tf_op | source)
XLA Modules:
  0.0 131.5 jit_solution(9411007963931525464)
XLA Ops:
  0.7 1.6 %add_bitcast_fusion = f32[1,32,32,256]{3,2,1,0:T(8,128)S(1)} fusion(s32[32,32,256]{2,1,0:T(8,128)} %param.8), kind=kLoop, calls=%fused_computation.110 | loop fusion | flops 2097152 | bytes 2097152 | tf_op jit(solution)/shard_map/stack | solution.py:288
  2.3 0.2 copy-done.1
  2.5 0.1 pad_maximum_fusion.7
  2.6 2.1 %collective-permute-start = (f32[3,4,32,256]{3,2,1,0:T(8,128)S(1)}, f32[3,4,32,256]{3,2,1,0:T(8,128)S(1)}, u32[]{:S(2)}, u32[]{:S(2)}) collective-permute-start(f32[3,4,32,256]{3,2,1,0:T(8,128)S(1)} %get-tuple-element.54), channel_id=1, source_target_pairs={{0,16},{16,32},{32,48},{48,64},{64,80},{80,96},{96,112},{112,128},... | collective-permute-start | bytes 1179656 | tf_op jit(solution)/shard_map/ppermute | solution.py:198
  4.6 5.8 %collective-permute-start.1 = (f32[3,4,32,256]{3,2,1,0:T(8,128)S(1)}, f32[3,4,32,256]{3,2,1,0:T(8,128)S(1)}, u32[]{:S(2)}, u32[]{:S(2)}) collective-permute-start(f32[3,4,32,256]{3,2,1,0:T(8,128)S(1)} %get-tuple-element.55), channel_id=1, source_target_pairs={{16,0},{32,16},{48,32},{64,48},{80,64},{96,80},{112,96},{128,112},... | collective-permute-start | bytes 1179656 | tf_op jit(solution)/shard_map/ppermute | solution.py:201
  10.4 0.1 pad_maximum_fusion.4
  10.5 3.4 %collective-permute-done = f32[3,4,32,256]{3,2,1,0:T(8,128)S(1)} collective-permute-done((f32[3,4,32,256]{3,2,1,0:T(8,128)S(1)}, f32[3,4,32,256]{3,2,1,0:T(8,128)S(1)}, u32[]{:S(2)}, u32[]{:S(2)}) %collective-permute-start) | collective-permute-done | bytes 393248 | tf_op jit(solution)/shard_map/ppermute | solution.py:198
  13.9 1.8 %collective-permute-done.1 = f32[3,4,32,256]{3,2,1,0:T(8,128)S(1)} collective-permute-done((f32[3,4,32,256]{3,2,1,0:T(8,128)S(1)}, f32[3,4,32,256]{3,2,1,0:T(8,128)S(1)}, u32[]{:S(2)}, u32[]{:S(2)}) %collective-permute-start.1) | collective-permute-done | bytes 393248 | tf_op jit(solution)/shard_map/ppermute | solution.py:201
  15.7 0.4 pad_maximum_fusion.1
  16.1 0.2 fusion.64
  16.2 3.9 %collective-permute-start.2 = (f32[3,40,4,256]{3,2,1,0:T(4,128)S(1)}, f32[3,40,4,256]{3,2,1,0:T(4,128)S(1)}, u32[]{:S(2)}, u32[]{:S(2)}) collective-permute-start(f32[3,40,4,256]{3,2,1,0:T(4,128)S(1)} %get-tuple-element.52), channel_id=1, source_target_pairs={{0,1},{1,2},{2,3},{3,4},{4,5},{5,6},{6,7},{7,8},{8,9},{9,10},{10,1... | collective-permute-start | bytes 1474568 | tf_op jit(solution)/shard_map/ppermute | solution.py:198
  20.1 1.3 collective-permute-start.3
  21.4 1.9 %collective-permute-start.4 = (f32[6,3,8,256]{3,2,1,0:T(8,128)S(1)}, f32[6,3,8,256]{3,2,1,0:T(8,128)S(1)}, u32[]{:S(2)}, u32[]{:S(2)}) collective-permute-start(f32[6,3,8,256]{3,2,1,0:T(8,128)S(1)} %get-tuple-element.60), channel_id=1, source_target_pairs={{0,16},{16,32},{32,48},{48,64},{64,80},{80,96},{96,112},{112,128},... | collective-permute-start | bytes 442376 | tf_op jit(solution)/shard_map/ppermute | solution.py:198
  23.4 5.8 %collective-permute-start.5 = (f32[6,3,8,256]{3,2,1,0:T(8,128)S(1)}, f32[6,3,8,256]{3,2,1,0:T(8,128)S(1)}, u32[]{:S(2)}, u32[]{:S(2)}) collective-permute-start(f32[6,3,8,256]{3,2,1,0:T(8,128)S(1)} %get-tuple-element.61), channel_id=1, source_target_pairs={{16,0},{32,16},{48,32},{64,48},{80,64},{96,80},{112,96},{128,112},... | collective-permute-start | bytes 442376 | tf_op jit(solution)/shard_map/ppermute | solution.py:201
  29.1 8.8 %collective-permute-done.4 = f32[6,3,8,256]{3,2,1,0:T(8,128)S(1)} collective-permute-done((f32[6,3,8,256]{3,2,1,0:T(8,128)S(1)}, f32[6,3,8,256]{3,2,1,0:T(8,128)S(1)}, u32[]{:S(2)}, u32[]{:S(2)}) %collective-permute-start.4) | collective-permute-done | bytes 147488 | tf_op jit(solution)/shard_map/ppermute | solution.py:198
  38.0 0.1 pad_maximum_fusion.3
  38.1 0.0 collective-permute-done.3
  38.1 0.9 pad_maximum_fusion
  39.0 0.3 slice_bitcast_fusion.1
  39.3 0.3 multiply_subtract_fusion
  39.6 4.5 %multiply_subtract_fusion.1 = (f32[38,38,256]{2,1,0:T(8,128)S(1)}, f32[38,38,256]{2,1,0:T(8,128)S(1)}, f32[38,38,256]{2,1,0:T(8,128)S(1)}) fusion(f32[40,40,256]{2,1,0:T(8,128)S(1)} %multiply_subtract_fusion, f32[40,40,256]{2,1,0:T(8,128)S(1)} %get-tuple-element.50, f32[40,40,256]{2,1,0:T(8,128)S(1)} %get-tuple-element.51, ...), kind=kLoop, calls=%fused_computation.43 | loop fusion | flops 13307904 | bytes 26390528 | tf_op jit(solution)/shard_map/sub | solution.py:216
  44.2 4.5 %multiply_subtract_fusion.2 = (f32[36,36,256]{2,1,0:T(8,128)S(1)}, f32[36,36,256]{2,1,0:T(8,128)S(1)}, f32[36,36,256]{2,1,0:T(8,128)S(1)}) fusion(f32[38,38,256]{2,1,0:T(8,128)S(1)} %get-tuple-element.46, f32[38,38,256]{2,1,0:T(8,128)S(1)} %get-tuple-element.47, f32[40,40,256]{2,1,0:T(8,128)S(1)} %get-tuple-element.51, f32[38,38,256]{2,1,0:T(8,128)S(1)} %get-tuple-element.48), kind=kLoop, calls=%fused_computation.64 | loop fusion | flops 11943936 | bytes 24788992 | tf_op jit(solution)/shard_map/sub | solution.py:216
  48.6 4.0 %multiply_subtract_fusion.3 = (f32[34,34,256]{2,1,0:T(8,128)S(1)}, f32[34,34,256]{2,1,0:T(8,128)S(1)}, f32[34,34,256]{2,1,0:T(8,128)S(1)}) fusion(f32[36,36,256]{2,1,0:T(8,128)S(1)} %get-tuple-element.43, f32[36,36,256]{2,1,0:T(8,128)S(1)} %get-tuple-element.44, f32[40,40,256]{2,1,0:T(8,128)S(1)} %get-tuple-element.51, f32[36,36,256]{2,1,0:T(8,128)S(1)} %get-tuple-element.45), kind=kLoop, calls=%fused_computation.85 | loop fusion | flops 10653696 | bytes 23212032 | tf_op jit(solution)/shard_map/sub | solution.py:216
  52.7 3.8 %fusion.56 = (f32[32,32,256]{2,1,0:T(8,128)S(1)}, f32[32,32,256]{2,1,0:T(8,128)}) fusion(f32[34,34,256]{2,1,0:T(8,128)S(1)} %get-tuple-element.41, f32[40,40,256]{2,1,0:T(8,128)S(1)} %get-tuple-element.51, f32[34,34,256]{2,1,0:T(8,128)S(1)} %get-tuple-element.40, f32[34,34,256]{2,1,0:T(8,128)S(1)} %get-tuple-element.42), kind=kLoop, calls=%fused_computation.102 | loop fusion | flops 7602176 | bytes 17465344 | tf_op jit(solution)/shard_map/add | solution.py:224
  56.5 1.3 fusion.65
  57.8 2.2 %collective-permute-start.6 = (f32[6,22,4,256]{3,2,1,0:T(4,128)}, f32[6,22,4,256]{3,2,1,0:T(4,128)}, u32[]{:S(2)}, u32[]{:S(2)}) collective-permute-start(f32[6,22,4,256]{3,2,1,0:T(4,128)} %get-tuple-element.58), channel_id=1, source_target_pairs={{0,1},{1,2},{2,3},{3,4},{4,5},{5,6},{6,7},{7,8},{8,9},{9,10},{10,1... | collective-permute-start | bytes 1622024 | tf_op jit(solution)/shard_map/ppermute | solution.py:198
  60.0 1.5 %collective-permute-start.7 = (f32[6,22,4,256]{3,2,1,0:T(4,128)}, f32[6,22,4,256]{3,2,1,0:T(4,128)}, u32[]{:S(2)}, u32[]{:S(2)}) collective-permute-start(f32[6,22,4,256]{3,2,1,0:T(4,128)} %get-tuple-element.59), channel_id=1, source_target_pairs={{1,0},{2,1},{3,2},{4,3},{5,4},{6,5},{7,6},{8,7},{9,8},{10,9},{11,1... | collective-permute-start | bytes 1622024 | tf_op jit(solution)/shard_map/ppermute | solution.py:201
  61.5 0.1 bitcast_reduce_fusion
  61.6 0.3 bitcast_reduce_fusion.1
  61.9 0.5 fusion.43
  62.4 0.5 copy.43
  62.9 0.4 reshape.18
  63.3 21.3 %all_to_all.33 = f32[16,1,2048]{2,1,0:T(1,128)S(1)} all-to-all(f32[16,1,2048]{2,1,0:T(1,128)S(1)} %reshape.18), channel_id=1, replica_groups=mesh['gx'=16,'gy'=16] {'gy'}, dimensions={0} | all-to-all | bytes 262144 | tf_op jit(solution)/shard_map/all_to_all | solution.py:303
  84.6 0.5 broadcast.141
  85.1 0.9 reduce
  86.0 0.4 reshape.19
  86.3 0.6 copy.45
  86.9 1.1 broadcast_in_dim.9.blk_ref
  88.0 11.3 %shard_map.93 = f32[1,22,24,256]{3,2,1,0:T(8,128)} custom-call(f32[1,16,8,256]{3,2,1,0:T(8,128)} %broadcast_in_dim.9.blk_ref), custom_call_target="tpu_custom_call" | custom-call | tf_op jit(solution)/shard_map/pallas_call | solution.py:94
  99.3 3.0 %pad_maximum_fusion.2.ub_ref = f32[6,22,16,256]{3,2,1,0:T(8,128)} fusion(f32[6,22,4,256]{3,2,1,0:T(4,128)} %collective-permute-done.7, f32[6,22,8,256]{3,2,1,0:T(8,128)S(1)} %pad_maximum_fusion.3, f32[6,22,4,256]{3,2,1,0:T(4,128)} %collective-permute-done.6), kind=kLoop, calls=%fused_computation.18 | loop fusion | flops 1081344 | bytes 4325376 | tf_op jit(solution)/shard_map/concatenate | solution.py:202
  102.2 9.9 %shard_map.94 = (f32[3,16,8,256]{3,2,1,0:T(8,128)}, f32[16,8,256]{2,1,0:T(8,128)}) custom-call(f32[22,24,256]{2,1,0:T(8,128)} %bitcast.47, f32[6,22,16,256]{3,2,1,0:T(8,128)} %pad_maximum_fusion.2.ub_ref), custom_call_target="tpu_custom_call" | custom-call | tf_op jit(solution)/shard_map/pallas_call | solution.py:182
  112.2 1.3 %copy.46 = f32[16,8,256]{0,1,2:T(8,128)S(1)} copy(f32[16,8,256]{2,1,0:T(8,128)} %get-tuple-element.15) | data formatting | bytes 262144 | tf_op jit(solution)/shard_map/pallas_call | solution.py:182
  113.5 0.4 reshape.20
  113.9 14.5 %all_to_all.34 = f32[16,1,2048]{2,1,0:T(1,128)S(1)} all-to-all(f32[16,1,2048]{2,1,0:T(1,128)S(1)} %reshape.20), channel_id=1, replica_groups=mesh['gx'=16,'gy'=16] {'gy'}, dimensions={0} | all-to-all | bytes 262144 | tf_op jit(solution)/shard_map/all_to_all | solution.py:307
  128.3 0.9 reduce.1
  129.2 0.4 reshape.21
  129.6 0.9 copy.47
  130.5 1.0 copy.48
  (16 shorter events, 0.1 us)
Async XLA Ops:
  0.6 1.7 %copy-start.2 = (f32[32,32,256]{2,1,0:T(8,128)S(1)}, f32[32,32,256]{2,1,0:T(8,128)}, u32[]{:S(2)}) copy-start(f32[32,32,256]{2,1,0:T(8,128)} %param.6) | copy-start | bytes 3145732
  0.6 1.8 %copy-start.1 = (f32[32,32,256]{2,1,0:T(8,128)S(1)}, f32[32,32,256]{2,1,0:T(8,128)}, u32[]{:S(2)}) copy-start(f32[32,32,256]{2,1,0:T(8,128)} %param.7) | copy-start | bytes 3145732
  2.5 7.9 %copy-start.3 = (f32[3,16,8,256]{3,2,1,0:T(8,128)S(1)}, f32[3,16,8,256]{3,2,1,0:T(8,128)}, u32[]{:S(2)}) copy-start(f32[3,16,8,256]{3,2,1,0:T(8,128)} %param.10) | copy-start | bytes 1179652
  2.5 7.9 %copy-start.4 = (f32[3,16,8,256]{3,2,1,0:T(8,128)S(1)}, f32[3,16,8,256]{3,2,1,0:T(8,128)}, u32[]{:S(2)}) copy-start(f32[3,16,8,256]{3,2,1,0:T(8,128)} %param.9) | copy-start | bytes 1179652
  2.6 11.3 %collective-permute-start = (f32[3,4,32,256]{3,2,1,0:T(8,128)S(1)}, f32[3,4,32,256]{3,2,1,0:T(8,128)S(1)}, u32[]{:S(2)}, u32[]{:S(2)}) collective-permute-start(f32[3,4,32,256]{3,2,1,0:T(8,128)S(1)} %get-tuple-element.54), channel_id=1, source_target_pairs={{0,16},{16,32},{32,48},{48,64},{64,80},{80,96},{96,112},{112,128},... | collective-permute-start | bytes 1179656 | tf_op jit(solution)/shard_map/ppermute | solution.py:198
  4.6 11.0 %collective-permute-start.1 = (f32[3,4,32,256]{3,2,1,0:T(8,128)S(1)}, f32[3,4,32,256]{3,2,1,0:T(8,128)S(1)}, u32[]{:S(2)}, u32[]{:S(2)}) collective-permute-start(f32[3,4,32,256]{3,2,1,0:T(8,128)S(1)} %get-tuple-element.55), channel_id=1, source_target_pairs={{16,0},{32,16},{48,32},{64,48},{80,64},{96,80},{112,96},{128,112},... | collective-permute-start | bytes 1179656 | tf_op jit(solution)/shard_map/ppermute | solution.py:201
  16.2 21.8 %collective-permute-start.2 = (f32[3,40,4,256]{3,2,1,0:T(4,128)S(1)}, f32[3,40,4,256]{3,2,1,0:T(4,128)S(1)}, u32[]{:S(2)}, u32[]{:S(2)}) collective-permute-start(f32[3,40,4,256]{3,2,1,0:T(4,128)S(1)} %get-tuple-element.52), channel_id=1, source_target_pairs={{0,1},{1,2},{2,3},{3,4},{4,5},{5,6},{6,7},{7,8},{8,9},{9,10},{10,1... | collective-permute-start | bytes 1474568 | tf_op jit(solution)/shard_map/ppermute | solution.py:198
  20.1 18.0 %collective-permute-start.3 = (f32[3,40,4,256]{3,2,1,0:T(4,128)S(1)}, f32[3,40,4,256]{3,2,1,0:T(4,128)S(1)}, u32[]{:S(2)}, u32[]{:S(2)}) collective-permute-start(f32[3,40,4,256]{3,2,1,0:T(4,128)S(1)} %get-tuple-element.53), channel_id=1, source_target_pairs={{1,0},{2,1},{3,2},{4,3},{5,4},{6,5},{7,6},{8,7},{9,8},{10,9},{11,1... | collective-permute-start | bytes 1474568 | tf_op jit(solution)/shard_map/ppermute | solution.py:201
  21.4 16.5 %collective-permute-start.4 = (f32[6,3,8,256]{3,2,1,0:T(8,128)S(1)}, f32[6,3,8,256]{3,2,1,0:T(8,128)S(1)}, u32[]{:S(2)}, u32[]{:S(2)}) collective-permute-start(f32[6,3,8,256]{3,2,1,0:T(8,128)S(1)} %get-tuple-element.60), channel_id=1, source_target_pairs={{0,16},{16,32},{32,48},{48,64},{64,80},{80,96},{96,112},{112,128},... | collective-permute-start | bytes 442376 | tf_op jit(solution)/shard_map/ppermute | solution.py:198
  23.4 14.6 %collective-permute-start.5 = (f32[6,3,8,256]{3,2,1,0:T(8,128)S(1)}, f32[6,3,8,256]{3,2,1,0:T(8,128)S(1)}, u32[]{:S(2)}, u32[]{:S(2)}) collective-permute-start(f32[6,3,8,256]{3,2,1,0:T(8,128)S(1)} %get-tuple-element.61), channel_id=1, source_target_pairs={{16,0},{32,16},{48,32},{64,48},{80,64},{96,80},{112,96},{128,112},... | collective-permute-start | bytes 442376 | tf_op jit(solution)/shard_map/ppermute | solution.py:201
  56.5 5.1 %copy-start = (f32[32,32,256]{2,1,0:T(8,128)}, f32[32,32,256]{2,1,0:T(8,128)S(1)}, u32[]{:S(2)}) copy-start(f32[32,32,256]{2,1,0:T(8,128)S(1)} %get-tuple-element.37) | copy-start | bytes 3145732
  57.8 4.1 %copy-start.5 = (f32[256,128,1]{1,0,2:T(8,128)S(1)}, f32[256,128,1]{1,0,2:T(8,128)}, u32[]{:S(2)}) copy-start(f32[256,128,1]{1,0,2:T(8,128)} %constant.36) | copy-start | bytes 393220
  57.8 41.5 %collective-permute-start.6 = (f32[6,22,4,256]{3,2,1,0:T(4,128)}, f32[6,22,4,256]{3,2,1,0:T(4,128)}, u32[]{:S(2)}, u32[]{:S(2)}) collective-permute-start(f32[6,22,4,256]{3,2,1,0:T(4,128)} %get-tuple-element.58), channel_id=1, source_target_pairs={{0,1},{1,2},{2,3},{3,4},{4,5},{5,6},{6,7},{7,8},{8,9},{9,10},{10,1... | collective-permute-start | bytes 1622024 | tf_op jit(solution)/shard_map/ppermute | solution.py:198
  60.0 39.3 %collective-permute-start.7 = (f32[6,22,4,256]{3,2,1,0:T(4,128)}, f32[6,22,4,256]{3,2,1,0:T(4,128)}, u32[]{:S(2)}, u32[]{:S(2)}) collective-permute-start(f32[6,22,4,256]{3,2,1,0:T(4,128)} %get-tuple-element.59), channel_id=1, source_target_pairs={{1,0},{2,1},{3,2},{4,3},{5,4},{6,5},{7,6},{8,7},{9,8},{10,9},{11,1... | collective-permute-start | bytes 1622024 | tf_op jit(solution)/shard_map/ppermute | solution.py:201

commit v12 on v11

--- a/solution.py
+++ b/solution.py
@@ -122,7 +122,7 @@
         fc[7, i] = s_ref[i, pl.ds(zoff, nz), :]
         return carry
 
-    lax.fori_loop(0, nxe, align, 0)
+    lax.fori_loop(0, nxe, align, 0, unroll=2)
 
     def faces_row(i, carry):
         c = fc[7, i]
@@ -135,7 +135,7 @@
         fc[6, i] = diag + spring_term * c
         return carry
 
-    lax.fori_loop(1, nxe - 1, faces_row, 0)
+    lax.fori_loop(1, nxe - 1, faces_row, 0, unroll=2)
 
     def sweep(src, dst, weight, i):
         c, diag = fc[7, i], fc[6, i]
@@ -156,8 +156,8 @@
         sweep(u1, u2, second_weight, i)
         return carry
 
-    lax.fori_loop(1, nxe - 1, first, 0)
-    lax.fori_loop(2, nxe - 2, second, 0)
+    lax.fori_loop(1, nxe - 1, first, 0, unroll=2)
+    lax.fori_loop(2, nxe - 2, second, 0, unroll=2)
 
     def energy_row(i, carry):
         parts = []
@@ -172,7 +172,7 @@
         u1[0, i] = 0.25 * (parts[0] + parts[1] + parts[2])
         return carry
 
-    lax.fori_loop(m, m + bx, energy_row, 0)
+    lax.fori_loop(m, m + bx, energy_row, 0, unroll=2)
     energy_out[...] = u1[0, pl.ds(m, bx), pl.ds(lo, bz), :]
     disp_out[...] = u2[:, pl.ds(m, bx), pl.ds(lo, bz), :]
 

time: 132 us -> 129 us (0.977)
  Pallas kernels: 21.2 us -> 18.5 us
    pallas_call x1, Pallas kernels: 9.92 us -> 7.2 us  [mechanics(): pl.pallas_call(functools.partial(mech_kernel, zoff), out_shape=(jax.Shape...]
where the time goes in v12:
time: 129 us
  blocking collectives  35.8 us (28%)
  other arithmetic  25.3 us (20%)
  starting transfers between devices  24.3 us (19%)
  Pallas kernels  18.5 us (14%)
  waiting for transfers between devices  14 us (11%)
  local copies, waits for them, and re-layouts  9.39 us (7%)
    all_to_all x1, blocking collectives, on_device(): lax.all_to_all(coarse, 'gy', split_axis=1, concat_axis=2, tiled=True)  21.3 us
    all_to_all x1, blocking collectives, on_device(): lax.all_to_all(energy, 'gy', split_axis=2, concat_axis=1, tiled=True)  14.5 us
    ppermute x4, starting transfers between devices, padded_2(): lax.ppermute(lax.slice_in_dim(block, 0, width, axis=dim), axis, backward)  14.3 us
    sub x4, other arithmetic, advance(): chem = conc_pad - order_pad * order_pad * (3.0 - 2.0 * order_pad)  13.3 us
    ppermute x4, waiting for transfers between devices, padded_2(): lax.ppermute(lax.slice_in_dim(block, block.shape[dim] - width, None, axis...  12.3 us
    pallas_call x1, Pallas kernels, halo_exchange(): pl.pallas_call(functools.partial(halo_kernel, hx, nx, ny), out_shape=jax....  11.3 us
    ppermute x4, starting transfers between devices, padded_2(): lax.ppermute(lax.slice_in_dim(block, block.shape[dim] - width, None, axis...  10 us
    pallas_call x1, Pallas kernels, mechanics(): pl.pallas_call(functools.partial(mech_kernel, zoff), out_shape=(jax.Shape...  7.2 us
  transfers between devices with their start and end apart: 8, of which 3 were waited for; matrix products, arithmetic and copies ran while one was open for 4% of the time, Pallas kernels for 9%

profile of v12, /device:TPU:2, one launch (start us, length us, event | category | flops | bytes accessed | tf_op | source)
XLA Modules:
  0.0 128.8 jit_solution(16711090433364045075)
XLA Ops:
  0.7 1.6 %add_bitcast_fusion = f32[1,32,32,256]{3,2,1,0:T(8,128)S(1)} fusion(s32[32,32,256]{2,1,0:T(8,128)} %param.8), kind=kLoop, calls=%fused_computation.110 | loop fusion | flops 2097152 | bytes 2097152 | tf_op jit(solution)/shard_map/stack | solution.py:288
  2.3 0.2 copy-done.1
  2.5 0.1 pad_maximum_fusion.7
  2.6 2.1 %collective-permute-start = (f32[3,4,32,256]{3,2,1,0:T(8,128)S(1)}, f32[3,4,32,256]{3,2,1,0:T(8,128)S(1)}, u32[]{:S(2)}, u32[]{:S(2)}) collective-permute-start(f32[3,4,32,256]{3,2,1,0:T(8,128)S(1)} %get-tuple-element.54), channel_id=1, source_target_pairs={{0,16},{16,32},{32,48},{48,64},{64,80},{80,96},{96,112},{112,128},... | collective-permute-start | bytes 1179656 | tf_op jit(solution)/shard_map/ppermute | solution.py:198
  4.6 5.8 %collective-permute-start.1 = (f32[3,4,32,256]{3,2,1,0:T(8,128)S(1)}, f32[3,4,32,256]{3,2,1,0:T(8,128)S(1)}, u32[]{:S(2)}, u32[]{:S(2)}) collective-permute-start(f32[3,4,32,256]{3,2,1,0:T(8,128)S(1)} %get-tuple-element.55), channel_id=1, source_target_pairs={{16,0},{32,16},{48,32},{64,48},{80,64},{96,80},{112,96},{128,112},... | collective-permute-start | bytes 1179656 | tf_op jit(solution)/shard_map/ppermute | solution.py:201
  10.4 0.1 pad_maximum_fusion.4
  10.5 3.4 %collective-permute-done = f32[3,4,32,256]{3,2,1,0:T(8,128)S(1)} collective-permute-done((f32[3,4,32,256]{3,2,1,0:T(8,128)S(1)}, f32[3,4,32,256]{3,2,1,0:T(8,128)S(1)}, u32[]{:S(2)}, u32[]{:S(2)}) %collective-permute-start) | collective-permute-done | bytes 393248 | tf_op jit(solution)/shard_map/ppermute | solution.py:198
  13.9 1.8 %collective-permute-done.1 = f32[3,4,32,256]{3,2,1,0:T(8,128)S(1)} collective-permute-done((f32[3,4,32,256]{3,2,1,0:T(8,128)S(1)}, f32[3,4,32,256]{3,2,1,0:T(8,128)S(1)}, u32[]{:S(2)}, u32[]{:S(2)}) %collective-permute-start.1) | collective-permute-done | bytes 393248 | tf_op jit(solution)/shard_map/ppermute | solution.py:201
  15.7 0.4 pad_maximum_fusion.1
  16.1 0.2 fusion.64
  16.2 3.9 %collective-permute-start.2 = (f32[3,40,4,256]{3,2,1,0:T(4,128)S(1)}, f32[3,40,4,256]{3,2,1,0:T(4,128)S(1)}, u32[]{:S(2)}, u32[]{:S(2)}) collective-permute-start(f32[3,40,4,256]{3,2,1,0:T(4,128)S(1)} %get-tuple-element.52), channel_id=1, source_target_pairs={{0,1},{1,2},{2,3},{3,4},{4,5},{5,6},{6,7},{7,8},{8,9},{9,10},{10,1... | collective-permute-start | bytes 1474568 | tf_op jit(solution)/shard_map/ppermute | solution.py:198
  20.1 1.3 %collective-permute-start.3 = (f32[3,40,4,256]{3,2,1,0:T(4,128)S(1)}, f32[3,40,4,256]{3,2,1,0:T(4,128)S(1)}, u32[]{:S(2)}, u32[]{:S(2)}) collective-permute-start(f32[3,40,4,256]{3,2,1,0:T(4,128)S(1)} %get-tuple-element.53), channel_id=1, source_target_pairs={{1,0},{2,1},{3,2},{4,3},{5,4},{6,5},{7,6},{8,7},{9,8},{10,9},{11,1... | collective-permute-start | bytes 1474568 | tf_op jit(solution)/shard_map/ppermute | solution.py:201
  21.4 1.9 %collective-permute-start.4 = (f32[6,3,8,256]{3,2,1,0:T(8,128)S(1)}, f32[6,3,8,256]{3,2,1,0:T(8,128)S(1)}, u32[]{:S(2)}, u32[]{:S(2)}) collective-permute-start(f32[6,3,8,256]{3,2,1,0:T(8,128)S(1)} %get-tuple-element.60), channel_id=1, source_target_pairs={{0,16},{16,32},{32,48},{48,64},{64,80},{80,96},{96,112},{112,128},... | collective-permute-start | bytes 442376 | tf_op jit(solution)/shard_map/ppermute | solution.py:198
  23.4 5.8 %collective-permute-start.5 = (f32[6,3,8,256]{3,2,1,0:T(8,128)S(1)}, f32[6,3,8,256]{3,2,1,0:T(8,128)S(1)}, u32[]{:S(2)}, u32[]{:S(2)}) collective-permute-start(f32[6,3,8,256]{3,2,1,0:T(8,128)S(1)} %get-tuple-element.61), channel_id=1, source_target_pairs={{16,0},{32,16},{48,32},{64,48},{80,64},{96,80},{112,96},{128,112},... | collective-permute-start | bytes 442376 | tf_op jit(solution)/shard_map/ppermute | solution.py:201
  29.1 8.8 %collective-permute-done.4 = f32[6,3,8,256]{3,2,1,0:T(8,128)S(1)} collective-permute-done((f32[6,3,8,256]{3,2,1,0:T(8,128)S(1)}, f32[6,3,8,256]{3,2,1,0:T(8,128)S(1)}, u32[]{:S(2)}, u32[]{:S(2)}) %collective-permute-start.4) | collective-permute-done | bytes 147488 | tf_op jit(solution)/shard_map/ppermute | solution.py:198
  38.0 0.1 pad_maximum_fusion.3
  38.1 0.0 collective-permute-done.3
  38.1 0.9 pad_maximum_fusion
  39.0 0.3 slice_bitcast_fusion.1
  39.3 0.3 multiply_subtract_fusion
  39.6 4.5 %multiply_subtract_fusion.1 = (f32[38,38,256]{2,1,0:T(8,128)S(1)}, f32[38,38,256]{2,1,0:T(8,128)S(1)}, f32[38,38,256]{2,1,0:T(8,128)S(1)}) fusion(f32[40,40,256]{2,1,0:T(8,128)S(1)} %multiply_subtract_fusion, f32[40,40,256]{2,1,0:T(8,128)S(1)} %get-tuple-element.50, f32[40,40,256]{2,1,0:T(8,128)S(1)} %get-tuple-element.51, ...), kind=kLoop, calls=%fused_computation.43 | loop fusion | flops 13307904 | bytes 26390528 | tf_op jit(solution)/shard_map/sub | solution.py:216
  44.2 4.5 %multiply_subtract_fusion.2 = (f32[36,36,256]{2,1,0:T(8,128)S(1)}, f32[36,36,256]{2,1,0:T(8,128)S(1)}, f32[36,36,256]{2,1,0:T(8,128)S(1)}) fusion(f32[38,38,256]{2,1,0:T(8,128)S(1)} %get-tuple-element.46, f32[38,38,256]{2,1,0:T(8,128)S(1)} %get-tuple-element.47, f32[40,40,256]{2,1,0:T(8,128)S(1)} %get-tuple-element.51, f32[38,38,256]{2,1,0:T(8,128)S(1)} %get-tuple-element.48), kind=kLoop, calls=%fused_computation.64 | loop fusion | flops 11943936 | bytes 24788992 | tf_op jit(solution)/shard_map/sub | solution.py:216
  48.6 4.0 %multiply_subtract_fusion.3 = (f32[34,34,256]{2,1,0:T(8,128)S(1)}, f32[34,34,256]{2,1,0:T(8,128)S(1)}, f32[34,34,256]{2,1,0:T(8,128)S(1)}) fusion(f32[36,36,256]{2,1,0:T(8,128)S(1)} %get-tuple-element.43, f32[36,36,256]{2,1,0:T(8,128)S(1)} %get-tuple-element.44, f32[40,40,256]{2,1,0:T(8,128)S(1)} %get-tuple-element.51, f32[36,36,256]{2,1,0:T(8,128)S(1)} %get-tuple-element.45), kind=kLoop, calls=%fused_computation.85 | loop fusion | flops 10653696 | bytes 23212032 | tf_op jit(solution)/shard_map/sub | solution.py:216
  52.7 3.8 %fusion.56 = (f32[32,32,256]{2,1,0:T(8,128)S(1)}, f32[32,32,256]{2,1,0:T(8,128)}) fusion(f32[34,34,256]{2,1,0:T(8,128)S(1)} %get-tuple-element.41, f32[40,40,256]{2,1,0:T(8,128)S(1)} %get-tuple-element.51, f32[34,34,256]{2,1,0:T(8,128)S(1)} %get-tuple-element.40, f32[34,34,256]{2,1,0:T(8,128)S(1)} %get-tuple-element.42), kind=kLoop, calls=%fused_computation.102 | loop fusion | flops 7602176 | bytes 17465344 | tf_op jit(solution)/shard_map/add | solution.py:224
  56.5 1.3 %fusion.65 = (f32[6,22,4,256]{3,2,1,0:T(4,128)}, f32[6,22,4,256]{3,2,1,0:T(4,128)}) fusion(f32[6,22,8,256]{3,2,1,0:T(8,128)S(1)} %pad_maximum_fusion.3), kind=kLoop, calls=%fused_computation.118 | loop fusion | bytes 2162688 | tf_op jit(solution)/shard_map/slice | solution.py:199
  57.8 2.2 %collective-permute-start.6 = (f32[6,22,4,256]{3,2,1,0:T(4,128)}, f32[6,22,4,256]{3,2,1,0:T(4,128)}, u32[]{:S(2)}, u32[]{:S(2)}) collective-permute-start(f32[6,22,4,256]{3,2,1,0:T(4,128)} %get-tuple-element.58), channel_id=1, source_target_pairs={{0,1},{1,2},{2,3},{3,4},{4,5},{5,6},{6,7},{7,8},{8,9},{9,10},{10,1... | collective-permute-start | bytes 1622024 | tf_op jit(solution)/shard_map/ppermute | solution.py:198
  60.0 1.5 %collective-permute-start.7 = (f32[6,22,4,256]{3,2,1,0:T(4,128)}, f32[6,22,4,256]{3,2,1,0:T(4,128)}, u32[]{:S(2)}, u32[]{:S(2)}) collective-permute-start(f32[6,22,4,256]{3,2,1,0:T(4,128)} %get-tuple-element.59), channel_id=1, source_target_pairs={{1,0},{2,1},{3,2},{4,3},{5,4},{6,5},{7,6},{8,7},{9,8},{10,9},{11,1... | collective-permute-start | bytes 1622024 | tf_op jit(solution)/shard_map/ppermute | solution.py:201
  61.5 0.1 bitcast_reduce_fusion
  61.6 0.3 bitcast_reduce_fusion.1
  61.9 0.5 fusion.43
  62.4 0.5 copy.43
  62.9 0.4 reshape.18
  63.3 21.3 %all_to_all.33 = f32[16,1,2048]{2,1,0:T(1,128)S(1)} all-to-all(f32[16,1,2048]{2,1,0:T(1,128)S(1)} %reshape.18), channel_id=1, replica_groups=mesh['gx'=16,'gy'=16] {'gy'}, dimensions={0} | all-to-all | bytes 262144 | tf_op jit(solution)/shard_map/all_to_all | solution.py:303
  84.6 0.5 broadcast.141
  85.1 0.9 reduce
  86.0 0.4 reshape.19
  86.3 0.6 copy.45
  86.9 1.1 broadcast_in_dim.9.blk_ref
  88.0 11.3 %shard_map.93 = f32[1,22,24,256]{3,2,1,0:T(8,128)} custom-call(f32[1,16,8,256]{3,2,1,0:T(8,128)} %broadcast_in_dim.9.blk_ref), custom_call_target="tpu_custom_call" | custom-call | tf_op jit(solution)/shard_map/pallas_call | solution.py:94
  99.3 3.0 %pad_maximum_fusion.2.ub_ref = f32[6,22,16,256]{3,2,1,0:T(8,128)} fusion(f32[6,22,4,256]{3,2,1,0:T(4,128)} %collective-permute-done.7, f32[6,22,8,256]{3,2,1,0:T(8,128)S(1)} %pad_maximum_fusion.3, f32[6,22,4,256]{3,2,1,0:T(4,128)} %collective-permute-done.6), kind=kLoop, calls=%fused_computation.18 | loop fusion | flops 1081344 | bytes 4325376 | tf_op jit(solution)/shard_map/concatenate | solution.py:202
  102.2 7.2 %shard_map.94 = (f32[3,16,8,256]{3,2,1,0:T(8,128)}, f32[16,8,256]{2,1,0:T(8,128)}) custom-call(f32[22,24,256]{2,1,0:T(8,128)} %bitcast.47, f32[6,22,16,256]{3,2,1,0:T(8,128)} %pad_maximum_fusion.2.ub_ref), custom_call_target="tpu_custom_call" | custom-call | tf_op jit(solution)/shard_map/pallas_call | solution.py:182
  109.4 1.3 %copy.46 = f32[16,8,256]{0,1,2:T(8,128)S(1)} copy(f32[16,8,256]{2,1,0:T(8,128)} %get-tuple-element.15) | data formatting | bytes 262144 | tf_op jit(solution)/shard_map/pallas_call | solution.py:182
  110.8 0.4 reshape.20
  111.2 14.5 %all_to_all.34 = f32[16,1,2048]{2,1,0:T(1,128)S(1)} all-to-all(f32[16,1,2048]{2,1,0:T(1,128)S(1)} %reshape.20), channel_id=1, replica_groups=mesh['gx'=16,'gy'=16] {'gy'}, dimensions={0} | all-to-all | bytes 262144 | tf_op jit(solution)/shard_map/all_to_all | solution.py:307
  125.6 0.9 reduce.1
  126.5 0.4 reshape.21
  126.9 0.9 copy.47
  127.8 1.0 copy.48
  (16 shorter events, 0.1 us)
Async XLA Ops:
  0.6 1.7 %copy-start.2 = (f32[32,32,256]{2,1,0:T(8,128)S(1)}, f32[32,32,256]{2,1,0:T(8,128)}, u32[]{:S(2)}) copy-start(f32[32,32,256]{2,1,0:T(8,128)} %param.6) | copy-start | bytes 3145732
  0.6 1.8 %copy-start.1 = (f32[32,32,256]{2,1,0:T(8,128)S(1)}, f32[32,32,256]{2,1,0:T(8,128)}, u32[]{:S(2)}) copy-start(f32[32,32,256]{2,1,0:T(8,128)} %param.7) | copy-start | bytes 3145732
  2.5 7.9 %copy-start.3 = (f32[3,16,8,256]{3,2,1,0:T(8,128)S(1)}, f32[3,16,8,256]{3,2,1,0:T(8,128)}, u32[]{:S(2)}) copy-start(f32[3,16,8,256]{3,2,1,0:T(8,128)} %param.10) | copy-start | bytes 1179652
  2.5 7.9 %copy-start.4 = (f32[3,16,8,256]{3,2,1,0:T(8,128)S(1)}, f32[3,16,8,256]{3,2,1,0:T(8,128)}, u32[]{:S(2)}) copy-start(f32[3,16,8,256]{3,2,1,0:T(8,128)} %param.9) | copy-start | bytes 1179652
  2.6 11.3 %collective-permute-start = (f32[3,4,32,256]{3,2,1,0:T(8,128)S(1)}, f32[3,4,32,256]{3,2,1,0:T(8,128)S(1)}, u32[]{:S(2)}, u32[]{:S(2)}) collective-permute-start(f32[3,4,32,256]{3,2,1,0:T(8,128)S(1)} %get-tuple-element.54), channel_id=1, source_target_pairs={{0,16},{16,32},{32,48},{48,64},{64,80},{80,96},{96,112},{112,128},... | collective-permute-start | bytes 1179656 | tf_op jit(solution)/shard_map/ppermute | solution.py:198
  4.6 11.0 %collective-permute-start.1 = (f32[3,4,32,256]{3,2,1,0:T(8,128)S(1)}, f32[3,4,32,256]{3,2,1,0:T(8,128)S(1)}, u32[]{:S(2)}, u32[]{:S(2)}) collective-permute-start(f32[3,4,32,256]{3,2,1,0:T(8,128)S(1)} %get-tuple-element.55), channel_id=1, source_target_pairs={{16,0},{32,16},{48,32},{64,48},{80,64},{96,80},{112,96},{128,112},... | collective-permute-start | bytes 1179656 | tf_op jit(solution)/shard_map/ppermute | solution.py:201
  16.2 21.8 %collective-permute-start.2 = (f32[3,40,4,256]{3,2,1,0:T(4,128)S(1)}, f32[3,40,4,256]{3,2,1,0:T(4,128)S(1)}, u32[]{:S(2)}, u32[]{:S(2)}) collective-permute-start(f32[3,40,4,256]{3,2,1,0:T(4,128)S(1)} %get-tuple-element.52), channel_id=1, source_target_pairs={{0,1},{1,2},{2,3},{3,4},{4,5},{5,6},{6,7},{7,8},{8,9},{9,10},{10,1... | collective-permute-start | bytes 1474568 | tf_op jit(solution)/shard_map/ppermute | solution.py:198
  20.1 18.0 %collective-permute-start.3 = (f32[3,40,4,256]{3,2,1,0:T(4,128)S(1)}, f32[3,40,4,256]{3,2,1,0:T(4,128)S(1)}, u32[]{:S(2)}, u32[]{:S(2)}) collective-permute-start(f32[3,40,4,256]{3,2,1,0:T(4,128)S(1)} %get-tuple-element.53), channel_id=1, source_target_pairs={{1,0},{2,1},{3,2},{4,3},{5,4},{6,5},{7,6},{8,7},{9,8},{10,9},{11,1... | collective-permute-start | bytes 1474568 | tf_op jit(solution)/shard_map/ppermute | solution.py:201
  21.4 16.5 %collective-permute-start.4 = (f32[6,3,8,256]{3,2,1,0:T(8,128)S(1)}, f32[6,3,8,256]{3,2,1,0:T(8,128)S(1)}, u32[]{:S(2)}, u32[]{:S(2)}) collective-permute-start(f32[6,3,8,256]{3,2,1,0:T(8,128)S(1)} %get-tuple-element.60), channel_id=1, source_target_pairs={{0,16},{16,32},{32,48},{48,64},{64,80},{80,96},{96,112},{112,128},... | collective-permute-start | bytes 442376 | tf_op jit(solution)/shard_map/ppermute | solution.py:198
  23.4 14.6 %collective-permute-start.5 = (f32[6,3,8,256]{3,2,1,0:T(8,128)S(1)}, f32[6,3,8,256]{3,2,1,0:T(8,128)S(1)}, u32[]{:S(2)}, u32[]{:S(2)}) collective-permute-start(f32[6,3,8,256]{3,2,1,0:T(8,128)S(1)} %get-tuple-element.61), channel_id=1, source_target_pairs={{16,0},{32,16},{48,32},{64,48},{80,64},{96,80},{112,96},{128,112},... | collective-permute-start | bytes 442376 | tf_op jit(solution)/shard_map/ppermute | solution.py:201
  56.5 5.1 %copy-start = (f32[32,32,256]{2,1,0:T(8,128)}, f32[32,32,256]{2,1,0:T(8,128)S(1)}, u32[]{:S(2)}) copy-start(f32[32,32,256]{2,1,0:T(8,128)S(1)} %get-tuple-element.37) | copy-start | bytes 3145732
  57.8 4.1 %copy-start.5 = (f32[256,128,1]{1,0,2:T(8,128)S(1)}, f32[256,128,1]{1,0,2:T(8,128)}, u32[]{:S(2)}) copy-start(f32[256,128,1]{1,0,2:T(8,128)} %constant.36) | copy-start | bytes 393220
  57.8 41.5 %collective-permute-start.6 = (f32[6,22,4,256]{3,2,1,0:T(4,128)}, f32[6,22,4,256]{3,2,1,0:T(4,128)}, u32[]{:S(2)}, u32[]{:S(2)}) collective-permute-start(f32[6,22,4,256]{3,2,1,0:T(4,128)} %get-tuple-element.58), channel_id=1, source_target_pairs={{0,1},{1,2},{2,3},{3,4},{4,5},{5,6},{6,7},{7,8},{8,9},{9,10},{10,1... | collective-permute-start | bytes 1622024 | tf_op jit(solution)/shard_map/ppermute | solution.py:198
  60.0 39.3 %collective-permute-start.7 = (f32[6,22,4,256]{3,2,1,0:T(4,128)}, f32[6,22,4,256]{3,2,1,0:T(4,128)}, u32[]{:S(2)}, u32[]{:S(2)}) collective-permute-start(f32[6,22,4,256]{3,2,1,0:T(4,128)} %get-tuple-element.59), channel_id=1, source_target_pairs={{1,0},{2,1},{3,2},{4,3},{5,4},{6,5},{7,6},{8,7},{9,8},{10,9},{11,1... | collective-permute-start | bytes 1622024 | tf_op jit(solution)/shard_map/ppermute | solution.py:201

commit v13 on v12

--- a/solution.py
+++ b/solution.py
@@ -122,7 +122,7 @@
         fc[7, i] = s_ref[i, pl.ds(zoff, nz), :]
         return carry
 
-    lax.fori_loop(0, nxe, align, 0, unroll=2)
+    lax.fori_loop(0, nxe, align, 0, unroll=4)
 
     def faces_row(i, carry):
         c = fc[7, i]
@@ -135,7 +135,7 @@
         fc[6, i] = diag + spring_term * c
         return carry
 
-    lax.fori_loop(1, nxe - 1, faces_row, 0, unroll=2)
+    lax.fori_loop(1, nxe - 1, faces_row, 0, unroll=4)
 
     def sweep(src, dst, weight, i):
         c, diag = fc[7, i], fc[6, i]
@@ -156,8 +156,8 @@
         sweep(u1, u2, second_weight, i)
         return carry
 
-    lax.fori_loop(1, nxe - 1, first, 0, unroll=2)
-    lax.fori_loop(2, nxe - 2, second, 0, unroll=2)
+    lax.fori_loop(1, nxe - 1, first, 0, unroll=4)
+    lax.fori_loop(2, nxe - 2, second, 0, unroll=4)
 
     def energy_row(i, carry):
         parts = []
@@ -172,7 +172,7 @@
         u1[0, i] = 0.25 * (parts[0] + parts[1] + parts[2])
         return carry
 
-    lax.fori_loop(m, m + bx, energy_row, 0, unroll=2)
+    lax.fori_loop(m, m + bx, energy_row, 0, unroll=4)
     energy_out[...] = u1[0, pl.ds(m, bx), pl.ds(lo, bz), :]
     disp_out[...] = u2[:, pl.ds(m, bx), pl.ds(lo, bz), :]
 

time: 129 us -> 128 us (level)
  no operation moved by 1% of the time
where the time goes in v13:
time: 128 us
  blocking collectives  35.8 us (28%)
  other arithmetic  25.3 us (20%)
  starting transfers between devices  24.3 us (19%)
  Pallas kernels  17.4 us (14%)
  waiting for transfers between devices  14 us (11%)
  local copies, waits for them, and re-layouts  9.39 us (7%)
    all_to_all x1, blocking collectives, on_device(): lax.all_to_all(coarse, 'gy', split_axis=1, concat_axis=2, tiled=True)  21.3 us
    all_to_all x1, blocking collectives, on_device(): lax.all_to_all(energy, 'gy', split_axis=2, concat_axis=1, tiled=True)  14.5 us
    ppermute x4, starting transfers between devices, padded_2(): lax.ppermute(lax.slice_in_dim(block, 0, width, axis=dim), axis, backward)  14.3 us
    sub x4, other arithmetic, advance(): chem = conc_pad - order_pad * order_pad * (3.0 - 2.0 * order_pad)  13.3 us
    ppermute x4, waiting for transfers between devices, padded_2(): lax.ppermute(lax.slice_in_dim(block, block.shape[dim] - width, None, axis...  12.3 us
    pallas_call x1, Pallas kernels, halo_exchange(): pl.pallas_call(functools.partial(halo_kernel, hx, nx, ny), out_shape=jax....  11.3 us
    ppermute x4, starting transfers between devices, padded_2(): lax.ppermute(lax.slice_in_dim(block, block.shape[dim] - width, None, axis...  10 us
    pallas_call x1, Pallas kernels, mechanics(): pl.pallas_call(functools.partial(mech_kernel, zoff), out_shape=(jax.Shape...  6.1 us
  transfers between devices with their start and end apart: 8, of which 3 were waited for; matrix products, arithmetic and copies ran while one was open for 4% of the time, Pallas kernels for 9%

profile of v13, /device:TPU:2, one launch (start us, length us, event | category | flops | bytes accessed | tf_op | source)
XLA Modules:
  0.0 127.7 jit_solution(13733536338847186415)
XLA Ops:
  0.7 1.6 %add_bitcast_fusion = f32[1,32,32,256]{3,2,1,0:T(8,128)S(1)} fusion(s32[32,32,256]{2,1,0:T(8,128)} %param.8), kind=kLoop, calls=%fused_computation.110 | loop fusion | flops 2097152 | bytes 2097152 | tf_op jit(solution)/shard_map/stack | solution.py:288
  2.3 0.2 copy-done.1
  2.5 0.1 pad_maximum_fusion.7
  2.6 2.1 %collective-permute-start = (f32[3,4,32,256]{3,2,1,0:T(8,128)S(1)}, f32[3,4,32,256]{3,2,1,0:T(8,128)S(1)}, u32[]{:S(2)}, u32[]{:S(2)}) collective-permute-start(f32[3,4,32,256]{3,2,1,0:T(8,128)S(1)} %get-tuple-element.54), channel_id=1, source_target_pairs={{0,16},{16,32},{32,48},{48,64},{64,80},{80,96},{96,112},{112,128},... | collective-permute-start | bytes 1179656 | tf_op jit(solution)/shard_map/ppermute | solution.py:198
  4.6 5.8 %collective-permute-start.1 = (f32[3,4,32,256]{3,2,1,0:T(8,128)S(1)}, f32[3,4,32,256]{3,2,1,0:T(8,128)S(1)}, u32[]{:S(2)}, u32[]{:S(2)}) collective-permute-start(f32[3,4,32,256]{3,2,1,0:T(8,128)S(1)} %get-tuple-element.55), channel_id=1, source_target_pairs={{16,0},{32,16},{48,32},{64,48},{80,64},{96,80},{112,96},{128,112},... | collective-permute-start | bytes 1179656 | tf_op jit(solution)/shard_map/ppermute | solution.py:201
  10.4 0.1 pad_maximum_fusion.4
  10.5 3.4 %collective-permute-done = f32[3,4,32,256]{3,2,1,0:T(8,128)S(1)} collective-permute-done((f32[3,4,32,256]{3,2,1,0:T(8,128)S(1)}, f32[3,4,32,256]{3,2,1,0:T(8,128)S(1)}, u32[]{:S(2)}, u32[]{:S(2)}) %collective-permute-start) | collective-permute-done | bytes 393248 | tf_op jit(solution)/shard_map/ppermute | solution.py:198
  13.9 1.8 %collective-permute-done.1 = f32[3,4,32,256]{3,2,1,0:T(8,128)S(1)} collective-permute-done((f32[3,4,32,256]{3,2,1,0:T(8,128)S(1)}, f32[3,4,32,256]{3,2,1,0:T(8,128)S(1)}, u32[]{:S(2)}, u32[]{:S(2)}) %collective-permute-start.1) | collective-permute-done | bytes 393248 | tf_op jit(solution)/shard_map/ppermute | solution.py:201
  15.7 0.4 pad_maximum_fusion.1
  16.1 0.2 fusion.64
  16.2 3.9 %collective-permute-start.2 = (f32[3,40,4,256]{3,2,1,0:T(4,128)S(1)}, f32[3,40,4,256]{3,2,1,0:T(4,128)S(1)}, u32[]{:S(2)}, u32[]{:S(2)}) collective-permute-start(f32[3,40,4,256]{3,2,1,0:T(4,128)S(1)} %get-tuple-element.52), channel_id=1, source_target_pairs={{0,1},{1,2},{2,3},{3,4},{4,5},{5,6},{6,7},{7,8},{8,9},{9,10},{10,1... | collective-permute-start | bytes 1474568 | tf_op jit(solution)/shard_map/ppermute | solution.py:198
  20.1 1.3 %collective-permute-start.3 = (f32[3,40,4,256]{3,2,1,0:T(4,128)S(1)}, f32[3,40,4,256]{3,2,1,0:T(4,128)S(1)}, u32[]{:S(2)}, u32[]{:S(2)}) collective-permute-start(f32[3,40,4,256]{3,2,1,0:T(4,128)S(1)} %get-tuple-element.53), channel_id=1, source_target_pairs={{1,0},{2,1},{3,2},{4,3},{5,4},{6,5},{7,6},{8,7},{9,8},{10,9},{11,1... | collective-permute-start | bytes 1474568 | tf_op jit(solution)/shard_map/ppermute | solution.py:201
  21.4 1.9 %collective-permute-start.4 = (f32[6,3,8,256]{3,2,1,0:T(8,128)S(1)}, f32[6,3,8,256]{3,2,1,0:T(8,128)S(1)}, u32[]{:S(2)}, u32[]{:S(2)}) collective-permute-start(f32[6,3,8,256]{3,2,1,0:T(8,128)S(1)} %get-tuple-element.60), channel_id=1, source_target_pairs={{0,16},{16,32},{32,48},{48,64},{64,80},{80,96},{96,112},{112,128},... | collective-permute-start | bytes 442376 | tf_op jit(solution)/shard_map/ppermute | solution.py:198
  23.4 5.8 %collective-permute-start.5 = (f32[6,3,8,256]{3,2,1,0:T(8,128)S(1)}, f32[6,3,8,256]{3,2,1,0:T(8,128)S(1)}, u32[]{:S(2)}, u32[]{:S(2)}) collective-permute-start(f32[6,3,8,256]{3,2,1,0:T(8,128)S(1)} %get-tuple-element.61), channel_id=1, source_target_pairs={{16,0},{32,16},{48,32},{64,48},{80,64},{96,80},{112,96},{128,112},... | collective-permute-start | bytes 442376 | tf_op jit(solution)/shard_map/ppermute | solution.py:201
  29.1 8.8 %collective-permute-done.4 = f32[6,3,8,256]{3,2,1,0:T(8,128)S(1)} collective-permute-done((f32[6,3,8,256]{3,2,1,0:T(8,128)S(1)}, f32[6,3,8,256]{3,2,1,0:T(8,128)S(1)}, u32[]{:S(2)}, u32[]{:S(2)}) %collective-permute-start.4) | collective-permute-done | bytes 147488 | tf_op jit(solution)/shard_map/ppermute | solution.py:198
  38.0 0.1 pad_maximum_fusion.3
  38.1 0.0 collective-permute-done.3
  38.1 0.9 pad_maximum_fusion
  39.0 0.3 slice_bitcast_fusion.1
  39.3 0.3 multiply_subtract_fusion
  39.6 4.5 %multiply_subtract_fusion.1 = (f32[38,38,256]{2,1,0:T(8,128)S(1)}, f32[38,38,256]{2,1,0:T(8,128)S(1)}, f32[38,38,256]{2,1,0:T(8,128)S(1)}) fusion(f32[40,40,256]{2,1,0:T(8,128)S(1)} %multiply_subtract_fusion, f32[40,40,256]{2,1,0:T(8,128)S(1)} %get-tuple-element.50, f32[40,40,256]{2,1,0:T(8,128)S(1)} %get-tuple-element.51, ...), kind=kLoop, calls=%fused_computation.43 | loop fusion | flops 13307904 | bytes 26390528 | tf_op jit(solution)/shard_map/sub | solution.py:216
  44.2 4.5 %multiply_subtract_fusion.2 = (f32[36,36,256]{2,1,0:T(8,128)S(1)}, f32[36,36,256]{2,1,0:T(8,128)S(1)}, f32[36,36,256]{2,1,0:T(8,128)S(1)}) fusion(f32[38,38,256]{2,1,0:T(8,128)S(1)} %get-tuple-element.46, f32[38,38,256]{2,1,0:T(8,128)S(1)} %get-tuple-element.47, f32[40,40,256]{2,1,0:T(8,128)S(1)} %get-tuple-element.51, f32[38,38,256]{2,1,0:T(8,128)S(1)} %get-tuple-element.48), kind=kLoop, calls=%fused_computation.64 | loop fusion | flops 11943936 | bytes 24788992 | tf_op jit(solution)/shard_map/sub | solution.py:216
  48.6 4.0 %multiply_subtract_fusion.3 = (f32[34,34,256]{2,1,0:T(8,128)S(1)}, f32[34,34,256]{2,1,0:T(8,128)S(1)}, f32[34,34,256]{2,1,0:T(8,128)S(1)}) fusion(f32[36,36,256]{2,1,0:T(8,128)S(1)} %get-tuple-element.43, f32[36,36,256]{2,1,0:T(8,128)S(1)} %get-tuple-element.44, f32[40,40,256]{2,1,0:T(8,128)S(1)} %get-tuple-element.51, f32[36,36,256]{2,1,0:T(8,128)S(1)} %get-tuple-element.45), kind=kLoop, calls=%fused_computation.85 | loop fusion | flops 10653696 | bytes 23212032 | tf_op jit(solution)/shard_map/sub | solution.py:216
  52.7 3.8 %fusion.56 = (f32[32,32,256]{2,1,0:T(8,128)S(1)}, f32[32,32,256]{2,1,0:T(8,128)}) fusion(f32[34,34,256]{2,1,0:T(8,128)S(1)} %get-tuple-element.41, f32[40,40,256]{2,1,0:T(8,128)S(1)} %get-tuple-element.51, f32[34,34,256]{2,1,0:T(8,128)S(1)} %get-tuple-element.40, f32[34,34,256]{2,1,0:T(8,128)S(1)} %get-tuple-element.42), kind=kLoop, calls=%fused_computation.102 | loop fusion | flops 7602176 | bytes 17465344 | tf_op jit(solution)/shard_map/add | solution.py:224
  56.5 1.3 %fusion.65 = (f32[6,22,4,256]{3,2,1,0:T(4,128)}, f32[6,22,4,256]{3,2,1,0:T(4,128)}) fusion(f32[6,22,8,256]{3,2,1,0:T(8,128)S(1)} %pad_maximum_fusion.3), kind=kLoop, calls=%fused_computation.118 | loop fusion | bytes 2162688 | tf_op jit(solution)/shard_map/slice | solution.py:199
  57.8 2.2 %collective-permute-start.6 = (f32[6,22,4,256]{3,2,1,0:T(4,128)}, f32[6,22,4,256]{3,2,1,0:T(4,128)}, u32[]{:S(2)}, u32[]{:S(2)}) collective-permute-start(f32[6,22,4,256]{3,2,1,0:T(4,128)} %get-tuple-element.58), channel_id=1, source_target_pairs={{0,1},{1,2},{2,3},{3,4},{4,5},{5,6},{6,7},{7,8},{8,9},{9,10},{10,1... | collective-permute-start | bytes 1622024 | tf_op jit(solution)/shard_map/ppermute | solution.py:198
  60.0 1.5 %collective-permute-start.7 = (f32[6,22,4,256]{3,2,1,0:T(4,128)}, f32[6,22,4,256]{3,2,1,0:T(4,128)}, u32[]{:S(2)}, u32[]{:S(2)}) collective-permute-start(f32[6,22,4,256]{3,2,1,0:T(4,128)} %get-tuple-element.59), channel_id=1, source_target_pairs={{1,0},{2,1},{3,2},{4,3},{5,4},{6,5},{7,6},{8,7},{9,8},{10,9},{11,1... | collective-permute-start | bytes 1622024 | tf_op jit(solution)/shard_map/ppermute | solution.py:201
  61.5 0.1 bitcast_reduce_fusion
  61.6 0.3 bitcast_reduce_fusion.1
  61.9 0.5 fusion.43
  62.4 0.5 copy.43
  62.9 0.4 reshape.18
  63.3 21.3 %all_to_all.33 = f32[16,1,2048]{2,1,0:T(1,128)S(1)} all-to-all(f32[16,1,2048]{2,1,0:T(1,128)S(1)} %reshape.18), channel_id=1, replica_groups=mesh['gx'=16,'gy'=16] {'gy'}, dimensions={0} | all-to-all | bytes 262144 | tf_op jit(solution)/shard_map/all_to_all | solution.py:303
  84.6 0.5 broadcast.141
  85.1 0.9 reduce
  86.0 0.4 reshape.19
  86.3 0.6 copy.45
  86.9 1.1 broadcast_in_dim.9.blk_ref
  88.0 11.3 %shard_map.93 = f32[1,22,24,256]{3,2,1,0:T(8,128)} custom-call(f32[1,16,8,256]{3,2,1,0:T(8,128)} %broadcast_in_dim.9.blk_ref), custom_call_target="tpu_custom_call" | custom-call | tf_op jit(solution)/shard_map/pallas_call | solution.py:94
  99.3 3.0 %pad_maximum_fusion.2.ub_ref = f32[6,22,16,256]{3,2,1,0:T(8,128)} fusion(f32[6,22,4,256]{3,2,1,0:T(4,128)} %collective-permute-done.7, f32[6,22,8,256]{3,2,1,0:T(8,128)S(1)} %pad_maximum_fusion.3, f32[6,22,4,256]{3,2,1,0:T(4,128)} %collective-permute-done.6), kind=kLoop, calls=%fused_computation.18 | loop fusion | flops 1081344 | bytes 4325376 | tf_op jit(solution)/shard_map/concatenate | solution.py:202
  102.2 6.1 %shard_map.94 = (f32[3,16,8,256]{3,2,1,0:T(8,128)}, f32[16,8,256]{2,1,0:T(8,128)}) custom-call(f32[22,24,256]{2,1,0:T(8,128)} %bitcast.47, f32[6,22,16,256]{3,2,1,0:T(8,128)} %pad_maximum_fusion.2.ub_ref), custom_call_target="tpu_custom_call" | custom-call | tf_op jit(solution)/shard_map/pallas_call | solution.py:182
  108.3 1.3 %copy.46 = f32[16,8,256]{0,1,2:T(8,128)S(1)} copy(f32[16,8,256]{2,1,0:T(8,128)} %get-tuple-element.15) | data formatting | bytes 262144 | tf_op jit(solution)/shard_map/pallas_call | solution.py:182
  109.7 0.4 reshape.20
  110.1 14.5 %all_to_all.34 = f32[16,1,2048]{2,1,0:T(1,128)S(1)} all-to-all(f32[16,1,2048]{2,1,0:T(1,128)S(1)} %reshape.20), channel_id=1, replica_groups=mesh['gx'=16,'gy'=16] {'gy'}, dimensions={0} | all-to-all | bytes 262144 | tf_op jit(solution)/shard_map/all_to_all | solution.py:307
  124.5 0.9 reduce.1
  125.4 0.4 reshape.21
  125.8 0.9 copy.47
  126.7 1.0 copy.48
  (16 shorter events, 0.1 us)
Async XLA Ops:
  0.6 1.7 %copy-start.2 = (f32[32,32,256]{2,1,0:T(8,128)S(1)}, f32[32,32,256]{2,1,0:T(8,128)}, u32[]{:S(2)}) copy-start(f32[32,32,256]{2,1,0:T(8,128)} %param.6) | copy-start | bytes 3145732
  0.6 1.8 %copy-start.1 = (f32[32,32,256]{2,1,0:T(8,128)S(1)}, f32[32,32,256]{2,1,0:T(8,128)}, u32[]{:S(2)}) copy-start(f32[32,32,256]{2,1,0:T(8,128)} %param.7) | copy-start | bytes 3145732
  2.5 7.9 %copy-start.3 = (f32[3,16,8,256]{3,2,1,0:T(8,128)S(1)}, f32[3,16,8,256]{3,2,1,0:T(8,128)}, u32[]{:S(2)}) copy-start(f32[3,16,8,256]{3,2,1,0:T(8,128)} %param.10) | copy-start | bytes 1179652
  2.5 7.9 %copy-start.4 = (f32[3,16,8,256]{3,2,1,0:T(8,128)S(1)}, f32[3,16,8,256]{3,2,1,0:T(8,128)}, u32[]{:S(2)}) copy-start(f32[3,16,8,256]{3,2,1,0:T(8,128)} %param.9) | copy-start | bytes 1179652
  2.6 11.3 %collective-permute-start = (f32[3,4,32,256]{3,2,1,0:T(8,128)S(1)}, f32[3,4,32,256]{3,2,1,0:T(8,128)S(1)}, u32[]{:S(2)}, u32[]{:S(2)}) collective-permute-start(f32[3,4,32,256]{3,2,1,0:T(8,128)S(1)} %get-tuple-element.54), channel_id=1, source_target_pairs={{0,16},{16,32},{32,48},{48,64},{64,80},{80,96},{96,112},{112,128},... | collective-permute-start | bytes 1179656 | tf_op jit(solution)/shard_map/ppermute | solution.py:198
  4.6 11.0 %collective-permute-start.1 = (f32[3,4,32,256]{3,2,1,0:T(8,128)S(1)}, f32[3,4,32,256]{3,2,1,0:T(8,128)S(1)}, u32[]{:S(2)}, u32[]{:S(2)}) collective-permute-start(f32[3,4,32,256]{3,2,1,0:T(8,128)S(1)} %get-tuple-element.55), channel_id=1, source_target_pairs={{16,0},{32,16},{48,32},{64,48},{80,64},{96,80},{112,96},{128,112},... | collective-permute-start | bytes 1179656 | tf_op jit(solution)/shard_map/ppermute | solution.py:201
  16.2 21.8 %collective-permute-start.2 = (f32[3,40,4,256]{3,2,1,0:T(4,128)S(1)}, f32[3,40,4,256]{3,2,1,0:T(4,128)S(1)}, u32[]{:S(2)}, u32[]{:S(2)}) collective-permute-start(f32[3,40,4,256]{3,2,1,0:T(4,128)S(1)} %get-tuple-element.52), channel_id=1, source_target_pairs={{0,1},{1,2},{2,3},{3,4},{4,5},{5,6},{6,7},{7,8},{8,9},{9,10},{10,1... | collective-permute-start | bytes 1474568 | tf_op jit(solution)/shard_map/ppermute | solution.py:198
  20.1 18.0 %collective-permute-start.3 = (f32[3,40,4,256]{3,2,1,0:T(4,128)S(1)}, f32[3,40,4,256]{3,2,1,0:T(4,128)S(1)}, u32[]{:S(2)}, u32[]{:S(2)}) collective-permute-start(f32[3,40,4,256]{3,2,1,0:T(4,128)S(1)} %get-tuple-element.53), channel_id=1, source_target_pairs={{1,0},{2,1},{3,2},{4,3},{5,4},{6,5},{7,6},{8,7},{9,8},{10,9},{11,1... | collective-permute-start | bytes 1474568 | tf_op jit(solution)/shard_map/ppermute | solution.py:201
  21.4 16.5 %collective-permute-start.4 = (f32[6,3,8,256]{3,2,1,0:T(8,128)S(1)}, f32[6,3,8,256]{3,2,1,0:T(8,128)S(1)}, u32[]{:S(2)}, u32[]{:S(2)}) collective-permute-start(f32[6,3,8,256]{3,2,1,0:T(8,128)S(1)} %get-tuple-element.60), channel_id=1, source_target_pairs={{0,16},{16,32},{32,48},{48,64},{64,80},{80,96},{96,112},{112,128},... | collective-permute-start | bytes 442376 | tf_op jit(solution)/shard_map/ppermute | solution.py:198
  23.4 14.6 %collective-permute-start.5 = (f32[6,3,8,256]{3,2,1,0:T(8,128)S(1)}, f32[6,3,8,256]{3,2,1,0:T(8,128)S(1)}, u32[]{:S(2)}, u32[]{:S(2)}) collective-permute-start(f32[6,3,8,256]{3,2,1,0:T(8,128)S(1)} %get-tuple-element.61), channel_id=1, source_target_pairs={{16,0},{32,16},{48,32},{64,48},{80,64},{96,80},{112,96},{128,112},... | collective-permute-start | bytes 442376 | tf_op jit(solution)/shard_map/ppermute | solution.py:201
  56.5 5.1 %copy-start = (f32[32,32,256]{2,1,0:T(8,128)}, f32[32,32,256]{2,1,0:T(8,128)S(1)}, u32[]{:S(2)}) copy-start(f32[32,32,256]{2,1,0:T(8,128)S(1)} %get-tuple-element.37) | copy-start | bytes 3145732
  57.8 4.1 %copy-start.5 = (f32[256,128,1]{1,0,2:T(8,128)S(1)}, f32[256,128,1]{1,0,2:T(8,128)}, u32[]{:S(2)}) copy-start(f32[256,128,1]{1,0,2:T(8,128)} %constant.36) | copy-start | bytes 393220
  57.8 41.5 %collective-permute-start.6 = (f32[6,22,4,256]{3,2,1,0:T(4,128)}, f32[6,22,4,256]{3,2,1,0:T(4,128)}, u32[]{:S(2)}, u32[]{:S(2)}) collective-permute-start(f32[6,22,4,256]{3,2,1,0:T(4,128)} %get-tuple-element.58), channel_id=1, source_target_pairs={{0,1},{1,2},{2,3},{3,4},{4,5},{5,6},{6,7},{7,8},{8,9},{9,10},{10,1... | collective-permute-start | bytes 1622024 | tf_op jit(solution)/shard_map/ppermute | solution.py:198
  60.0 39.3 %collective-permute-start.7 = (f32[6,22,4,256]{3,2,1,0:T(4,128)}, f32[6,22,4,256]{3,2,1,0:T(4,128)}, u32[]{:S(2)}, u32[]{:S(2)}) collective-permute-start(f32[6,22,4,256]{3,2,1,0:T(4,128)} %get-tuple-element.59), channel_id=1, source_target_pairs={{1,0},{2,1},{3,2},{4,3},{5,4},{6,5},{7,6},{8,7},{9,8},{10,9},{11,1... | collective-permute-start | bytes 1622024 | tf_op jit(solution)/shard_map/ppermute | solution.py:201

commit v14 on v13

--- a/solution.py
+++ b/solution.py
@@ -112,14 +112,16 @@
             jnp.where(lane == last, 0.0, pltpu.roll(v, last, 1)), jnp.where(lane == 0, 0.0, pltpu.roll(v, 1, 1)))
 
 
-def mech_kernel(zoff, s_ref, ub_ref, disp_out, energy_out, u1, u2, fc):
+def mech_kernel(zoff, ext_ref, disp_out, energy_out, u1, u2, fc, ub_ref):
     _, nxe, nz, _ = ub_ref.shape
     bx, bz = disp_out.shape[1], disp_out.shape[2]
     m = (nxe - bx) // 2
     lo = (nz - bz) // 2
 
     def align(i, carry):
-        fc[7, i] = s_ref[i, pl.ds(zoff, nz), :]
+        fc[7, i] = ext_ref[0, i, pl.ds(zoff, nz), :]
+        for k in range(6):
+            ub_ref[k, i] = ext_ref[1 + k, i, pl.ds(zoff, nz), :]
         return carry
 
     lax.fori_loop(0, nxe, align, 0, unroll=4)
@@ -177,17 +179,17 @@
     disp_out[...] = u2[:, pl.ds(m, bx), pl.ds(lo, bz), :]
 
 
-def mechanics(stiff_ext, ub, zoff, bx, bz):
-    _, nxe, nz, ny = ub.shape
+def mechanics(ext, zoff, nz, bx, bz):
+    _, nxe, _, ny = ext.shape
     return pl.pallas_call(
         functools.partial(mech_kernel, zoff),
         out_shape=(jax.ShapeDtypeStruct((3, bx, bz, ny), jnp.float32),
                    jax.ShapeDtypeStruct((bx, bz, ny), jnp.float32)),
-        in_specs=[pl.BlockSpec(memory_space=pltpu.VMEM)] * 2,
+        in_specs=[pl.BlockSpec(memory_space=pltpu.VMEM)],
         out_specs=(pl.BlockSpec(memory_space=pltpu.VMEM), pl.BlockSpec(memory_space=pltpu.VMEM)),
         scratch_shapes=[pltpu.VMEM((3, nxe, nz, ny), jnp.float32), pltpu.VMEM((3, nxe, nz, ny), jnp.float32),
-                        pltpu.VMEM((8, nxe, nz, ny), jnp.float32)],
-    )(stiff_ext, ub)
+                        pltpu.VMEM((8, nxe, nz, ny), jnp.float32), pltpu.VMEM((6, nxe, nz, ny), jnp.float32)],
+    )(ext)
 
 
 def padded_2(block, sides, width):
@@ -287,23 +289,17 @@
     h = FINE_HALO
     fields = jnp.stack([concentration, order_field, mobility_of(phase_labels)])
     m = MECH_HALO
-    fields = padded_2(fields, (("gx", 1),), h)
-    fields, ub = lax.optimization_barrier((fields, jnp.concatenate([displacement, body_load])))
-    ub = padded_2(ub, (("gx", 1),), m)
-    fields = padded_2(fields, (("gy", 2),), h)
+    fields = padded_2(fields, (("gx", 1), ("gy", 2)), h)
     conc, order, mob = fields[0], fields[1], fields[2]
     for step in range(STEPS):
         conc, order, mob = advance(conc, order, mob, step == STEPS - 1)
 
-    order, ub = lax.optimization_barrier((order, ub))
-    ub = padded_2(ub, (("gy", 2),), m + 1)
-    disp, load = ub[:3], ub[3:]
 
     coarse = restrict_xzy(order)
     stiff = lax.all_to_all(coarse, "gy", split_axis=1, concat_axis=2, tiled=True)
-    stiff_ext = halo_exchange(stiff[None], m, 0)[0]
+    ext = halo_exchange(jnp.concatenate([stiff[None], displacement, body_load]), m, 0)
     bx, bz = stiff.shape[0], stiff.shape[1]
-    disp, energy = mechanics(stiff_ext, ub, TILE - (m + 1), bx, bz)
+    disp, energy = mechanics(ext, TILE - (m + 1), bz + 2 * (m + 1), bx, bz)
     tiles = lax.all_to_all(energy, "gy", split_axis=2, concat_axis=1, tiled=True)
     return (conc, order, disp, jnp.transpose(tiles, (0, 2, 1)))
 

time: 128 us -> 151 us (1.18)
  Pallas kernels: 17.4 us -> 44.7 us
  blocking collectives: 35.8 us -> 19.7 us
  waiting for transfers between devices: 14 us -> 27 us
  starting transfers between devices: 24.3 us -> 16.3 us
  local copies, waits for them, and re-layouts: 9.39 us -> 16.6 us
    pallas_call x1, Pallas kernels: 11.3 us -> 38.1 us  [halo_exchange(): pl.pallas_call(functools.partial(halo_kernel, hx, nx, ny), out_shape=jax....]
    all_to_all x1 -> x0, blocking collectives: 14.5 us -> none  [on_device(): lax.all_to_all(energy, 'gy', split_axis=2, concat_axis=1, tiled=True)]
    all_to_all x0 -> x1, waiting for transfers between devices: none -> 8.35 us  [on_device(): lax.all_to_all(energy, 'gy', split_axis=2, concat_axis=1, tiled=True)]
    ppermute x4 -> x2, starting transfers between devices: 14.3 us -> 7.04 us  [padded_2(): lax.ppermute(lax.slice_in_dim(block, 0, width, axis=dim), axis, backward)]
    ppermute x4 -> x2, waiting for transfers between devices: 1.76 us -> 6.06 us  [padded_2(): lax.ppermute(lax.slice_in_dim(block, 0, width, axis=dim), axis, backward)]
    ppermute x4 -> x2, starting transfers between devices: 10 us -> 5.77 us  [padded_2(): lax.ppermute(lax.slice_in_dim(block, block.shape[dim] - width, None, axis...]
    unnamed x17 -> x13, local copies, waits for them, and re-layouts: 2.66 us -> 6.74 us
    all_to_all x0 -> x1, starting transfers between devices: none -> 3.51 us  [on_device(): lax.all_to_all(energy, 'gy', split_axis=2, concat_axis=1, tiled=True)]
  transfers between devices with their start and end apart: 8 -> 5, of which waited for: 3 -> 5; matrix products, arithmetic and copies ran while one was open for 4% -> 1% of each run, Pallas kernels for 9% -> 0%
where the time goes in v14:
time: 151 us; the launch traced here: 150 us
  Pallas kernels  44.7 us (30%)
  waiting for transfers between devices  27 us (18%)
  other arithmetic  24.5 us (16%)
  blocking collectives  19.7 us (13%)
  local copies, waits for them, and re-layouts  16.6 us (11%)
  starting transfers between devices  16.3 us (11%)
    pallas_call x1, Pallas kernels, halo_exchange(): pl.pallas_call(functools.partial(halo_kernel, hx, nx, ny), out_shape=jax....  38.1 us
    all_to_all x1, blocking collectives, on_device(): lax.all_to_all(coarse, 'gy', split_axis=1, concat_axis=2, tiled=True)  19.7 us
    sub x4, other arithmetic, advance(): chem = conc_pad - order_pad * order_pad * (3.0 - 2.0 * order_pad)  13.3 us
    ppermute x2, waiting for transfers between devices, padded_2(): lax.ppermute(lax.slice_in_dim(block, block.shape[dim] - width, None, axis...  12.6 us
    all_to_all x1, waiting for transfers between devices, on_device(): lax.all_to_all(energy, 'gy', split_axis=2, concat_axis=1, tiled=True)  8.35 us
    ppermute x2, starting transfers between devices, padded_2(): lax.ppermute(lax.slice_in_dim(block, 0, width, axis=dim), axis, backward)  7.04 us
    unnamed x13, local copies, waits for them, and re-layouts  6.74 us
    pallas_call x1, Pallas kernels, mechanics(): pl.pallas_call(functools.partial(mech_kernel, zoff), out_shape=(jax.Shape...  6.61 us
  transfers between devices with their start and end apart: 5, of which 5 were waited for; matrix products, arithmetic and copies ran while one was open for 1% of the time, Pallas kernels for 0%

profile of v14, /device:TPU:2, one launch (start us, length us, event | category | flops | bytes accessed | tf_op | source)
XLA Modules:
  0.0 150.1 jit_solution(10340756439944898653)
XLA Ops:
  0.6 0.0 copy-start.1
  0.6 0.0 copy-start
  0.7 1.6 %add_bitcast_fusion = f32[1,32,32,256]{3,2,1,0:T(8,128)S(1)} fusion(s32[32,32,256]{2,1,0:T(8,128)} %param.8), kind=kLoop, calls=%fused_computation.107 | loop fusion | flops 2097152 | bytes 2097152 | tf_op jit(solution)/shard_map/stack | solution.py:290
  2.3 0.0 copy-done.1
  2.3 0.2 copy-done
  2.5 0.1 pad_maximum_fusion.9
  2.6 1.9 %collective-permute-start = (f32[3,4,32,256]{3,2,1,0:T(8,128)S(1)}, f32[3,4,32,256]{3,2,1,0:T(8,128)S(1)}, u32[]{:S(2)}, u32[]{:S(2)}) collective-permute-start(f32[3,4,32,256]{3,2,1,0:T(8,128)S(1)} %get-tuple-element.48), channel_id=1, source_target_pairs={{0,16},{16,32},{32,48},{48,64},{64,80},{80,96},{96,112},{112,128},... | collective-permute-start | bytes 1179656 | tf_op jit(solution)/shard_map/ppermute | solution.py:200
  4.5 5.8 %collective-permute-start.1 = (f32[3,4,32,256]{3,2,1,0:T(8,128)S(1)}, f32[3,4,32,256]{3,2,1,0:T(8,128)S(1)}, u32[]{:S(2)}, u32[]{:S(2)}) collective-permute-start(f32[3,4,32,256]{3,2,1,0:T(8,128)S(1)} %get-tuple-element.49), channel_id=1, source_target_pairs={{16,0},{32,16},{48,32},{64,48},{80,64},{96,80},{112,96},{128,112},... | collective-permute-start | bytes 1179656 | tf_op jit(solution)/shard_map/ppermute | solution.py:203
  10.2 3.5 %collective-permute-done = f32[3,4,32,256]{3,2,1,0:T(8,128)S(1)} collective-permute-done((f32[3,4,32,256]{3,2,1,0:T(8,128)S(1)}, f32[3,4,32,256]{3,2,1,0:T(8,128)S(1)}, u32[]{:S(2)}, u32[]{:S(2)}) %collective-permute-start) | collective-permute-done | bytes 393248 | tf_op jit(solution)/shard_map/ppermute | solution.py:200
  13.8 1.8 %collective-permute-done.1 = f32[3,4,32,256]{3,2,1,0:T(8,128)S(1)} collective-permute-done((f32[3,4,32,256]{3,2,1,0:T(8,128)S(1)}, f32[3,4,32,256]{3,2,1,0:T(8,128)S(1)}, u32[]{:S(2)}, u32[]{:S(2)}) %collective-permute-start.1) | collective-permute-done | bytes 393248 | tf_op jit(solution)/shard_map/ppermute | solution.py:203
  15.5 0.2 pad_maximum_fusion.6
  15.7 3.9 %collective-permute-start.2 = (f32[3,40,4,256]{3,2,1,0:T(4,128)S(1)}, f32[3,40,4,256]{3,2,1,0:T(4,128)S(1)}, u32[]{:S(2)}, u32[]{:S(2)}) collective-permute-start(f32[3,40,4,256]{3,2,1,0:T(4,128)S(1)} %get-tuple-element.46), channel_id=1, source_target_pairs={{0,1},{1,2},{2,3},{3,4},{4,5},{5,6},{6,7},{7,8},{8,9},{9,10},{10,1... | collective-permute-start | bytes 1474568 | tf_op jit(solution)/shard_map/ppermute | solution.py:200
  19.5 1.3 collective-permute-start.3
  20.8 9.0 %collective-permute-done.2 = f32[3,40,4,256]{3,2,1,0:T(4,128)S(1)} collective-permute-done((f32[3,40,4,256]{3,2,1,0:T(4,128)S(1)}, f32[3,40,4,256]{3,2,1,0:T(4,128)S(1)}, u32[]{:S(2)}, u32[]{:S(2)}) %collective-permute-start.2) | collective-permute-done | bytes 491552 | tf_op jit(solution)/shard_map/ppermute | solution.py:200
  29.9 4.3 %collective-permute-done.3 = f32[3,40,4,256]{3,2,1,0:T(4,128)S(1)} collective-permute-done((f32[3,40,4,256]{3,2,1,0:T(4,128)S(1)}, f32[3,40,4,256]{3,2,1,0:T(4,128)S(1)}, u32[]{:S(2)}, u32[]{:S(2)}) %collective-permute-start.3) | collective-permute-done | bytes 491552 | tf_op jit(solution)/shard_map/ppermute | solution.py:203
  34.2 1.0 pad_maximum_fusion
  35.2 0.3 slice_bitcast_fusion.1
  35.6 0.3 multiply_subtract_fusion
  35.9 4.5 %multiply_subtract_fusion.1 = (f32[38,38,256]{2,1,0:T(8,128)S(1)}, f32[38,38,256]{2,1,0:T(8,128)S(1)}, f32[38,38,256]{2,1,0:T(8,128)S(1)}) fusion(f32[40,40,256]{2,1,0:T(8,128)S(1)} %multiply_subtract_fusion, f32[40,40,256]{2,1,0:T(8,128)S(1)} %get-tuple-element.44, f32[40,40,256]{2,1,0:T(8,128)S(1)} %get-tuple-element.45, ...), kind=kLoop, calls=%fused_computation.41 | loop fusion | flops 13307904 | bytes 26390528 | tf_op jit(solution)/shard_map/sub | solution.py:218
  40.4 4.5 %multiply_subtract_fusion.2 = (f32[36,36,256]{2,1,0:T(8,128)S(1)}, f32[36,36,256]{2,1,0:T(8,128)S(1)}, f32[36,36,256]{2,1,0:T(8,128)S(1)}) fusion(f32[38,38,256]{2,1,0:T(8,128)S(1)} %get-tuple-element.40, f32[38,38,256]{2,1,0:T(8,128)S(1)} %get-tuple-element.41, f32[40,40,256]{2,1,0:T(8,128)S(1)} %get-tuple-element.45, f32[38,38,256]{2,1,0:T(8,128)S(1)} %get-tuple-element.42), kind=kLoop, calls=%fused_computation.62 | loop fusion | flops 11943936 | bytes 24788992 | tf_op jit(solution)/shard_map/sub | solution.py:218
  44.9 4.0 %multiply_subtract_fusion.3 = (f32[34,34,256]{2,1,0:T(8,128)S(1)}, f32[34,34,256]{2,1,0:T(8,128)S(1)}, f32[34,34,256]{2,1,0:T(8,128)S(1)}) fusion(f32[36,36,256]{2,1,0:T(8,128)S(1)} %get-tuple-element.37, f32[36,36,256]{2,1,0:T(8,128)S(1)} %get-tuple-element.38, f32[40,40,256]{2,1,0:T(8,128)S(1)} %get-tuple-element.45, f32[36,36,256]{2,1,0:T(8,128)S(1)} %get-tuple-element.39), kind=kLoop, calls=%fused_computation.83 | loop fusion | flops 10653696 | bytes 23212032 | tf_op jit(solution)/shard_map/sub | solution.py:218
  48.9 0.0 copy-start.3
  48.9 2.4 %bitcast_reduce_fusion = (f32[16,32,256]{2,1,0:T(8,128)S(1)}, f32[32,32,256]{2,1,0:T(8,128)}) fusion(f32[34,34,256]{2,1,0:T(8,128)S(1)} %get-tuple-element.34, f32[34,34,256]{2,1,0:T(8,128)S(1)} %get-tuple-element.35, f32[40,40,256]{2,1,0:T(8,128)S(1)} %get-tuple-element.45), kind=kLoop, calls=%fused_computation.106 | loop fusion | flops 5636096 | bytes 10305536 | tf_op jit(solution)/shard_map/reduce_sum | solution.py:243
  51.3 0.3 bitcast_reduce_fusion.1
  51.6 0.0 copy-done.3
  51.6 0.5 fusion.43
  52.1 1.4 copy.43
  53.4 1.6 %reshape.18 = f32[16,1,2048]{2,1,0:T(1,128)S(1)} reshape(f32[128,16,16]{2,1,0:T(8,128)} %bitcast.43) | data formatting | bytes 262144
  55.1 19.7 %all_to_all.33 = f32[16,1,2048]{2,1,0:T(1,128)S(1)} all-to-all(f32[16,1,2048]{2,1,0:T(1,128)S(1)} %reshape.18), channel_id=1, replica_groups=mesh['gx'=16,'gy'=16] {'gy'}, dimensions={0} | all-to-all | bytes 262144 | tf_op jit(solution)/shard_map/all_to_all | solution.py:299
  74.7 0.6 broadcast.146
  75.3 0.9 reduce
  76.2 1.3 reshape.19
  77.6 0.0 copy-start.2
  77.6 2.9 %copy.45 = f32[16,8,16,16]{3,2,1,0:T(8,128)} copy(f32[16,8,16,16]{3,0,1,2:T(8,128)} %bitcast.45) | data formatting | bytes 262144 | tf_op jit(solution)/shard_map/all_to_all | solution.py:299
  80.4 1.6 %broadcast_in_dim.9 = f32[1,16,8,256]{3,2,1,0:T(8,128)S(1)} reshape(f32[16,8,16,16]{3,2,1,0:T(8,128)} %copy.45) | data formatting | bytes 262144 | tf_op jit(solution)/shard_map/broadcast_in_dim | solution.py:300
  82.1 0.0 copy-done.2
  82.1 2.0 %pad_maximum_fusion.1.blk_ref = f32[7,16,8,256]{3,2,1,0:T(8,128)} fusion(f32[3,16,8,256]{3,2,1,0:T(8,128)S(1)} %copy-done.2, f32[3,16,8,256]{3,2,1,0:T(8,128)} %param.9, f32[1,16,8,256]{3,2,1,0:T(8,128)S(1)} %broadcast_in_dim.9), kind=kLoop, calls=%fused_computation.108 | loop fusion | flops 458752 | bytes 1835008 | tf_op jit(solution)/shard_map/concatenate | solution.py:300
  84.1 38.1 %shard_map.93.ext_ref = f32[7,22,24,256]{3,2,1,0:T(8,128)} custom-call(f32[7,16,8,256]{3,2,1,0:T(8,128)} %pad_maximum_fusion.1.blk_ref), custom_call_target="tpu_custom_call" | custom-call | tf_op jit(solution)/shard_map/pallas_call | solution.py:94
  122.2 6.6 %shard_map.94 = (f32[3,16,8,256]{3,2,1,0:T(8,128)}, f32[16,8,256]{2,1,0:T(8,128)}) custom-call(f32[7,22,24,256]{3,2,1,0:T(8,128)} %shard_map.93.ext_ref), custom_call_target="tpu_custom_call" | custom-call | tf_op jit(solution)/shard_map/pallas_call | solution.py:184
  128.8 2.2 %copy.46 = f32[16,8,256]{0,1,2:T(8,128)} copy(f32[16,8,256]{2,1,0:T(8,128)} %get-tuple-element.7) | data formatting | bytes 262144 | tf_op jit(solution)/shard_map/pallas_call | solution.py:184
  131.0 2.3 %reshape.20 = f32[16,1,2048]{2,1,0:T(1,128)} reshape(f32[256,8,16]{2,1,0:T(8,128)} %bitcast.44) | data formatting | bytes 262144
  133.3 3.5 %all-to-all-start.1 = ((f32[16,1,2048]{2,1,0:T(1,128)}), f32[16,1,2048]{2,1,0:T(1,128)S(1)}, u32[]{:S(2)}, u32[]{:S(2)}) async-start(f32[16,1,2048]{2,1,0:T(1,128)} %reshape.20), calls=%async_computation.1 | async-start | bytes 262144 | tf_op jit(solution)/shard_map/all_to_all | solution.py:303
  136.8 1.7 %fusion.48 = f32[32,32,256]{2,1,0:T(8,128)} fusion(f32[34,34,256]{2,1,0:T(8,128)S(1)} %get-tuple-element.34, f32[34,34,256]{2,1,0:T(8,128)S(1)} %get-tuple-element.36), kind=kLoop, calls=%fused_computation.91 | loop fusion | flops 2359296 | bytes 8732672 | tf_op jit(solution)/shard_map/add | solution.py:223
  138.5 8.4 %all-to-all-done.1 = f32[16,1,2048]{2,1,0:T(1,128)S(1)} async-done(((f32[16,1,2048]{2,1,0:T(1,128)}), f32[16,1,2048]{2,1,0:T(1,128)S(1)}, u32[]{:S(2)}, u32[]{:S(2)}) %all-to-all-start.1) | async-done | bytes 131104 | tf_op jit(solution)/shard_map/all_to_all | solution.py:303
  146.9 0.9 reduce.1
  147.8 0.4 reshape.21
  148.2 0.9 copy.47
  149.1 1.0 copy.48
Async XLA Ops:
  0.6 1.7 %copy-start.1 = (f32[32,32,256]{2,1,0:T(8,128)S(1)}, f32[32,32,256]{2,1,0:T(8,128)}, u32[]{:S(2)}) copy-start(f32[32,32,256]{2,1,0:T(8,128)} %param.6) | copy-start | bytes 3145732
  0.6 1.8 %copy-start = (f32[32,32,256]{2,1,0:T(8,128)S(1)}, f32[32,32,256]{2,1,0:T(8,128)}, u32[]{:S(2)}) copy-start(f32[32,32,256]{2,1,0:T(8,128)} %param.7) | copy-start | bytes 3145732
  2.6 11.2 %collective-permute-start = (f32[3,4,32,256]{3,2,1,0:T(8,128)S(1)}, f32[3,4,32,256]{3,2,1,0:T(8,128)S(1)}, u32[]{:S(2)}, u32[]{:S(2)}) collective-permute-start(f32[3,4,32,256]{3,2,1,0:T(8,128)S(1)} %get-tuple-element.48), channel_id=1, source_target_pairs={{0,16},{16,32},{32,48},{48,64},{64,80},{80,96},{96,112},{112,128},... | collective-permute-start | bytes 1179656 | tf_op jit(solution)/shard_map/ppermute | solution.py:200
  4.5 11.0 %collective-permute-start.1 = (f32[3,4,32,256]{3,2,1,0:T(8,128)S(1)}, f32[3,4,32,256]{3,2,1,0:T(8,128)S(1)}, u32[]{:S(2)}, u32[]{:S(2)}) collective-permute-start(f32[3,4,32,256]{3,2,1,0:T(8,128)S(1)} %get-tuple-element.49), channel_id=1, source_target_pairs={{16,0},{32,16},{48,32},{64,48},{80,64},{96,80},{112,96},{128,112},... | collective-permute-start | bytes 1179656 | tf_op jit(solution)/shard_map/ppermute | solution.py:203
  15.7 14.2 %collective-permute-start.2 = (f32[3,40,4,256]{3,2,1,0:T(4,128)S(1)}, f32[3,40,4,256]{3,2,1,0:T(4,128)S(1)}, u32[]{:S(2)}, u32[]{:S(2)}) collective-permute-start(f32[3,40,4,256]{3,2,1,0:T(4,128)S(1)} %get-tuple-element.46), channel_id=1, source_target_pairs={{0,1},{1,2},{2,3},{3,4},{4,5},{5,6},{6,7},{7,8},{8,9},{9,10},{10,1... | collective-permute-start | bytes 1474568 | tf_op jit(solution)/shard_map/ppermute | solution.py:200
  19.5 14.6 %collective-permute-start.3 = (f32[3,40,4,256]{3,2,1,0:T(4,128)S(1)}, f32[3,40,4,256]{3,2,1,0:T(4,128)S(1)}, u32[]{:S(2)}, u32[]{:S(2)}) collective-permute-start(f32[3,40,4,256]{3,2,1,0:T(4,128)S(1)} %get-tuple-element.47), channel_id=1, source_target_pairs={{1,0},{2,1},{3,2},{4,3},{5,4},{6,5},{7,6},{8,7},{9,8},{10,9},{11,1... | collective-permute-start | bytes 1474568 | tf_op jit(solution)/shard_map/ppermute | solution.py:203
  48.9 2.7 %copy-start.3 = (f32[256,128,1]{1,0,2:T(8,128)S(1)}, f32[256,128,1]{1,0,2:T(8,128)}, u32[]{:S(2)}) copy-start(f32[256,128,1]{1,0,2:T(8,128)} %constant.36) | copy-start | bytes 393220
  77.6 4.5 %copy-start.2 = (f32[3,16,8,256]{3,2,1,0:T(8,128)S(1)}, f32[3,16,8,256]{3,2,1,0:T(8,128)}, u32[]{:S(2)}) copy-start(f32[3,16,8,256]{3,2,1,0:T(8,128)} %param.10) | copy-start | bytes 1179652
  133.3 13.6 %all-to-all-start.1 = ((f32[16,1,2048]{2,1,0:T(1,128)}), f32[16,1,2048]{2,1,0:T(1,128)S(1)}, u32[]{:S(2)}, u32[]{:S(2)}) async-start(f32[16,1,2048]{2,1,0:T(1,128)} %reshape.20), calls=%async_computation.1 | async-start | bytes 262144 | tf_op jit(solution)/shard_map/all_to_all | solution.py:303

commit v15 on v13

--- a/solution.py
+++ b/solution.py
@@ -295,11 +295,9 @@
     for step in range(STEPS):
         conc, order, mob = advance(conc, order, mob, step == STEPS - 1)
 
-    order, ub = lax.optimization_barrier((order, ub))
+    coarse = restrict_xzy(order)
+    coarse, ub = lax.optimization_barrier((coarse, ub))
     ub = padded_2(ub, (("gy", 2),), m + 1)
-    disp, load = ub[:3], ub[3:]
-
-    coarse = restrict_xzy(order)
     stiff = lax.all_to_all(coarse, "gy", split_axis=1, concat_axis=2, tiled=True)
     stiff_ext = halo_exchange(stiff[None], m, 0)[0]
     bx, bz = stiff.shape[0], stiff.shape[1]

time: 128 us -> 137 us (1.070)
  blocking collectives: 35.8 us -> 21.5 us
  waiting for transfers between devices: 14 us -> 22.5 us
  local copies, waits for them, and re-layouts: 9.39 us -> 16.8 us
  starting transfers between devices: 24.3 us -> 28.1 us
  other arithmetic: 25.3 us -> 27.3 us
    all_to_all x1 -> x0, blocking collectives: 14.5 us -> none  [on_device(): lax.all_to_all(energy, 'gy', split_axis=2, concat_axis=1, tiled=True)]
    all_to_all x0 -> x1, waiting for transfers between devices: none -> 8.52 us  [on_device(): lax.all_to_all(energy, 'gy', split_axis=2, concat_axis=1, tiled=True)]
    all_to_all x0 -> x1, starting transfers between devices: none -> 3.97 us  [on_device(): lax.all_to_all(energy, 'gy', split_axis=2, concat_axis=1, tiled=True)]
    unnamed x17, local copies, waits for them, and re-layouts: 2.66 us -> 6.1 us
    reduce_sum x1, other arithmetic: 0.09 us -> 2.4 us  [restrict_xzy(): sq = sq.reshape(sx // 2, 2, sy, sz).sum(axis=1)]
    add x1, other arithmetic: 3.8 us -> 1.75 us  [advance(): conc_new = conc_in + rate_conc * fine_laplace(chem)]
    optimization_barrier x0 -> x1, local copies, waits for them, and re-layouts: none -> 1.39 us  [on_device(): coarse, ub = lax.optimization_barrier((coarse, ub))]
  transfers between devices with their start and end apart: 8 -> 9, of which waited for: 3 -> 4; matrix products, arithmetic and copies ran while one was open for 4% -> 9% of each run, Pallas kernels for 9% -> 8%
where the time goes in v15:
time: 137 us; the launch traced here: 136 us
  starting transfers between devices  28.1 us (21%)
  other arithmetic  27.3 us (20%)
  waiting for transfers between devices  22.5 us (16%)
  blocking collectives  21.5 us (16%)
  Pallas kernels  17.4 us (13%)
  local copies, waits for them, and re-layouts  16.8 us (12%)
    all_to_all x1, blocking collectives, on_device(): lax.all_to_all(coarse, 'gy', split_axis=1, concat_axis=2, tiled=True)  21.5 us
    ppermute x4, starting transfers between devices, padded_2(): lax.ppermute(lax.slice_in_dim(block, 0, width, axis=dim), axis, backward)  14.3 us
    sub x4, other arithmetic, advance(): chem = conc_pad - order_pad * order_pad * (3.0 - 2.0 * order_pad)  14.2 us
    ppermute x4, waiting for transfers between devices, padded_2(): lax.ppermute(lax.slice_in_dim(block, block.shape[dim] - width, None, axis...  12.3 us
    pallas_call x1, Pallas kernels, halo_exchange(): pl.pallas_call(functools.partial(halo_kernel, hx, nx, ny), out_shape=jax....  11.3 us
    ppermute x4, starting transfers between devices, padded_2(): lax.ppermute(lax.slice_in_dim(block, block.shape[dim] - width, None, axis...  9.93 us
    all_to_all x1, waiting for transfers between devices, on_device(): lax.all_to_all(energy, 'gy', split_axis=2, concat_axis=1, tiled=True)  8.52 us
    pallas_call x1, Pallas kernels, mechanics(): pl.pallas_call(functools.partial(mech_kernel, zoff), out_shape=(jax.Shape...  6.1 us
  transfers between devices with their start and end apart: 9, of which 4 were waited for; matrix products, arithmetic and copies ran while one was open for 9% of the time, Pallas kernels for 8%

profile of v15, /device:TPU:2, one launch (start us, length us, event | category | flops | bytes accessed | tf_op | source)
XLA Modules:
  0.0 135.8 jit_solution(7200427617653475923)
XLA Ops:
  0.7 1.6 %add_bitcast_fusion = f32[1,32,32,256]{3,2,1,0:T(8,128)S(1)} fusion(s32[32,32,256]{2,1,0:T(8,128)} %param.8), kind=kLoop, calls=%fused_computation.110 | loop fusion | flops 2097152 | bytes 2097152 | tf_op jit(solution)/shard_map/stack | solution.py:288
  2.3 0.2 copy-done.1
  2.5 0.1 pad_maximum_fusion.7
  2.6 2.1 %collective-permute-start = (f32[3,4,32,256]{3,2,1,0:T(8,128)S(1)}, f32[3,4,32,256]{3,2,1,0:T(8,128)S(1)}, u32[]{:S(2)}, u32[]{:S(2)}) collective-permute-start(f32[3,4,32,256]{3,2,1,0:T(8,128)S(1)} %get-tuple-element.56), channel_id=1, source_target_pairs={{0,16},{16,32},{32,48},{48,64},{64,80},{80,96},{96,112},{112,128},... | collective-permute-start | bytes 1179656 | tf_op jit(solution)/shard_map/ppermute | solution.py:198
  4.6 5.8 %collective-permute-start.1 = (f32[3,4,32,256]{3,2,1,0:T(8,128)S(1)}, f32[3,4,32,256]{3,2,1,0:T(8,128)S(1)}, u32[]{:S(2)}, u32[]{:S(2)}) collective-permute-start(f32[3,4,32,256]{3,2,1,0:T(8,128)S(1)} %get-tuple-element.57), channel_id=1, source_target_pairs={{16,0},{32,16},{48,32},{64,48},{80,64},{96,80},{112,96},{128,112},... | collective-permute-start | bytes 1179656 | tf_op jit(solution)/shard_map/ppermute | solution.py:201
  10.4 0.1 pad_maximum_fusion.4
  10.5 3.4 %collective-permute-done = f32[3,4,32,256]{3,2,1,0:T(8,128)S(1)} collective-permute-done((f32[3,4,32,256]{3,2,1,0:T(8,128)S(1)}, f32[3,4,32,256]{3,2,1,0:T(8,128)S(1)}, u32[]{:S(2)}, u32[]{:S(2)}) %collective-permute-start) | collective-permute-done | bytes 393248 | tf_op jit(solution)/shard_map/ppermute | solution.py:198
  13.9 1.8 %collective-permute-done.1 = f32[3,4,32,256]{3,2,1,0:T(8,128)S(1)} collective-permute-done((f32[3,4,32,256]{3,2,1,0:T(8,128)S(1)}, f32[3,4,32,256]{3,2,1,0:T(8,128)S(1)}, u32[]{:S(2)}, u32[]{:S(2)}) %collective-permute-start.1) | collective-permute-done | bytes 393248 | tf_op jit(solution)/shard_map/ppermute | solution.py:201
  15.7 0.4 pad_maximum_fusion.1
  16.1 0.2 fusion.65
  16.2 3.9 %collective-permute-start.2 = (f32[3,40,4,256]{3,2,1,0:T(4,128)S(1)}, f32[3,40,4,256]{3,2,1,0:T(4,128)S(1)}, u32[]{:S(2)}, u32[]{:S(2)}) collective-permute-start(f32[3,40,4,256]{3,2,1,0:T(4,128)S(1)} %get-tuple-element.54), channel_id=1, source_target_pairs={{0,1},{1,2},{2,3},{3,4},{4,5},{5,6},{6,7},{7,8},{8,9},{9,10},{10,1... | collective-permute-start | bytes 1474568 | tf_op jit(solution)/shard_map/ppermute | solution.py:198
  20.1 1.3 collective-permute-start.3
  21.4 1.9 %collective-permute-start.4 = (f32[6,3,8,256]{3,2,1,0:T(8,128)S(1)}, f32[6,3,8,256]{3,2,1,0:T(8,128)S(1)}, u32[]{:S(2)}, u32[]{:S(2)}) collective-permute-start(f32[6,3,8,256]{3,2,1,0:T(8,128)S(1)} %get-tuple-element.60), channel_id=1, source_target_pairs={{0,16},{16,32},{32,48},{48,64},{64,80},{80,96},{96,112},{112,128},... | collective-permute-start | bytes 442376 | tf_op jit(solution)/shard_map/ppermute | solution.py:198
  23.4 5.8 %collective-permute-start.5 = (f32[6,3,8,256]{3,2,1,0:T(8,128)S(1)}, f32[6,3,8,256]{3,2,1,0:T(8,128)S(1)}, u32[]{:S(2)}, u32[]{:S(2)}) collective-permute-start(f32[6,3,8,256]{3,2,1,0:T(8,128)S(1)} %get-tuple-element.61), channel_id=1, source_target_pairs={{16,0},{32,16},{48,32},{64,48},{80,64},{96,80},{112,96},{128,112},... | collective-permute-start | bytes 442376 | tf_op jit(solution)/shard_map/ppermute | solution.py:201
  29.1 8.8 %collective-permute-done.4 = f32[6,3,8,256]{3,2,1,0:T(8,128)S(1)} collective-permute-done((f32[6,3,8,256]{3,2,1,0:T(8,128)S(1)}, f32[6,3,8,256]{3,2,1,0:T(8,128)S(1)}, u32[]{:S(2)}, u32[]{:S(2)}) %collective-permute-start.4) | collective-permute-done | bytes 147488 | tf_op jit(solution)/shard_map/ppermute | solution.py:198
  38.0 0.1 pad_maximum_fusion.3
  38.1 0.9 pad_maximum_fusion
  39.0 0.3 slice_bitcast_fusion.1
  39.3 0.3 multiply_subtract_fusion
  39.6 4.5 %multiply_subtract_fusion.1 = (f32[38,38,256]{2,1,0:T(8,128)S(1)}, f32[38,38,256]{2,1,0:T(8,128)S(1)}, f32[38,38,256]{2,1,0:T(8,128)S(1)}) fusion(f32[40,40,256]{2,1,0:T(8,128)S(1)} %multiply_subtract_fusion, f32[40,40,256]{2,1,0:T(8,128)S(1)} %get-tuple-element.52, f32[40,40,256]{2,1,0:T(8,128)S(1)} %get-tuple-element.53, ...), kind=kLoop, calls=%fused_computation.43 | loop fusion | flops 13307904 | bytes 26390528 | tf_op jit(solution)/shard_map/sub | solution.py:216
  44.2 4.5 %multiply_subtract_fusion.2 = (f32[36,36,256]{2,1,0:T(8,128)S(1)}, f32[36,36,256]{2,1,0:T(8,128)S(1)}, f32[36,36,256]{2,1,0:T(8,128)S(1)}) fusion(f32[38,38,256]{2,1,0:T(8,128)S(1)} %get-tuple-element.48, f32[38,38,256]{2,1,0:T(8,128)S(1)} %get-tuple-element.49, f32[40,40,256]{2,1,0:T(8,128)S(1)} %get-tuple-element.53, f32[38,38,256]{2,1,0:T(8,128)S(1)} %get-tuple-element.50), kind=kLoop, calls=%fused_computation.64 | loop fusion | flops 11943936 | bytes 24788992 | tf_op jit(solution)/shard_map/sub | solution.py:216
  48.6 4.9 %multiply_subtract_fusion.3 = (f32[34,34,256]{2,1,0:T(8,128)S(1)}, f32[34,34,256]{2,1,0:T(8,128)S(1)}, f32[34,34,256]{2,1,0:T(8,128)}) fusion(f32[36,36,256]{2,1,0:T(8,128)S(1)} %get-tuple-element.45, f32[36,36,256]{2,1,0:T(8,128)S(1)} %get-tuple-element.46, f32[40,40,256]{2,1,0:T(8,128)S(1)} %get-tuple-element.53, f32[36,36,256]{2,1,0:T(8,128)S(1)} %get-tuple-element.47), kind=kLoop, calls=%fused_computation.85 | loop fusion | flops 10653696 | bytes 23212032 | tf_op jit(solution)/shard_map/sub | solution.py:216
  53.5 2.4 %bitcast_reduce_fusion = (f32[16,32,256]{2,1,0:T(8,128)S(1)}, f32[32,32,256]{2,1,0:T(8,128)}) fusion(f32[34,34,256]{2,1,0:T(8,128)S(1)} %get-tuple-element.42, f32[34,34,256]{2,1,0:T(8,128)S(1)} %get-tuple-element.43, f32[40,40,256]{2,1,0:T(8,128)S(1)} %get-tuple-element.53), kind=kLoop, calls=%fused_computation.109 | loop fusion | flops 5636096 | bytes 10305536 | tf_op jit(solution)/shard_map/reduce_sum | solution.py:241
  55.9 0.3 bitcast_reduce_fusion.1
  56.2 1.1 fusion.43
  57.4 1.1 fusion.66
  58.5 2.1 %collective-permute-start.6 = (f32[6,22,4,256]{3,2,1,0:T(4,128)}, f32[6,22,4,256]{3,2,1,0:T(4,128)}, u32[]{:S(2)}, u32[]{:S(2)}) collective-permute-start(f32[6,22,4,256]{3,2,1,0:T(4,128)} %get-tuple-element.58), channel_id=1, source_target_pairs={{0,1},{1,2},{2,3},{3,4},{4,5},{5,6},{6,7},{7,8},{8,9},{9,10},{10,1... | collective-permute-start | bytes 1622024 | tf_op jit(solution)/shard_map/ppermute | solution.py:198
  60.6 1.5 %collective-permute-start.7 = (f32[6,22,4,256]{3,2,1,0:T(4,128)}, f32[6,22,4,256]{3,2,1,0:T(4,128)}, u32[]{:S(2)}, u32[]{:S(2)}) collective-permute-start(f32[6,22,4,256]{3,2,1,0:T(4,128)} %get-tuple-element.59), channel_id=1, source_target_pairs={{1,0},{2,1},{3,2},{4,3},{5,4},{6,5},{7,6},{8,7},{9,8},{10,9},{11,1... | collective-permute-start | bytes 1622024 | tf_op jit(solution)/shard_map/ppermute | solution.py:201
  62.1 1.4 %copy.43 = f32[16,128,16]{2,0,1:T(8,128)S(1)} copy(f32[16,128,16]{1,2,0:T(8,128)} %fusion.43) | data formatting | bytes 262144 | tf_op jit(solution)/shard_map/optimization_barrier | solution.py:299
  63.5 1.0 reshape.18
  64.5 21.5 %all_to_all.33 = f32[16,1,2048]{2,1,0:T(1,128)S(1)} all-to-all(f32[16,1,2048]{2,1,0:T(1,128)} %reshape.18), channel_id=1, replica_groups=mesh['gx'=16,'gy'=16] {'gy'}, dimensions={0} | all-to-all | bytes 262144 | tf_op jit(solution)/shard_map/all_to_all | solution.py:301
  86.0 0.6 broadcast.146
  86.6 1.6 %reduce = f32[16,2048]{1,0:T(8,128)} reduce(f32[16,1,2048]{2,1,0:T(1,128)S(1)} %all_to_all.33, f32[]{:T(128)} %broadcast.146), dimensions={1}, to_apply=%all_to_all.24.reduce_sub_computation | reduce | bytes 262148 | tf_op jit(solution)/shard_map/all_to_all | solution.py:301
  88.2 1.3 reshape.19
  89.5 1.6 %copy.45 = f32[16,8,16,16]{3,2,1,0:T(8,128)} copy(f32[16,8,16,16]{3,0,1,2:T(8,128)S(1)} %bitcast.44) | data formatting | bytes 262144 | tf_op jit(solution)/shard_map/all_to_all | solution.py:301
  91.1 2.3 %broadcast_in_dim.9.blk_ref = f32[1,16,8,256]{3,2,1,0:T(8,128)} reshape(f32[16,8,16,16]{3,2,1,0:T(8,128)} %copy.45) | data formatting | bytes 262144 | tf_op jit(solution)/shard_map/broadcast_in_dim | solution.py:302
  93.3 11.3 %shard_map.93 = f32[1,22,24,256]{3,2,1,0:T(8,128)} custom-call(f32[1,16,8,256]{3,2,1,0:T(8,128)} %broadcast_in_dim.9.blk_ref), custom_call_target="tpu_custom_call" | custom-call | tf_op jit(solution)/shard_map/pallas_call | solution.py:94
  104.6 3.0 %pad_maximum_fusion.2.ub_ref = f32[6,22,16,256]{3,2,1,0:T(8,128)} fusion(f32[6,22,4,256]{3,2,1,0:T(4,128)} %collective-permute-done.7, f32[6,22,8,256]{3,2,1,0:T(8,128)S(1)} %pad_maximum_fusion.3, f32[6,22,4,256]{3,2,1,0:T(4,128)} %collective-permute-done.6), kind=kLoop, calls=%fused_computation.18 | loop fusion | flops 1081344 | bytes 4325376 | tf_op jit(solution)/shard_map/concatenate | solution.py:202
  107.6 6.1 %shard_map.94 = (f32[3,16,8,256]{3,2,1,0:T(8,128)}, f32[16,8,256]{2,1,0:T(8,128)}) custom-call(f32[22,24,256]{2,1,0:T(8,128)} %bitcast.47, f32[6,22,16,256]{3,2,1,0:T(8,128)} %pad_maximum_fusion.2.ub_ref), custom_call_target="tpu_custom_call" | custom-call | tf_op jit(solution)/shard_map/pallas_call | solution.py:182
  113.7 2.3 %copy.46 = f32[16,8,256]{0,1,2:T(8,128)} copy(f32[16,8,256]{2,1,0:T(8,128)} %get-tuple-element.15) | data formatting | bytes 262144 | tf_op jit(solution)/shard_map/pallas_call | solution.py:182
  116.0 2.3 %reshape.20 = f32[16,1,2048]{2,1,0:T(1,128)} reshape(f32[256,8,16]{2,1,0:T(8,128)} %bitcast.39) | data formatting | bytes 262144
  118.3 4.0 %all-to-all-start.1 = ((f32[16,1,2048]{2,1,0:T(1,128)}), f32[16,1,2048]{2,1,0:T(1,128)S(1)}, u32[]{:S(2)}, u32[]{:S(2)}) async-start(f32[16,1,2048]{2,1,0:T(1,128)} %reshape.20), calls=%async_computation.1 | async-start | bytes 262144 | tf_op jit(solution)/shard_map/all_to_all | solution.py:305
  122.3 1.7 %fusion.48 = f32[32,32,256]{2,1,0:T(8,128)} fusion(f32[34,34,256]{2,1,0:T(8,128)S(1)} %get-tuple-element.42, f32[34,34,256]{2,1,0:T(8,128)S(1)} %copy-done), kind=kLoop, calls=%fused_computation.94 | loop fusion | flops 2359296 | bytes 8732672 | tf_op jit(solution)/shard_map/add | solution.py:221
  124.0 8.5 %all-to-all-done.1 = f32[16,1,2048]{2,1,0:T(1,128)S(1)} async-done(((f32[16,1,2048]{2,1,0:T(1,128)}), f32[16,1,2048]{2,1,0:T(1,128)S(1)}, u32[]{:S(2)}, u32[]{:S(2)}) %all-to-all-start.1) | async-done | bytes 131104 | tf_op jit(solution)/shard_map/all_to_all | solution.py:305
  132.6 1.0 reduce.1
  133.5 0.4 reshape.21
  133.9 0.9 copy.47
  134.8 1.0 copy.48
  (17 shorter events, 0.1 us)
Async XLA Ops:
  0.6 1.7 %copy-start.2 = (f32[32,32,256]{2,1,0:T(8,128)S(1)}, f32[32,32,256]{2,1,0:T(8,128)}, u32[]{:S(2)}) copy-start(f32[32,32,256]{2,1,0:T(8,128)} %param.6) | copy-start | bytes 3145732
  0.6 1.8 %copy-start.1 = (f32[32,32,256]{2,1,0:T(8,128)S(1)}, f32[32,32,256]{2,1,0:T(8,128)}, u32[]{:S(2)}) copy-start(f32[32,32,256]{2,1,0:T(8,128)} %param.7) | copy-start | bytes 3145732
  2.5 7.9 %copy-start.3 = (f32[3,16,8,256]{3,2,1,0:T(8,128)S(1)}, f32[3,16,8,256]{3,2,1,0:T(8,128)}, u32[]{:S(2)}) copy-start(f32[3,16,8,256]{3,2,1,0:T(8,128)} %param.10) | copy-start | bytes 1179652
  2.5 7.9 %copy-start.4 = (f32[3,16,8,256]{3,2,1,0:T(8,128)S(1)}, f32[3,16,8,256]{3,2,1,0:T(8,128)}, u32[]{:S(2)}) copy-start(f32[3,16,8,256]{3,2,1,0:T(8,128)} %param.9) | copy-start | bytes 1179652
  2.6 11.3 %collective-permute-start = (f32[3,4,32,256]{3,2,1,0:T(8,128)S(1)}, f32[3,4,32,256]{3,2,1,0:T(8,128)S(1)}, u32[]{:S(2)}, u32[]{:S(2)}) collective-permute-start(f32[3,4,32,256]{3,2,1,0:T(8,128)S(1)} %get-tuple-element.56), channel_id=1, source_target_pairs={{0,16},{16,32},{32,48},{48,64},{64,80},{80,96},{96,112},{112,128},... | collective-permute-start | bytes 1179656 | tf_op jit(solution)/shard_map/ppermute | solution.py:198
  4.6 11.0 %collective-permute-start.1 = (f32[3,4,32,256]{3,2,1,0:T(8,128)S(1)}, f32[3,4,32,256]{3,2,1,0:T(8,128)S(1)}, u32[]{:S(2)}, u32[]{:S(2)}) collective-permute-start(f32[3,4,32,256]{3,2,1,0:T(8,128)S(1)} %get-tuple-element.57), channel_id=1, source_target_pairs={{16,0},{32,16},{48,32},{64,48},{80,64},{96,80},{112,96},{128,112},... | collective-permute-start | bytes 1179656 | tf_op jit(solution)/shard_map/ppermute | solution.py:201
  16.2 21.8 %collective-permute-start.2 = (f32[3,40,4,256]{3,2,1,0:T(4,128)S(1)}, f32[3,40,4,256]{3,2,1,0:T(4,128)S(1)}, u32[]{:S(2)}, u32[]{:S(2)}) collective-permute-start(f32[3,40,4,256]{3,2,1,0:T(4,128)S(1)} %get-tuple-element.54), channel_id=1, source_target_pairs={{0,1},{1,2},{2,3},{3,4},{4,5},{5,6},{6,7},{7,8},{8,9},{9,10},{10,1... | collective-permute-start | bytes 1474568 | tf_op jit(solution)/shard_map/ppermute | solution.py:198
  20.1 18.0 %collective-permute-start.3 = (f32[3,40,4,256]{3,2,1,0:T(4,128)S(1)}, f32[3,40,4,256]{3,2,1,0:T(4,128)S(1)}, u32[]{:S(2)}, u32[]{:S(2)}) collective-permute-start(f32[3,40,4,256]{3,2,1,0:T(4,128)S(1)} %get-tuple-element.55), channel_id=1, source_target_pairs={{1,0},{2,1},{3,2},{4,3},{5,4},{6,5},{7,6},{8,7},{9,8},{10,9},{11,1... | collective-permute-start | bytes 1474568 | tf_op jit(solution)/shard_map/ppermute | solution.py:201
  21.4 16.5 %collective-permute-start.4 = (f32[6,3,8,256]{3,2,1,0:T(8,128)S(1)}, f32[6,3,8,256]{3,2,1,0:T(8,128)S(1)}, u32[]{:S(2)}, u32[]{:S(2)}) collective-permute-start(f32[6,3,8,256]{3,2,1,0:T(8,128)S(1)} %get-tuple-element.60), channel_id=1, source_target_pairs={{0,16},{16,32},{32,48},{48,64},{64,80},{80,96},{96,112},{112,128},... | collective-permute-start | bytes 442376 | tf_op jit(solution)/shard_map/ppermute | solution.py:198
  23.4 14.6 %collective-permute-start.5 = (f32[6,3,8,256]{3,2,1,0:T(8,128)S(1)}, f32[6,3,8,256]{3,2,1,0:T(8,128)S(1)}, u32[]{:S(2)}, u32[]{:S(2)}) collective-permute-start(f32[6,3,8,256]{3,2,1,0:T(8,128)S(1)} %get-tuple-element.61), channel_id=1, source_target_pairs={{16,0},{32,16},{48,32},{64,48},{80,64},{96,80},{112,96},{128,112},... | collective-permute-start | bytes 442376 | tf_op jit(solution)/shard_map/ppermute | solution.py:201
  53.5 2.7 %copy-start.5 = (f32[256,128,1]{1,0,2:T(8,128)S(1)}, f32[256,128,1]{1,0,2:T(8,128)}, u32[]{:S(2)}) copy-start(f32[256,128,1]{1,0,2:T(8,128)} %constant.36) | copy-start | bytes 393220
  58.5 46.1 %collective-permute-start.6 = (f32[6,22,4,256]{3,2,1,0:T(4,128)}, f32[6,22,4,256]{3,2,1,0:T(4,128)}, u32[]{:S(2)}, u32[]{:S(2)}) collective-permute-start(f32[6,22,4,256]{3,2,1,0:T(4,128)} %get-tuple-element.58), channel_id=1, source_target_pairs={{0,1},{1,2},{2,3},{3,4},{4,5},{5,6},{6,7},{7,8},{8,9},{9,10},{10,1... | collective-permute-start | bytes 1622024 | tf_op jit(solution)/shard_map/ppermute | solution.py:198
  60.6 44.0 %collective-permute-start.7 = (f32[6,22,4,256]{3,2,1,0:T(4,128)}, f32[6,22,4,256]{3,2,1,0:T(4,128)}, u32[]{:S(2)}, u32[]{:S(2)}) collective-permute-start(f32[6,22,4,256]{3,2,1,0:T(4,128)} %get-tuple-element.59), channel_id=1, source_target_pairs={{1,0},{2,1},{3,2},{4,3},{5,4},{6,5},{7,6},{8,7},{9,8},{10,9},{11,1... | collective-permute-start | bytes 1622024 | tf_op jit(solution)/shard_map/ppermute | solution.py:201
  113.7 8.6 %copy-start = (f32[34,34,256]{2,1,0:T(8,128)S(1)}, f32[34,34,256]{2,1,0:T(8,128)}, u32[]{:S(2)}) copy-start(f32[34,34,256]{2,1,0:T(8,128)} %get-tuple-element.44) | copy-start | bytes 3551236
  118.3 14.2 %all-to-all-start.1 = ((f32[16,1,2048]{2,1,0:T(1,128)}), f32[16,1,2048]{2,1,0:T(1,128)S(1)}, u32[]{:S(2)}, u32[]{:S(2)}) async-start(f32[16,1,2048]{2,1,0:T(1,128)} %reshape.20), calls=%async_computation.1 | async-start | bytes 262144 | tf_op jit(solution)/shard_map/all_to_all | solution.py:305

commit v16 on v13

--- a/solution.py
+++ b/solution.py
@@ -122,7 +122,7 @@
         fc[7, i] = s_ref[i, pl.ds(zoff, nz), :]
         return carry
 
-    lax.fori_loop(0, nxe, align, 0, unroll=4)
+    lax.fori_loop(0, nxe, align, 0, unroll=True)
 
     def faces_row(i, carry):
         c = fc[7, i]
@@ -135,7 +135,7 @@
         fc[6, i] = diag + spring_term * c
         return carry
 
-    lax.fori_loop(1, nxe - 1, faces_row, 0, unroll=4)
+    lax.fori_loop(1, nxe - 1, faces_row, 0, unroll=True)
 
     def sweep(src, dst, weight, i):
         c, diag = fc[7, i], fc[6, i]
@@ -156,8 +156,8 @@
         sweep(u1, u2, second_weight, i)
         return carry
 
-    lax.fori_loop(1, nxe - 1, first, 0, unroll=4)
-    lax.fori_loop(2, nxe - 2, second, 0, unroll=4)
+    lax.fori_loop(1, nxe - 1, first, 0, unroll=True)
+    lax.fori_loop(2, nxe - 2, second, 0, unroll=True)
 
     def energy_row(i, carry):
         parts = []
@@ -172,7 +172,7 @@
         u1[0, i] = 0.25 * (parts[0] + parts[1] + parts[2])
         return carry
 
-    lax.fori_loop(m, m + bx, energy_row, 0, unroll=4)
+    lax.fori_loop(m, m + bx, energy_row, 0, unroll=True)
     energy_out[...] = u1[0, pl.ds(m, bx), pl.ds(lo, bz), :]
     disp_out[...] = u2[:, pl.ds(m, bx), pl.ds(lo, bz), :]
 

time: 128 us -> 128 us (level)
  no operation moved by 1% of the time
where the time goes in v16:
time: 128 us; the launch traced here: 127 us
  blocking collectives  35.8 us (28%)
  other arithmetic  25.3 us (20%)
  starting transfers between devices  24.3 us (19%)
  Pallas kernels  17.2 us (13%)
  waiting for transfers between devices  14 us (11%)
  local copies, waits for them, and re-layouts  9.39 us (7%)
    all_to_all x1, blocking collectives, on_device(): lax.all_to_all(coarse, 'gy', split_axis=1, concat_axis=2, tiled=True)  21.3 us
    all_to_all x1, blocking collectives, on_device(): lax.all_to_all(energy, 'gy', split_axis=2, concat_axis=1, tiled=True)  14.5 us
    ppermute x4, starting transfers between devices, padded_2(): lax.ppermute(lax.slice_in_dim(block, 0, width, axis=dim), axis, backward)  14.3 us
    sub x4, other arithmetic, advance(): chem = conc_pad - order_pad * order_pad * (3.0 - 2.0 * order_pad)  13.3 us
    ppermute x4, waiting for transfers between devices, padded_2(): lax.ppermute(lax.slice_in_dim(block, block.shape[dim] - width, None, axis...  12.3 us
    pallas_call x1, Pallas kernels, halo_exchange(): pl.pallas_call(functools.partial(halo_kernel, hx, nx, ny), out_shape=jax....  11.3 us
    ppermute x4, starting transfers between devices, padded_2(): lax.ppermute(lax.slice_in_dim(block, block.shape[dim] - width, None, axis...  10 us
    pallas_call x1, Pallas kernels, mechanics(): pl.pallas_call(functools.partial(mech_kernel, zoff), out_shape=(jax.Shape...  5.9 us
  transfers between devices with their start and end apart: 8, of which 3 were waited for; matrix products, arithmetic and copies ran while one was open for 4% of the time, Pallas kernels for 9%

profile of v16, /device:TPU:2, one launch (start us, length us, event | category | flops | bytes accessed | tf_op | source)
XLA Modules:
  0.0 127.5 jit_solution(7586997080831720596)
XLA Ops:
  0.7 1.6 %add_bitcast_fusion = f32[1,32,32,256]{3,2,1,0:T(8,128)S(1)} fusion(s32[32,32,256]{2,1,0:T(8,128)} %param.8), kind=kLoop, calls=%fused_computation.110 | loop fusion | flops 2097152 | bytes 2097152 | tf_op jit(solution)/shard_map/stack | solution.py:288
  2.3 0.2 copy-done.1
  2.5 0.1 pad_maximum_fusion.7
  2.6 2.1 %collective-permute-start = (f32[3,4,32,256]{3,2,1,0:T(8,128)S(1)}, f32[3,4,32,256]{3,2,1,0:T(8,128)S(1)}, u32[]{:S(2)}, u32[]{:S(2)}) collective-permute-start(f32[3,4,32,256]{3,2,1,0:T(8,128)S(1)} %get-tuple-element.54), channel_id=1, source_target_pairs={{0,16},{16,32},{32,48},{48,64},{64,80},{80,96},{96,112},{112,128},... | collective-permute-start | bytes 1179656 | tf_op jit(solution)/shard_map/ppermute | solution.py:198
  4.6 5.8 %collective-permute-start.1 = (f32[3,4,32,256]{3,2,1,0:T(8,128)S(1)}, f32[3,4,32,256]{3,2,1,0:T(8,128)S(1)}, u32[]{:S(2)}, u32[]{:S(2)}) collective-permute-start(f32[3,4,32,256]{3,2,1,0:T(8,128)S(1)} %get-tuple-element.55), channel_id=1, source_target_pairs={{16,0},{32,16},{48,32},{64,48},{80,64},{96,80},{112,96},{128,112},... | collective-permute-start | bytes 1179656 | tf_op jit(solution)/shard_map/ppermute | solution.py:201
  10.4 0.1 pad_maximum_fusion.4
  10.5 3.4 %collective-permute-done = f32[3,4,32,256]{3,2,1,0:T(8,128)S(1)} collective-permute-done((f32[3,4,32,256]{3,2,1,0:T(8,128)S(1)}, f32[3,4,32,256]{3,2,1,0:T(8,128)S(1)}, u32[]{:S(2)}, u32[]{:S(2)}) %collective-permute-start) | collective-permute-done | bytes 393248 | tf_op jit(solution)/shard_map/ppermute | solution.py:198
  13.9 1.8 %collective-permute-done.1 = f32[3,4,32,256]{3,2,1,0:T(8,128)S(1)} collective-permute-done((f32[3,4,32,256]{3,2,1,0:T(8,128)S(1)}, f32[3,4,32,256]{3,2,1,0:T(8,128)S(1)}, u32[]{:S(2)}, u32[]{:S(2)}) %collective-permute-start.1) | collective-permute-done | bytes 393248 | tf_op jit(solution)/shard_map/ppermute | solution.py:201
  15.7 0.4 pad_maximum_fusion.1
  16.1 0.2 fusion.64
  16.2 3.9 %collective-permute-start.2 = (f32[3,40,4,256]{3,2,1,0:T(4,128)S(1)}, f32[3,40,4,256]{3,2,1,0:T(4,128)S(1)}, u32[]{:S(2)}, u32[]{:S(2)}) collective-permute-start(f32[3,40,4,256]{3,2,1,0:T(4,128)S(1)} %get-tuple-element.52), channel_id=1, source_target_pairs={{0,1},{1,2},{2,3},{3,4},{4,5},{5,6},{6,7},{7,8},{8,9},{9,10},{10,1... | collective-permute-start | bytes 1474568 | tf_op jit(solution)/shard_map/ppermute | solution.py:198
  20.1 1.3 %collective-permute-start.3 = (f32[3,40,4,256]{3,2,1,0:T(4,128)S(1)}, f32[3,40,4,256]{3,2,1,0:T(4,128)S(1)}, u32[]{:S(2)}, u32[]{:S(2)}) collective-permute-start(f32[3,40,4,256]{3,2,1,0:T(4,128)S(1)} %get-tuple-element.53), channel_id=1, source_target_pairs={{1,0},{2,1},{3,2},{4,3},{5,4},{6,5},{7,6},{8,7},{9,8},{10,9},{11,1... | collective-permute-start | bytes 1474568 | tf_op jit(solution)/shard_map/ppermute | solution.py:201
  21.4 1.9 %collective-permute-start.4 = (f32[6,3,8,256]{3,2,1,0:T(8,128)S(1)}, f32[6,3,8,256]{3,2,1,0:T(8,128)S(1)}, u32[]{:S(2)}, u32[]{:S(2)}) collective-permute-start(f32[6,3,8,256]{3,2,1,0:T(8,128)S(1)} %get-tuple-element.60), channel_id=1, source_target_pairs={{0,16},{16,32},{32,48},{48,64},{64,80},{80,96},{96,112},{112,128},... | collective-permute-start | bytes 442376 | tf_op jit(solution)/shard_map/ppermute | solution.py:198
  23.4 5.8 %collective-permute-start.5 = (f32[6,3,8,256]{3,2,1,0:T(8,128)S(1)}, f32[6,3,8,256]{3,2,1,0:T(8,128)S(1)}, u32[]{:S(2)}, u32[]{:S(2)}) collective-permute-start(f32[6,3,8,256]{3,2,1,0:T(8,128)S(1)} %get-tuple-element.61), channel_id=1, source_target_pairs={{16,0},{32,16},{48,32},{64,48},{80,64},{96,80},{112,96},{128,112},... | collective-permute-start | bytes 442376 | tf_op jit(solution)/shard_map/ppermute | solution.py:201
  29.1 8.8 %collective-permute-done.4 = f32[6,3,8,256]{3,2,1,0:T(8,128)S(1)} collective-permute-done((f32[6,3,8,256]{3,2,1,0:T(8,128)S(1)}, f32[6,3,8,256]{3,2,1,0:T(8,128)S(1)}, u32[]{:S(2)}, u32[]{:S(2)}) %collective-permute-start.4) | collective-permute-done | bytes 147488 | tf_op jit(solution)/shard_map/ppermute | solution.py:198
  38.0 0.0 collective-permute-done.5
  38.0 0.1 pad_maximum_fusion.3
  38.1 0.9 pad_maximum_fusion
  39.0 0.3 slice_bitcast_fusion.1
  39.3 0.3 multiply_subtract_fusion
  39.6 4.5 %multiply_subtract_fusion.1 = (f32[38,38,256]{2,1,0:T(8,128)S(1)}, f32[38,38,256]{2,1,0:T(8,128)S(1)}, f32[38,38,256]{2,1,0:T(8,128)S(1)}) fusion(f32[40,40,256]{2,1,0:T(8,128)S(1)} %multiply_subtract_fusion, f32[40,40,256]{2,1,0:T(8,128)S(1)} %get-tuple-element.50, f32[40,40,256]{2,1,0:T(8,128)S(1)} %get-tuple-element.51, ...), kind=kLoop, calls=%fused_computation.43 | loop fusion | flops 13307904 | bytes 26390528 | tf_op jit(solution)/shard_map/sub | solution.py:216
  44.2 4.5 %multiply_subtract_fusion.2 = (f32[36,36,256]{2,1,0:T(8,128)S(1)}, f32[36,36,256]{2,1,0:T(8,128)S(1)}, f32[36,36,256]{2,1,0:T(8,128)S(1)}) fusion(f32[38,38,256]{2,1,0:T(8,128)S(1)} %get-tuple-element.46, f32[38,38,256]{2,1,0:T(8,128)S(1)} %get-tuple-element.47, f32[40,40,256]{2,1,0:T(8,128)S(1)} %get-tuple-element.51, f32[38,38,256]{2,1,0:T(8,128)S(1)} %get-tuple-element.48), kind=kLoop, calls=%fused_computation.64 | loop fusion | flops 11943936 | bytes 24788992 | tf_op jit(solution)/shard_map/sub | solution.py:216
  48.6 4.0 %multiply_subtract_fusion.3 = (f32[34,34,256]{2,1,0:T(8,128)S(1)}, f32[34,34,256]{2,1,0:T(8,128)S(1)}, f32[34,34,256]{2,1,0:T(8,128)S(1)}) fusion(f32[36,36,256]{2,1,0:T(8,128)S(1)} %get-tuple-element.43, f32[36,36,256]{2,1,0:T(8,128)S(1)} %get-tuple-element.44, f32[40,40,256]{2,1,0:T(8,128)S(1)} %get-tuple-element.51, f32[36,36,256]{2,1,0:T(8,128)S(1)} %get-tuple-element.45), kind=kLoop, calls=%fused_computation.85 | loop fusion | flops 10653696 | bytes 23212032 | tf_op jit(solution)/shard_map/sub | solution.py:216
  52.7 3.8 %fusion.56 = (f32[32,32,256]{2,1,0:T(8,128)S(1)}, f32[32,32,256]{2,1,0:T(8,128)}) fusion(f32[34,34,256]{2,1,0:T(8,128)S(1)} %get-tuple-element.41, f32[40,40,256]{2,1,0:T(8,128)S(1)} %get-tuple-element.51, f32[34,34,256]{2,1,0:T(8,128)S(1)} %get-tuple-element.40, f32[34,34,256]{2,1,0:T(8,128)S(1)} %get-tuple-element.42), kind=kLoop, calls=%fused_computation.102 | loop fusion | flops 7602176 | bytes 17465344 | tf_op jit(solution)/shard_map/add | solution.py:224
  56.5 1.3 %fusion.65 = (f32[6,22,4,256]{3,2,1,0:T(4,128)}, f32[6,22,4,256]{3,2,1,0:T(4,128)}) fusion(f32[6,22,8,256]{3,2,1,0:T(8,128)S(1)} %pad_maximum_fusion.3), kind=kLoop, calls=%fused_computation.118 | loop fusion | bytes 2162688 | tf_op jit(solution)/shard_map/slice | solution.py:199
  57.8 2.2 %collective-permute-start.6 = (f32[6,22,4,256]{3,2,1,0:T(4,128)}, f32[6,22,4,256]{3,2,1,0:T(4,128)}, u32[]{:S(2)}, u32[]{:S(2)}) collective-permute-start(f32[6,22,4,256]{3,2,1,0:T(4,128)} %get-tuple-element.58), channel_id=1, source_target_pairs={{0,1},{1,2},{2,3},{3,4},{4,5},{5,6},{6,7},{7,8},{8,9},{9,10},{10,1... | collective-permute-start | bytes 1622024 | tf_op jit(solution)/shard_map/ppermute | solution.py:198
  60.0 1.5 %collective-permute-start.7 = (f32[6,22,4,256]{3,2,1,0:T(4,128)}, f32[6,22,4,256]{3,2,1,0:T(4,128)}, u32[]{:S(2)}, u32[]{:S(2)}) collective-permute-start(f32[6,22,4,256]{3,2,1,0:T(4,128)} %get-tuple-element.59), channel_id=1, source_target_pairs={{1,0},{2,1},{3,2},{4,3},{5,4},{6,5},{7,6},{8,7},{9,8},{10,9},{11,1... | collective-permute-start | bytes 1622024 | tf_op jit(solution)/shard_map/ppermute | solution.py:201
  61.5 0.1 bitcast_reduce_fusion
  61.6 0.3 bitcast_reduce_fusion.1
  61.9 0.5 fusion.43
  62.4 0.5 copy.43
  62.9 0.4 reshape.18
  63.3 21.3 %all_to_all.33 = f32[16,1,2048]{2,1,0:T(1,128)S(1)} all-to-all(f32[16,1,2048]{2,1,0:T(1,128)S(1)} %reshape.18), channel_id=1, replica_groups=mesh['gx'=16,'gy'=16] {'gy'}, dimensions={0} | all-to-all | bytes 262144 | tf_op jit(solution)/shard_map/all_to_all | solution.py:303
  84.6 0.5 broadcast.141
  85.1 0.9 reduce
  86.0 0.4 reshape.19
  86.3 0.6 copy.45
  86.9 1.1 broadcast_in_dim.9.blk_ref
  88.0 11.3 %shard_map.93 = f32[1,22,24,256]{3,2,1,0:T(8,128)} custom-call(f32[1,16,8,256]{3,2,1,0:T(8,128)} %broadcast_in_dim.9.blk_ref), custom_call_target="tpu_custom_call" | custom-call | tf_op jit(solution)/shard_map/pallas_call | solution.py:94
  99.3 3.0 %pad_maximum_fusion.2.ub_ref = f32[6,22,16,256]{3,2,1,0:T(8,128)} fusion(f32[6,22,4,256]{3,2,1,0:T(4,128)} %collective-permute-done.7, f32[6,22,8,256]{3,2,1,0:T(8,128)S(1)} %pad_maximum_fusion.3, f32[6,22,4,256]{3,2,1,0:T(4,128)} %collective-permute-done.6), kind=kLoop, calls=%fused_computation.18 | loop fusion | flops 1081344 | bytes 4325376 | tf_op jit(solution)/shard_map/concatenate | solution.py:202
  102.2 5.9 %shard_map.94 = (f32[3,16,8,256]{3,2,1,0:T(8,128)}, f32[16,8,256]{2,1,0:T(8,128)}) custom-call(f32[22,24,256]{2,1,0:T(8,128)} %bitcast.47, f32[6,22,16,256]{3,2,1,0:T(8,128)} %pad_maximum_fusion.2.ub_ref), custom_call_target="tpu_custom_call" | custom-call | tf_op jit(solution)/shard_map/pallas_call | solution.py:182
  108.1 1.3 %copy.46 = f32[16,8,256]{0,1,2:T(8,128)S(1)} copy(f32[16,8,256]{2,1,0:T(8,128)} %get-tuple-element.15) | data formatting | bytes 262144 | tf_op jit(solution)/shard_map/pallas_call | solution.py:182
  109.5 0.4 reshape.20
  109.9 14.5 %all_to_all.34 = f32[16,1,2048]{2,1,0:T(1,128)S(1)} all-to-all(f32[16,1,2048]{2,1,0:T(1,128)S(1)} %reshape.20), channel_id=1, replica_groups=mesh['gx'=16,'gy'=16] {'gy'}, dimensions={0} | all-to-all | bytes 262144 | tf_op jit(solution)/shard_map/all_to_all | solution.py:307
  124.3 0.9 reduce.1
  125.2 0.4 reshape.21
  125.6 0.9 copy.47
  126.5 1.0 copy.48
  (16 shorter events, 0.1 us)
Async XLA Ops:
  0.6 1.7 %copy-start.2 = (f32[32,32,256]{2,1,0:T(8,128)S(1)}, f32[32,32,256]{2,1,0:T(8,128)}, u32[]{:S(2)}) copy-start(f32[32,32,256]{2,1,0:T(8,128)} %param.6) | copy-start | bytes 3145732
  0.6 1.8 %copy-start.1 = (f32[32,32,256]{2,1,0:T(8,128)S(1)}, f32[32,32,256]{2,1,0:T(8,128)}, u32[]{:S(2)}) copy-start(f32[32,32,256]{2,1,0:T(8,128)} %param.7) | copy-start | bytes 3145732
  2.5 7.9 %copy-start.3 = (f32[3,16,8,256]{3,2,1,0:T(8,128)S(1)}, f32[3,16,8,256]{3,2,1,0:T(8,128)}, u32[]{:S(2)}) copy-start(f32[3,16,8,256]{3,2,1,0:T(8,128)} %param.10) | copy-start | bytes 1179652
  2.5 7.9 %copy-start.4 = (f32[3,16,8,256]{3,2,1,0:T(8,128)S(1)}, f32[3,16,8,256]{3,2,1,0:T(8,128)}, u32[]{:S(2)}) copy-start(f32[3,16,8,256]{3,2,1,0:T(8,128)} %param.9) | copy-start | bytes 1179652
  2.6 11.3 %collective-permute-start = (f32[3,4,32,256]{3,2,1,0:T(8,128)S(1)}, f32[3,4,32,256]{3,2,1,0:T(8,128)S(1)}, u32[]{:S(2)}, u32[]{:S(2)}) collective-permute-start(f32[3,4,32,256]{3,2,1,0:T(8,128)S(1)} %get-tuple-element.54), channel_id=1, source_target_pairs={{0,16},{16,32},{32,48},{48,64},{64,80},{80,96},{96,112},{112,128},... | collective-permute-start | bytes 1179656 | tf_op jit(solution)/shard_map/ppermute | solution.py:198
  4.6 11.0 %collective-permute-start.1 = (f32[3,4,32,256]{3,2,1,0:T(8,128)S(1)}, f32[3,4,32,256]{3,2,1,0:T(8,128)S(1)}, u32[]{:S(2)}, u32[]{:S(2)}) collective-permute-start(f32[3,4,32,256]{3,2,1,0:T(8,128)S(1)} %get-tuple-element.55), channel_id=1, source_target_pairs={{16,0},{32,16},{48,32},{64,48},{80,64},{96,80},{112,96},{128,112},... | collective-permute-start | bytes 1179656 | tf_op jit(solution)/shard_map/ppermute | solution.py:201
  16.2 21.8 %collective-permute-start.2 = (f32[3,40,4,256]{3,2,1,0:T(4,128)S(1)}, f32[3,40,4,256]{3,2,1,0:T(4,128)S(1)}, u32[]{:S(2)}, u32[]{:S(2)}) collective-permute-start(f32[3,40,4,256]{3,2,1,0:T(4,128)S(1)} %get-tuple-element.52), channel_id=1, source_target_pairs={{0,1},{1,2},{2,3},{3,4},{4,5},{5,6},{6,7},{7,8},{8,9},{9,10},{10,1... | collective-permute-start | bytes 1474568 | tf_op jit(solution)/shard_map/ppermute | solution.py:198
  20.1 18.0 %collective-permute-start.3 = (f32[3,40,4,256]{3,2,1,0:T(4,128)S(1)}, f32[3,40,4,256]{3,2,1,0:T(4,128)S(1)}, u32[]{:S(2)}, u32[]{:S(2)}) collective-permute-start(f32[3,40,4,256]{3,2,1,0:T(4,128)S(1)} %get-tuple-element.53), channel_id=1, source_target_pairs={{1,0},{2,1},{3,2},{4,3},{5,4},{6,5},{7,6},{8,7},{9,8},{10,9},{11,1... | collective-permute-start | bytes 1474568 | tf_op jit(solution)/shard_map/ppermute | solution.py:201
  21.4 16.5 %collective-permute-start.4 = (f32[6,3,8,256]{3,2,1,0:T(8,128)S(1)}, f32[6,3,8,256]{3,2,1,0:T(8,128)S(1)}, u32[]{:S(2)}, u32[]{:S(2)}) collective-permute-start(f32[6,3,8,256]{3,2,1,0:T(8,128)S(1)} %get-tuple-element.60), channel_id=1, source_target_pairs={{0,16},{16,32},{32,48},{48,64},{64,80},{80,96},{96,112},{112,128},... | collective-permute-start | bytes 442376 | tf_op jit(solution)/shard_map/ppermute | solution.py:198
  23.4 14.6 %collective-permute-start.5 = (f32[6,3,8,256]{3,2,1,0:T(8,128)S(1)}, f32[6,3,8,256]{3,2,1,0:T(8,128)S(1)}, u32[]{:S(2)}, u32[]{:S(2)}) collective-permute-start(f32[6,3,8,256]{3,2,1,0:T(8,128)S(1)} %get-tuple-element.61), channel_id=1, source_target_pairs={{16,0},{32,16},{48,32},{64,48},{80,64},{96,80},{112,96},{128,112},... | collective-permute-start | bytes 442376 | tf_op jit(solution)/shard_map/ppermute | solution.py:201
  56.5 5.1 %copy-start = (f32[32,32,256]{2,1,0:T(8,128)}, f32[32,32,256]{2,1,0:T(8,128)S(1)}, u32[]{:S(2)}) copy-start(f32[32,32,256]{2,1,0:T(8,128)S(1)} %get-tuple-element.37) | copy-start | bytes 3145732
  57.8 4.1 %copy-start.5 = (f32[256,128,1]{1,0,2:T(8,128)S(1)}, f32[256,128,1]{1,0,2:T(8,128)}, u32[]{:S(2)}) copy-start(f32[256,128,1]{1,0,2:T(8,128)} %constant.36) | copy-start | bytes 393220
  57.8 41.5 %collective-permute-start.6 = (f32[6,22,4,256]{3,2,1,0:T(4,128)}, f32[6,22,4,256]{3,2,1,0:T(4,128)}, u32[]{:S(2)}, u32[]{:S(2)}) collective-permute-start(f32[6,22,4,256]{3,2,1,0:T(4,128)} %get-tuple-element.58), channel_id=1, source_target_pairs={{0,1},{1,2},{2,3},{3,4},{4,5},{5,6},{6,7},{7,8},{8,9},{9,10},{10,1... | collective-permute-start | bytes 1622024 | tf_op jit(solution)/shard_map/ppermute | solution.py:198
  60.0 39.3 %collective-permute-start.7 = (f32[6,22,4,256]{3,2,1,0:T(4,128)}, f32[6,22,4,256]{3,2,1,0:T(4,128)}, u32[]{:S(2)}, u32[]{:S(2)}) collective-permute-start(f32[6,22,4,256]{3,2,1,0:T(4,128)} %get-tuple-element.59), channel_id=1, source_target_pairs={{1,0},{2,1},{3,2},{4,3},{5,4},{6,5},{7,6},{8,7},{9,8},{10,9},{11,1... | collective-permute-start | bytes 1622024 | tf_op jit(solution)/shard_map/ppermute | solution.py:201

commit v17 on v16

--- a/solution.py
+++ b/solution.py
@@ -112,14 +112,20 @@
             jnp.where(lane == last, 0.0, pltpu.roll(v, last, 1)), jnp.where(lane == 0, 0.0, pltpu.roll(v, 1, 1)))
 
 
-def mech_kernel(zoff, s_ref, ub_ref, disp_out, energy_out, u1, u2, fc):
+def mech_kernel(zoff, s_ref, low_ref, mid_ref, high_ref, disp_out, energy_out, u1, u2, fc, ub_ref, z3):
     _, nxe, nz, _ = ub_ref.shape
     bx, bz = disp_out.shape[1], disp_out.shape[2]
     m = (nxe - bx) // 2
     lo = (nz - bz) // 2
+    t = mid_ref.shape[2]
 
     def align(i, carry):
         fc[7, i] = s_ref[i, pl.ds(zoff, nz), :]
+        for k in range(6):
+            z3[k, i, pl.ds(0, t), :] = low_ref[k, i]
+            z3[k, i, pl.ds(t, t), :] = mid_ref[k, i]
+            z3[k, i, pl.ds(2 * t, t), :] = high_ref[k, i]
+            ub_ref[k, i] = z3[k, i, pl.ds(zoff, nz), :]
         return carry
 
     lax.fori_loop(0, nxe, align, 0, unroll=True)
@@ -177,17 +183,18 @@
     disp_out[...] = u2[:, pl.ds(m, bx), pl.ds(lo, bz), :]
 
 
-def mechanics(stiff_ext, ub, zoff, bx, bz):
-    _, nxe, nz, ny = ub.shape
+def mechanics(stiff_ext, low, mid, high, zoff, nz, bx, bz):
+    _, nxe, t, ny = mid.shape
     return pl.pallas_call(
         functools.partial(mech_kernel, zoff),
         out_shape=(jax.ShapeDtypeStruct((3, bx, bz, ny), jnp.float32),
                    jax.ShapeDtypeStruct((bx, bz, ny), jnp.float32)),
-        in_specs=[pl.BlockSpec(memory_space=pltpu.VMEM)] * 2,
+        in_specs=[pl.BlockSpec(memory_space=pltpu.VMEM)] * 4,
         out_specs=(pl.BlockSpec(memory_space=pltpu.VMEM), pl.BlockSpec(memory_space=pltpu.VMEM)),
         scratch_shapes=[pltpu.VMEM((3, nxe, nz, ny), jnp.float32), pltpu.VMEM((3, nxe, nz, ny), jnp.float32),
-                        pltpu.VMEM((8, nxe, nz, ny), jnp.float32)],
-    )(stiff_ext, ub)
+                        pltpu.VMEM((8, nxe, nz, ny), jnp.float32), pltpu.VMEM((6, nxe, nz, ny), jnp.float32),
+                        pltpu.VMEM((6, nxe, 3 * t, ny), jnp.float32)],
+    )(stiff_ext, low, mid, high)
 
 
 def padded_2(block, sides, width):
@@ -296,14 +303,16 @@
         conc, order, mob = advance(conc, order, mob, step == STEPS - 1)
 
     order, ub = lax.optimization_barrier((order, ub))
-    ub = padded_2(ub, (("gy", 2),), m + 1)
-    disp, load = ub[:3], ub[3:]
+    count = lax.axis_size("gy")
+    forward = [(i, i + 1) for i in range(count - 1)]
+    ub_low = lax.ppermute(ub, "gy", forward)
+    ub_high = lax.ppermute(ub, "gy", [(b, a) for a, b in forward])
 
     coarse = restrict_xzy(order)
     stiff = lax.all_to_all(coarse, "gy", split_axis=1, concat_axis=2, tiled=True)
     stiff_ext = halo_exchange(stiff[None], m, 0)[0]
     bx, bz = stiff.shape[0], stiff.shape[1]
-    disp, energy = mechanics(stiff_ext, ub, TILE - (m + 1), bx, bz)
+    disp, energy = mechanics(stiff_ext, ub_low, ub, ub_high, TILE - (m + 1), bz + 2 * (m + 1), bx, bz)
     tiles = lax.all_to_all(energy, "gy", split_axis=2, concat_axis=1, tiled=True)
     return (conc, order, disp, jnp.transpose(tiles, (0, 2, 1)))
 

time: 128 us -> 135 us (1.055)
  blocking collectives: 35.8 us -> 45.7 us
  other arithmetic: 25.3 us -> 22.4 us
  Pallas kernels: 17.2 us -> 18.8 us
    all_to_all x1, blocking collectives: 21.3 us -> 29.4 us  [on_device(): lax.all_to_all(coarse, 'gy', split_axis=1, concat_axis=2, tiled=True)]
    ppermute x0 -> x2, starting transfers between devices: none -> 3.87 us  [the longest x1 2.41 us: on_device(): ub_low = lax.ppermute(ub, 'gy', forward)]
    concatenate x4 -> x3, other arithmetic: 4.35 us -> 1.39 us  [padded_2(): block = jnp.concatenate([low, block, high], axis=dim)]
    ppermute x4 -> x3, starting transfers between devices: 10 us -> 7.82 us  [padded_2(): lax.ppermute(lax.slice_in_dim(block, block.shape[dim] - width, None, axis...]
    all_to_all x1, blocking collectives: 14.5 us -> 16.3 us  [on_device(): lax.all_to_all(energy, 'gy', split_axis=2, concat_axis=1, tiled=True)]
    ppermute x4 -> x3, starting transfers between devices: 14.3 us -> 12.8 us  [padded_2(): lax.ppermute(lax.slice_in_dim(block, 0, width, axis=dim), axis, backward)]
    ppermute x4 -> x3, waiting for transfers between devices: 12.3 us -> 12.3 us  [padded_2(): lax.ppermute(lax.slice_in_dim(block, block.shape[dim] - width, None, axis...]
where the time goes in v17:
time: 135 us
  blocking collectives  45.7 us (34%)
  starting transfers between devices  24.5 us (18%)
  other arithmetic  22.4 us (17%)
  Pallas kernels  18.8 us (14%)
  waiting for transfers between devices  14 us (10%)
  local copies, waits for them, and re-layouts  8.1 us (6%)
    all_to_all x1, blocking collectives, on_device(): lax.all_to_all(coarse, 'gy', split_axis=1, concat_axis=2, tiled=True)  29.4 us
    all_to_all x1, blocking collectives, on_device(): lax.all_to_all(energy, 'gy', split_axis=2, concat_axis=1, tiled=True)  16.3 us
    sub x4, other arithmetic, advance(): chem = conc_pad - order_pad * order_pad * (3.0 - 2.0 * order_pad)  13.3 us
    ppermute x3, starting transfers between devices, padded_2(): lax.ppermute(lax.slice_in_dim(block, 0, width, axis=dim), axis, backward)  12.8 us
    pallas_call x1, Pallas kernels, halo_exchange(): pl.pallas_call(functools.partial(halo_kernel, hx, nx, ny), out_shape=jax....  12.4 us
    ppermute x3, waiting for transfers between devices, padded_2(): lax.ppermute(lax.slice_in_dim(block, block.shape[dim] - width, None, axis...  12.3 us
    ppermute x3, starting transfers between devices, padded_2(): lax.ppermute(lax.slice_in_dim(block, block.shape[dim] - width, None, axis...  7.82 us
    pallas_call x1, Pallas kernels, mechanics(): pl.pallas_call(functools.partial(mech_kernel, zoff), out_shape=(jax.Shape...  6.33 us
  transfers between devices with their start and end apart: 8, of which 3 were waited for; matrix products, arithmetic and copies ran while one was open for 4% of the time, Pallas kernels for 9%

profile of v17, /device:TPU:2, one launch (start us, length us, event | category | flops | bytes accessed | tf_op | source)
XLA Modules:
  0.0 135.0 jit_solution(835292803907929816)
XLA Ops:
  0.7 1.6 %add_bitcast_fusion = f32[1,32,32,256]{3,2,1,0:T(8,128)S(1)} fusion(s32[32,32,256]{2,1,0:T(8,128)} %param.8), kind=kLoop, calls=%fused_computation.109 | loop fusion | flops 2097152 | bytes 2097152 | tf_op jit(solution)/shard_map/stack | solution.py:295
  2.3 0.2 copy-done.2
  2.5 0.1 pad_maximum_fusion.6
  2.6 2.1 %collective-permute-start = (f32[3,4,32,256]{3,2,1,0:T(8,128)S(1)}, f32[3,4,32,256]{3,2,1,0:T(8,128)S(1)}, u32[]{:S(2)}, u32[]{:S(2)}) collective-permute-start(f32[3,4,32,256]{3,2,1,0:T(8,128)S(1)} %get-tuple-element.54), channel_id=1, source_target_pairs={{0,16},{16,32},{32,48},{48,64},{64,80},{80,96},{96,112},{112,128},... | collective-permute-start | bytes 1179656 | tf_op jit(solution)/shard_map/ppermute | solution.py:205
  4.6 5.8 %collective-permute-start.1 = (f32[3,4,32,256]{3,2,1,0:T(8,128)S(1)}, f32[3,4,32,256]{3,2,1,0:T(8,128)S(1)}, u32[]{:S(2)}, u32[]{:S(2)}) collective-permute-start(f32[3,4,32,256]{3,2,1,0:T(8,128)S(1)} %get-tuple-element.55), channel_id=1, source_target_pairs={{16,0},{32,16},{48,32},{64,48},{80,64},{96,80},{112,96},{128,112},... | collective-permute-start | bytes 1179656 | tf_op jit(solution)/shard_map/ppermute | solution.py:208
  10.4 0.1 pad_maximum_fusion.3
  10.5 3.4 %collective-permute-done = f32[3,4,32,256]{3,2,1,0:T(8,128)S(1)} collective-permute-done((f32[3,4,32,256]{3,2,1,0:T(8,128)S(1)}, f32[3,4,32,256]{3,2,1,0:T(8,128)S(1)}, u32[]{:S(2)}, u32[]{:S(2)}) %collective-permute-start) | collective-permute-done | bytes 393248 | tf_op jit(solution)/shard_map/ppermute | solution.py:205
  13.9 1.8 %collective-permute-done.1 = f32[3,4,32,256]{3,2,1,0:T(8,128)S(1)} collective-permute-done((f32[3,4,32,256]{3,2,1,0:T(8,128)S(1)}, f32[3,4,32,256]{3,2,1,0:T(8,128)S(1)}, u32[]{:S(2)}, u32[]{:S(2)}) %collective-permute-start.1) | collective-permute-done | bytes 393248 | tf_op jit(solution)/shard_map/ppermute | solution.py:208
  15.7 0.4 pad_maximum_fusion.1
  16.1 0.2 fusion.64
  16.2 3.9 %collective-permute-start.2 = (f32[3,40,4,256]{3,2,1,0:T(4,128)S(1)}, f32[3,40,4,256]{3,2,1,0:T(4,128)S(1)}, u32[]{:S(2)}, u32[]{:S(2)}) collective-permute-start(f32[3,40,4,256]{3,2,1,0:T(4,128)S(1)} %get-tuple-element.52), channel_id=1, source_target_pairs={{0,1},{1,2},{2,3},{3,4},{4,5},{5,6},{6,7},{7,8},{8,9},{9,10},{10,1... | collective-permute-start | bytes 1474568 | tf_op jit(solution)/shard_map/ppermute | solution.py:205
  20.1 1.3 collective-permute-start.3
  21.4 1.9 %collective-permute-start.4 = (f32[6,3,8,256]{3,2,1,0:T(8,128)S(1)}, f32[6,3,8,256]{3,2,1,0:T(8,128)S(1)}, u32[]{:S(2)}, u32[]{:S(2)}) collective-permute-start(f32[6,3,8,256]{3,2,1,0:T(8,128)S(1)} %get-tuple-element.58), channel_id=1, source_target_pairs={{0,16},{16,32},{32,48},{48,64},{64,80},{80,96},{96,112},{112,128},... | collective-permute-start | bytes 442376 | tf_op jit(solution)/shard_map/ppermute | solution.py:205
  23.4 5.8 %collective-permute-start.5 = (f32[6,3,8,256]{3,2,1,0:T(8,128)S(1)}, f32[6,3,8,256]{3,2,1,0:T(8,128)S(1)}, u32[]{:S(2)}, u32[]{:S(2)}) collective-permute-start(f32[6,3,8,256]{3,2,1,0:T(8,128)S(1)} %get-tuple-element.59), channel_id=1, source_target_pairs={{16,0},{32,16},{48,32},{64,48},{80,64},{96,80},{112,96},{128,112},... | collective-permute-start | bytes 442376 | tf_op jit(solution)/shard_map/ppermute | solution.py:208
  29.1 8.8 %collective-permute-done.4 = f32[6,3,8,256]{3,2,1,0:T(8,128)S(1)} collective-permute-done((f32[6,3,8,256]{3,2,1,0:T(8,128)S(1)}, f32[6,3,8,256]{3,2,1,0:T(8,128)S(1)}, u32[]{:S(2)}, u32[]{:S(2)}) %collective-permute-start.4) | collective-permute-done | bytes 147488 | tf_op jit(solution)/shard_map/ppermute | solution.py:205
  38.0 0.0 collective-permute-done.5
  38.0 0.1 pad_maximum_fusion.2.mid_ref
  38.1 0.0 collective-permute-done.3
  38.1 0.9 pad_maximum_fusion
  39.0 0.3 slice_bitcast_fusion.1
  39.4 0.3 multiply_subtract_fusion
  39.6 4.5 %multiply_subtract_fusion.1 = (f32[38,38,256]{2,1,0:T(8,128)S(1)}, f32[38,38,256]{2,1,0:T(8,128)S(1)}, f32[38,38,256]{2,1,0:T(8,128)S(1)}) fusion(f32[40,40,256]{2,1,0:T(8,128)S(1)} %multiply_subtract_fusion, f32[40,40,256]{2,1,0:T(8,128)S(1)} %get-tuple-element.50, f32[40,40,256]{2,1,0:T(8,128)S(1)} %get-tuple-element.51, ...), kind=kLoop, calls=%fused_computation.42 | loop fusion | flops 13307904 | bytes 26390528 | tf_op jit(solution)/shard_map/sub | solution.py:223
  44.2 4.5 %multiply_subtract_fusion.2 = (f32[36,36,256]{2,1,0:T(8,128)S(1)}, f32[36,36,256]{2,1,0:T(8,128)S(1)}, f32[36,36,256]{2,1,0:T(8,128)S(1)}) fusion(f32[38,38,256]{2,1,0:T(8,128)S(1)} %get-tuple-element.46, f32[38,38,256]{2,1,0:T(8,128)S(1)} %get-tuple-element.47, f32[40,40,256]{2,1,0:T(8,128)S(1)} %get-tuple-element.51, f32[38,38,256]{2,1,0:T(8,128)S(1)} %get-tuple-element.48), kind=kLoop, calls=%fused_computation.63 | loop fusion | flops 11943936 | bytes 24788992 | tf_op jit(solution)/shard_map/sub | solution.py:223
  48.6 4.0 %multiply_subtract_fusion.3 = (f32[34,34,256]{2,1,0:T(8,128)S(1)}, f32[34,34,256]{2,1,0:T(8,128)S(1)}, f32[34,34,256]{2,1,0:T(8,128)S(1)}) fusion(f32[36,36,256]{2,1,0:T(8,128)S(1)} %get-tuple-element.43, f32[36,36,256]{2,1,0:T(8,128)S(1)} %get-tuple-element.44, f32[40,40,256]{2,1,0:T(8,128)S(1)} %get-tuple-element.51, f32[36,36,256]{2,1,0:T(8,128)S(1)} %get-tuple-element.45), kind=kLoop, calls=%fused_computation.84 | loop fusion | flops 10653696 | bytes 23212032 | tf_op jit(solution)/shard_map/sub | solution.py:223
  52.7 3.8 %fusion.56 = (f32[32,32,256]{2,1,0:T(8,128)S(1)}, f32[32,32,256]{2,1,0:T(8,128)}) fusion(f32[34,34,256]{2,1,0:T(8,128)S(1)} %get-tuple-element.41, f32[40,40,256]{2,1,0:T(8,128)S(1)} %get-tuple-element.51, f32[34,34,256]{2,1,0:T(8,128)S(1)} %get-tuple-element.40, f32[34,34,256]{2,1,0:T(8,128)S(1)} %get-tuple-element.42), kind=kLoop, calls=%fused_computation.101 | loop fusion | flops 7602176 | bytes 17465344 | tf_op jit(solution)/shard_map/add | solution.py:231
  56.5 2.4 %collective-permute-start.6 = (f32[6,22,8,256]{3,2,1,0:T(8,128)S(1)}, f32[6,22,8,256]{3,2,1,0:T(8,128)}, u32[]{:S(2)}, u32[]{:S(2)}) collective-permute-start(f32[6,22,8,256]{3,2,1,0:T(8,128)S(1)} %pad_maximum_fusion.2.mid_ref), channel_id=1, source_target_pairs={{0,1},{1,2},{2,3},{3,4},{4,5},{5,6},{6,7},{7,8},{8,9},{9,10},{10,1... | collective-permute-start | bytes 3244040 | tf_op jit(solution)/shard_map/ppermute | solution.py:308
  58.9 1.5 %collective-permute-start.7 = (f32[6,22,8,256]{3,2,1,0:T(8,128)S(1)}, f32[6,22,8,256]{3,2,1,0:T(8,128)}, u32[]{:S(2)}, u32[]{:S(2)}) collective-permute-start(f32[6,22,8,256]{3,2,1,0:T(8,128)S(1)} %pad_maximum_fusion.2.mid_ref), channel_id=1, source_target_pairs={{1,0},{2,1},{3,2},{4,3},{5,4},{6,5},{7,6},{8,7},{9,8},{10,9},{11,1... | collective-permute-start | bytes 3244040 | tf_op jit(solution)/shard_map/ppermute | solution.py:309
  60.4 0.1 bitcast_reduce_fusion
  60.5 0.3 bitcast_reduce_fusion.1
  60.8 0.5 fusion.43
  61.3 0.5 copy.43
  61.8 0.4 reshape.18
  62.2 29.4 %all_to_all.33 = f32[16,1,2048]{2,1,0:T(1,128)S(1)} all-to-all(f32[16,1,2048]{2,1,0:T(1,128)S(1)} %reshape.18), channel_id=1, replica_groups=mesh['gx'=16,'gy'=16] {'gy'}, dimensions={0} | all-to-all | bytes 262144 | tf_op jit(solution)/shard_map/all_to_all | solution.py:312
  91.6 0.5 broadcast.141
  92.1 0.9 reduce
  93.0 0.4 reshape.19
  93.4 0.6 copy.45
  94.0 1.1 broadcast_in_dim.9.blk_ref
  95.0 12.4 %shard_map.93 = f32[1,22,24,256]{3,2,1,0:T(8,128)} custom-call(f32[1,16,8,256]{3,2,1,0:T(8,128)} %broadcast_in_dim.9.blk_ref), custom_call_target="tpu_custom_call" | custom-call | tf_op jit(solution)/shard_map/pallas_call | solution.py:94
  107.5 0.0 collective-permute-done.6.low_ref
  107.5 6.3 %shard_map.94 = (f32[3,16,8,256]{3,2,1,0:T(8,128)}, f32[16,8,256]{2,1,0:T(8,128)}) custom-call(f32[22,24,256]{2,1,0:T(8,128)} %bitcast.47, f32[6,22,8,256]{3,2,1,0:T(8,128)} %collective-permute-done.6.low_ref, f32[6,22,8,256]{3,2,1,0:T(8,128)} %copy-done, f32[6,22,8,256]{3,2,1,0:T(8,128)} %collective-permute-done.7.high_ref), custom_call_target="tpu_custom_call" | custom-call | tf_op jit(solution)/shard_map/pallas_call | solution.py:188
  113.8 1.3 copy.46
  115.2 0.4 reshape.20
  115.6 16.3 %all_to_all.34 = f32[16,1,2048]{2,1,0:T(1,128)S(1)} all-to-all(f32[16,1,2048]{2,1,0:T(1,128)S(1)} %reshape.20), channel_id=1, replica_groups=mesh['gx'=16,'gy'=16] {'gy'}, dimensions={0} | all-to-all | bytes 262144 | tf_op jit(solution)/shard_map/all_to_all | solution.py:316
  131.9 0.9 reduce.1
  132.7 0.4 reshape.21
  133.1 0.9 copy.47
  134.0 1.0 copy.48
  (16 shorter events, 0.1 us)
Async XLA Ops:
  0.6 1.7 %copy-start.3 = (f32[32,32,256]{2,1,0:T(8,128)S(1)}, f32[32,32,256]{2,1,0:T(8,128)}, u32[]{:S(2)}) copy-start(f32[32,32,256]{2,1,0:T(8,128)} %param.6) | copy-start | bytes 3145732
  0.6 1.8 %copy-start.2 = (f32[32,32,256]{2,1,0:T(8,128)S(1)}, f32[32,32,256]{2,1,0:T(8,128)}, u32[]{:S(2)}) copy-start(f32[32,32,256]{2,1,0:T(8,128)} %param.7) | copy-start | bytes 3145732
  2.5 7.9 %copy-start.4 = (f32[3,16,8,256]{3,2,1,0:T(8,128)S(1)}, f32[3,16,8,256]{3,2,1,0:T(8,128)}, u32[]{:S(2)}) copy-start(f32[3,16,8,256]{3,2,1,0:T(8,128)} %param.10) | copy-start | bytes 1179652
  2.5 7.9 %copy-start.5 = (f32[3,16,8,256]{3,2,1,0:T(8,128)S(1)}, f32[3,16,8,256]{3,2,1,0:T(8,128)}, u32[]{:S(2)}) copy-start(f32[3,16,8,256]{3,2,1,0:T(8,128)} %param.9) | copy-start | bytes 1179652
  2.6 11.3 %collective-permute-start = (f32[3,4,32,256]{3,2,1,0:T(8,128)S(1)}, f32[3,4,32,256]{3,2,1,0:T(8,128)S(1)}, u32[]{:S(2)}, u32[]{:S(2)}) collective-permute-start(f32[3,4,32,256]{3,2,1,0:T(8,128)S(1)} %get-tuple-element.54), channel_id=1, source_target_pairs={{0,16},{16,32},{32,48},{48,64},{64,80},{80,96},{96,112},{112,128},... | collective-permute-start | bytes 1179656 | tf_op jit(solution)/shard_map/ppermute | solution.py:205
  4.6 11.0 %collective-permute-start.1 = (f32[3,4,32,256]{3,2,1,0:T(8,128)S(1)}, f32[3,4,32,256]{3,2,1,0:T(8,128)S(1)}, u32[]{:S(2)}, u32[]{:S(2)}) collective-permute-start(f32[3,4,32,256]{3,2,1,0:T(8,128)S(1)} %get-tuple-element.55), channel_id=1, source_target_pairs={{16,0},{32,16},{48,32},{64,48},{80,64},{96,80},{112,96},{128,112},... | collective-permute-start | bytes 1179656 | tf_op jit(solution)/shard_map/ppermute | solution.py:208
  16.2 21.8 %collective-permute-start.2 = (f32[3,40,4,256]{3,2,1,0:T(4,128)S(1)}, f32[3,40,4,256]{3,2,1,0:T(4,128)S(1)}, u32[]{:S(2)}, u32[]{:S(2)}) collective-permute-start(f32[3,40,4,256]{3,2,1,0:T(4,128)S(1)} %get-tuple-element.52), channel_id=1, source_target_pairs={{0,1},{1,2},{2,3},{3,4},{4,5},{5,6},{6,7},{7,8},{8,9},{9,10},{10,1... | collective-permute-start | bytes 1474568 | tf_op jit(solution)/shard_map/ppermute | solution.py:205
  20.1 18.0 %collective-permute-start.3 = (f32[3,40,4,256]{3,2,1,0:T(4,128)S(1)}, f32[3,40,4,256]{3,2,1,0:T(4,128)S(1)}, u32[]{:S(2)}, u32[]{:S(2)}) collective-permute-start(f32[3,40,4,256]{3,2,1,0:T(4,128)S(1)} %get-tuple-element.53), channel_id=1, source_target_pairs={{1,0},{2,1},{3,2},{4,3},{5,4},{6,5},{7,6},{8,7},{9,8},{10,9},{11,1... | collective-permute-start | bytes 1474568 | tf_op jit(solution)/shard_map/ppermute | solution.py:208
  21.4 16.5 %collective-permute-start.4 = (f32[6,3,8,256]{3,2,1,0:T(8,128)S(1)}, f32[6,3,8,256]{3,2,1,0:T(8,128)S(1)}, u32[]{:S(2)}, u32[]{:S(2)}) collective-permute-start(f32[6,3,8,256]{3,2,1,0:T(8,128)S(1)} %get-tuple-element.58), channel_id=1, source_target_pairs={{0,16},{16,32},{32,48},{48,64},{64,80},{80,96},{96,112},{112,128},... | collective-permute-start | bytes 442376 | tf_op jit(solution)/shard_map/ppermute | solution.py:205
  23.4 14.6 %collective-permute-start.5 = (f32[6,3,8,256]{3,2,1,0:T(8,128)S(1)}, f32[6,3,8,256]{3,2,1,0:T(8,128)S(1)}, u32[]{:S(2)}, u32[]{:S(2)}) collective-permute-start(f32[6,3,8,256]{3,2,1,0:T(8,128)S(1)} %get-tuple-element.59), channel_id=1, source_target_pairs={{16,0},{32,16},{48,32},{64,48},{80,64},{96,80},{112,96},{128,112},... | collective-permute-start | bytes 442376 | tf_op jit(solution)/shard_map/ppermute | solution.py:208
  38.1 20.8 %copy-start = (f32[6,22,8,256]{3,2,1,0:T(8,128)}, f32[6,22,8,256]{3,2,1,0:T(8,128)S(1)}, u32[]{:S(2)}) copy-start(f32[6,22,8,256]{3,2,1,0:T(8,128)S(1)} %pad_maximum_fusion.2.mid_ref) | copy-start | bytes 3244036
  56.5 5.3 %copy-start.1 = (f32[32,32,256]{2,1,0:T(8,128)}, f32[32,32,256]{2,1,0:T(8,128)S(1)}, u32[]{:S(2)}) copy-start(f32[32,32,256]{2,1,0:T(8,128)S(1)} %get-tuple-element.37) | copy-start | bytes 3145732
  56.5 4.3 %copy-start.6 = (f32[256,128,1]{1,0,2:T(8,128)S(1)}, f32[256,128,1]{1,0,2:T(8,128)}, u32[]{:S(2)}) copy-start(f32[256,128,1]{1,0,2:T(8,128)} %constant.36) | copy-start | bytes 393220
  56.5 51.0 %collective-permute-start.6 = (f32[6,22,8,256]{3,2,1,0:T(8,128)S(1)}, f32[6,22,8,256]{3,2,1,0:T(8,128)}, u32[]{:S(2)}, u32[]{:S(2)}) collective-permute-start(f32[6,22,8,256]{3,2,1,0:T(8,128)S(1)} %pad_maximum_fusion.2.mid_ref), channel_id=1, source_target_pairs={{0,1},{1,2},{2,3},{3,4},{4,5},{5,6},{6,7},{7,8},{8,9},{9,10},{10,1... | collective-permute-start | bytes 3244040 | tf_op jit(solution)/shard_map/ppermute | solution.py:308
  58.9 48.6 %collective-permute-start.7 = (f32[6,22,8,256]{3,2,1,0:T(8,128)S(1)}, f32[6,22,8,256]{3,2,1,0:T(8,128)}, u32[]{:S(2)}, u32[]{:S(2)}) collective-permute-start(f32[6,22,8,256]{3,2,1,0:T(8,128)S(1)} %pad_maximum_fusion.2.mid_ref), channel_id=1, source_target_pairs={{1,0},{2,1},{3,2},{4,3},{5,4},{6,5},{7,6},{8,7},{9,8},{10,9},{11,1... | collective-permute-start | bytes 3244040 | tf_op jit(solution)/shard_map/ppermute | solution.py:309

commit v18 on v16

--- a/solution.py
+++ b/solution.py
@@ -287,10 +287,10 @@
     h = FINE_HALO
     fields = jnp.stack([concentration, order_field, mobility_of(phase_labels)])
     m = MECH_HALO
-    fields = padded_2(fields, (("gx", 1),), h)
+    fields = padded_2(fields, (("gy", 2),), h)
     fields, ub = lax.optimization_barrier((fields, jnp.concatenate([displacement, body_load])))
     ub = padded_2(ub, (("gx", 1),), m)
-    fields = padded_2(fields, (("gy", 2),), h)
+    fields = padded_2(fields, (("gx", 1),), h)
     conc, order, mob = fields[0], fields[1], fields[2]
     for step in range(STEPS):
         conc, order, mob = advance(conc, order, mob, step == STEPS - 1)

time: 128 us -> 131 us (1.023)
  waiting for transfers between devices: 14 us -> 17.1 us
    ppermute x4, waiting for transfers between devices: 1.76 us -> 8.35 us  [padded_2(): lax.ppermute(lax.slice_in_dim(block, 0, width, axis=dim), axis, backward)]
    ppermute x4, starting transfers between devices: 14.3 us -> 9.24 us  [padded_2(): lax.ppermute(lax.slice_in_dim(block, 0, width, axis=dim), axis, backward)]
    ppermute x4, starting transfers between devices: 10 us -> 14.2 us  [padded_2(): lax.ppermute(lax.slice_in_dim(block, block.shape[dim] - width, None, axis...]
    ppermute x4, waiting for transfers between devices: 12.3 us -> 8.71 us  [padded_2(): lax.ppermute(lax.slice_in_dim(block, block.shape[dim] - width, None, axis...]
    all_to_all x1, blocking collectives: 14.5 us -> 16 us  [on_device(): lax.all_to_all(energy, 'gy', split_axis=2, concat_axis=1, tiled=True)]
    concatenate x4 -> x3, other arithmetic: 4.35 us -> 3.75 us  [padded_2(): block = jnp.concatenate([low, block, high], axis=dim)]
    unnamed x17 -> x19, local copies, waits for them, and re-layouts: 2.66 us -> 3.02 us
  transfers between devices with their start and end apart: 8 -> 8, of which waited for: 3 -> 4; matrix products, arithmetic and copies ran while one was open for 4% -> 4% of each run, Pallas kernels for 9% -> 9%
where the time goes in v18:
time: 131 us
  blocking collectives  36.3 us (28%)
  other arithmetic  24.8 us (19%)
  starting transfers between devices  23.5 us (18%)
  Pallas kernels  17.9 us (14%)
  waiting for transfers between devices  17.1 us (13%)
  local copies, waits for them, and re-layouts  9.67 us (7%)
    all_to_all x1, blocking collectives, on_device(): lax.all_to_all(coarse, 'gy', split_axis=1, concat_axis=2, tiled=True)  20.3 us
    all_to_all x1, blocking collectives, on_device(): lax.all_to_all(energy, 'gy', split_axis=2, concat_axis=1, tiled=True)  16 us
    ppermute x4, starting transfers between devices, padded_2(): lax.ppermute(lax.slice_in_dim(block, block.shape[dim] - width, None, axis...  14.2 us
    sub x4, other arithmetic, advance(): chem = conc_pad - order_pad * order_pad * (3.0 - 2.0 * order_pad)  13.3 us
    pallas_call x1, Pallas kernels, halo_exchange(): pl.pallas_call(functools.partial(halo_kernel, hx, nx, ny), out_shape=jax....  12 us
    ppermute x4, starting transfers between devices, padded_2(): lax.ppermute(lax.slice_in_dim(block, 0, width, axis=dim), axis, backward)  9.24 us
    ppermute x4, waiting for transfers between devices, padded_2(): lax.ppermute(lax.slice_in_dim(block, block.shape[dim] - width, None, axis...  8.71 us
    ppermute x4, waiting for transfers between devices, padded_2(): lax.ppermute(lax.slice_in_dim(block, 0, width, axis=dim), axis, backward)  8.35 us
  transfers between devices with their start and end apart: 8, of which 4 were waited for; matrix products, arithmetic and copies ran while one was open for 4% of the time, Pallas kernels for 9%

profile of v18, /device:TPU:2, one launch (start us, length us, event | category | flops | bytes accessed | tf_op | source)
XLA Modules:
  0.0 130.6 jit_solution(13075127600376555784)
XLA Ops:
  0.7 1.6 %add_bitcast_fusion = f32[1,32,32,256]{3,2,1,0:T(8,128)S(1)} fusion(s32[32,32,256]{2,1,0:T(8,128)} %param.8), kind=kLoop, calls=%fused_computation.109 | loop fusion | flops 2097152 | bytes 2097152 | tf_op jit(solution)/shard_map/stack | solution.py:288
  2.3 0.2 copy-done.1
  2.5 0.1 pad_maximum_fusion.6
  2.6 4.0 %collective-permute-start = (f32[3,32,4,256]{3,2,1,0:T(4,128)S(1)}, f32[3,32,4,256]{3,2,1,0:T(4,128)S(1)}, u32[]{:S(2)}, u32[]{:S(2)}) collective-permute-start(f32[3,32,4,256]{3,2,1,0:T(4,128)S(1)} %get-tuple-element.54), channel_id=1, source_target_pairs={{0,1},{1,2},{2,3},{3,4},{4,5},{5,6},{6,7},{7,8},{8,9},{9,10},{10,1... | collective-permute-start | bytes 1179656 | tf_op jit(solution)/shard_map/ppermute | solution.py:198
  6.6 1.3 collective-permute-start.1
  7.9 0.1 pad_maximum_fusion.3
  8.0 6.9 %collective-permute-done = f32[3,32,4,256]{3,2,1,0:T(4,128)S(1)} collective-permute-done((f32[3,32,4,256]{3,2,1,0:T(4,128)S(1)}, f32[3,32,4,256]{3,2,1,0:T(4,128)S(1)}, u32[]{:S(2)}, u32[]{:S(2)}) %collective-permute-start) | collective-permute-done | bytes 393248 | tf_op jit(solution)/shard_map/ppermute | solution.py:198
  15.0 4.3 %collective-permute-done.1 = f32[3,32,4,256]{3,2,1,0:T(4,128)S(1)} collective-permute-done((f32[3,32,4,256]{3,2,1,0:T(4,128)S(1)}, f32[3,32,4,256]{3,2,1,0:T(4,128)S(1)}, u32[]{:S(2)}, u32[]{:S(2)}) %collective-permute-start.1) | collective-permute-done | bytes 393248 | tf_op jit(solution)/shard_map/ppermute | solution.py:201
  19.3 0.7 pad_maximum_fusion
  20.0 0.1 fusion.64
  20.0 1.9 %collective-permute-start.2 = (f32[3,4,40,256]{3,2,1,0:T(8,128)S(1)}, f32[3,4,40,256]{3,2,1,0:T(8,128)S(1)}, u32[]{:S(2)}, u32[]{:S(2)}) collective-permute-start(f32[3,4,40,256]{3,2,1,0:T(8,128)S(1)} %get-tuple-element.53), channel_id=1, source_target_pairs={{0,16},{16,32},{32,48},{48,64},{64,80},{80,96},{96,112},{112,128},... | collective-permute-start | bytes 1474568 | tf_op jit(solution)/shard_map/ppermute | solution.py:198
  22.0 3.6 %collective-permute-start.4 = (f32[6,3,8,256]{3,2,1,0:T(8,128)S(1)}, f32[6,3,8,256]{3,2,1,0:T(8,128)S(1)}, u32[]{:S(2)}, u32[]{:S(2)}) collective-permute-start(f32[6,3,8,256]{3,2,1,0:T(8,128)S(1)} %get-tuple-element.60), channel_id=1, source_target_pairs={{0,16},{16,32},{32,48},{48,64},{64,80},{80,96},{96,112},{112,128},... | collective-permute-start | bytes 442376 | tf_op jit(solution)/shard_map/ppermute | solution.py:198
  25.6 4.1 %collective-permute-start.5 = (f32[6,3,8,256]{3,2,1,0:T(8,128)S(1)}, f32[6,3,8,256]{3,2,1,0:T(8,128)S(1)}, u32[]{:S(2)}, u32[]{:S(2)}) collective-permute-start(f32[6,3,8,256]{3,2,1,0:T(8,128)S(1)} %get-tuple-element.61), channel_id=1, source_target_pairs={{16,0},{32,16},{48,32},{64,48},{80,64},{96,80},{112,96},{128,112},... | collective-permute-start | bytes 442376 | tf_op jit(solution)/shard_map/ppermute | solution.py:201
  29.7 2.4 %collective-permute-start.3 = (f32[3,4,40,256]{3,2,1,0:T(8,128)S(1)}, f32[3,4,40,256]{3,2,1,0:T(8,128)S(1)}, u32[]{:S(2)}, u32[]{:S(2)}) collective-permute-start(f32[3,4,40,256]{3,2,1,0:T(8,128)S(1)} %get-tuple-element.52), channel_id=1, source_target_pairs={{16,0},{32,16},{48,32},{64,48},{80,64},{96,80},{112,96},{128,112},... | collective-permute-start | bytes 1474568 | tf_op jit(solution)/shard_map/ppermute | solution.py:201
  32.1 1.8 %collective-permute-done.4 = f32[6,3,8,256]{3,2,1,0:T(8,128)S(1)} collective-permute-done((f32[6,3,8,256]{3,2,1,0:T(8,128)S(1)}, f32[6,3,8,256]{3,2,1,0:T(8,128)S(1)}, u32[]{:S(2)}, u32[]{:S(2)}) %collective-permute-start.4) | collective-permute-done | bytes 147488 | tf_op jit(solution)/shard_map/ppermute | solution.py:198
  33.9 0.1 pad_maximum_fusion.2
  34.0 0.3 constant_dynamic-update-slice_fusion.1
  34.4 4.0 %collective-permute-done.3 = f32[3,4,40,256]{3,2,1,0:T(8,128)S(1)} collective-permute-done((f32[3,4,40,256]{3,2,1,0:T(8,128)S(1)}, f32[3,4,40,256]{3,2,1,0:T(8,128)S(1)}, u32[]{:S(2)}, u32[]{:S(2)}) %collective-permute-start.3) | collective-permute-done | bytes 491552 | tf_op jit(solution)/shard_map/ppermute | solution.py:201
  38.5 0.3 slice_bitcast_fusion.1
  38.8 0.3 multiply_subtract_fusion
  39.1 4.5 %multiply_subtract_fusion.1 = (f32[38,38,256]{2,1,0:T(8,128)S(1)}, f32[38,38,256]{2,1,0:T(8,128)S(1)}, f32[38,38,256]{2,1,0:T(8,128)S(1)}) fusion(f32[40,40,256]{2,1,0:T(8,128)S(1)} %multiply_subtract_fusion, f32[40,40,256]{2,1,0:T(8,128)S(1)} %get-tuple-element.50, f32[40,40,256]{2,1,0:T(8,128)S(1)} %get-tuple-element.51, ...), kind=kLoop, calls=%fused_computation.42 | loop fusion | flops 13307904 | bytes 26390528 | tf_op jit(solution)/shard_map/sub | solution.py:216
  43.6 4.5 %multiply_subtract_fusion.2 = (f32[36,36,256]{2,1,0:T(8,128)S(1)}, f32[36,36,256]{2,1,0:T(8,128)S(1)}, f32[36,36,256]{2,1,0:T(8,128)S(1)}) fusion(f32[38,38,256]{2,1,0:T(8,128)S(1)} %get-tuple-element.46, f32[38,38,256]{2,1,0:T(8,128)S(1)} %get-tuple-element.47, f32[40,40,256]{2,1,0:T(8,128)S(1)} %get-tuple-element.51, f32[38,38,256]{2,1,0:T(8,128)S(1)} %get-tuple-element.48), kind=kLoop, calls=%fused_computation.63 | loop fusion | flops 11943936 | bytes 24788992 | tf_op jit(solution)/shard_map/sub | solution.py:216
  48.1 4.0 %multiply_subtract_fusion.3 = (f32[34,34,256]{2,1,0:T(8,128)S(1)}, f32[34,34,256]{2,1,0:T(8,128)S(1)}, f32[34,34,256]{2,1,0:T(8,128)S(1)}) fusion(f32[36,36,256]{2,1,0:T(8,128)S(1)} %get-tuple-element.43, f32[36,36,256]{2,1,0:T(8,128)S(1)} %get-tuple-element.44, f32[40,40,256]{2,1,0:T(8,128)S(1)} %get-tuple-element.51, f32[36,36,256]{2,1,0:T(8,128)S(1)} %get-tuple-element.45), kind=kLoop, calls=%fused_computation.84 | loop fusion | flops 10653696 | bytes 23212032 | tf_op jit(solution)/shard_map/sub | solution.py:216
  52.1 3.8 %fusion.56 = (f32[32,32,256]{2,1,0:T(8,128)S(1)}, f32[32,32,256]{2,1,0:T(8,128)}) fusion(f32[34,34,256]{2,1,0:T(8,128)S(1)} %get-tuple-element.41, f32[40,40,256]{2,1,0:T(8,128)S(1)} %get-tuple-element.51, f32[34,34,256]{2,1,0:T(8,128)S(1)} %get-tuple-element.40, f32[34,34,256]{2,1,0:T(8,128)S(1)} %get-tuple-element.42), kind=kLoop, calls=%fused_computation.101 | loop fusion | flops 7602176 | bytes 17465344 | tf_op jit(solution)/shard_map/add | solution.py:224
  55.9 1.3 fusion.65
  57.2 4.8 %collective-permute-start.6 = (f32[6,22,4,256]{3,2,1,0:T(4,128)}, f32[6,22,4,256]{3,2,1,0:T(4,128)}, u32[]{:S(2)}, u32[]{:S(2)}) collective-permute-start(f32[6,22,4,256]{3,2,1,0:T(4,128)} %get-tuple-element.58), channel_id=1, source_target_pairs={{0,1},{1,2},{2,3},{3,4},{4,5},{5,6},{6,7},{7,8},{8,9},{9,10},{10,1... | collective-permute-start | bytes 1622024 | tf_op jit(solution)/shard_map/ppermute | solution.py:198
  62.0 1.5 %collective-permute-start.7 = (f32[6,22,4,256]{3,2,1,0:T(4,128)}, f32[6,22,4,256]{3,2,1,0:T(4,128)}, u32[]{:S(2)}, u32[]{:S(2)}) collective-permute-start(f32[6,22,4,256]{3,2,1,0:T(4,128)} %get-tuple-element.59), channel_id=1, source_target_pairs={{1,0},{2,1},{3,2},{4,3},{5,4},{6,5},{7,6},{8,7},{9,8},{10,9},{11,1... | collective-permute-start | bytes 1622024 | tf_op jit(solution)/shard_map/ppermute | solution.py:201
  63.4 0.1 bitcast_reduce_fusion
  63.5 0.3 bitcast_reduce_fusion.1
  63.9 0.5 fusion.43
  64.3 0.5 copy.43
  64.8 0.4 reshape.18
  65.2 20.3 %all_to_all.33 = f32[16,1,2048]{2,1,0:T(1,128)S(1)} all-to-all(f32[16,1,2048]{2,1,0:T(1,128)S(1)} %reshape.18), channel_id=1, replica_groups=mesh['gx'=16,'gy'=16] {'gy'}, dimensions={0} | all-to-all | bytes 262144 | tf_op jit(solution)/shard_map/all_to_all | solution.py:303
  85.5 0.5 broadcast.141
  86.0 0.9 reduce
  86.9 0.4 reshape.19
  87.3 0.6 copy.45
  87.9 1.1 broadcast_in_dim.9.blk_ref
  88.9 12.0 %shard_map.93 = f32[1,22,24,256]{3,2,1,0:T(8,128)} custom-call(f32[1,16,8,256]{3,2,1,0:T(8,128)} %broadcast_in_dim.9.blk_ref), custom_call_target="tpu_custom_call" | custom-call | tf_op jit(solution)/shard_map/pallas_call | solution.py:94
  100.9 3.0 %pad_maximum_fusion.1.ub_ref = f32[6,22,16,256]{3,2,1,0:T(8,128)} fusion(f32[6,22,4,256]{3,2,1,0:T(4,128)} %collective-permute-done.7, f32[6,22,8,256]{3,2,1,0:T(8,128)S(1)} %pad_maximum_fusion.2, f32[6,22,4,256]{3,2,1,0:T(4,128)} %collective-permute-done.6), kind=kLoop, calls=%fused_computation.17 | loop fusion | flops 1081344 | bytes 4325376 | tf_op jit(solution)/shard_map/concatenate | solution.py:202
  103.9 5.9 %shard_map.94 = (f32[3,16,8,256]{3,2,1,0:T(8,128)}, f32[16,8,256]{2,1,0:T(8,128)}) custom-call(f32[22,24,256]{2,1,0:T(8,128)} %bitcast.47, f32[6,22,16,256]{3,2,1,0:T(8,128)} %pad_maximum_fusion.1.ub_ref), custom_call_target="tpu_custom_call" | custom-call | tf_op jit(solution)/shard_map/pallas_call | solution.py:182
  109.8 1.3 %copy.46 = f32[16,8,256]{0,1,2:T(8,128)S(1)} copy(f32[16,8,256]{2,1,0:T(8,128)} %get-tuple-element.15) | data formatting | bytes 262144 | tf_op jit(solution)/shard_map/pallas_call | solution.py:182
  111.1 0.4 reshape.20
  111.5 16.0 %all_to_all.34 = f32[16,1,2048]{2,1,0:T(1,128)S(1)} all-to-all(f32[16,1,2048]{2,1,0:T(1,128)S(1)} %reshape.20), channel_id=1, replica_groups=mesh['gx'=16,'gy'=16] {'gy'}, dimensions={0} | all-to-all | bytes 262144 | tf_op jit(solution)/shard_map/all_to_all | solution.py:307
  127.5 0.9 reduce.1
  128.4 0.4 reshape.21
  128.7 0.9 copy.47
  129.7 1.0 copy.48
  (18 shorter events, 0.1 us)
Async XLA Ops:
  0.6 1.7 %copy-start.2 = (f32[32,32,256]{2,1,0:T(8,128)S(1)}, f32[32,32,256]{2,1,0:T(8,128)}, u32[]{:S(2)}) copy-start(f32[32,32,256]{2,1,0:T(8,128)} %param.6) | copy-start | bytes 3145732
  0.6 1.8 %copy-start.1 = (f32[32,32,256]{2,1,0:T(8,128)S(1)}, f32[32,32,256]{2,1,0:T(8,128)}, u32[]{:S(2)}) copy-start(f32[32,32,256]{2,1,0:T(8,128)} %param.7) | copy-start | bytes 3145732
  2.5 5.4 %copy-start.3 = (f32[3,16,8,256]{3,2,1,0:T(8,128)S(1)}, f32[3,16,8,256]{3,2,1,0:T(8,128)}, u32[]{:S(2)}) copy-start(f32[3,16,8,256]{3,2,1,0:T(8,128)} %param.10) | copy-start | bytes 1179652
  2.5 5.4 %copy-start.4 = (f32[3,16,8,256]{3,2,1,0:T(8,128)S(1)}, f32[3,16,8,256]{3,2,1,0:T(8,128)}, u32[]{:S(2)}) copy-start(f32[3,16,8,256]{3,2,1,0:T(8,128)} %param.9) | copy-start | bytes 1179652
  2.6 12.3 %collective-permute-start = (f32[3,32,4,256]{3,2,1,0:T(4,128)S(1)}, f32[3,32,4,256]{3,2,1,0:T(4,128)S(1)}, u32[]{:S(2)}, u32[]{:S(2)}) collective-permute-start(f32[3,32,4,256]{3,2,1,0:T(4,128)S(1)} %get-tuple-element.54), channel_id=1, source_target_pairs={{0,1},{1,2},{2,3},{3,4},{4,5},{5,6},{6,7},{7,8},{8,9},{9,10},{10,1... | collective-permute-start | bytes 1179656 | tf_op jit(solution)/shard_map/ppermute | solution.py:198
  6.6 12.6 %collective-permute-start.1 = (f32[3,32,4,256]{3,2,1,0:T(4,128)S(1)}, f32[3,32,4,256]{3,2,1,0:T(4,128)S(1)}, u32[]{:S(2)}, u32[]{:S(2)}) collective-permute-start(f32[3,32,4,256]{3,2,1,0:T(4,128)S(1)} %get-tuple-element.55), channel_id=1, source_target_pairs={{1,0},{2,1},{3,2},{4,3},{5,4},{6,5},{7,6},{8,7},{9,8},{10,9},{11,1... | collective-permute-start | bytes 1179656 | tf_op jit(solution)/shard_map/ppermute | solution.py:201
  20.0 14.0 %collective-permute-start.2 = (f32[3,4,40,256]{3,2,1,0:T(8,128)S(1)}, f32[3,4,40,256]{3,2,1,0:T(8,128)S(1)}, u32[]{:S(2)}, u32[]{:S(2)}) collective-permute-start(f32[3,4,40,256]{3,2,1,0:T(8,128)S(1)} %get-tuple-element.53), channel_id=1, source_target_pairs={{0,16},{16,32},{32,48},{48,64},{64,80},{80,96},{96,112},{112,128},... | collective-permute-start | bytes 1474568 | tf_op jit(solution)/shard_map/ppermute | solution.py:198
  22.0 11.9 %collective-permute-start.4 = (f32[6,3,8,256]{3,2,1,0:T(8,128)S(1)}, f32[6,3,8,256]{3,2,1,0:T(8,128)S(1)}, u32[]{:S(2)}, u32[]{:S(2)}) collective-permute-start(f32[6,3,8,256]{3,2,1,0:T(8,128)S(1)} %get-tuple-element.60), channel_id=1, source_target_pairs={{0,16},{16,32},{32,48},{48,64},{64,80},{80,96},{96,112},{112,128},... | collective-permute-start | bytes 442376 | tf_op jit(solution)/shard_map/ppermute | solution.py:198
  25.6 8.3 %collective-permute-start.5 = (f32[6,3,8,256]{3,2,1,0:T(8,128)S(1)}, f32[6,3,8,256]{3,2,1,0:T(8,128)S(1)}, u32[]{:S(2)}, u32[]{:S(2)}) collective-permute-start(f32[6,3,8,256]{3,2,1,0:T(8,128)S(1)} %get-tuple-element.61), channel_id=1, source_target_pairs={{16,0},{32,16},{48,32},{64,48},{80,64},{96,80},{112,96},{128,112},... | collective-permute-start | bytes 442376 | tf_op jit(solution)/shard_map/ppermute | solution.py:201
  29.7 8.7 %collective-permute-start.3 = (f32[3,4,40,256]{3,2,1,0:T(8,128)S(1)}, f32[3,4,40,256]{3,2,1,0:T(8,128)S(1)}, u32[]{:S(2)}, u32[]{:S(2)}) collective-permute-start(f32[3,4,40,256]{3,2,1,0:T(8,128)S(1)} %get-tuple-element.52), channel_id=1, source_target_pairs={{16,0},{32,16},{48,32},{64,48},{80,64},{96,80},{112,96},{128,112},... | collective-permute-start | bytes 1474568 | tf_op jit(solution)/shard_map/ppermute | solution.py:201
  55.9 7.6 %copy-start = (f32[32,32,256]{2,1,0:T(8,128)}, f32[32,32,256]{2,1,0:T(8,128)S(1)}, u32[]{:S(2)}) copy-start(f32[32,32,256]{2,1,0:T(8,128)S(1)} %get-tuple-element.37) | copy-start | bytes 3145732
  57.2 6.6 %copy-start.5 = (f32[256,128,1]{1,0,2:T(8,128)S(1)}, f32[256,128,1]{1,0,2:T(8,128)}, u32[]{:S(2)}) copy-start(f32[256,128,1]{1,0,2:T(8,128)} %constant.36) | copy-start | bytes 393220
  57.2 43.7 %collective-permute-start.6 = (f32[6,22,4,256]{3,2,1,0:T(4,128)}, f32[6,22,4,256]{3,2,1,0:T(4,128)}, u32[]{:S(2)}, u32[]{:S(2)}) collective-permute-start(f32[6,22,4,256]{3,2,1,0:T(4,128)} %get-tuple-element.58), channel_id=1, source_target_pairs={{0,1},{1,2},{2,3},{3,4},{4,5},{5,6},{6,7},{7,8},{8,9},{9,10},{10,1... | collective-permute-start | bytes 1622024 | tf_op jit(solution)/shard_map/ppermute | solution.py:198
  62.0 39.0 %collective-permute-start.7 = (f32[6,22,4,256]{3,2,1,0:T(4,128)}, f32[6,22,4,256]{3,2,1,0:T(4,128)}, u32[]{:S(2)}, u32[]{:S(2)}) collective-permute-start(f32[6,22,4,256]{3,2,1,0:T(4,128)} %get-tuple-element.59), channel_id=1, source_target_pairs={{1,0},{2,1},{3,2},{4,3},{5,4},{6,5},{7,6},{8,7},{9,8},{10,9},{11,1... | collective-permute-start | bytes 1622024 | tf_op jit(solution)/shard_map/ppermute | solution.py:201

commit v19 on v16

--- a/solution.py
+++ b/solution.py
@@ -291,7 +291,7 @@
     fields, ub = lax.optimization_barrier((fields, jnp.concatenate([displacement, body_load])))
     ub = padded_2(ub, (("gx", 1),), m)
     fields = padded_2(fields, (("gy", 2),), h)
-    conc, order, mob = fields[0], fields[1], fields[2]
+    conc, order, mob = fields[0], fields[1], fields[2].astype(jnp.bfloat16)
     for step in range(STEPS):
         conc, order, mob = advance(conc, order, mob, step == STEPS - 1)
 

time: 128 us -> 128 us (level)
  no operation moved by 1% of the time
where the time goes in v19:
time: 128 us
  blocking collectives  35.8 us (28%)
  other arithmetic  25.6 us (20%)
  starting transfers between devices  24.3 us (19%)
  Pallas kernels  17.2 us (13%)
  waiting for transfers between devices  14 us (11%)
  local copies, waits for them, and re-layouts  9.36 us (7%)
    all_to_all x1, blocking collectives, on_device(): lax.all_to_all(coarse, 'gy', split_axis=1, concat_axis=2, tiled=True)  21.3 us
    all_to_all x1, blocking collectives, on_device(): lax.all_to_all(energy, 'gy', split_axis=2, concat_axis=1, tiled=True)  14.5 us
    ppermute x4, starting transfers between devices, padded_2(): lax.ppermute(lax.slice_in_dim(block, 0, width, axis=dim), axis, backward)  14.3 us
    sub x4, other arithmetic, advance(): chem = conc_pad - order_pad * order_pad * (3.0 - 2.0 * order_pad)  13.5 us
    ppermute x4, waiting for transfers between devices, padded_2(): lax.ppermute(lax.slice_in_dim(block, block.shape[dim] - width, None, axis...  12.3 us
    pallas_call x1, Pallas kernels, halo_exchange(): pl.pallas_call(functools.partial(halo_kernel, hx, nx, ny), out_shape=jax....  11.3 us
    ppermute x4, starting transfers between devices, padded_2(): lax.ppermute(lax.slice_in_dim(block, block.shape[dim] - width, None, axis...  10 us
    pallas_call x1, Pallas kernels, mechanics(): pl.pallas_call(functools.partial(mech_kernel, zoff), out_shape=(jax.Shape...  5.9 us
  transfers between devices with their start and end apart: 8, of which 3 were waited for; matrix products, arithmetic and copies ran while one was open for 4% of the time, Pallas kernels for 9%

profile of v19, /device:TPU:2, one launch (start us, length us, event | category | flops | bytes accessed | tf_op | source)
XLA Modules:
  0.0 127.7 jit_solution(5141352204321756242)
XLA Ops:
  0.7 1.6 %add_bitcast_fusion = f32[1,32,32,256]{3,2,1,0:T(8,128)S(1)} fusion(s32[32,32,256]{2,1,0:T(8,128)} %param.8), kind=kLoop, calls=%fused_computation.110 | loop fusion | flops 2097152 | bytes 2097152 | tf_op jit(solution)/shard_map/stack | solution.py:288
  2.3 0.2 copy-done.1
  2.5 0.1 pad_maximum_fusion.7
  2.6 2.1 %collective-permute-start = (f32[3,4,32,256]{3,2,1,0:T(8,128)S(1)}, f32[3,4,32,256]{3,2,1,0:T(8,128)S(1)}, u32[]{:S(2)}, u32[]{:S(2)}) collective-permute-start(f32[3,4,32,256]{3,2,1,0:T(8,128)S(1)} %get-tuple-element.53), channel_id=1, source_target_pairs={{0,16},{16,32},{32,48},{48,64},{64,80},{80,96},{96,112},{112,128},... | collective-permute-start | bytes 1179656 | tf_op jit(solution)/shard_map/ppermute | solution.py:198
  4.6 5.8 %collective-permute-start.1 = (f32[3,4,32,256]{3,2,1,0:T(8,128)S(1)}, f32[3,4,32,256]{3,2,1,0:T(8,128)S(1)}, u32[]{:S(2)}, u32[]{:S(2)}) collective-permute-start(f32[3,4,32,256]{3,2,1,0:T(8,128)S(1)} %get-tuple-element.54), channel_id=1, source_target_pairs={{16,0},{32,16},{48,32},{64,48},{80,64},{96,80},{112,96},{128,112},... | collective-permute-start | bytes 1179656 | tf_op jit(solution)/shard_map/ppermute | solution.py:201
  10.4 0.1 pad_maximum_fusion.4
  10.5 3.4 %collective-permute-done = f32[3,4,32,256]{3,2,1,0:T(8,128)S(1)} collective-permute-done((f32[3,4,32,256]{3,2,1,0:T(8,128)S(1)}, f32[3,4,32,256]{3,2,1,0:T(8,128)S(1)}, u32[]{:S(2)}, u32[]{:S(2)}) %collective-permute-start) | collective-permute-done | bytes 393248 | tf_op jit(solution)/shard_map/ppermute | solution.py:198
  13.9 1.8 %collective-permute-done.1 = f32[3,4,32,256]{3,2,1,0:T(8,128)S(1)} collective-permute-done((f32[3,4,32,256]{3,2,1,0:T(8,128)S(1)}, f32[3,4,32,256]{3,2,1,0:T(8,128)S(1)}, u32[]{:S(2)}, u32[]{:S(2)}) %collective-permute-start.1) | collective-permute-done | bytes 393248 | tf_op jit(solution)/shard_map/ppermute | solution.py:201
  15.7 0.4 pad_maximum_fusion.1
  16.1 0.2 fusion.65
  16.2 3.9 %collective-permute-start.2 = (f32[3,40,4,256]{3,2,1,0:T(4,128)S(1)}, f32[3,40,4,256]{3,2,1,0:T(4,128)S(1)}, u32[]{:S(2)}, u32[]{:S(2)}) collective-permute-start(f32[3,40,4,256]{3,2,1,0:T(4,128)S(1)} %get-tuple-element.51), channel_id=1, source_target_pairs={{0,1},{1,2},{2,3},{3,4},{4,5},{5,6},{6,7},{7,8},{8,9},{9,10},{10,1... | collective-permute-start | bytes 1474568 | tf_op jit(solution)/shard_map/ppermute | solution.py:198
  20.1 1.3 %collective-permute-start.3 = (f32[3,40,4,256]{3,2,1,0:T(4,128)S(1)}, f32[3,40,4,256]{3,2,1,0:T(4,128)S(1)}, u32[]{:S(2)}, u32[]{:S(2)}) collective-permute-start(f32[3,40,4,256]{3,2,1,0:T(4,128)S(1)} %get-tuple-element.52), channel_id=1, source_target_pairs={{1,0},{2,1},{3,2},{4,3},{5,4},{6,5},{7,6},{8,7},{9,8},{10,9},{11,1... | collective-permute-start | bytes 1474568 | tf_op jit(solution)/shard_map/ppermute | solution.py:201
  21.4 1.9 %collective-permute-start.4 = (f32[6,3,8,256]{3,2,1,0:T(8,128)S(1)}, f32[6,3,8,256]{3,2,1,0:T(8,128)S(1)}, u32[]{:S(2)}, u32[]{:S(2)}) collective-permute-start(f32[6,3,8,256]{3,2,1,0:T(8,128)S(1)} %get-tuple-element.59), channel_id=1, source_target_pairs={{0,16},{16,32},{32,48},{48,64},{64,80},{80,96},{96,112},{112,128},... | collective-permute-start | bytes 442376 | tf_op jit(solution)/shard_map/ppermute | solution.py:198
  23.4 5.8 %collective-permute-start.5 = (f32[6,3,8,256]{3,2,1,0:T(8,128)S(1)}, f32[6,3,8,256]{3,2,1,0:T(8,128)S(1)}, u32[]{:S(2)}, u32[]{:S(2)}) collective-permute-start(f32[6,3,8,256]{3,2,1,0:T(8,128)S(1)} %get-tuple-element.60), channel_id=1, source_target_pairs={{16,0},{32,16},{48,32},{64,48},{80,64},{96,80},{112,96},{128,112},... | collective-permute-start | bytes 442376 | tf_op jit(solution)/shard_map/ppermute | solution.py:201
  29.1 8.8 %collective-permute-done.4 = f32[6,3,8,256]{3,2,1,0:T(8,128)S(1)} collective-permute-done((f32[6,3,8,256]{3,2,1,0:T(8,128)S(1)}, f32[6,3,8,256]{3,2,1,0:T(8,128)S(1)}, u32[]{:S(2)}, u32[]{:S(2)}) %collective-permute-start.4) | collective-permute-done | bytes 147488 | tf_op jit(solution)/shard_map/ppermute | solution.py:198
  38.0 0.1 pad_maximum_fusion.3
  38.1 0.9 pad_maximum_fusion
  39.0 0.1 fusion.57
  39.1 0.2 slice_bitcast_fusion.1
  39.3 0.3 multiply_subtract_fusion
  39.6 4.6 %multiply_subtract_fusion.1 = (f32[38,38,256]{2,1,0:T(8,128)S(1)}, f32[38,38,256]{2,1,0:T(8,128)S(1)}, f32[38,38,256]{2,1,0:T(8,128)S(1)}) fusion(f32[40,40,256]{2,1,0:T(8,128)S(1)} %multiply_subtract_fusion, f32[40,40,256]{2,1,0:T(8,128)S(1)} %get-tuple-element.50, bf16[40,40,256]{2,1,0:T(8,128)(2,1)S(1)} %fusion.57, f32[40,40,256]{2,1,0:T(8,128)S(1)} %get-tuple-element.49), kind=kLoop, calls=%fused_computation.43 | loop fusion | flops 13677568 | bytes 25612288 | tf_op jit(solution)/shard_map/sub | solution.py:216
  44.2 4.5 %multiply_subtract_fusion.2 = (f32[36,36,256]{2,1,0:T(8,128)S(1)}, f32[36,36,256]{2,1,0:T(8,128)S(1)}, f32[36,36,256]{2,1,0:T(8,128)S(1)}) fusion(f32[38,38,256]{2,1,0:T(8,128)S(1)} %get-tuple-element.46, f32[38,38,256]{2,1,0:T(8,128)S(1)} %get-tuple-element.47, bf16[40,40,256]{2,1,0:T(8,128)(2,1)S(1)} %fusion.57, f32[38,38,256]{2,1,0:T(8,128)S(1)} %get-tuple-element.48), kind=kLoop, calls=%fused_computation.64 | loop fusion | flops 12275712 | bytes 24051712 | tf_op jit(solution)/shard_map/sub | solution.py:216
  48.7 4.2 %multiply_subtract_fusion.3 = (f32[34,34,256]{2,1,0:T(8,128)S(1)}, f32[34,34,256]{2,1,0:T(8,128)S(1)}, f32[34,34,256]{2,1,0:T(8,128)S(1)}) fusion(f32[36,36,256]{2,1,0:T(8,128)S(1)} %get-tuple-element.43, f32[36,36,256]{2,1,0:T(8,128)S(1)} %get-tuple-element.44, bf16[40,40,256]{2,1,0:T(8,128)(2,1)S(1)} %fusion.57, f32[36,36,256]{2,1,0:T(8,128)S(1)} %get-tuple-element.45), kind=kLoop, calls=%fused_computation.85 | loop fusion | flops 10949632 | bytes 22515712 | tf_op jit(solution)/shard_map/sub | solution.py:216
  52.9 3.9 %fusion.56 = (f32[32,32,256]{2,1,0:T(8,128)S(1)}, f32[32,32,256]{2,1,0:T(8,128)}) fusion(f32[34,34,256]{2,1,0:T(8,128)S(1)} %get-tuple-element.41, f32[34,34,256]{2,1,0:T(8,128)S(1)} %get-tuple-element.40, bf16[40,40,256]{2,1,0:T(8,128)(2,1)S(1)} %fusion.57, f32[34,34,256]{2,1,0:T(8,128)S(1)} %get-tuple-element.42), kind=kLoop, calls=%fused_computation.102 | loop fusion | flops 7864320 | bytes 16941056 | tf_op jit(solution)/shard_map/add | solution.py:224
  56.7 1.3 %fusion.66 = (f32[6,22,4,256]{3,2,1,0:T(4,128)}, f32[6,22,4,256]{3,2,1,0:T(4,128)}) fusion(f32[6,22,8,256]{3,2,1,0:T(8,128)S(1)} %pad_maximum_fusion.3), kind=kLoop, calls=%fused_computation.119 | loop fusion | bytes 2162688 | tf_op jit(solution)/shard_map/slice | solution.py:199
  58.0 2.2 %collective-permute-start.6 = (f32[6,22,4,256]{3,2,1,0:T(4,128)}, f32[6,22,4,256]{3,2,1,0:T(4,128)}, u32[]{:S(2)}, u32[]{:S(2)}) collective-permute-start(f32[6,22,4,256]{3,2,1,0:T(4,128)} %get-tuple-element.57), channel_id=1, source_target_pairs={{0,1},{1,2},{2,3},{3,4},{4,5},{5,6},{6,7},{7,8},{8,9},{9,10},{10,1... | collective-permute-start | bytes 1622024 | tf_op jit(solution)/shard_map/ppermute | solution.py:198
  60.3 1.5 %collective-permute-start.7 = (f32[6,22,4,256]{3,2,1,0:T(4,128)}, f32[6,22,4,256]{3,2,1,0:T(4,128)}, u32[]{:S(2)}, u32[]{:S(2)}) collective-permute-start(f32[6,22,4,256]{3,2,1,0:T(4,128)} %get-tuple-element.58), channel_id=1, source_target_pairs={{1,0},{2,1},{3,2},{4,3},{5,4},{6,5},{7,6},{8,7},{9,8},{10,9},{11,1... | collective-permute-start | bytes 1622024 | tf_op jit(solution)/shard_map/ppermute | solution.py:201
  61.7 0.1 bitcast_reduce_fusion
  61.8 0.3 bitcast_reduce_fusion.1
  62.2 0.5 fusion.43
  62.6 0.5 copy.43
  63.1 0.4 reshape.19
  63.5 21.3 %all_to_all.33 = f32[16,1,2048]{2,1,0:T(1,128)S(1)} all-to-all(f32[16,1,2048]{2,1,0:T(1,128)S(1)} %reshape.19), channel_id=1, replica_groups=mesh['gx'=16,'gy'=16] {'gy'}, dimensions={0} | all-to-all | bytes 262144 | tf_op jit(solution)/shard_map/all_to_all | solution.py:303
  84.8 0.5 broadcast.141
  85.4 0.9 reduce
  86.2 0.4 reshape.20
  86.6 0.6 copy.45
  87.2 1.1 broadcast_in_dim.18.blk_ref
  88.3 11.3 %shard_map.93 = f32[1,22,24,256]{3,2,1,0:T(8,128)} custom-call(f32[1,16,8,256]{3,2,1,0:T(8,128)} %broadcast_in_dim.18.blk_ref), custom_call_target="tpu_custom_call" | custom-call | tf_op jit(solution)/shard_map/pallas_call | solution.py:94
  99.6 3.0 %pad_maximum_fusion.2.ub_ref = f32[6,22,16,256]{3,2,1,0:T(8,128)} fusion(f32[6,22,4,256]{3,2,1,0:T(4,128)} %collective-permute-done.7, f32[6,22,8,256]{3,2,1,0:T(8,128)S(1)} %pad_maximum_fusion.3, f32[6,22,4,256]{3,2,1,0:T(4,128)} %collective-permute-done.6), kind=kLoop, calls=%fused_computation.18 | loop fusion | flops 1081344 | bytes 4325376 | tf_op jit(solution)/shard_map/concatenate | solution.py:202
  102.5 5.9 %shard_map.94 = (f32[3,16,8,256]{3,2,1,0:T(8,128)}, f32[16,8,256]{2,1,0:T(8,128)}) custom-call(f32[22,24,256]{2,1,0:T(8,128)} %bitcast.47, f32[6,22,16,256]{3,2,1,0:T(8,128)} %pad_maximum_fusion.2.ub_ref), custom_call_target="tpu_custom_call" | custom-call | tf_op jit(solution)/shard_map/pallas_call | solution.py:182
  108.4 1.3 %copy.46 = f32[16,8,256]{0,1,2:T(8,128)S(1)} copy(f32[16,8,256]{2,1,0:T(8,128)} %get-tuple-element.15) | data formatting | bytes 262144 | tf_op jit(solution)/shard_map/pallas_call | solution.py:182
  109.7 0.4 reshape.21
  110.1 14.5 %all_to_all.34 = f32[16,1,2048]{2,1,0:T(1,128)S(1)} all-to-all(f32[16,1,2048]{2,1,0:T(1,128)S(1)} %reshape.21), channel_id=1, replica_groups=mesh['gx'=16,'gy'=16] {'gy'}, dimensions={0} | all-to-all | bytes 262144 | tf_op jit(solution)/shard_map/all_to_all | solution.py:307
  124.6 0.9 reduce.1
  125.5 0.4 reshape.22
  125.8 0.9 copy.47
  126.8 1.0 copy.48
  (17 shorter events, 0.1 us)
Async XLA Ops:
  0.6 1.7 %copy-start.2 = (f32[32,32,256]{2,1,0:T(8,128)S(1)}, f32[32,32,256]{2,1,0:T(8,128)}, u32[]{:S(2)}) copy-start(f32[32,32,256]{2,1,0:T(8,128)} %param.6) | copy-start | bytes 3145732
  0.6 1.8 %copy-start.1 = (f32[32,32,256]{2,1,0:T(8,128)S(1)}, f32[32,32,256]{2,1,0:T(8,128)}, u32[]{:S(2)}) copy-start(f32[32,32,256]{2,1,0:T(8,128)} %param.7) | copy-start | bytes 3145732
  2.5 7.9 %copy-start.3 = (f32[3,16,8,256]{3,2,1,0:T(8,128)S(1)}, f32[3,16,8,256]{3,2,1,0:T(8,128)}, u32[]{:S(2)}) copy-start(f32[3,16,8,256]{3,2,1,0:T(8,128)} %param.10) | copy-start | bytes 1179652
  2.5 7.9 %copy-start.4 = (f32[3,16,8,256]{3,2,1,0:T(8,128)S(1)}, f32[3,16,8,256]{3,2,1,0:T(8,128)}, u32[]{:S(2)}) copy-start(f32[3,16,8,256]{3,2,1,0:T(8,128)} %param.9) | copy-start | bytes 1179652
  2.6 11.3 %collective-permute-start = (f32[3,4,32,256]{3,2,1,0:T(8,128)S(1)}, f32[3,4,32,256]{3,2,1,0:T(8,128)S(1)}, u32[]{:S(2)}, u32[]{:S(2)}) collective-permute-start(f32[3,4,32,256]{3,2,1,0:T(8,128)S(1)} %get-tuple-element.53), channel_id=1, source_target_pairs={{0,16},{16,32},{32,48},{48,64},{64,80},{80,96},{96,112},{112,128},... | collective-permute-start | bytes 1179656 | tf_op jit(solution)/shard_map/ppermute | solution.py:198
  4.6 11.0 %collective-permute-start.1 = (f32[3,4,32,256]{3,2,1,0:T(8,128)S(1)}, f32[3,4,32,256]{3,2,1,0:T(8,128)S(1)}, u32[]{:S(2)}, u32[]{:S(2)}) collective-permute-start(f32[3,4,32,256]{3,2,1,0:T(8,128)S(1)} %get-tuple-element.54), channel_id=1, source_target_pairs={{16,0},{32,16},{48,32},{64,48},{80,64},{96,80},{112,96},{128,112},... | collective-permute-start | bytes 1179656 | tf_op jit(solution)/shard_map/ppermute | solution.py:201
  16.2 21.8 %collective-permute-start.2 = (f32[3,40,4,256]{3,2,1,0:T(4,128)S(1)}, f32[3,40,4,256]{3,2,1,0:T(4,128)S(1)}, u32[]{:S(2)}, u32[]{:S(2)}) collective-permute-start(f32[3,40,4,256]{3,2,1,0:T(4,128)S(1)} %get-tuple-element.51), channel_id=1, source_target_pairs={{0,1},{1,2},{2,3},{3,4},{4,5},{5,6},{6,7},{7,8},{8,9},{9,10},{10,1... | collective-permute-start | bytes 1474568 | tf_op jit(solution)/shard_map/ppermute | solution.py:198
  20.1 18.0 %collective-permute-start.3 = (f32[3,40,4,256]{3,2,1,0:T(4,128)S(1)}, f32[3,40,4,256]{3,2,1,0:T(4,128)S(1)}, u32[]{:S(2)}, u32[]{:S(2)}) collective-permute-start(f32[3,40,4,256]{3,2,1,0:T(4,128)S(1)} %get-tuple-element.52), channel_id=1, source_target_pairs={{1,0},{2,1},{3,2},{4,3},{5,4},{6,5},{7,6},{8,7},{9,8},{10,9},{11,1... | collective-permute-start | bytes 1474568 | tf_op jit(solution)/shard_map/ppermute | solution.py:201
  21.4 16.5 %collective-permute-start.4 = (f32[6,3,8,256]{3,2,1,0:T(8,128)S(1)}, f32[6,3,8,256]{3,2,1,0:T(8,128)S(1)}, u32[]{:S(2)}, u32[]{:S(2)}) collective-permute-start(f32[6,3,8,256]{3,2,1,0:T(8,128)S(1)} %get-tuple-element.59), channel_id=1, source_target_pairs={{0,16},{16,32},{32,48},{48,64},{64,80},{80,96},{96,112},{112,128},... | collective-permute-start | bytes 442376 | tf_op jit(solution)/shard_map/ppermute | solution.py:198
  23.4 14.6 %collective-permute-start.5 = (f32[6,3,8,256]{3,2,1,0:T(8,128)S(1)}, f32[6,3,8,256]{3,2,1,0:T(8,128)S(1)}, u32[]{:S(2)}, u32[]{:S(2)}) collective-permute-start(f32[6,3,8,256]{3,2,1,0:T(8,128)S(1)} %get-tuple-element.60), channel_id=1, source_target_pairs={{16,0},{32,16},{48,32},{64,48},{80,64},{96,80},{112,96},{128,112},... | collective-permute-start | bytes 442376 | tf_op jit(solution)/shard_map/ppermute | solution.py:201
  56.7 5.1 %copy-start = (f32[32,32,256]{2,1,0:T(8,128)}, f32[32,32,256]{2,1,0:T(8,128)S(1)}, u32[]{:S(2)}) copy-start(f32[32,32,256]{2,1,0:T(8,128)S(1)} %get-tuple-element.37) | copy-start | bytes 3145732
  58.0 4.1 %copy-start.5 = (f32[256,128,1]{1,0,2:T(8,128)S(1)}, f32[256,128,1]{1,0,2:T(8,128)}, u32[]{:S(2)}) copy-start(f32[256,128,1]{1,0,2:T(8,128)} %constant.74) | copy-start | bytes 393220
  58.0 41.5 %collective-permute-start.6 = (f32[6,22,4,256]{3,2,1,0:T(4,128)}, f32[6,22,4,256]{3,2,1,0:T(4,128)}, u32[]{:S(2)}, u32[]{:S(2)}) collective-permute-start(f32[6,22,4,256]{3,2,1,0:T(4,128)} %get-tuple-element.57), channel_id=1, source_target_pairs={{0,1},{1,2},{2,3},{3,4},{4,5},{5,6},{6,7},{7,8},{8,9},{9,10},{10,1... | collective-permute-start | bytes 1622024 | tf_op jit(solution)/shard_map/ppermute | solution.py:198
  60.3 39.3 %collective-permute-start.7 = (f32[6,22,4,256]{3,2,1,0:T(4,128)}, f32[6,22,4,256]{3,2,1,0:T(4,128)}, u32[]{:S(2)}, u32[]{:S(2)}) collective-permute-start(f32[6,22,4,256]{3,2,1,0:T(4,128)} %get-tuple-element.58), channel_id=1, source_target_pairs={{1,0},{2,1},{3,2},{4,3},{5,4},{6,5},{7,6},{8,7},{9,8},{10,9},{11,1... | collective-permute-start | bytes 1622024 | tf_op jit(solution)/shard_map/ppermute | solution.py:201

commit v20 on v19

--- a/solution.py
+++ b/solution.py
@@ -139,13 +139,14 @@
 
     def sweep(src, dst, weight, i):
         c, diag = fc[7, i], fc[6, i]
+        inv = 1.0 / diag
         for k in range(3):
             u = src[k, i]
             others = (src[k, i + 1], src[k, i - 1]) + _rolls(u)
             result = diag * u
             for f, other in enumerate(others):
                 result = result - fc[f, i] * other
-            new = u + weight * (ub_ref[3 + k, i] - result) / diag
+            new = u + weight * (ub_ref[3 + k, i] - result) * inv
             dst[k, i] = jnp.where(c > 0, new, 0.0)
 
     def first(i, carry):

time: 128 us -> 128 us (level)
  no operation moved by 1% of the time
where the time goes in v20:
time: 128 us
  blocking collectives  35.8 us (28%)
  other arithmetic  25.6 us (20%)
  starting transfers between devices  24.3 us (19%)
  Pallas kernels  17.2 us (13%)
  waiting for transfers between devices  14 us (11%)
  local copies, waits for them, and re-layouts  9.36 us (7%)
    all_to_all x1, blocking collectives, on_device(): lax.all_to_all(coarse, 'gy', split_axis=1, concat_axis=2, tiled=True)  21.3 us
    all_to_all x1, blocking collectives, on_device(): lax.all_to_all(energy, 'gy', split_axis=2, concat_axis=1, tiled=True)  14.5 us
    ppermute x4, starting transfers between devices, padded_2(): lax.ppermute(lax.slice_in_dim(block, 0, width, axis=dim), axis, backward)  14.3 us
    sub x4, other arithmetic, advance(): chem = conc_pad - order_pad * order_pad * (3.0 - 2.0 * order_pad)  13.5 us
    ppermute x4, waiting for transfers between devices, padded_2(): lax.ppermute(lax.slice_in_dim(block, block.shape[dim] - width, None, axis...  12.3 us
    pallas_call x1, Pallas kernels, halo_exchange(): pl.pallas_call(functools.partial(halo_kernel, hx, nx, ny), out_shape=jax....  11.3 us
    ppermute x4, starting transfers between devices, padded_2(): lax.ppermute(lax.slice_in_dim(block, block.shape[dim] - width, None, axis...  10 us
    pallas_call x1, Pallas kernels, mechanics(): pl.pallas_call(functools.partial(mech_kernel, zoff), out_shape=(jax.Shape...  5.89 us
  transfers between devices with their start and end apart: 8, of which 3 were waited for; matrix products, arithmetic and copies ran while one was open for 4% of the time, Pallas kernels for 9%

profile of v20, /device:TPU:2, one launch (start us, length us, event | category | flops | bytes accessed | tf_op | source)
XLA Modules:
  0.0 127.7 jit_solution(13716255474716716143)
XLA Ops:
  0.7 1.6 %add_bitcast_fusion = f32[1,32,32,256]{3,2,1,0:T(8,128)S(1)} fusion(s32[32,32,256]{2,1,0:T(8,128)} %param.8), kind=kLoop, calls=%fused_computation.110 | loop fusion | flops 2097152 | bytes 2097152 | tf_op jit(solution)/shard_map/stack | solution.py:289
  2.3 0.2 copy-done.1
  2.5 0.1 pad_maximum_fusion.7
  2.6 2.1 %collective-permute-start = (f32[3,4,32,256]{3,2,1,0:T(8,128)S(1)}, f32[3,4,32,256]{3,2,1,0:T(8,128)S(1)}, u32[]{:S(2)}, u32[]{:S(2)}) collective-permute-start(f32[3,4,32,256]{3,2,1,0:T(8,128)S(1)} %get-tuple-element.53), channel_id=1, source_target_pairs={{0,16},{16,32},{32,48},{48,64},{64,80},{80,96},{96,112},{112,128},... | collective-permute-start | bytes 1179656 | tf_op jit(solution)/shard_map/ppermute | solution.py:199
  4.6 5.8 %collective-permute-start.1 = (f32[3,4,32,256]{3,2,1,0:T(8,128)S(1)}, f32[3,4,32,256]{3,2,1,0:T(8,128)S(1)}, u32[]{:S(2)}, u32[]{:S(2)}) collective-permute-start(f32[3,4,32,256]{3,2,1,0:T(8,128)S(1)} %get-tuple-element.54), channel_id=1, source_target_pairs={{16,0},{32,16},{48,32},{64,48},{80,64},{96,80},{112,96},{128,112},... | collective-permute-start | bytes 1179656 | tf_op jit(solution)/shard_map/ppermute | solution.py:202
  10.4 0.1 pad_maximum_fusion.4
  10.5 3.4 %collective-permute-done = f32[3,4,32,256]{3,2,1,0:T(8,128)S(1)} collective-permute-done((f32[3,4,32,256]{3,2,1,0:T(8,128)S(1)}, f32[3,4,32,256]{3,2,1,0:T(8,128)S(1)}, u32[]{:S(2)}, u32[]{:S(2)}) %collective-permute-start) | collective-permute-done | bytes 393248 | tf_op jit(solution)/shard_map/ppermute | solution.py:199
  13.9 1.8 %collective-permute-done.1 = f32[3,4,32,256]{3,2,1,0:T(8,128)S(1)} collective-permute-done((f32[3,4,32,256]{3,2,1,0:T(8,128)S(1)}, f32[3,4,32,256]{3,2,1,0:T(8,128)S(1)}, u32[]{:S(2)}, u32[]{:S(2)}) %collective-permute-start.1) | collective-permute-done | bytes 393248 | tf_op jit(solution)/shard_map/ppermute | solution.py:202
  15.7 0.4 pad_maximum_fusion.1
  16.1 0.2 fusion.65
  16.2 3.9 %collective-permute-start.2 = (f32[3,40,4,256]{3,2,1,0:T(4,128)S(1)}, f32[3,40,4,256]{3,2,1,0:T(4,128)S(1)}, u32[]{:S(2)}, u32[]{:S(2)}) collective-permute-start(f32[3,40,4,256]{3,2,1,0:T(4,128)S(1)} %get-tuple-element.51), channel_id=1, source_target_pairs={{0,1},{1,2},{2,3},{3,4},{4,5},{5,6},{6,7},{7,8},{8,9},{9,10},{10,1... | collective-permute-start | bytes 1474568 | tf_op jit(solution)/shard_map/ppermute | solution.py:199
  20.1 1.3 %collective-permute-start.3 = (f32[3,40,4,256]{3,2,1,0:T(4,128)S(1)}, f32[3,40,4,256]{3,2,1,0:T(4,128)S(1)}, u32[]{:S(2)}, u32[]{:S(2)}) collective-permute-start(f32[3,40,4,256]{3,2,1,0:T(4,128)S(1)} %get-tuple-element.52), channel_id=1, source_target_pairs={{1,0},{2,1},{3,2},{4,3},{5,4},{6,5},{7,6},{8,7},{9,8},{10,9},{11,1... | collective-permute-start | bytes 1474568 | tf_op jit(solution)/shard_map/ppermute | solution.py:202
  21.4 1.9 %collective-permute-start.4 = (f32[6,3,8,256]{3,2,1,0:T(8,128)S(1)}, f32[6,3,8,256]{3,2,1,0:T(8,128)S(1)}, u32[]{:S(2)}, u32[]{:S(2)}) collective-permute-start(f32[6,3,8,256]{3,2,1,0:T(8,128)S(1)} %get-tuple-element.59), channel_id=1, source_target_pairs={{0,16},{16,32},{32,48},{48,64},{64,80},{80,96},{96,112},{112,128},... | collective-permute-start | bytes 442376 | tf_op jit(solution)/shard_map/ppermute | solution.py:199
  23.4 5.8 %collective-permute-start.5 = (f32[6,3,8,256]{3,2,1,0:T(8,128)S(1)}, f32[6,3,8,256]{3,2,1,0:T(8,128)S(1)}, u32[]{:S(2)}, u32[]{:S(2)}) collective-permute-start(f32[6,3,8,256]{3,2,1,0:T(8,128)S(1)} %get-tuple-element.60), channel_id=1, source_target_pairs={{16,0},{32,16},{48,32},{64,48},{80,64},{96,80},{112,96},{128,112},... | collective-permute-start | bytes 442376 | tf_op jit(solution)/shard_map/ppermute | solution.py:202
  29.1 8.8 %collective-permute-done.4 = f32[6,3,8,256]{3,2,1,0:T(8,128)S(1)} collective-permute-done((f32[6,3,8,256]{3,2,1,0:T(8,128)S(1)}, f32[6,3,8,256]{3,2,1,0:T(8,128)S(1)}, u32[]{:S(2)}, u32[]{:S(2)}) %collective-permute-start.4) | collective-permute-done | bytes 147488 | tf_op jit(solution)/shard_map/ppermute | solution.py:199
  38.0 0.1 pad_maximum_fusion.3
  38.1 0.9 pad_maximum_fusion
  39.0 0.1 fusion.57
  39.1 0.2 slice_bitcast_fusion.1
  39.3 0.3 multiply_subtract_fusion
  39.6 4.6 %multiply_subtract_fusion.1 = (f32[38,38,256]{2,1,0:T(8,128)S(1)}, f32[38,38,256]{2,1,0:T(8,128)S(1)}, f32[38,38,256]{2,1,0:T(8,128)S(1)}) fusion(f32[40,40,256]{2,1,0:T(8,128)S(1)} %multiply_subtract_fusion, f32[40,40,256]{2,1,0:T(8,128)S(1)} %get-tuple-element.50, bf16[40,40,256]{2,1,0:T(8,128)(2,1)S(1)} %fusion.57, f32[40,40,256]{2,1,0:T(8,128)S(1)} %get-tuple-element.49), kind=kLoop, calls=%fused_computation.43 | loop fusion | flops 13677568 | bytes 25612288 | tf_op jit(solution)/shard_map/sub | solution.py:217
  44.2 4.5 %multiply_subtract_fusion.2 = (f32[36,36,256]{2,1,0:T(8,128)S(1)}, f32[36,36,256]{2,1,0:T(8,128)S(1)}, f32[36,36,256]{2,1,0:T(8,128)S(1)}) fusion(f32[38,38,256]{2,1,0:T(8,128)S(1)} %get-tuple-element.46, f32[38,38,256]{2,1,0:T(8,128)S(1)} %get-tuple-element.47, bf16[40,40,256]{2,1,0:T(8,128)(2,1)S(1)} %fusion.57, f32[38,38,256]{2,1,0:T(8,128)S(1)} %get-tuple-element.48), kind=kLoop, calls=%fused_computation.64 | loop fusion | flops 12275712 | bytes 24051712 | tf_op jit(solution)/shard_map/sub | solution.py:217
  48.7 4.2 %multiply_subtract_fusion.3 = (f32[34,34,256]{2,1,0:T(8,128)S(1)}, f32[34,34,256]{2,1,0:T(8,128)S(1)}, f32[34,34,256]{2,1,0:T(8,128)S(1)}) fusion(f32[36,36,256]{2,1,0:T(8,128)S(1)} %get-tuple-element.43, f32[36,36,256]{2,1,0:T(8,128)S(1)} %get-tuple-element.44, bf16[40,40,256]{2,1,0:T(8,128)(2,1)S(1)} %fusion.57, f32[36,36,256]{2,1,0:T(8,128)S(1)} %get-tuple-element.45), kind=kLoop, calls=%fused_computation.85 | loop fusion | flops 10949632 | bytes 22515712 | tf_op jit(solution)/shard_map/sub | solution.py:217
  52.9 3.9 %fusion.56 = (f32[32,32,256]{2,1,0:T(8,128)S(1)}, f32[32,32,256]{2,1,0:T(8,128)}) fusion(f32[34,34,256]{2,1,0:T(8,128)S(1)} %get-tuple-element.41, f32[34,34,256]{2,1,0:T(8,128)S(1)} %get-tuple-element.40, bf16[40,40,256]{2,1,0:T(8,128)(2,1)S(1)} %fusion.57, f32[34,34,256]{2,1,0:T(8,128)S(1)} %get-tuple-element.42), kind=kLoop, calls=%fused_computation.102 | loop fusion | flops 7864320 | bytes 16941056 | tf_op jit(solution)/shard_map/add | solution.py:225
  56.7 1.3 %fusion.66 = (f32[6,22,4,256]{3,2,1,0:T(4,128)}, f32[6,22,4,256]{3,2,1,0:T(4,128)}) fusion(f32[6,22,8,256]{3,2,1,0:T(8,128)S(1)} %pad_maximum_fusion.3), kind=kLoop, calls=%fused_computation.119 | loop fusion | bytes 2162688 | tf_op jit(solution)/shard_map/slice | solution.py:200
  58.0 2.2 %collective-permute-start.6 = (f32[6,22,4,256]{3,2,1,0:T(4,128)}, f32[6,22,4,256]{3,2,1,0:T(4,128)}, u32[]{:S(2)}, u32[]{:S(2)}) collective-permute-start(f32[6,22,4,256]{3,2,1,0:T(4,128)} %get-tuple-element.57), channel_id=1, source_target_pairs={{0,1},{1,2},{2,3},{3,4},{4,5},{5,6},{6,7},{7,8},{8,9},{9,10},{10,1... | collective-permute-start | bytes 1622024 | tf_op jit(solution)/shard_map/ppermute | solution.py:199
  60.3 1.5 %collective-permute-start.7 = (f32[6,22,4,256]{3,2,1,0:T(4,128)}, f32[6,22,4,256]{3,2,1,0:T(4,128)}, u32[]{:S(2)}, u32[]{:S(2)}) collective-permute-start(f32[6,22,4,256]{3,2,1,0:T(4,128)} %get-tuple-element.58), channel_id=1, source_target_pairs={{1,0},{2,1},{3,2},{4,3},{5,4},{6,5},{7,6},{8,7},{9,8},{10,9},{11,1... | collective-permute-start | bytes 1622024 | tf_op jit(solution)/shard_map/ppermute | solution.py:202
  61.7 0.1 bitcast_reduce_fusion
  61.8 0.3 bitcast_reduce_fusion.1
  62.2 0.5 fusion.43
  62.6 0.5 copy.43
  63.1 0.4 reshape.19
  63.5 21.3 %all_to_all.33 = f32[16,1,2048]{2,1,0:T(1,128)S(1)} all-to-all(f32[16,1,2048]{2,1,0:T(1,128)S(1)} %reshape.19), channel_id=1, replica_groups=mesh['gx'=16,'gy'=16] {'gy'}, dimensions={0} | all-to-all | bytes 262144 | tf_op jit(solution)/shard_map/all_to_all | solution.py:304
  84.8 0.5 broadcast.141
  85.4 0.9 reduce
  86.2 0.4 reshape.20
  86.6 0.6 copy.45
  87.2 1.1 broadcast_in_dim.18.blk_ref
  88.3 11.3 %shard_map.93 = f32[1,22,24,256]{3,2,1,0:T(8,128)} custom-call(f32[1,16,8,256]{3,2,1,0:T(8,128)} %broadcast_in_dim.18.blk_ref), custom_call_target="tpu_custom_call" | custom-call | tf_op jit(solution)/shard_map/pallas_call | solution.py:94
  99.6 3.0 %pad_maximum_fusion.2.ub_ref = f32[6,22,16,256]{3,2,1,0:T(8,128)} fusion(f32[6,22,4,256]{3,2,1,0:T(4,128)} %collective-permute-done.7, f32[6,22,8,256]{3,2,1,0:T(8,128)S(1)} %pad_maximum_fusion.3, f32[6,22,4,256]{3,2,1,0:T(4,128)} %collective-permute-done.6), kind=kLoop, calls=%fused_computation.18 | loop fusion | flops 1081344 | bytes 4325376 | tf_op jit(solution)/shard_map/concatenate | solution.py:203
  102.5 5.9 %shard_map.94 = (f32[3,16,8,256]{3,2,1,0:T(8,128)}, f32[16,8,256]{2,1,0:T(8,128)}) custom-call(f32[22,24,256]{2,1,0:T(8,128)} %bitcast.47, f32[6,22,16,256]{3,2,1,0:T(8,128)} %pad_maximum_fusion.2.ub_ref), custom_call_target="tpu_custom_call" | custom-call | tf_op jit(solution)/shard_map/pallas_call | solution.py:183
  108.4 1.3 %copy.46 = f32[16,8,256]{0,1,2:T(8,128)S(1)} copy(f32[16,8,256]{2,1,0:T(8,128)} %get-tuple-element.15) | data formatting | bytes 262144 | tf_op jit(solution)/shard_map/pallas_call | solution.py:183
  109.7 0.4 reshape.21
  110.1 14.5 %all_to_all.34 = f32[16,1,2048]{2,1,0:T(1,128)S(1)} all-to-all(f32[16,1,2048]{2,1,0:T(1,128)S(1)} %reshape.21), channel_id=1, replica_groups=mesh['gx'=16,'gy'=16] {'gy'}, dimensions={0} | all-to-all | bytes 262144 | tf_op jit(solution)/shard_map/all_to_all | solution.py:308
  124.6 0.9 reduce.1
  125.5 0.4 reshape.22
  125.8 0.9 copy.47
  126.8 1.0 copy.48
  (17 shorter events, 0.1 us)
Async XLA Ops:
  0.6 1.7 %copy-start.2 = (f32[32,32,256]{2,1,0:T(8,128)S(1)}, f32[32,32,256]{2,1,0:T(8,128)}, u32[]{:S(2)}) copy-start(f32[32,32,256]{2,1,0:T(8,128)} %param.6) | copy-start | bytes 3145732
  0.6 1.8 %copy-start.1 = (f32[32,32,256]{2,1,0:T(8,128)S(1)}, f32[32,32,256]{2,1,0:T(8,128)}, u32[]{:S(2)}) copy-start(f32[32,32,256]{2,1,0:T(8,128)} %param.7) | copy-start | bytes 3145732
  2.5 7.9 %copy-start.3 = (f32[3,16,8,256]{3,2,1,0:T(8,128)S(1)}, f32[3,16,8,256]{3,2,1,0:T(8,128)}, u32[]{:S(2)}) copy-start(f32[3,16,8,256]{3,2,1,0:T(8,128)} %param.10) | copy-start | bytes 1179652
  2.5 7.9 %copy-start.4 = (f32[3,16,8,256]{3,2,1,0:T(8,128)S(1)}, f32[3,16,8,256]{3,2,1,0:T(8,128)}, u32[]{:S(2)}) copy-start(f32[3,16,8,256]{3,2,1,0:T(8,128)} %param.9) | copy-start | bytes 1179652
  2.6 11.3 %collective-permute-start = (f32[3,4,32,256]{3,2,1,0:T(8,128)S(1)}, f32[3,4,32,256]{3,2,1,0:T(8,128)S(1)}, u32[]{:S(2)}, u32[]{:S(2)}) collective-permute-start(f32[3,4,32,256]{3,2,1,0:T(8,128)S(1)} %get-tuple-element.53), channel_id=1, source_target_pairs={{0,16},{16,32},{32,48},{48,64},{64,80},{80,96},{96,112},{112,128},... | collective-permute-start | bytes 1179656 | tf_op jit(solution)/shard_map/ppermute | solution.py:199
  4.6 11.0 %collective-permute-start.1 = (f32[3,4,32,256]{3,2,1,0:T(8,128)S(1)}, f32[3,4,32,256]{3,2,1,0:T(8,128)S(1)}, u32[]{:S(2)}, u32[]{:S(2)}) collective-permute-start(f32[3,4,32,256]{3,2,1,0:T(8,128)S(1)} %get-tuple-element.54), channel_id=1, source_target_pairs={{16,0},{32,16},{48,32},{64,48},{80,64},{96,80},{112,96},{128,112},... | collective-permute-start | bytes 1179656 | tf_op jit(solution)/shard_map/ppermute | solution.py:202
  16.2 21.8 %collective-permute-start.2 = (f32[3,40,4,256]{3,2,1,0:T(4,128)S(1)}, f32[3,40,4,256]{3,2,1,0:T(4,128)S(1)}, u32[]{:S(2)}, u32[]{:S(2)}) collective-permute-start(f32[3,40,4,256]{3,2,1,0:T(4,128)S(1)} %get-tuple-element.51), channel_id=1, source_target_pairs={{0,1},{1,2},{2,3},{3,4},{4,5},{5,6},{6,7},{7,8},{8,9},{9,10},{10,1... | collective-permute-start | bytes 1474568 | tf_op jit(solution)/shard_map/ppermute | solution.py:199
  20.1 18.0 %collective-permute-start.3 = (f32[3,40,4,256]{3,2,1,0:T(4,128)S(1)}, f32[3,40,4,256]{3,2,1,0:T(4,128)S(1)}, u32[]{:S(2)}, u32[]{:S(2)}) collective-permute-start(f32[3,40,4,256]{3,2,1,0:T(4,128)S(1)} %get-tuple-element.52), channel_id=1, source_target_pairs={{1,0},{2,1},{3,2},{4,3},{5,4},{6,5},{7,6},{8,7},{9,8},{10,9},{11,1... | collective-permute-start | bytes 1474568 | tf_op jit(solution)/shard_map/ppermute | solution.py:202
  21.4 16.5 %collective-permute-start.4 = (f32[6,3,8,256]{3,2,1,0:T(8,128)S(1)}, f32[6,3,8,256]{3,2,1,0:T(8,128)S(1)}, u32[]{:S(2)}, u32[]{:S(2)}) collective-permute-start(f32[6,3,8,256]{3,2,1,0:T(8,128)S(1)} %get-tuple-element.59), channel_id=1, source_target_pairs={{0,16},{16,32},{32,48},{48,64},{64,80},{80,96},{96,112},{112,128},... | collective-permute-start | bytes 442376 | tf_op jit(solution)/shard_map/ppermute | solution.py:199
  23.4 14.6 %collective-permute-start.5 = (f32[6,3,8,256]{3,2,1,0:T(8,128)S(1)}, f32[6,3,8,256]{3,2,1,0:T(8,128)S(1)}, u32[]{:S(2)}, u32[]{:S(2)}) collective-permute-start(f32[6,3,8,256]{3,2,1,0:T(8,128)S(1)} %get-tuple-element.60), channel_id=1, source_target_pairs={{16,0},{32,16},{48,32},{64,48},{80,64},{96,80},{112,96},{128,112},... | collective-permute-start | bytes 442376 | tf_op jit(solution)/shard_map/ppermute | solution.py:202
  56.7 5.1 %copy-start = (f32[32,32,256]{2,1,0:T(8,128)}, f32[32,32,256]{2,1,0:T(8,128)S(1)}, u32[]{:S(2)}) copy-start(f32[32,32,256]{2,1,0:T(8,128)S(1)} %get-tuple-element.37) | copy-start | bytes 3145732
  58.0 4.1 %copy-start.5 = (f32[256,128,1]{1,0,2:T(8,128)S(1)}, f32[256,128,1]{1,0,2:T(8,128)}, u32[]{:S(2)}) copy-start(f32[256,128,1]{1,0,2:T(8,128)} %constant.74) | copy-start | bytes 393220
  58.0 41.5 %collective-permute-start.6 = (f32[6,22,4,256]{3,2,1,0:T(4,128)}, f32[6,22,4,256]{3,2,1,0:T(4,128)}, u32[]{:S(2)}, u32[]{:S(2)}) collective-permute-start(f32[6,22,4,256]{3,2,1,0:T(4,128)} %get-tuple-element.57), channel_id=1, source_target_pairs={{0,1},{1,2},{2,3},{3,4},{4,5},{5,6},{6,7},{7,8},{8,9},{9,10},{10,1... | collective-permute-start | bytes 1622024 | tf_op jit(solution)/shard_map/ppermute | solution.py:199
  60.3 39.3 %collective-permute-start.7 = (f32[6,22,4,256]{3,2,1,0:T(4,128)}, f32[6,22,4,256]{3,2,1,0:T(4,128)}, u32[]{:S(2)}, u32[]{:S(2)}) collective-permute-start(f32[6,22,4,256]{3,2,1,0:T(4,128)} %get-tuple-element.58), channel_id=1, source_target_pairs={{1,0},{2,1},{3,2},{4,3},{5,4},{6,5},{7,6},{8,7},{9,8},{10,9},{11,1... | collective-permute-start | bytes 1622024 | tf_op jit(solution)/shard_map/ppermute | solution.py:202
